TPU v7x, 32 devices: a whole 2x2x4 slice. The times are simulated.
32 devices in a mesh: dp: 4 (over y, x), space: 8 (over z, core).
Axes of the slice: x: 2, y: 2, z: 4, core: 2. Of those that a mesh axis runs over, the one named last changes fastest.
Arguments:
- latent: bfloat16 [4, 32, 512, 320], P('dp', 'space'), may hold values from -40 to 40
- timesteps: int32 [4], P('dp'), may hold values from 0 to 999
- norm_gain: float32 [320], replicated, may hold values from 0.1 to 1.9
- norm_bias: float32 [320], replicated, may hold values from -3 to 3
- conv_weight: bfloat16 [3, 3, 320, 320], replicated, may hold values from -0.109375 to 0.109375
- conv_bias: float32 [320], replicated, may hold values from -3 to 3
- time_weight: bfloat16 [320, 320], replicated, may hold values from -0.5 to 0.5
- cotangent: bfloat16 [4, 32, 512, 320], P('dp', 'space'), may hold values from -40 to 40
Outputs:
- block_out: bfloat16 [4, 32, 512, 320], P('dp', 'space')
- latent_grad: bfloat16 [4, 32, 512, 320], P('dp', 'space')
- weight_grad: float32 [3, 3, 320, 320], replicated
- time_grad: float32 [320, 320], replicated
All inputs are finite; a program needn't handle non-finite values.
Results may differ from a plain program's by a relative error of at most 0.001.
The roundings to bfloat16 on the way count: a program that leaves them out, or rounds other values in their place, can miss the bound.
Values may be sent and summed in bfloat16 or wider, within the bound.
No kernel may reach another device: no remote copies, remote signals or barrier semaphores. Data moves between devices by JAX's collectives and lax.ppermute only.
A program may use at most 128 MiB of HBM per device.

v0:
```python
import functools
import math

import jax
import jax.numpy as jnp
from jax import lax
from jax.experimental import pallas as pl
from jax.experimental.pallas import tpu as pltpu
from jax.sharding import PartitionSpec as P


GROUPS = 32
epsilon = 1e-05
f32 = jnp.float32
bf16 = jnp.bfloat16
f16 = jnp.float16
HIGHEST = lax.Precision.HIGHEST
LANES = 128


def contract(a, b, dims, precision=None):
    return lax.dot_general(a, b, (dims, ((), ())), preferred_element_type=f32, precision=precision)


def call(body, outs, args, specs=None, scratch=(), flops=0, moved=0, limit=40 << 20):
    vmem = pl.BlockSpec(memory_space=pltpu.VMEM)
    many = isinstance(outs, (list, tuple))
    return pl.pallas_call(
        body,
        out_shape=tuple(outs) if many else outs,
        in_specs=list(specs) if specs else [vmem] * len(args),
        out_specs=tuple([vmem] * len(outs)) if many else vmem,
        scratch_shapes=list(scratch),
        compiler_params=pltpu.CompilerParams(vmem_limit_bytes=limit),
        cost_estimate=pl.CostEstimate(flops=flops, bytes_accessed=moved, transcendentals=0),
    )(*args)


def member_matrix(channels):
    per_group = channels // GROUPS
    row = lax.broadcasted_iota(jnp.int32, (channels, channels), 0).astype(f32)
    col = lax.broadcasted_iota(jnp.int32, (channels, channels), 1).astype(f32)
    same = jnp.floor((row + 0.5) / per_group) == jnp.floor((col + 0.5) / per_group)
    return jnp.where(same, 1.0, 0.0).astype(f32)


def lane_form(cells):
    ones = jnp.ones((8, cells.shape[1]), f32)
    return contract(ones, cells, ((1,), (1,)), HIGHEST)


def rows_of(*rows):
    height = lax.broadcasted_iota(jnp.int32, rows[0].shape, 0)
    packed = jnp.zeros(rows[0].shape, f32)
    for number, row in enumerate(rows):
        packed = jnp.where(height == number, row, packed)
    return packed


def fold_lanes(cells):
    total = cells[:, :LANES]
    for start in range(LANES, cells.shape[1], LANES):
        total = total + cells[:, start : start + LANES]
    return total


def stats_body(count, step_ref, latent_ref, cot_ref, out_ref):
    row_count, channels, cols = latent_ref.shape
    member = member_matrix(channels)
    ones = jnp.ones((cols, LANES), bf16)
    tall = jnp.ones((8, cols), bf16)
    sums = jnp.zeros((channels, LANES), f32)
    grads = jnp.zeros((8, channels), f32)
    top = jnp.zeros((channels, LANES), f32)
    for row in range(row_count):
        sums = sums + contract(latent_ref[row], ones, ((1,), (0,)))
        grads = grads + contract(tall, cot_ref[row], ((1,), (1,)))
        size = jnp.abs(cot_ref[row].astype(f32))
        for start in range(0, cols, LANES):
            top = jnp.maximum(top, size[:, start : start + LANES])
    mean = contract(member, sums, ((1,), (0,)), HIGHEST) / count
    squares = jnp.zeros((channels, LANES), f32)
    for row in range(row_count):
        centered = latent_ref[row].astype(f32) - mean[:, :1]
        squares = squares + fold_lanes(centered * centered)
    grouped = contract(member, squares, ((1,), (0,)), HIGHEST)
    step = jnp.full((8, channels), step_ref[0].astype(f32))
    largest = jnp.broadcast_to(jnp.max(top), (8, channels))
    out_ref[...] = rows_of(
        lane_form(mean) * (1.0 / LANES), lane_form(grouped), grads, largest, step
    )


def tree_sum(parts):
    while len(parts) > 1:
        parts = [parts[i] + parts[i + 1] for i in range(0, len(parts), 2)]
    return parts[0]


def merge_body(count, total, *refs):
    out_ref = refs[-1]
    parts = [ref[...] for ref in refs[:-1]]
    mean = tree_sum([part[0:1] for part in parts]) / len(parts)
    squares = tree_sum([part[1:2] + count * (part[0:1] - mean) ** 2 for part in parts])
    grads = tree_sum([part[2:3] for part in parts])
    largest = functools.reduce(jnp.maximum, [part[3:4] for part in parts])
    if total:
        squares = lax.rsqrt(squares / total + epsilon)
    shape = parts[0].shape
    out_ref[...] = rows_of(
        *[
            jnp.broadcast_to(row, shape)
            for row in (mean, squares, grads, largest, parts[0][4:5])
        ]
    )


def column_values(stats_ref, gain_ref, bias_ref):
    channels = gain_ref.shape[1]
    shape = (8, channels)
    table = rows_of(
        jnp.broadcast_to(stats_ref[0:1], shape),
        jnp.broadcast_to(stats_ref[1:2], shape),
        jnp.broadcast_to(gain_ref[...], shape),
        jnp.broadcast_to(bias_ref[...], shape),
    ).T
    return [table[:, i : i + 1] for i in range(4)]


def normalized(cells, values):
    mean, inverse, gain, bias = values
    normed = (cells.astype(f32) - mean) * inverse
    shifted = normed * gain + bias
    return normed, shifted, jax.nn.sigmoid(shifted)


def activate(cells, values):
    _, shifted, sigmoid = normalized(cells, values)
    return (shifted * sigmoid).astype(bf16)


def shifted_cols(cells):
    cols = cells.shape[1]
    lane = lax.broadcasted_iota(jnp.int32, cells.shape, 1)
    zero = jnp.zeros_like(cells)
    after = jnp.where(lane == cols - 1, zero, pltpu.roll(cells, cols - 1, 1))
    before = jnp.where(lane == 0, zero, pltpu.roll(cells, 1, 1))
    return after, before


def put_taps(buffer_ref, place, cells, flip):
    channels, cols = cells.shape
    wide = cells.astype(f32)
    after, before = shifted_cols(wide)
    order = (after, cells, before) if flip else (before, cells, after)
    for tap, piece in enumerate(order):
        buffer_ref[tap * channels : (tap + 1) * channels, place * cols : (place + 1) * cols] = (
            piece.astype(bf16)
        )


def put_gradient(taps_ref, cot_ref, above_ref, below_ref):
    row_count = cot_ref.shape[0]
    put_taps(taps_ref, 0, above_ref[...], True)
    for row in range(row_count):
        put_taps(taps_ref, row + 1, cot_ref[row], True)
    put_taps(taps_ref, row_count + 1, below_ref[...], True)


def weight_body(
    shape, where_ref, latent_ref, cot_ref, above_ref, below_ref, stats_ref, gain_ref, bias_ref,
    act_ref, near_ref, far_ref, taps_ref,
):
    blocks, zones, height, width = shape
    row_count, channels, cols = latent_ref.shape
    core, mine, other, zone_index = [where_ref[i] for i in range(4)]
    values = column_values(stats_ref, gain_ref, bias_ref)
    for row in range(row_count):
        act_ref[:, row * cols : (row + 1) * cols] = activate(latent_ref[row], values)
    put_gradient(taps_ref, cot_ref, above_ref, below_ref)
    tap_width = zones * width // 3

    def store(ref, place, found, block, tap_row):
        first = block * height
        size = max(min(height, channels - first), 0)
        for zone in range(zones):
            low = max(zone * width, tap_row * tap_width)
            high = min((zone + 1) * width, (tap_row + 1) * tap_width)
            if low >= high:
                continue
            at = zone_index ^ zone
            left, right = low - zone * width, high - zone * width
            source = low - tap_row * tap_width
            used = max(min(right - left, 3 * channels - source), 0)
            if size and used:
                ref[place, at, :size, left : left + used] = found[
                    first : first + size, source : source + used
                ]
            if used < right - left:
                ref[place, at, :, left + used : right] = jnp.zeros(
                    (height, right - left - used), f32
                )
            if size < height and used:
                ref[place, at, size:, left : left + used] = jnp.zeros((height - size, used), f32)

    for tap_row in range(3):
        start = (2 - tap_row) * cols
        found = contract(
            act_ref[...], taps_ref[:, start : start + row_count * cols], ((1,), (1,))
        )
        for half in range(2):

            @pl.when(core == half)
            def _():
                for rest in range(blocks // 2):
                    store(near_ref, mine ^ rest, found, half * blocks // 2 + rest, tap_row)

            @pl.when(core != half)
            def _():
                for rest in range(blocks // 2):
                    store(far_ref, other ^ rest, found, half * blocks // 2 + rest, tap_row)


def conv_body(
    ends_ref, act_ref, latent_ref, above_ref, below_ref, stats_ref, gain_ref, bias_ref,
    weight_ref, extra_ref, out_ref, taps_ref, flat_ref,
):
    row_count, channels, cols = latent_ref.shape
    values = column_values(stats_ref, gain_ref, bias_ref)
    for place, ref, end in ((0, above_ref, 0), (row_count + 1, below_ref, 1)):
        keep = ends_ref[end].astype(f32)
        put_taps(taps_ref, place, (activate(ref[...], values).astype(f32) * keep).astype(bf16), False)
    for row in range(row_count):
        put_taps(taps_ref, row + 1, act_ref[:, row * cols : (row + 1) * cols], False)
    for tap_row in range(3):
        flat_ref[tap_row] = weight_ref[tap_row].reshape(3 * channels, channels).T
    extra = jnp.broadcast_to(extra_ref[...], (8, channels)).T[:, :1]
    for row in range(row_count):
        total = latent_ref[row].astype(f32) + extra
        for tap_row in range(3):
            start = (row + tap_row) * cols
            total = total + contract(
                flat_ref[tap_row], taps_ref[:, start : start + cols], ((1,), (0,))
            )
        out_ref[row] = total.astype(bf16)


def backward_body(
    latent_ref, cot_ref, above_ref, below_ref, stats_ref, gain_ref, bias_ref, weight_ref,
    grad_ref, sums_ref, taps_ref, flat_ref,
):
    row_count, channels, cols = latent_ref.shape
    values = column_values(stats_ref, gain_ref, bias_ref)
    put_gradient(taps_ref, cot_ref, above_ref, below_ref)
    for tap_row in range(3):
        flat_ref[tap_row] = jnp.concatenate([weight_ref[tap_row, j] for j in range(3)], axis=1)
    first = jnp.zeros((channels, LANES), f32)
    second = jnp.zeros((channels, LANES), f32)
    for row in range(row_count):
        total = jnp.zeros((channels, cols), f32)
        for tap_row in range(3):
            start = (row + 2 - tap_row) * cols
            total = total + contract(
                flat_ref[tap_row], taps_ref[:, start : start + cols], ((1,), (0,))
            )
        normed, shifted, sigmoid = normalized(latent_ref[row], values)
        grad = total * sigmoid * (1.0 + shifted * (1.0 - sigmoid)) * values[2]
        grad_ref[row] = grad
        first = first + fold_lanes(grad)
        second = second + fold_lanes(grad * normed)
    member = member_matrix(channels)
    first = contract(member, first, ((1,), (0,)), HIGHEST)
    second = contract(member, second, ((1,), (0,)), HIGHEST)
    sums_ref[...] = rows_of(lane_form(first), lane_form(second))


def latent_body(
    total, parts, grad_ref, latent_ref, cot_ref, stats_ref, *refs,
):
    out_ref = refs[-1]
    row_count, channels, _ = latent_ref.shape
    sums = tree_sum([ref[...] for ref in refs[:parts]]) / total
    shape = (8, channels)
    table = rows_of(
        *[
            jnp.broadcast_to(row, shape)
            for row in (stats_ref[0:1], stats_ref[1:2], sums[0:1], sums[1:2])
        ]
    ).T
    mean, inverse, first, second = [table[:, i : i + 1] for i in range(4)]
    for row in range(row_count):
        normed = (latent_ref[row].astype(f32) - mean) * inverse
        change = inverse * (grad_ref[row] - first - normed * second)
        out_ref[row] = (cot_ref[row].astype(f32) + change).astype(bf16)


def place_body(shape, places_ref, cells_ref, *refs):
    blocks, zones, height, width = shape
    out_ref, flat_ref, rows_ref, sem = refs[-4:]
    channels = out_ref.shape[1]
    for block in range(blocks):
        top = pl.multiple_of(places_ref[block] * height, 8)
        for zone in range(zones):
            left = pl.multiple_of(places_ref[blocks + zone] * width, LANES)
            flat_ref[pl.ds(top, height), pl.ds(left, width)] = cells_ref[block, zone]
    tap_width = zones * width // 3
    half = places_ref[blocks + zones]
    first = blocks * height
    sizes = (min(first, channels), channels - min(first, channels))
    for tap in range(9):
        left = (tap // 3) * tap_width + (tap % 3) * channels
        rows_ref[tap] = flat_ref[:, left : left + channels]
        for index in range(2):

            @pl.when(half == index)
            def _():
                pltpu.make_async_copy(
                    rows_ref.at[tap, pl.ds(0, sizes[index])],
                    out_ref.at[tap, pl.ds(index * first, sizes[index])],
                    sem,
                ).start()

    for tap in range(9):
        for index in range(2):

            @pl.when(half == index)
            def _():
                pltpu.make_async_copy(
                    rows_ref.at[tap, pl.ds(0, sizes[index])],
                    out_ref.at[tap, pl.ds(index * first, sizes[index])],
                    sem,
                ).wait()


def scale_body(factor, spread, gain_ref, bias_ref, *refs):
    parts, (scale_ref, steps_ref) = refs[:-2], refs[-2:]
    largest = functools.reduce(jnp.maximum, [ref[3:4] for ref in parts])
    top = jnp.max(largest, axis=1, keepdims=True)
    reach = spread * jnp.max(jnp.abs(gain_ref[...]), axis=1, keepdims=True) + jnp.max(
        jnp.abs(bias_ref[...]), axis=1, keepdims=True
    )
    bound = jnp.maximum(top * reach * factor, 1e-30)
    power = jnp.clip(jnp.floor(jnp.log2(30000.0 / bound)), -100.0, 100.0)
    shape = scale_ref.shape
    scale = jnp.broadcast_to(jnp.exp2(power), shape)
    scale_ref[...] = rows_of(scale, 1.0 / scale)
    steps_ref[...] = rows_of(*[jnp.broadcast_to(ref[4:5], steps_ref.shape) for ref in parts])


def time_body(embed_ref, *refs):
    out_ref = refs[-1]
    columns = embed_ref[...].T
    terms = [
        columns[:, image : image + 1] * ref[2:3] for image, ref in enumerate(refs[:-1])
    ]
    out_ref[...] = tree_sum(terms)


def swap_space(cells, mask):
    count = lax.axis_size("space")
    return lax.ppermute(cells, "space", [(i, i ^ mask) for i in range(count)])


def swap_image(cells, masks):
    images = lax.axis_size("dp")
    count = lax.axis_size("space")
    pairs = [
        (i * count + j, (i ^ masks[j % 2]) * count + j) for i in range(images) for j in range(count)
    ]
    return lax.ppermute(cells, ("dp", "space"), pairs)


def slab_program(
    latent, timesteps, norm_gain, norm_bias, conv_weight, conv_bias, time_weight, cotangent
):
    images, row_count, col_count, channels = latent.shape
    assert images == 1
    per_group = channels // GROUPS
    image_count = lax.axis_size("dp")
    slab_count = lax.axis_size("space")
    zones = slab_count // 2
    bits = image_count.bit_length() - 1
    blocks = 2 * image_count
    height = -(-channels // (8 * blocks)) * 8
    tap_width = -(-3 * channels // LANES) * LANES
    width = 3 * tap_width // zones
    local_count = row_count * col_count * per_group
    total_count = local_count * slab_count
    positions = row_count * col_count

    image_index = lax.axis_index("dp")
    slab_index = lax.axis_index("space")
    core = slab_index % 2
    zone_index = slab_index // 2

    lat = latent.transpose(0, 1, 3, 2)[0]
    cot = cotangent.transpose(0, 1, 3, 2)[0]
    gain = norm_gain.reshape(1, channels)
    bias = norm_bias.reshape(1, channels)
    smem = pl.BlockSpec(memory_space=pltpu.SMEM)
    vmem = pl.BlockSpec(memory_space=pltpu.VMEM)
    small = jax.ShapeDtypeStruct((8, channels), f32)

    down = [(i, i + 1) for i in range(slab_count - 1)]
    up = [(i + 1, i) for i in range(slab_count - 1)]

    flops = 2 * positions * channels * channels * 9
    taps = pltpu.VMEM((3 * channels, (row_count + 2) * col_count), bf16)
    flat = pltpu.VMEM((3, channels, 3 * channels), bf16)

    edges = [
        lax.ppermute(jnp.stack([cot[row], lat[row]]), "space", way)
        for row, way in ((row_count - 1, down), (0, up))
    ]
    (cot_above, lat_above), (cot_below, lat_below) = edges
    own = call(
        functools.partial(stats_body, local_count),
        small,
        (timesteps, lat, cot),
        specs=(smem, vmem, vmem),
        moved=2 * lat.size * 2,
        flops=positions * channels * 60,
    )
    partner = swap_space(own, 1)
    pair = call(functools.partial(merge_body, local_count, None), small, (own, partner))
    parts = [pair]
    for mask in range(1, zones):
        parts.append(swap_space(pair, 2 * mask))
    stats = call(
        functools.partial(merge_body, 2 * local_count, total_count), small, tuple(parts)
    )

    orders = [list(range(bits)), list(range(bits))[::-1]]

    def rest_index(which):
        index = 0
        for step in range(bits):
            shift = jnp.where(which == 0, orders[0][step], orders[1][step])
            index = index * 2 + ((image_index >> shift) & 1)
        return index

    mine, other = rest_index(core), rest_index(1 - core)
    where = jnp.stack([core, mine, other, zone_index]).astype(jnp.int32)
    share_shape = jax.ShapeDtypeStruct((blocks // 2, zones, height, width), f32)
    act, near, far = call(
        functools.partial(weight_body, (blocks, zones, height, width)),
        (jax.ShapeDtypeStruct((channels, positions), bf16), share_shape, share_shape),
        (where, lat, cot, cot_above, cot_below, stats, gain, bias),
        specs=(smem,) + (vmem,) * 7,
        scratch=(taps,),
        flops=flops,
        moved=8 * lat.size,
    )
    everyone = [stats]
    for mask in range(1, image_count):
        everyone.append(swap_image(stats, (mask, mask)))
    scales, steps = call(
        functools.partial(
            scale_body, float(positions * slab_count * image_count), math.sqrt(per_group)
        ),
        (jax.ShapeDtypeStruct((8, LANES), f32), small),
        (gain, bias, *everyone),
    )
    scale, back = scales[0, 0], scales[1, 0]

    middle = blocks // 4
    far_in = swap_space(far[middle:], 1)
    near_in = swap_space(far[:middle], 1)
    sending = near[middle:] + far_in
    keeping = near[:middle] + near_in
    for step in range(bits):
        masks = (1 << orders[0][step], 1 << orders[1][step])
        arrived = swap_image((sending * scale).astype(f16), masks)
        total = keeping + arrived.astype(f32) * back
        middle = total.shape[0] // 2
        sending, keeping = total[middle:], total[:middle]
    total = keeping[0] if bits == 0 else total[0]
    share = total[0]
    arrivals = []
    for mask in range(1, zones):
        arrivals.append(swap_space((total[mask] * scale).astype(f16), 2 * mask))
    for arrived in arrivals:
        share = share + arrived.astype(f32) * back
    share = (share * scale).astype(f16)
    collected = [share]
    for mask in range(1, zones):
        collected.append(swap_space(share, 2 * mask))
    full = jnp.stack(collected)[None]
    for step in reversed(range(bits)):
        masks = (1 << orders[0][step], 1 << orders[1][step])
        full = jnp.concatenate([full, swap_image(full, masks)])
    crossed = swap_space(full, 1)

    def place(cells, whose, half, before):
        spots = [whose ^ rest for rest in range(blocks // 2)]
        spots += [zone_index ^ mask for mask in range(zones)] + [half]
        spots = jnp.stack(spots).astype(jnp.int32)
        anywhere = pl.BlockSpec(memory_space=pl.ANY)
        args = (spots, cells.astype(f32) * back) + before
        rows = blocks // 2 * height
        return pl.pallas_call(
            functools.partial(place_body, (blocks // 2, zones, height, width)),
            out_shape=jax.ShapeDtypeStruct((9, channels, channels), f32),
            in_specs=[smem, vmem] + [anywhere] * len(before),
            out_specs=anywhere,
            scratch_shapes=[
                pltpu.VMEM((rows, zones * width), f32),
                pltpu.VMEM((9, rows, channels), f32),
                pltpu.SemaphoreType.DMA(()),
            ],
            input_output_aliases={2: 0} if before else {},
            compiler_params=pltpu.CompilerParams(vmem_limit_bytes=40 << 20),
            cost_estimate=pl.CostEstimate(
                flops=0, bytes_accessed=36 * channels * channels, transcendentals=0
            ),
        )(*args)

    weight_grad = place(full, mine, core, ())
    weight_grad = place(crossed, other, 1 - core, (weight_grad,))
    weight_grad = weight_grad.reshape(3, 3, channels, channels)

    half_count = channels // 2
    frequency = jnp.exp(-math.log(10000.0) * jnp.arange(half_count, dtype=f32) / half_count)
    angles = steps[:, :half_count] * frequency[None, :]
    embedding = jnp.concatenate([jnp.cos(angles), jnp.sin(angles)], axis=1).astype(bf16)
    time_bias = jnp.dot(embedding[:1], time_weight, preferred_element_type=f32)
    extra = time_bias + conv_bias.reshape(1, channels)
    ends = jnp.stack([slab_index > 0, slab_index < slab_count - 1]).astype(jnp.int32)
    time_grad = call(
        time_body,
        jax.ShapeDtypeStruct((channels, channels), f32),
        (embedding.astype(f32), *everyone),
    )

    grad, sums = call(
        backward_body,
        (jax.ShapeDtypeStruct((row_count, channels, col_count), f32), small),
        (lat, cot, cot_above, cot_below, stats, gain, bias, conv_weight),
        scratch=(taps, flat),
        flops=flops,
        moved=8 * lat.size,
    )
    block_out = call(
        conv_body,
        jax.ShapeDtypeStruct((row_count, channels, col_count), bf16),
        (ends, act, lat, lat_above, lat_below, stats, gain, bias, conv_weight, extra),
        specs=(smem,) + (vmem,) * 9,
        scratch=(taps, flat),
        flops=flops,
        moved=8 * lat.size,
    )
    sums = sums + swap_space(sums, 1)
    others = [sums]
    for mask in range(1, zones):
        others.append(swap_space(sums, 2 * mask))
    latent_grad = call(
        functools.partial(latent_body, total_count, len(others)),
        jax.ShapeDtypeStruct((row_count, channels, col_count), bf16),
        (grad, lat, cot, stats, *others),
        flops=lat.size * 20,
        moved=10 * lat.size,
    )

    block_out = block_out[None].transpose(0, 1, 3, 2)
    latent_grad = latent_grad[None].transpose(0, 1, 3, 2)
    return (block_out, latent_grad, weight_grad, time_grad)


def solution(mesh):
    return jax.shard_map(
        slab_program,
        mesh=mesh,
        in_specs=(
            P("dp", "space", None, None),
            P("dp"),
            P(),
            P(),
            P(),
            P(),
            P(),
            P("dp", "space", None, None),
        ),
        out_specs=(P("dp", "space", None, None), P("dp", "space", None, None), P(), P()),
        check_vma=False,
    )
```

profile of v0, /device:TPU:0, one launch (start us, length us, event | category | flops | bytes accessed | tf_op | source)
XLA Modules:
  0.0 134.3 jit_solution(6946723035774648041)
XLA Ops:
  3.0 3.4 %collective-permute-start = (bf16[2,320,512]{2,1,0:T(8,128)(2,1)}, bf16[2,320,512]{2,1,0:T(8,128)(2,1)}, u32[]{:S(2)}, u32[]{:S(2)}) collective-permute-start(bf16[2,320,512]{2,1,0:T(8,128)(2,1)} %pad_maximum_fusion.1), channel_id=1, source_target_pairs={{0,1},{1,2},{2,3},{3,4},{4,5},{5,6},{6,7},{8,9},{9,10},{10,11},{11... | collective-permute-start | bytes 1966088 | tf_op jit(solution)/shard_map/ppermute | solution.py:412
  9.2 2.7 %shard_map.111.refs_0_ = f32[8,320]{1,0:T(8,128)S(1)} custom-call(s32[1]{0:T(128)S(6)} %copy.14.step_ref, bf16[4,320,512]{2,1,0:T(8,128)(2,1)S(1)} %bitcast.76, bf16[4,320,512]{2,1,0:T(8,128)(2,1)S(1)} %bitcast.82), custom_call_target="tpu_custom_call" | custom-call | flops 39321600 | bytes 2621440 | tf_op jit(solution)/shard_map/pallas_call | solution.py:28
  11.9 2.5 %collective-permute-start.2 = (f32[8,320]{1,0:T(8,128)S(1)}, f32[8,320]{1,0:T(8,128)S(1)}, u32[]{:S(2)}, u32[]{:S(2)}) collective-permute-start(f32[8,320]{1,0:T(8,128)S(1)} %shard_map.111.refs_0_), channel_id=1, source_target_pairs={{0,1},{1,0},{2,3},{3,2},{4,5},{5,4},{6,7},{7,6},{8,9},{9,8},{10,11... | collective-permute-start | bytes 30728 | tf_op jit(solution)/shard_map/ppermute | solution.py:361
  15.2 2.0 %collective-permute-start.3 = (f32[8,320]{1,0:T(8,128)S(1)}, f32[8,320]{1,0:T(8,128)S(1)}, u32[]{:S(2)}, u32[]{:S(2)}) collective-permute-start(f32[8,320]{1,0:T(8,128)S(1)} %shard_map.112.refs_0_), channel_id=1, source_target_pairs={{0,2},{1,3},{2,0},{3,1},{4,6},{5,7},{6,4},{7,5},{8,10},{9,11},{10,... | collective-permute-start | bytes 30728 | tf_op jit(solution)/shard_map/ppermute | solution.py:361
  17.3 2.6 %collective-permute-start.4 = (f32[8,320]{1,0:T(8,128)S(1)}, f32[8,320]{1,0:T(8,128)S(1)}, u32[]{:S(2)}, u32[]{:S(2)}) collective-permute-start(f32[8,320]{1,0:T(8,128)S(1)} %shard_map.112.refs_0_), channel_id=1, source_target_pairs={{0,4},{1,5},{2,6},{3,7},{4,0},{5,1},{6,2},{7,3},{8,12},{9,13},{10,... | collective-permute-start | bytes 30728 | tf_op jit(solution)/shard_map/ppermute | solution.py:361
  22.9 2.4 %collective-permute-done.5.refs_3_ = f32[8,320]{1,0:T(8,128)S(1)} collective-permute-done((f32[8,320]{1,0:T(8,128)S(1)}, f32[8,320]{1,0:T(8,128)S(1)}, u32[]{:S(2)}, u32[]{:S(2)}) %collective-permute-start.5) | collective-permute-done | bytes 10272 | tf_op jit(solution)/shard_map/ppermute | solution.py:361
  27.8 7.2 %shard_map.114 = (bf16[320,2048]{1,0:T(8,128)(2,1)S(1)}, f32[4,4,40,768]{3,2,1,0:T(8,128)S(1)}, f32[4,4,40,768]{3,2,1,0:T(8,128)S(1)}) custom-call(s32[4]{0:T(128)S(1)} %pad_add_fusion.where_ref, bf16[4,320,512]{2,1,0:T(8,128)(2,1)S(1)} %bitcast.77, bf16[4,320,512]{2,1,0:T(8,128)(2,1)S(1)} %bitcast.83, bf16[320,512]{1,0:T(8,128)(2,1)S(1)} %get-tuple-element.27.above_ref, ...), custom_call_target="tpu_custom_call" | custom-call | flops 3774873600 | bytes 5242880 | tf_op jit(solution)/shard_map/pallas_call | solution.py:28
  41.8 2.4 %collective-permute-done.8.refs_3_ = f32[8,320]{1,0:T(8,128)S(1)} collective-permute-done((f32[8,320]{1,0:T(8,128)S(1)}, f32[8,320]{1,0:T(8,128)S(1)}, u32[]{:S(2)}, u32[]{:S(2)}) %collective-permute-start.8) | collective-permute-done | bytes 10272 | tf_op jit(solution)/shard_map/ppermute | solution.py:370
  46.3 8.3 %collective-permute-done.15 = f16[2,4,40,768]{3,2,1,0:T(8,128)(2,1)S(1)} collective-permute-done((f16[2,4,40,768]{3,2,1,0:T(8,128)(2,1)S(1)}, f16[2,4,40,768]{3,2,1,0:T(8,128)(2,1)S(1)}, u32[]{:S(2)}, u32[]{:S(2)}) %collective-permute-start.15) | collective-permute-done | bytes 491552 | tf_op jit(solution)/shard_map/ppermute | solution.py:370
  56.7 5.7 %collective-permute-done.16 = f16[1,4,40,768]{3,2,1,0:T(8,128)(2,1)S(1)} collective-permute-done((f16[1,4,40,768]{3,2,1,0:T(8,128)(2,1)S(1)}, f16[1,4,40,768]{3,2,1,0:T(8,128)(2,1)S(1)}, u32[]{:S(2)}, u32[]{:S(2)}) %collective-permute-start.16) | collective-permute-done | bytes 245792 | tf_op jit(solution)/shard_map/ppermute | solution.py:370
  64.5 3.7 %collective-permute-start.17 = (f16[40,768]{1,0:T(8,128)(2,1)S(1)}, f16[40,768]{1,0:T(8,128)(2,1)S(1)}, u32[]{:S(2)}, u32[]{:S(2)}) collective-permute-start(f16[40,768]{1,0:T(8,128)(2,1)S(1)} %get-tuple-element.28), channel_id=1, source_target_pairs={{0,2},{1,3},{2,0},{3,1},{4,6},{5,7},{6,4},{7,5},{8,10},{9,11},{10,... | collective-permute-start | bytes 184328 | tf_op jit(solution)/shard_map/ppermute | solution.py:361
  71.8 2.9 %collective-permute-start.22 = (f16[40,768]{1,0:T(8,128)(2,1)S(1)}, f16[40,768]{1,0:T(8,128)(2,1)S(1)}, u32[]{:S(2)}, u32[]{:S(2)}) collective-permute-start(f16[40,768]{1,0:T(8,128)(2,1)S(1)} %fusion.8), channel_id=1, source_target_pairs={{0,6},{1,7},{2,4},{3,5},{4,2},{5,3},{6,0},{7,1},{8,14},{9,15},{10,... | collective-permute-start | bytes 184328 | tf_op jit(solution)/shard_map/ppermute | solution.py:361
  78.0 1.9 %collective-permute-done.21 = f16[40,768]{1,0:T(8,128)(2,1)S(1)} collective-permute-done((f16[40,768]{1,0:T(8,128)(2,1)S(1)}, f16[40,768]{1,0:T(8,128)(2,1)S(1)}, u32[]{:S(2)}, u32[]{:S(2)}) %collective-permute-start.21) | collective-permute-done | bytes 61472 | tf_op jit(solution)/shard_map/ppermute | solution.py:361
  81.9 8.6 %collective-permute-done.23 = f16[1,4,40,768]{3,2,1,0:T(8,128)(2,1)} collective-permute-done((f16[1,4,40,768]{3,2,1,0:T(8,128)(2,1)}, f16[1,4,40,768]{3,2,1,0:T(8,128)(2,1)}, u32[]{:S(2)}, u32[]{:S(2)}) %collective-permute-start.23) | collective-permute-done | bytes 245792 | tf_op jit(solution)/shard_map/ppermute | solution.py:370
  90.5 2.0 %pad_maximum_fusion.3 = f16[2,4,40,768]{3,2,1,0:T(8,128)(2,1)} fusion(f16[1,4,40,768]{3,2,1,0:T(8,128)(2,1)} %collective-permute-done.23, f16[1,4,40,768]{3,2,1,0:T(8,128)(2,1)} %maximum_bitcast_fusion), kind=kLoop, calls=%fused_computation.11 | loop fusion | flops 245760 | bytes 983040 | tf_op jit(solution)/shard_map/concatenate | solution.py:491
  95.9 5.7 %collective-permute-done.24 = f16[2,4,40,768]{3,2,1,0:T(8,128)(2,1)} collective-permute-done((f16[2,4,40,768]{3,2,1,0:T(8,128)(2,1)}, f16[2,4,40,768]{3,2,1,0:T(8,128)(2,1)}, u32[]{:S(2)}, u32[]{:S(2)}) %collective-permute-start.24) | collective-permute-done | bytes 491552 | tf_op jit(solution)/shard_map/ppermute | solution.py:370
  104.8 6.5 %shard_map.117 = (f32[4,320,512]{2,1,0:T(8,128)S(1)}, f32[8,320]{1,0:T(8,128)S(1)}) custom-call(bf16[4,320,512]{2,1,0:T(8,128)(2,1)S(1)} %bitcast.78, bf16[4,320,512]{2,1,0:T(8,128)(2,1)S(1)} %bitcast.84, bf16[320,512]{1,0:T(8,128)(2,1)S(1)} %copy-done.4, bf16[320,512]{1,0:T(8,128)(2,1)S(1)} %copy-done.6, f32[8,320]{1,0:T(8,128)S(1)} %shard_map.113.stats_ref.refs_0_, ...), custom_call_target="tpu_custom_call" | custom-call | flops 3774873600 | bytes 5242880 | tf_op jit(solution)/shard_map/pallas_call | solution.py:28
  113.1 1.9 %collective-permute-start.11 = (f32[8,320]{1,0:T(8,128)S(1)}, f32[8,320]{1,0:T(8,128)S(1)}, u32[]{:S(2)}, u32[]{:S(2)}) collective-permute-start(f32[8,320]{1,0:T(8,128)S(1)} %add.45.refs_0_), channel_id=1, source_target_pairs={{0,4},{1,5},{2,6},{3,7},{4,0},{5,1},{6,2},{7,3},{8,12},{9,13},{10,... | collective-permute-start | bytes 30728 | tf_op jit(solution)/shard_map/ppermute | solution.py:361
  115.1 2.4 %collective-permute-start.12 = (f32[8,320]{1,0:T(8,128)S(1)}, f32[8,320]{1,0:T(8,128)S(1)}, u32[]{:S(2)}, u32[]{:S(2)}) collective-permute-start(f32[8,320]{1,0:T(8,128)S(1)} %add.45.refs_0_), channel_id=1, source_target_pairs={{0,6},{1,7},{2,4},{3,5},{4,2},{5,3},{6,0},{7,1},{8,14},{9,15},{10,... | collective-permute-start | bytes 30728 | tf_op jit(solution)/shard_map/ppermute | solution.py:361
  117.5 7.3 %shard_map.116 = bf16[4,320,512]{2,1,0:T(8,128)(2,1)} custom-call(s32[2]{0:T(128)S(1)} %copy-done.16, bf16[320,2048]{1,0:T(8,128)(2,1)S(1)} %copy-done.18, bf16[4,320,512]{2,1,0:T(8,128)(2,1)S(1)} %bitcast.79, bf16[320,512]{1,0:T(8,128)(2,1)S(1)} %get-tuple-element.26.above_ref, bf16[320,512]{1,0:T(8,128)(2,1)S(1)} %get-tuple-element.24.below_ref, ...), custom_call_target="tpu_custom_call" | custom-call | flops 3774873600 | bytes 5242880 | tf_op jit(solution)/shard_map/pallas_call | solution.py:28
  124.8 2.3 %shard_map.118 = bf16[4,320,512]{2,1,0:T(8,128)(2,1)} custom-call(f32[4,320,512]{2,1,0:T(8,128)S(1)} %get-tuple-element.13.grad_ref, bf16[4,320,512]{2,1,0:T(8,128)(2,1)S(1)} %bitcast.80, bf16[4,320,512]{2,1,0:T(8,128)(2,1)S(1)} %bitcast.85, f32[8,320]{1,0:T(8,128)S(1)} %shard_map.113.stats_ref.refs_0_, f32[8,320]{1,0:T(8,128)S(1)} %add.45.refs_0_, ...), custom_call_target="tpu_custom_call" | custom-call | flops 13107200 | bytes 6553600 | tf_op jit(solution)/shard_map/pallas_call | solution.py:28
  127.1 2.1 %convert_multiply_fusion.cells_ref = f32[4,4,40,768]{3,2,1,0:T(8,128)S(1)} fusion(f32[]{:T(128)} %bitcast.32, f16[2,4,40,768]{3,2,1,0:T(8,128)(2,1)} %collective-permute-done.24, f16[1,4,40,768]{3,2,1,0:T(8,128)(2,1)} %collective-permute-done.23, f16[1,4,40,768]{3,2,1,0:T(8,128)(2,1)} %maximum_bitcast_fusion), kind=kLoop, calls=%fused_computation | loop fusion | flops 1966080 | bytes 2949124 | tf_op jit(solution)/shard_map/mul | solution.py:499
  129.2 2.1 %shard_map.119.refs_0_ = f32[9,320,320]{2,1,0:T(8,128)} custom-call(s32[9]{0:T(128)S(1)} %copy-done.13, f32[4,4,40,768]{3,2,1,0:T(8,128)S(1)} %convert_multiply_fusion.cells_ref), custom_call_target="tpu_custom_call" | custom-call | bytes 3686400 | tf_op jit(solution)/shard_map/pallas_call | solution.py:501
  132.1 2.1 %shard_map.120 = f32[9,320,320]{2,1,0:T(8,128)} custom-call(s32[9]{0:T(128)S(1)} %copy-done.12, f32[4,4,40,768]{3,2,1,0:T(8,128)S(1)} %convert_multiply_fusion.1.cells_ref, f32[9,320,320]{2,1,0:T(8,128)} %shard_map.119.refs_0_), custom_call_target="tpu_custom_call", output_to_operand_aliasing={{}: (2, {})} | custom-call | bytes 3686400 | tf_op jit(solution)/shard_map/pallas_call | solution.py:501
  (114 shorter events, 41.8 us)
Async XLA Ops:
  3.0 22.4 %collective-permute-start = (bf16[2,320,512]{2,1,0:T(8,128)(2,1)}, bf16[2,320,512]{2,1,0:T(8,128)(2,1)}, u32[]{:S(2)}, u32[]{:S(2)}) collective-permute-start(bf16[2,320,512]{2,1,0:T(8,128)(2,1)} %pad_maximum_fusion.1), channel_id=1, source_target_pairs={{0,1},{1,2},{2,3},{3,4},{4,5},{5,6},{6,7},{8,9},{9,10},{10,11},{11... | collective-permute-start | bytes 1966088 | tf_op jit(solution)/shard_map/ppermute | solution.py:412
  7.3 19.3 %collective-permute-start.1 = (bf16[2,320,512]{2,1,0:T(8,128)(2,1)}, bf16[2,320,512]{2,1,0:T(8,128)(2,1)}, u32[]{:S(2)}, u32[]{:S(2)}) collective-permute-start(bf16[2,320,512]{2,1,0:T(8,128)(2,1)} %pad_maximum_fusion.2), channel_id=1, source_target_pairs={{1,0},{2,1},{3,2},{4,3},{5,4},{6,5},{7,6},{9,8},{10,9},{11,10},{12... | collective-permute-start | bytes 1966088 | tf_op jit(solution)/shard_map/ppermute | solution.py:412
  15.2 6.5 %collective-permute-start.3 = (f32[8,320]{1,0:T(8,128)S(1)}, f32[8,320]{1,0:T(8,128)S(1)}, u32[]{:S(2)}, u32[]{:S(2)}) collective-permute-start(f32[8,320]{1,0:T(8,128)S(1)} %shard_map.112.refs_0_), channel_id=1, source_target_pairs={{0,2},{1,3},{2,0},{3,1},{4,6},{5,7},{6,4},{7,5},{8,10},{9,11},{10,... | collective-permute-start | bytes 30728 | tf_op jit(solution)/shard_map/ppermute | solution.py:361
  17.3 5.6 %collective-permute-start.4 = (f32[8,320]{1,0:T(8,128)S(1)}, f32[8,320]{1,0:T(8,128)S(1)}, u32[]{:S(2)}, u32[]{:S(2)}) collective-permute-start(f32[8,320]{1,0:T(8,128)S(1)} %shard_map.112.refs_0_), channel_id=1, source_target_pairs={{0,4},{1,5},{2,6},{3,7},{4,0},{5,1},{6,2},{7,3},{8,12},{9,13},{10,... | collective-permute-start | bytes 30728 | tf_op jit(solution)/shard_map/ppermute | solution.py:361
  19.9 5.5 %collective-permute-start.5 = (f32[8,320]{1,0:T(8,128)S(1)}, f32[8,320]{1,0:T(8,128)S(1)}, u32[]{:S(2)}, u32[]{:S(2)}) collective-permute-start(f32[8,320]{1,0:T(8,128)S(1)} %shard_map.112.refs_0_), channel_id=1, source_target_pairs={{0,6},{1,7},{2,4},{3,5},{4,2},{5,3},{6,0},{7,1},{8,14},{9,15},{10,... | collective-permute-start | bytes 30728 | tf_op jit(solution)/shard_map/ppermute | solution.py:361
  36.1 8.8 %collective-permute-start.14 = (f32[2,4,40,768]{3,2,1,0:T(8,128)S(1)}, f32[2,4,40,768]{3,2,1,0:T(8,128)S(1)}, u32[]{:S(2)}, u32[]{:S(2)}) collective-permute-start(f32[2,4,40,768]{3,2,1,0:T(8,128)S(1)} %get-tuple-element.19), channel_id=1, source_target_pairs={{0,1},{1,0},{2,3},{3,2},{4,5},{5,4},{6,7},{7,6},{8,9},{9,8},{10,11... | collective-permute-start | bytes 2949128 | tf_op jit(solution)/shard_map/ppermute | solution.py:361
  36.1 10.2 %collective-permute-start.13 = (f32[2,4,40,768]{3,2,1,0:T(8,128)S(1)}, f32[2,4,40,768]{3,2,1,0:T(8,128)S(1)}, u32[]{:S(2)}, u32[]{:S(2)}) collective-permute-start(f32[2,4,40,768]{3,2,1,0:T(8,128)S(1)} %get-tuple-element.18), channel_id=1, source_target_pairs={{0,1},{1,0},{2,3},{3,2},{4,5},{5,4},{6,7},{7,6},{8,9},{9,8},{10,11... | collective-permute-start | bytes 2949128 | tf_op jit(solution)/shard_map/ppermute | solution.py:361
  36.6 3.7 %collective-permute-start.6 = (f32[8,320]{1,0:T(8,128)S(1)}, f32[8,320]{1,0:T(8,128)S(1)}, u32[]{:S(2)}, u32[]{:S(2)}) collective-permute-start(f32[8,320]{1,0:T(8,128)S(1)} %shard_map.113.stats_ref.refs_0_), channel_id=1, source_target_pairs={{0,8},{1,9},{2,10},{3,11},{4,12},{5,13},{6,14},{7,15},{8,0},{9,1},... | collective-permute-start | bytes 30728 | tf_op jit(solution)/shard_map/ppermute | solution.py:370
  38.1 3.7 %collective-permute-start.7 = (f32[8,320]{1,0:T(8,128)S(1)}, f32[8,320]{1,0:T(8,128)S(1)}, u32[]{:S(2)}, u32[]{:S(2)}) collective-permute-start(f32[8,320]{1,0:T(8,128)S(1)} %shard_map.113.stats_ref.refs_0_), channel_id=1, source_target_pairs={{0,16},{1,17},{2,18},{3,19},{4,20},{5,21},{6,22},{7,23},{8,24},{9,... | collective-permute-start | bytes 30728 | tf_op jit(solution)/shard_map/ppermute | solution.py:370
  39.6 4.6 %collective-permute-start.8 = (f32[8,320]{1,0:T(8,128)S(1)}, f32[8,320]{1,0:T(8,128)S(1)}, u32[]{:S(2)}, u32[]{:S(2)}) collective-permute-start(f32[8,320]{1,0:T(8,128)S(1)} %shard_map.113.stats_ref.refs_0_), channel_id=1, source_target_pairs={{0,24},{1,25},{2,26},{3,27},{4,28},{5,29},{6,30},{7,31},{8,16},{9,... | collective-permute-start | bytes 30728 | tf_op jit(solution)/shard_map/ppermute | solution.py:370
  45.7 8.9 %collective-permute-start.15 = (f16[2,4,40,768]{3,2,1,0:T(8,128)(2,1)S(1)}, f16[2,4,40,768]{3,2,1,0:T(8,128)(2,1)S(1)}, u32[]{:S(2)}, u32[]{:S(2)}) collective-permute-start(f16[2,4,40,768]{3,2,1,0:T(8,128)(2,1)S(1)} %multiply_convert_fusion), channel_id=1, source_target_pairs={{0,8},{1,17},{2,10},{3,19},{4,12},{5,21},{6,14},{7,23},{8,0},{9,25... | collective-permute-start | bytes 1474568 | tf_op jit(solution)/shard_map/ppermute | solution.py:370
  56.1 6.3 %collective-permute-start.16 = (f16[1,4,40,768]{3,2,1,0:T(8,128)(2,1)S(1)}, f16[1,4,40,768]{3,2,1,0:T(8,128)(2,1)S(1)}, u32[]{:S(2)}, u32[]{:S(2)}) collective-permute-start(f16[1,4,40,768]{3,2,1,0:T(8,128)(2,1)S(1)} %fusion), channel_id=1, source_target_pairs={{0,16},{1,9},{2,18},{3,11},{4,20},{5,13},{6,22},{7,15},{8,24},{9,1... | collective-permute-start | bytes 737288 | tf_op jit(solution)/shard_map/ppermute | solution.py:370
  63.8 6.1 %collective-permute-start.19 = (f16[40,768]{1,0:T(8,128)(2,1)S(1)}, f16[40,768]{1,0:T(8,128)(2,1)S(1)}, u32[]{:S(2)}, u32[]{:S(2)}) collective-permute-start(f16[40,768]{1,0:T(8,128)(2,1)S(1)} %get-tuple-element.29), channel_id=1, source_target_pairs={{0,6},{1,7},{2,4},{3,5},{4,2},{5,3},{6,0},{7,1},{8,14},{9,15},{10,... | collective-permute-start | bytes 184328 | tf_op jit(solution)/shard_map/ppermute | solution.py:361
  64.0 5.9 %collective-permute-start.18 = (f16[40,768]{1,0:T(8,128)(2,1)S(1)}, f16[40,768]{1,0:T(8,128)(2,1)S(1)}, u32[]{:S(2)}, u32[]{:S(2)}) collective-permute-start(f16[40,768]{1,0:T(8,128)(2,1)S(1)} %get-tuple-element.30), channel_id=1, source_target_pairs={{0,4},{1,5},{2,6},{3,7},{4,0},{5,1},{6,2},{7,3},{8,12},{9,13},{10,... | collective-permute-start | bytes 184328 | tf_op jit(solution)/shard_map/ppermute | solution.py:361
  64.5 6.0 %collective-permute-start.17 = (f16[40,768]{1,0:T(8,128)(2,1)S(1)}, f16[40,768]{1,0:T(8,128)(2,1)S(1)}, u32[]{:S(2)}, u32[]{:S(2)}) collective-permute-start(f16[40,768]{1,0:T(8,128)(2,1)S(1)} %get-tuple-element.28), channel_id=1, source_target_pairs={{0,2},{1,3},{2,0},{3,1},{4,6},{5,7},{6,4},{7,5},{8,10},{9,11},{10,... | collective-permute-start | bytes 184328 | tf_op jit(solution)/shard_map/ppermute | solution.py:361
  71.8 6.2 %collective-permute-start.22 = (f16[40,768]{1,0:T(8,128)(2,1)S(1)}, f16[40,768]{1,0:T(8,128)(2,1)S(1)}, u32[]{:S(2)}, u32[]{:S(2)}) collective-permute-start(f16[40,768]{1,0:T(8,128)(2,1)S(1)} %fusion.8), channel_id=1, source_target_pairs={{0,6},{1,7},{2,4},{3,5},{4,2},{5,3},{6,0},{7,1},{8,14},{9,15},{10,... | collective-permute-start | bytes 184328 | tf_op jit(solution)/shard_map/ppermute | solution.py:361
  74.8 5.2 %collective-permute-start.21 = (f16[40,768]{1,0:T(8,128)(2,1)S(1)}, f16[40,768]{1,0:T(8,128)(2,1)S(1)}, u32[]{:S(2)}, u32[]{:S(2)}) collective-permute-start(f16[40,768]{1,0:T(8,128)(2,1)S(1)} %fusion.8), channel_id=1, source_target_pairs={{0,4},{1,5},{2,6},{3,7},{4,0},{5,1},{6,2},{7,3},{8,12},{9,13},{10,... | collective-permute-start | bytes 184328 | tf_op jit(solution)/shard_map/ppermute | solution.py:361
  75.7 4.9 %collective-permute-start.20 = (f16[40,768]{1,0:T(8,128)(2,1)S(1)}, f16[40,768]{1,0:T(8,128)(2,1)S(1)}, u32[]{:S(2)}, u32[]{:S(2)}) collective-permute-start(f16[40,768]{1,0:T(8,128)(2,1)S(1)} %fusion.8), channel_id=1, source_target_pairs={{0,2},{1,3},{2,0},{3,1},{4,6},{5,7},{6,4},{7,5},{8,10},{9,11},{10,... | collective-permute-start | bytes 184328 | tf_op jit(solution)/shard_map/ppermute | solution.py:361
  81.3 9.1 %collective-permute-start.23 = (f16[1,4,40,768]{3,2,1,0:T(8,128)(2,1)}, f16[1,4,40,768]{3,2,1,0:T(8,128)(2,1)}, u32[]{:S(2)}, u32[]{:S(2)}) collective-permute-start(f16[1,4,40,768]{3,2,1,0:T(8,128)(2,1)} %maximum_bitcast_fusion), channel_id=1, source_target_pairs={{0,16},{1,9},{2,18},{3,11},{4,20},{5,13},{6,22},{7,15},{8,24},{9,1... | collective-permute-start | bytes 737288 | tf_op jit(solution)/shard_map/ppermute | solution.py:370
  92.4 9.1 %collective-permute-start.24 = (f16[2,4,40,768]{3,2,1,0:T(8,128)(2,1)}, f16[2,4,40,768]{3,2,1,0:T(8,128)(2,1)}, u32[]{:S(2)}, u32[]{:S(2)}) collective-permute-start(f16[2,4,40,768]{3,2,1,0:T(8,128)(2,1)} %pad_maximum_fusion.3), channel_id=1, source_target_pairs={{0,8},{1,17},{2,10},{3,19},{4,12},{5,21},{6,14},{7,23},{8,0},{9,25... | collective-permute-start | bytes 1474568 | tf_op jit(solution)/shard_map/ppermute | solution.py:370
  103.1 28.2 %collective-permute-start.25 = (f16[4,4,40,768]{3,2,1,0:T(8,128)(2,1)S(1)}, f16[4,4,40,768]{3,2,1,0:T(8,128)(2,1)S(1)}, u32[]{:S(2)}, u32[]{:S(2)}) collective-permute-start(f16[4,4,40,768]{3,2,1,0:T(8,128)(2,1)S(1)} %pad_maximum_fusion), channel_id=1, source_target_pairs={{0,1},{1,0},{2,3},{3,2},{4,5},{5,4},{6,7},{7,6},{8,9},{9,8},{10,11... | collective-permute-start | bytes 2949128 | tf_op jit(solution)/shard_map/ppermute | solution.py:361
  113.1 11.7 %collective-permute-start.10 = (f32[8,320]{1,0:T(8,128)S(1)}, f32[8,320]{1,0:T(8,128)S(1)}, u32[]{:S(2)}, u32[]{:S(2)}) collective-permute-start(f32[8,320]{1,0:T(8,128)S(1)} %add.45.refs_0_), channel_id=1, source_target_pairs={{0,2},{1,3},{2,0},{3,1},{4,6},{5,7},{6,4},{7,5},{8,10},{9,11},{10,... | collective-permute-start | bytes 30728 | tf_op jit(solution)/shard_map/ppermute | solution.py:361
  113.1 11.7 %collective-permute-start.11 = (f32[8,320]{1,0:T(8,128)S(1)}, f32[8,320]{1,0:T(8,128)S(1)}, u32[]{:S(2)}, u32[]{:S(2)}) collective-permute-start(f32[8,320]{1,0:T(8,128)S(1)} %add.45.refs_0_), channel_id=1, source_target_pairs={{0,4},{1,5},{2,6},{3,7},{4,0},{5,1},{6,2},{7,3},{8,12},{9,13},{10,... | collective-permute-start | bytes 30728 | tf_op jit(solution)/shard_map/ppermute | solution.py:361
  115.1 9.7 %collective-permute-start.12 = (f32[8,320]{1,0:T(8,128)S(1)}, f32[8,320]{1,0:T(8,128)S(1)}, u32[]{:S(2)}, u32[]{:S(2)}) collective-permute-start(f32[8,320]{1,0:T(8,128)S(1)} %add.45.refs_0_), channel_id=1, source_target_pairs={{0,6},{1,7},{2,4},{3,5},{4,2},{5,3},{6,0},{7,1},{8,14},{9,15},{10,... | collective-permute-start | bytes 30728 | tf_op jit(solution)/shard_map/ppermute | solution.py:361
  (24 other events, 278.4 us)
where the time goes:
time: 135 us; the launch traced here: 134 us
  waiting for transfers between devices  45.2 us (33%)
  starting transfers between devices  31.9 us (24%)
  Pallas kernels  31.4 us (23%)
  other arithmetic  15.5 us (11%)
  local copies, waits for them, and re-layouts  8.39 us (6%)
  between operations  1.85 us (1%)
    ppermute x7, waiting for transfers between devices, swap_image(): return lax.ppermute(cells, ('dp', 'space'), pairs)  32.4 us
    pallas_call x9, Pallas kernels, call(): pl.pallas_call(body, out_shape=tuple(outs) if many else outs, in_specs=li...  27.2 us
    ppermute x17, starting transfers between devices, swap_space(): return lax.ppermute(cells, 'space', [(i, i ^ mask) for i in range(count)])  21.5 us
    ppermute x17, waiting for transfers between devices, swap_space(): return lax.ppermute(cells, 'space', [(i, i ^ mask) for i in range(count)])  12.8 us
    ppermute x7, starting transfers between devices, swap_image(): return lax.ppermute(cells, ('dp', 'space'), pairs)  5.7 us
    ppermute x2, starting transfers between devices, slab_program(): lax.ppermute(jnp.stack([cot[row], lat[row]]), 'space', way)  4.67 us
    pallas_call x2, Pallas kernels, place(): pl.pallas_call(functools.partial(place_body, (blocks // 2, zones, height,...  4.14 us
    concatenate x2, other arithmetic, slab_program(): full = jnp.concatenate([full, swap_image(full, masks)])  3.44 us
  transfers between devices with their start and end apart: 26, of which 16 were waited for; matrix products, arithmetic and copies ran while one was open for 6% of the time, Pallas kernels for 16%

commit v1 on v0

--- a/solution.py
+++ b/solution.py
@@ -274,12 +274,9 @@
     sums_ref[...] = rows_of(lane_form(first), lane_form(second))
 
 
-def latent_body(
-    total, parts, grad_ref, latent_ref, cot_ref, stats_ref, *refs,
-):
-    out_ref = refs[-1]
+def latent_body(total, grad_ref, latent_ref, cot_ref, stats_ref, sums_ref, out_ref):
     row_count, channels, _ = latent_ref.shape
-    sums = tree_sum([ref[...] for ref in refs[:parts]]) / total
+    sums = sums_ref[0:2] / total
     shape = (8, channels)
     table = rows_of(
         *[
@@ -294,65 +291,81 @@
         out_ref[row] = (cot_ref[row].astype(f32) + change).astype(bf16)
 
 
-def place_body(shape, places_ref, cells_ref, *refs):
-    blocks, zones, height, width = shape
+def place_body(shape, count, places_ref, *refs):
+    zones, height, width = shape
+    cells = refs[:count]
     out_ref, flat_ref, rows_ref, sem = refs[-4:]
     channels = out_ref.shape[1]
-    for block in range(blocks):
-        top = pl.multiple_of(places_ref[block] * height, 8)
+    tap_width = zones * width // 3
+    whole, part = channels // height, channels % height
+
+    def copies(index, act):
+        block = places_ref[index]
+
+        def copy(size):
+            return pltpu.make_async_copy(
+                rows_ref.at[index, :, pl.ds(0, size)],
+                out_ref.at[:, pl.ds(pl.multiple_of(block * height, 8), size)],
+                sem.at[index],
+            )
+
+        @pl.when(block < whole)
+        def _():
+            act(copy(height))
+
+        if part:
+
+            @pl.when(block == whole)
+            def _():
+                act(copy(part))
+
+    for index in range(count):
         for zone in range(zones):
-            left = pl.multiple_of(places_ref[blocks + zone] * width, LANES)
-            flat_ref[pl.ds(top, height), pl.ds(left, width)] = cells_ref[block, zone]
-    tap_width = zones * width // 3
-    half = places_ref[blocks + zones]
-    first = blocks * height
-    sizes = (min(first, channels), channels - min(first, channels))
-    for tap in range(9):
-        left = (tap // 3) * tap_width + (tap % 3) * channels
-        rows_ref[tap] = flat_ref[:, left : left + channels]
-        for index in range(2):
-
-            @pl.when(half == index)
-            def _():
-                pltpu.make_async_copy(
-                    rows_ref.at[tap, pl.ds(0, sizes[index])],
-                    out_ref.at[tap, pl.ds(index * first, sizes[index])],
-                    sem,
-                ).start()
-
-    for tap in range(9):
-        for index in range(2):
-
-            @pl.when(half == index)
-            def _():
-                pltpu.make_async_copy(
-                    rows_ref.at[tap, pl.ds(0, sizes[index])],
-                    out_ref.at[tap, pl.ds(index * first, sizes[index])],
-                    sem,
-                ).wait()
+            left = pl.multiple_of(places_ref[count + zone] * width, LANES)
+            flat_ref[index, :, pl.ds(left, width)] = cells[index][zone]
+        for tap in range(9):
+            left = (tap // 3) * tap_width + (tap % 3) * channels
+            rows_ref[index, tap] = flat_ref[index, :, left : left + channels]
+        copies(index, lambda copy: copy.start())
+    for index in range(count):
+        copies(index, lambda copy: copy.wait())
+
+
+def power_of_two(top, factor, spread, gain_ref, bias_ref, shape):
+    reach = spread * jnp.max(jnp.abs(gain_ref[...]), axis=1, keepdims=True) + jnp.max(
+        jnp.abs(bias_ref[...]), axis=1, keepdims=True
+    )
+    bound = jnp.maximum(jnp.max(top, axis=1, keepdims=True) * reach * factor, 1e-30)
+    power = jnp.clip(jnp.floor(jnp.log2(30000.0 / bound)), -100.0, 100.0)
+    scale = jnp.broadcast_to(jnp.exp2(power), shape)
+    return rows_of(scale, 1.0 / scale)
 
 
 def scale_body(factor, spread, gain_ref, bias_ref, *refs):
     parts, (scale_ref, steps_ref) = refs[:-2], refs[-2:]
-    largest = functools.reduce(jnp.maximum, [ref[3:4] for ref in parts])
-    top = jnp.max(largest, axis=1, keepdims=True)
-    reach = spread * jnp.max(jnp.abs(gain_ref[...]), axis=1, keepdims=True) + jnp.max(
-        jnp.abs(bias_ref[...]), axis=1, keepdims=True
-    )
-    bound = jnp.maximum(top * reach * factor, 1e-30)
-    power = jnp.clip(jnp.floor(jnp.log2(30000.0 / bound)), -100.0, 100.0)
-    shape = scale_ref.shape
-    scale = jnp.broadcast_to(jnp.exp2(power), shape)
-    scale_ref[...] = rows_of(scale, 1.0 / scale)
+    top = functools.reduce(jnp.maximum, [ref[3:4] for ref in parts])
+    scale_ref[...] = power_of_two(top, factor, spread, gain_ref, bias_ref, scale_ref.shape)
     steps_ref[...] = rows_of(*[jnp.broadcast_to(ref[4:5], steps_ref.shape) for ref in parts])
 
 
-def time_body(embed_ref, *refs):
-    out_ref = refs[-1]
+def gather_body(sums_ref, partner_ref, *refs):
+    parts, out_ref = refs[:-1], refs[-1]
+    top = functools.reduce(jnp.maximum, [ref[3:4] for ref in parts])
+    rows = [sums_ref[0:1] + partner_ref[0:1], sums_ref[1:2] + partner_ref[1:2], top]
+    rows += [ref[2:3] for ref in parts]
+    out_ref[...] = rows_of(*[jnp.broadcast_to(row, out_ref.shape) for row in rows])
+
+
+def total_body(factor, spread, gain_ref, bias_ref, *refs):
+    parts, (total_ref, scale_ref) = refs[:-2], refs[-2:]
+    top = functools.reduce(jnp.maximum, [ref[2:3] for ref in parts])
+    scale_ref[...] = power_of_two(top, factor, spread, gain_ref, bias_ref, scale_ref.shape)
+    total_ref[...] = tree_sum([ref[...] for ref in parts])
+
+
+def time_body(count, embed_ref, total_ref, out_ref):
     columns = embed_ref[...].T
-    terms = [
-        columns[:, image : image + 1] * ref[2:3] for image, ref in enumerate(refs[:-1])
-    ]
+    terms = [columns[:, i : i + 1] * total_ref[3 + i : 4 + i] for i in range(count)]
     out_ref[...] = tree_sum(terms)
 
 
@@ -408,11 +421,10 @@
     taps = pltpu.VMEM((3 * channels, (row_count + 2) * col_count), bf16)
     flat = pltpu.VMEM((3, channels, 3 * channels), bf16)
 
-    edges = [
-        lax.ppermute(jnp.stack([cot[row], lat[row]]), "space", way)
-        for row, way in ((row_count - 1, down), (0, up))
-    ]
-    (cot_above, lat_above), (cot_below, lat_below) = edges
+    cot_above = lax.ppermute(cot[row_count - 1], "space", down)
+    cot_below = lax.ppermute(cot[0], "space", up)
+    lat_above = lax.ppermute(lat[row_count - 1], "space", down)
+    lat_below = lax.ppermute(lat[0], "space", up)
     own = call(
         functools.partial(stats_body, local_count),
         small,
@@ -451,17 +463,37 @@
         flops=flops,
         moved=8 * lat.size,
     )
-    everyone = [stats]
+    everyone = [pair]
     for mask in range(1, image_count):
-        everyone.append(swap_image(stats, (mask, mask)))
+        everyone.append(swap_image(pair, (mask, mask)))
+    factor, spread = float(positions * slab_count * image_count), math.sqrt(per_group)
+    scales_shape = jax.ShapeDtypeStruct((8, LANES), f32)
     scales, steps = call(
-        functools.partial(
-            scale_body, float(positions * slab_count * image_count), math.sqrt(per_group)
-        ),
-        (jax.ShapeDtypeStruct((8, LANES), f32), small),
+        functools.partial(scale_body, factor, spread),
+        (scales_shape, jax.ShapeDtypeStruct((-(-image_count // 8) * 8, channels), f32)),
         (gain, bias, *everyone),
     )
     scale, back = scales[0, 0], scales[1, 0]
+
+    grad, sums = call(
+        backward_body,
+        (jax.ShapeDtypeStruct((row_count, channels, col_count), f32), small),
+        (lat, cot, cot_above, cot_below, stats, gain, bias, conv_weight),
+        scratch=(taps, flat),
+        flops=flops,
+        moved=8 * lat.size,
+    )
+    sums_partner = swap_space(sums, 1)
+    message = jax.ShapeDtypeStruct((-(-(3 + image_count) // 8) * 8, channels), f32)
+    gathered = [call(gather_body, message, (sums, sums_partner, *everyone))]
+    for mask in range(1, zones):
+        gathered.append(swap_space(gathered[0], 2 * mask))
+    totals, line_scales = call(
+        functools.partial(total_body, factor, spread),
+        (message, scales_shape),
+        (gain, bias, *gathered),
+    )
+    line_scale, line_back = line_scales[0, 0], line_scales[1, 0]
 
     middle = blocks // 4
     far_in = swap_space(far[middle:], 1)
@@ -474,49 +506,59 @@
         total = keeping + arrived.astype(f32) * back
         middle = total.shape[0] // 2
         sending, keeping = total[middle:], total[:middle]
-    total = keeping[0] if bits == 0 else total[0]
+    total = total[0] if bits else keeping[0]
     share = total[0]
     arrivals = []
     for mask in range(1, zones):
-        arrivals.append(swap_space((total[mask] * scale).astype(f16), 2 * mask))
+        arrivals.append(swap_space((total[mask] * line_scale).astype(f16), 2 * mask))
     for arrived in arrivals:
-        share = share + arrived.astype(f32) * back
-    share = (share * scale).astype(f16)
+        share = share + arrived.astype(f32) * line_back
+    share = (share * line_scale).astype(f16)
     collected = [share]
     for mask in range(1, zones):
         collected.append(swap_space(share, 2 * mask))
-    full = jnp.stack(collected)[None]
+    pieces = [jnp.stack(collected)]
     for step in reversed(range(bits)):
         masks = (1 << orders[0][step], 1 << orders[1][step])
-        full = jnp.concatenate([full, swap_image(full, masks)])
-    crossed = swap_space(full, 1)
-
-    def place(cells, whose, half, before):
-        spots = [whose ^ rest for rest in range(blocks // 2)]
-        spots += [zone_index ^ mask for mask in range(zones)] + [half]
-        spots = jnp.stack(spots).astype(jnp.int32)
+        arrived = []
+        for piece in pieces:
+            arrived.append(swap_image(piece, masks))
+        pieces = pieces + arrived
+    crossed = []
+    for piece in pieces:
+        crossed.append(swap_space(piece, 1))
+    half_blocks = blocks // 2
+    spots = [core * half_blocks + (mine ^ rest) for rest in range(half_blocks)]
+    cross_spots = [(1 - core) * half_blocks + (other ^ rest) for rest in range(half_blocks)]
+    zone_spots = [zone_index ^ mask for mask in range(zones)]
+
+    def place(cells, at, before):
+        table = jnp.stack(at + zone_spots).astype(jnp.int32)
         anywhere = pl.BlockSpec(memory_space=pl.ANY)
-        args = (spots, cells.astype(f32) * back) + before
-        rows = blocks // 2 * height
+        count = len(cells)
         return pl.pallas_call(
-            functools.partial(place_body, (blocks // 2, zones, height, width)),
+            functools.partial(place_body, (zones, height, width), count),
             out_shape=jax.ShapeDtypeStruct((9, channels, channels), f32),
-            in_specs=[smem, vmem] + [anywhere] * len(before),
+            in_specs=[smem] + [vmem] * count + [anywhere] * len(before),
             out_specs=anywhere,
             scratch_shapes=[
-                pltpu.VMEM((rows, zones * width), f32),
-                pltpu.VMEM((9, rows, channels), f32),
-                pltpu.SemaphoreType.DMA(()),
+                pltpu.VMEM((count, height, zones * width), f32),
+                pltpu.VMEM((count, 9, height, channels), f32),
+                pltpu.SemaphoreType.DMA((count,)),
             ],
-            input_output_aliases={2: 0} if before else {},
+            input_output_aliases={1 + count: 0} if before else {},
             compiler_params=pltpu.CompilerParams(vmem_limit_bytes=40 << 20),
             cost_estimate=pl.CostEstimate(
-                flops=0, bytes_accessed=36 * channels * channels, transcendentals=0
+                flops=0,
+                bytes_accessed=8 * count * zones * height * width,
+                transcendentals=0,
             ),
-        )(*args)
-
-    weight_grad = place(full, mine, core, ())
-    weight_grad = place(crossed, other, 1 - core, (weight_grad,))
+        )(table, *[piece.astype(f32) * line_back for piece in cells], *before)
+
+    weight_grad = place(
+        pieces[:-1] + crossed[:-1], spots[:-1] + cross_spots[:-1], ()
+    )
+    weight_grad = place(pieces[-1:] + crossed[-1:], spots[-1:] + cross_spots[-1:], (weight_grad,))
     weight_grad = weight_grad.reshape(3, 3, channels, channels)
 
     half_count = channels // 2
@@ -527,18 +569,9 @@
     extra = time_bias + conv_bias.reshape(1, channels)
     ends = jnp.stack([slab_index > 0, slab_index < slab_count - 1]).astype(jnp.int32)
     time_grad = call(
-        time_body,
+        functools.partial(time_body, image_count),
         jax.ShapeDtypeStruct((channels, channels), f32),
-        (embedding.astype(f32), *everyone),
-    )
-
-    grad, sums = call(
-        backward_body,
-        (jax.ShapeDtypeStruct((row_count, channels, col_count), f32), small),
-        (lat, cot, cot_above, cot_below, stats, gain, bias, conv_weight),
-        scratch=(taps, flat),
-        flops=flops,
-        moved=8 * lat.size,
+        (embedding.astype(f32), totals),
     )
     block_out = call(
         conv_body,
@@ -549,14 +582,10 @@
         flops=flops,
         moved=8 * lat.size,
     )
-    sums = sums + swap_space(sums, 1)
-    others = [sums]
-    for mask in range(1, zones):
-        others.append(swap_space(sums, 2 * mask))
     latent_grad = call(
-        functools.partial(latent_body, total_count, len(others)),
+        functools.partial(latent_body, total_count),
         jax.ShapeDtypeStruct((row_count, channels, col_count), bf16),
-        (grad, lat, cot, stats, *others),
+        (grad, lat, cot, stats, totals),
         flops=lat.size * 20,
         moved=10 * lat.size,
     )

time: 135 us -> 118 us (0.87)
  waiting for transfers between devices: 45.2 us -> 20.1 us
  starting transfers between devices: 31.9 us -> 39 us
  other arithmetic: 15.5 us -> 12.5 us
  local copies, waits for them, and re-layouts: 8.39 us -> 11.1 us
    ppermute x7 -> x8, waiting for transfers between devices: 32.4 us -> 7.12 us  [swap_image(): return lax.ppermute(cells, ('dp', 'space'), pairs)]
    ppermute x7 -> x8, starting transfers between devices: 5.7 us -> 9.65 us  [swap_image(): return lax.ppermute(cells, ('dp', 'space'), pairs)]
    another operation x4 -> x2, local copies, waits for them, and re-layouts: 3.63 us -> 0.17 us  [place(): table = jnp.stack(at + zone_spots).astype(jnp.int32)]
    concatenate x2 -> x0, other arithmetic: 3.44 us -> none  [slab_program(): full = jnp.concatenate([full, swap_image(full, masks)])]
    ppermute x2 -> x4, starting transfers between devices: 4.67 us -> 7.81 us  [the longest x1 2.6 us: slab_program(): lat_above = lax.ppermute(lat[row_count - 1], 'space', down)]
    unnamed x44 -> x34, local copies, waits for them, and re-layouts: 2.58 us -> 5.57 us
    squeeze x0 -> x2, local copies, waits for them, and re-layouts: none -> 2.95 us  [the longest x1 2.06 us: slab_program(): cot_below = lax.ppermute(cot[0], 'space', up)]
    another operation x3 -> x2, other arithmetic: 2.6 us -> 0.13 us  [the longest x1 0.08 us: slab_program(): pieces = [jnp.stack(collected)]]
  transfers between devices with their start and end apart: 26 -> 32, of which waited for: 16 -> 13; matrix products, arithmetic and copies ran while one was open for 6% -> 12% of each run, Pallas kernels for 16% -> 20%
where the time goes in v1:
time: 118 us; the launch traced here: 117 us
  starting transfers between devices  39 us (33%)
  Pallas kernels  32.4 us (27%)
  waiting for transfers between devices  20.1 us (17%)
  other arithmetic  12.5 us (11%)
  local copies, waits for them, and re-layouts  11.1 us (9%)
  between operations  1.93 us (2%)
    pallas_call x11, Pallas kernels, call(): pl.pallas_call(body, out_shape=tuple(outs) if many else outs, in_specs=li...  28.1 us
    ppermute x20, starting transfers between devices, swap_space(): return lax.ppermute(cells, 'space', [(i, i ^ mask) for i in range(count)])  21.5 us
    ppermute x20, waiting for transfers between devices, swap_space(): return lax.ppermute(cells, 'space', [(i, i ^ mask) for i in range(count)])  13 us
    ppermute x8, starting transfers between devices, swap_image(): return lax.ppermute(cells, ('dp', 'space'), pairs)  9.65 us
    ppermute x8, waiting for transfers between devices, swap_image(): return lax.ppermute(cells, ('dp', 'space'), pairs)  7.12 us
    unnamed x34, local copies, waits for them, and re-layouts  5.57 us
    mul x8, other arithmetic, place(): piece.astype(f32) * line_back  4.67 us
    pallas_call x2, Pallas kernels, place(): pl.pallas_call(functools.partial(place_body, (zones, height, width), coun...  4.25 us
  transfers between devices with their start and end apart: 32, of which 13 were waited for; matrix products, arithmetic and copies ran while one was open for 12% of the time, Pallas kernels for 20%

profile of v1, /device:TPU:0, one launch (start us, length us, event | category | flops | bytes accessed | tf_op | source)
XLA Modules:
  0.0 117.3 jit_solution(5714187429190667744)
XLA Ops:
  0.7 2.1 %slice_bitcast_fusion.2 = (bf16[320,512]{1,0:T(8,128)(2,1)}, bf16[320,512]{1,0:T(8,128)(2,1)}) fusion(bf16[1,4,320,512]{3,2,1,0:T(8,128)(2,1)} %bitcast.74), kind=kLoop, calls=%fused_computation.16 | loop fusion | bytes 1310720 | tf_op jit(solution)/shard_map/squeeze | solution.py:425
  2.7 2.4 %collective-permute-start = (bf16[320,512]{1,0:T(8,128)(2,1)}, bf16[320,512]{1,0:T(8,128)(2,1)S(1)}, u32[]{:S(2)}, u32[]{:S(2)}) collective-permute-start(bf16[320,512]{1,0:T(8,128)(2,1)} %get-tuple-element.27), channel_id=1, source_target_pairs={{0,1},{1,2},{2,3},{3,4},{4,5},{5,6},{6,7},{8,9},{9,10},{10,11},{11... | collective-permute-start | bytes 983048 | tf_op jit(solution)/shard_map/ppermute | solution.py:424
  8.4 2.7 %shard_map.111.refs_0_ = f32[8,320]{1,0:T(8,128)S(1)} custom-call(s32[1]{0:T(128)S(6)} %copy.14.step_ref, bf16[4,320,512]{2,1,0:T(8,128)(2,1)S(1)} %bitcast.68, bf16[4,320,512]{2,1,0:T(8,128)(2,1)S(1)} %bitcast.75), custom_call_target="tpu_custom_call" | custom-call | flops 39321600 | bytes 2621440 | tf_op jit(solution)/shard_map/pallas_call | solution.py:28
  11.1 3.3 %collective-permute-start.2 = (f32[8,320]{1,0:T(8,128)S(1)}, f32[8,320]{1,0:T(8,128)S(1)}, u32[]{:S(2)}, u32[]{:S(2)}) collective-permute-start(f32[8,320]{1,0:T(8,128)S(1)} %shard_map.111.refs_0_), channel_id=1, source_target_pairs={{0,1},{1,0},{2,3},{3,2},{4,5},{5,4},{6,7},{7,6},{8,9},{9,8},{10,11... | collective-permute-start | bytes 30728 | tf_op jit(solution)/shard_map/ppermute | solution.py:374
  15.3 2.0 %collective-permute-start.3 = (f32[8,320]{1,0:T(8,128)S(1)}, f32[8,320]{1,0:T(8,128)S(1)}, u32[]{:S(2)}, u32[]{:S(2)}) collective-permute-start(f32[8,320]{1,0:T(8,128)S(1)} %shard_map.112.refs_0_), channel_id=1, source_target_pairs={{0,2},{1,3},{2,0},{3,1},{4,6},{5,7},{6,4},{7,5},{8,10},{9,11},{10,... | collective-permute-start | bytes 30728 | tf_op jit(solution)/shard_map/ppermute | solution.py:374
  17.3 2.6 %collective-permute-start.4 = (f32[8,320]{1,0:T(8,128)S(1)}, f32[8,320]{1,0:T(8,128)S(1)}, u32[]{:S(2)}, u32[]{:S(2)}) collective-permute-start(f32[8,320]{1,0:T(8,128)S(1)} %shard_map.112.refs_0_), channel_id=1, source_target_pairs={{0,4},{1,5},{2,6},{3,7},{4,0},{5,1},{6,2},{7,3},{8,12},{9,13},{10,... | collective-permute-start | bytes 30728 | tf_op jit(solution)/shard_map/ppermute | solution.py:374
  20.0 1.9 %collective-permute-done.4.refs_2_ = f32[8,320]{1,0:T(8,128)S(1)} collective-permute-done((f32[8,320]{1,0:T(8,128)S(1)}, f32[8,320]{1,0:T(8,128)S(1)}, u32[]{:S(2)}, u32[]{:S(2)}) %collective-permute-start.4) | collective-permute-done | bytes 10272 | tf_op jit(solution)/shard_map/ppermute | solution.py:374
  21.9 3.5 %collective-permute-done.5.refs_3_ = f32[8,320]{1,0:T(8,128)S(1)} collective-permute-done((f32[8,320]{1,0:T(8,128)S(1)}, f32[8,320]{1,0:T(8,128)S(1)}, u32[]{:S(2)}, u32[]{:S(2)}) %collective-permute-start.5) | collective-permute-done | bytes 10272 | tf_op jit(solution)/shard_map/ppermute | solution.py:374
  25.5 7.5 %shard_map.114 = (bf16[320,2048]{1,0:T(8,128)(2,1)S(1)}, f32[4,4,40,768]{3,2,1,0:T(8,128)S(1)}, f32[4,4,40,768]{3,2,1,0:T(8,128)S(1)}) custom-call(s32[4]{0:T(128)S(1)} %pad_add_fusion.where_ref, bf16[4,320,512]{2,1,0:T(8,128)(2,1)S(1)} %bitcast.69, bf16[4,320,512]{2,1,0:T(8,128)(2,1)S(1)} %bitcast.76, bf16[320,512]{1,0:T(8,128)(2,1)S(1)} %collective-permute-done.above_ref, ...), custom_call_target="tpu_custom_call" | custom-call | flops 3774873600 | bytes 5242880 | tf_op jit(solution)/shard_map/pallas_call | solution.py:28
  38.8 2.6 %collective-permute-start.6 = (bf16[320,512]{1,0:T(8,128)(2,1)}, bf16[320,512]{1,0:T(8,128)(2,1)S(1)}, u32[]{:S(2)}, u32[]{:S(2)}) collective-permute-start(bf16[320,512]{1,0:T(8,128)(2,1)} %get-tuple-element.25), channel_id=1, source_target_pairs={{0,1},{1,2},{2,3},{3,4},{4,5},{5,6},{6,7},{8,9},{9,10},{10,11},{11... | collective-permute-start | bytes 983048 | tf_op jit(solution)/shard_map/ppermute | solution.py:426
  42.7 1.6 %multiply_convert_fusion = f16[2,4,40,768]{3,2,1,0:T(8,128)(2,1)} fusion(f32[2,4,40,768]{3,2,1,0:T(8,128)S(1)} %collective-permute-done.16, f32[4,4,40,768]{3,2,1,0:T(8,128)S(1)} %get-tuple-element.18, f32[]{:T(128)} %bitcast.25), kind=kLoop, calls=%fused_computation.2 | loop fusion | flops 737280 | bytes 2457604 | tf_op jit(solution)/shard_map/convert_element_type | solution.py:505
  45.2 1.6 %copy-done.7 = bf16[3,3,320,320]{3,2,1,0:T(8,128)(2,1)S(1)} copy-done((bf16[3,3,320,320]{3,2,1,0:T(8,128)(2,1)S(1)}, bf16[3,3,320,320]{3,2,1,0:T(8,128)(2,1)}, u32[]{:S(2)}) %copy-start.7) | copy-done | bytes 1843224
  47.8 7.3 %shard_map.117 = (f32[4,320,512]{2,1,0:T(8,128)S(1)}, f32[8,320]{1,0:T(8,128)S(1)}) custom-call(bf16[4,320,512]{2,1,0:T(8,128)(2,1)S(1)} %bitcast.71, bf16[4,320,512]{2,1,0:T(8,128)(2,1)S(1)} %bitcast.77, bf16[320,512]{1,0:T(8,128)(2,1)S(1)} %copy-done.10, bf16[320,512]{1,0:T(8,128)(2,1)} %collective-permute-done.1.below_ref, ...), custom_call_target="tpu_custom_call" | custom-call | flops 3774873600 | bytes 5242880 | tf_op jit(solution)/shard_map/pallas_call | solution.py:28
  58.6 3.7 %collective-permute-start.14 = (f32[8,320]{1,0:T(8,128)S(1)}, f32[8,320]{1,0:T(8,128)S(1)}, u32[]{:S(2)}, u32[]{:S(2)}) collective-permute-start(f32[8,320]{1,0:T(8,128)S(1)} %shard_map.118.refs_0_), channel_id=1, source_target_pairs={{0,6},{1,7},{2,4},{3,5},{4,2},{5,3},{6,0},{7,1},{8,14},{9,15},{10,... | collective-permute-start | bytes 30728 | tf_op jit(solution)/shard_map/ppermute | solution.py:374
  62.3 2.4 %multiply_add_fusion = f32[2,4,40,768]{3,2,1,0:T(8,128)S(1)} fusion(f16[2,4,40,768]{3,2,1,0:T(8,128)(2,1)} %collective-permute-done.17, f32[2,4,40,768]{3,2,1,0:T(8,128)} %collective-permute-done.15, f32[4,4,40,768]{3,2,1,0:T(8,128)} %copy-done.6, f32[]{:T(128)} %bitcast.26), kind=kLoop, calls=%fused_computation.1 | loop fusion | flops 983040 | bytes 3440644 | tf_op jit(solution)/shard_map/add | solution.py:506
  69.5 2.4 %collective-permute-done.18 = f16[1,4,40,768]{3,2,1,0:T(8,128)(2,1)S(1)} collective-permute-done((f16[1,4,40,768]{3,2,1,0:T(8,128)(2,1)S(1)}, f16[1,4,40,768]{3,2,1,0:T(8,128)(2,1)S(1)}, u32[]{:S(2)}, u32[]{:S(2)}) %collective-permute-start.18) | collective-permute-done | bytes 245792 | tf_op jit(solution)/shard_map/ppermute | solution.py:383
  74.0 3.7 %collective-permute-start.19 = (f16[40,768]{1,0:T(8,128)(2,1)S(1)}, f16[40,768]{1,0:T(8,128)(2,1)S(1)}, u32[]{:S(2)}, u32[]{:S(2)}) collective-permute-start(f16[40,768]{1,0:T(8,128)(2,1)S(1)} %get-tuple-element.28), channel_id=1, source_target_pairs={{0,2},{1,3},{2,0},{3,1},{4,6},{5,7},{6,4},{7,5},{8,10},{9,11},{10,... | collective-permute-start | bytes 184328 | tf_op jit(solution)/shard_map/ppermute | solution.py:374
  81.4 2.2 %collective-permute-start.24 = (f16[40,768]{1,0:T(8,128)(2,1)S(1)}, f16[40,768]{1,0:T(8,128)(2,1)S(1)}, u32[]{:S(2)}, u32[]{:S(2)}) collective-permute-start(f16[40,768]{1,0:T(8,128)(2,1)S(1)} %fusion.8), channel_id=1, source_target_pairs={{0,6},{1,7},{2,4},{3,5},{4,2},{5,3},{6,0},{7,1},{8,14},{9,15},{10,... | collective-permute-start | bytes 184328 | tf_op jit(solution)/shard_map/ppermute | solution.py:374
  85.9 1.7 %collective-permute-done.24 = f16[40,768]{1,0:T(8,128)(2,1)S(1)} collective-permute-done((f16[40,768]{1,0:T(8,128)(2,1)S(1)}, f16[40,768]{1,0:T(8,128)(2,1)S(1)}, u32[]{:S(2)}, u32[]{:S(2)}) %collective-permute-start.24) | collective-permute-done | bytes 61472 | tf_op jit(solution)/shard_map/ppermute | solution.py:374
  91.3 6.9 %shard_map.116 = bf16[4,320,512]{2,1,0:T(8,128)(2,1)} custom-call(s32[2]{0:T(128)S(1)} %add_convert_fusion.ends_ref, bf16[320,2048]{1,0:T(8,128)(2,1)S(1)} %copy-done.12, bf16[4,320,512]{2,1,0:T(8,128)(2,1)S(1)} %bitcast.72, bf16[320,512]{1,0:T(8,128)(2,1)S(1)} %collective-permute-done.6.above_ref, bf16[320,512]{1,0:T(8,128)(2,1)S(1)} %collective-permute-done.7.below_ref, ...), custom_call_target="tpu_custom_call" | custom-call | flops 3774873600 | bytes 5242880 | tf_op jit(solution)/shard_map/pallas_call | solution.py:28
  99.4 2.2 %shard_map.120 = bf16[4,320,512]{2,1,0:T(8,128)(2,1)} custom-call(f32[4,320,512]{2,1,0:T(8,128)S(1)} %copy-done.5, bf16[4,320,512]{2,1,0:T(8,128)(2,1)S(1)} %bitcast.73, bf16[4,320,512]{2,1,0:T(8,128)(2,1)S(1)} %bitcast.78, f32[8,320]{1,0:T(8,128)S(1)} %shard_map.113.stats_ref, f32[8,320]{1,0:T(8,128)S(1)} %get-tuple-element.17.sums_ref.total_ref), custom_call_target="tpu_custom_call" | custom-call | flops 13107200 | bytes 6553600 | tf_op jit(solution)/shard_map/pallas_call | solution.py:28
  105.1 2.7 %collective-permute-done.28 = f16[4,40,768]{2,1,0:T(8,128)(2,1)S(1)} collective-permute-done((f16[4,40,768]{2,1,0:T(8,128)(2,1)S(1)}, f16[4,40,768]{2,1,0:T(8,128)(2,1)S(1)}, u32[]{:S(2)}, u32[]{:S(2)}) %collective-permute-start.28) | collective-permute-done | bytes 245792 | tf_op jit(solution)/shard_map/ppermute | solution.py:383
  111.6 2.5 %shard_map.121.refs_2_ = f32[9,320,320]{2,1,0:T(8,128)} custom-call(s32[10]{0:T(128)S(1)} %stack.108.places_ref, f32[4,40,768]{2,1,0:T(8,128)S(1)} %convert_multiply_fusion.5.refs_0_, f32[4,40,768]{2,1,0:T(8,128)S(1)} %convert_multiply_fusion.4.refs_1_, f32[4,40,768]{2,1,0:T(8,128)S(1)} %convert_multiply_fusion.3.refs_2_, ...), custom_call_target="tpu_custom_call" | custom-call | bytes 5898240 | tf_op jit(solution)/shard_map/pallas_call | solution.py:539
  115.4 1.7 %shard_map.122 = f32[9,320,320]{2,1,0:T(8,128)} custom-call(s32[6]{0:T(128)S(1)} %stack.96.places_ref, f32[4,40,768]{2,1,0:T(8,128)S(1)} %convert_multiply_fusion.7.refs_0_, f32[4,40,768]{2,1,0:T(8,128)S(1)} %convert_multiply_fusion.6.refs_1_, f32[9,320,320]{2,1,0:T(8,128)} %shard_map.121.refs_2_), custom_call_target="tpu_custom_call", output_to_operand_aliasing={{}: (3, {})} | custom-call | bytes 1966080 | tf_op jit(solution)/shard_map/pallas_call | solution.py:539
  (119 shorter events, 41.8 us)
Async XLA Ops:
  2.7 22.7 %collective-permute-start = (bf16[320,512]{1,0:T(8,128)(2,1)}, bf16[320,512]{1,0:T(8,128)(2,1)S(1)}, u32[]{:S(2)}, u32[]{:S(2)}) collective-permute-start(bf16[320,512]{1,0:T(8,128)(2,1)} %get-tuple-element.27), channel_id=1, source_target_pairs={{0,1},{1,2},{2,3},{3,4},{4,5},{5,6},{6,7},{8,9},{9,10},{10,11},{11... | collective-permute-start | bytes 983048 | tf_op jit(solution)/shard_map/ppermute | solution.py:424
  5.2 20.3 %collective-permute-start.1 = (bf16[320,512]{1,0:T(8,128)(2,1)}, bf16[320,512]{1,0:T(8,128)(2,1)}, u32[]{:S(2)}, u32[]{:S(2)}) collective-permute-start(bf16[320,512]{1,0:T(8,128)(2,1)} %get-tuple-element.26), channel_id=1, source_target_pairs={{1,0},{2,1},{3,2},{4,3},{5,4},{6,5},{7,6},{9,8},{10,9},{11,10},{12... | collective-permute-start | bytes 983048 | tf_op jit(solution)/shard_map/ppermute | solution.py:425
  19.9 5.5 %collective-permute-start.5 = (f32[8,320]{1,0:T(8,128)S(1)}, f32[8,320]{1,0:T(8,128)S(1)}, u32[]{:S(2)}, u32[]{:S(2)}) collective-permute-start(f32[8,320]{1,0:T(8,128)S(1)} %shard_map.112.refs_0_), channel_id=1, source_target_pairs={{0,6},{1,7},{2,4},{3,5},{4,2},{5,3},{6,0},{7,1},{8,14},{9,15},{10,... | collective-permute-start | bytes 30728 | tf_op jit(solution)/shard_map/ppermute | solution.py:374
  34.4 8.3 %collective-permute-start.16 = (f32[2,4,40,768]{3,2,1,0:T(8,128)S(1)}, f32[2,4,40,768]{3,2,1,0:T(8,128)S(1)}, u32[]{:S(2)}, u32[]{:S(2)}) collective-permute-start(f32[2,4,40,768]{3,2,1,0:T(8,128)S(1)} %get-tuple-element.23), channel_id=1, source_target_pairs={{0,1},{1,0},{2,3},{3,2},{4,5},{5,4},{6,7},{7,6},{8,9},{9,8},{10,11... | collective-permute-start | bytes 2949128 | tf_op jit(solution)/shard_map/ppermute | solution.py:374
  35.9 5.5 %collective-permute-start.9 = (f32[8,320]{1,0:T(8,128)S(1)}, f32[8,320]{1,0:T(8,128)S(1)}, u32[]{:S(2)}, u32[]{:S(2)}) collective-permute-start(f32[8,320]{1,0:T(8,128)S(1)} %shard_map.112.refs_0_), channel_id=1, source_target_pairs={{0,16},{1,17},{2,18},{3,19},{4,20},{5,21},{6,22},{7,23},{8,24},{9,... | collective-permute-start | bytes 30728 | tf_op jit(solution)/shard_map/ppermute | solution.py:383
  37.9 20.7 %collective-permute-start.15 = (f32[2,4,40,768]{3,2,1,0:T(8,128)}, f32[2,4,40,768]{3,2,1,0:T(8,128)}, u32[]{:S(2)}, u32[]{:S(2)}) collective-permute-start(f32[2,4,40,768]{3,2,1,0:T(8,128)} %get-tuple-element.22), channel_id=1, source_target_pairs={{0,1},{1,0},{2,3},{3,2},{4,5},{5,4},{6,7},{7,6},{8,9},{9,8},{10,11... | collective-permute-start | bytes 2949128 | tf_op jit(solution)/shard_map/ppermute | solution.py:374
  38.8 52.4 %collective-permute-start.6 = (bf16[320,512]{1,0:T(8,128)(2,1)}, bf16[320,512]{1,0:T(8,128)(2,1)S(1)}, u32[]{:S(2)}, u32[]{:S(2)}) collective-permute-start(bf16[320,512]{1,0:T(8,128)(2,1)} %get-tuple-element.25), channel_id=1, source_target_pairs={{0,1},{1,2},{2,3},{3,4},{4,5},{5,6},{6,7},{8,9},{9,10},{10,11},{11... | collective-permute-start | bytes 983048 | tf_op jit(solution)/shard_map/ppermute | solution.py:426
  44.3 18.0 %collective-permute-start.17 = (f16[2,4,40,768]{3,2,1,0:T(8,128)(2,1)}, f16[2,4,40,768]{3,2,1,0:T(8,128)(2,1)}, u32[]{:S(2)}, u32[]{:S(2)}) collective-permute-start(f16[2,4,40,768]{3,2,1,0:T(8,128)(2,1)} %multiply_convert_fusion), channel_id=1, source_target_pairs={{0,8},{1,17},{2,10},{3,19},{4,12},{5,21},{6,14},{7,23},{8,0},{9,25... | collective-permute-start | bytes 1474568 | tf_op jit(solution)/shard_map/ppermute | solution.py:383
  57.9 9.4 %collective-permute-start.12 = (f32[8,320]{1,0:T(8,128)S(1)}, f32[8,320]{1,0:T(8,128)S(1)}, u32[]{:S(2)}, u32[]{:S(2)}) collective-permute-start(f32[8,320]{1,0:T(8,128)S(1)} %shard_map.118.refs_0_), channel_id=1, source_target_pairs={{0,2},{1,3},{2,0},{3,1},{4,6},{5,7},{6,4},{7,5},{8,10},{9,11},{10,... | collective-permute-start | bytes 30728 | tf_op jit(solution)/shard_map/ppermute | solution.py:374
  57.9 10.9 %collective-permute-start.13 = (f32[8,320]{1,0:T(8,128)S(1)}, f32[8,320]{1,0:T(8,128)S(1)}, u32[]{:S(2)}, u32[]{:S(2)}) collective-permute-start(f32[8,320]{1,0:T(8,128)S(1)} %shard_map.118.refs_0_), channel_id=1, source_target_pairs={{0,4},{1,5},{2,6},{3,7},{4,0},{5,1},{6,2},{7,3},{8,12},{9,13},{10,... | collective-permute-start | bytes 30728 | tf_op jit(solution)/shard_map/ppermute | solution.py:374
  58.6 10.2 %collective-permute-start.14 = (f32[8,320]{1,0:T(8,128)S(1)}, f32[8,320]{1,0:T(8,128)S(1)}, u32[]{:S(2)}, u32[]{:S(2)}) collective-permute-start(f32[8,320]{1,0:T(8,128)S(1)} %shard_map.118.refs_0_), channel_id=1, source_target_pairs={{0,6},{1,7},{2,4},{3,5},{4,2},{5,3},{6,0},{7,1},{8,14},{9,15},{10,... | collective-permute-start | bytes 30728 | tf_op jit(solution)/shard_map/ppermute | solution.py:374
  65.7 6.3 %collective-permute-start.18 = (f16[1,4,40,768]{3,2,1,0:T(8,128)(2,1)S(1)}, f16[1,4,40,768]{3,2,1,0:T(8,128)(2,1)S(1)}, u32[]{:S(2)}, u32[]{:S(2)}) collective-permute-start(f16[1,4,40,768]{3,2,1,0:T(8,128)(2,1)S(1)} %fusion), channel_id=1, source_target_pairs={{0,16},{1,9},{2,18},{3,11},{4,20},{5,13},{6,22},{7,15},{8,24},{9,1... | collective-permute-start | bytes 737288 | tf_op jit(solution)/shard_map/ppermute | solution.py:383
  67.3 23.9 %collective-permute-start.7 = (bf16[320,512]{1,0:T(8,128)(2,1)S(1)}, bf16[320,512]{1,0:T(8,128)(2,1)S(1)}, u32[]{:S(2)}, u32[]{:S(2)}) collective-permute-start(bf16[320,512]{1,0:T(8,128)(2,1)S(1)} %copy-done.13), channel_id=1, source_target_pairs={{1,0},{2,1},{3,2},{4,3},{5,4},{6,5},{7,6},{9,8},{10,9},{11,10},{12... | collective-permute-start | bytes 983048 | tf_op jit(solution)/shard_map/ppermute | solution.py:427
  73.2 6.2 %collective-permute-start.21 = (f16[40,768]{1,0:T(8,128)(2,1)S(1)}, f16[40,768]{1,0:T(8,128)(2,1)S(1)}, u32[]{:S(2)}, u32[]{:S(2)}) collective-permute-start(f16[40,768]{1,0:T(8,128)(2,1)S(1)} %get-tuple-element.29), channel_id=1, source_target_pairs={{0,6},{1,7},{2,4},{3,5},{4,2},{5,3},{6,0},{7,1},{8,14},{9,15},{10,... | collective-permute-start | bytes 184328 | tf_op jit(solution)/shard_map/ppermute | solution.py:374
  73.4 6.7 %collective-permute-start.20 = (f16[40,768]{1,0:T(8,128)(2,1)S(1)}, f16[40,768]{1,0:T(8,128)(2,1)S(1)}, u32[]{:S(2)}, u32[]{:S(2)}) collective-permute-start(f16[40,768]{1,0:T(8,128)(2,1)S(1)} %get-tuple-element.30), channel_id=1, source_target_pairs={{0,4},{1,5},{2,6},{3,7},{4,0},{5,1},{6,2},{7,3},{8,12},{9,13},{10,... | collective-permute-start | bytes 184328 | tf_op jit(solution)/shard_map/ppermute | solution.py:374
  74.0 6.1 %collective-permute-start.19 = (f16[40,768]{1,0:T(8,128)(2,1)S(1)}, f16[40,768]{1,0:T(8,128)(2,1)S(1)}, u32[]{:S(2)}, u32[]{:S(2)}) collective-permute-start(f16[40,768]{1,0:T(8,128)(2,1)S(1)} %get-tuple-element.28), channel_id=1, source_target_pairs={{0,2},{1,3},{2,0},{3,1},{4,6},{5,7},{6,4},{7,5},{8,10},{9,11},{10,... | collective-permute-start | bytes 184328 | tf_op jit(solution)/shard_map/ppermute | solution.py:374
  81.4 6.3 %collective-permute-start.24 = (f16[40,768]{1,0:T(8,128)(2,1)S(1)}, f16[40,768]{1,0:T(8,128)(2,1)S(1)}, u32[]{:S(2)}, u32[]{:S(2)}) collective-permute-start(f16[40,768]{1,0:T(8,128)(2,1)S(1)} %fusion.8), channel_id=1, source_target_pairs={{0,6},{1,7},{2,4},{3,5},{4,2},{5,3},{6,0},{7,1},{8,14},{9,15},{10,... | collective-permute-start | bytes 184328 | tf_op jit(solution)/shard_map/ppermute | solution.py:374
  83.6 5.5 %collective-permute-start.23 = (f16[40,768]{1,0:T(8,128)(2,1)S(1)}, f16[40,768]{1,0:T(8,128)(2,1)S(1)}, u32[]{:S(2)}, u32[]{:S(2)}) collective-permute-start(f16[40,768]{1,0:T(8,128)(2,1)S(1)} %fusion.8), channel_id=1, source_target_pairs={{0,4},{1,5},{2,6},{3,7},{4,0},{5,1},{6,2},{7,3},{8,12},{9,13},{10,... | collective-permute-start | bytes 184328 | tf_op jit(solution)/shard_map/ppermute | solution.py:374
  84.7 4.9 %collective-permute-start.22 = (f16[40,768]{1,0:T(8,128)(2,1)S(1)}, f16[40,768]{1,0:T(8,128)(2,1)S(1)}, u32[]{:S(2)}, u32[]{:S(2)}) collective-permute-start(f16[40,768]{1,0:T(8,128)(2,1)S(1)} %fusion.8), channel_id=1, source_target_pairs={{0,2},{1,3},{2,0},{3,1},{4,6},{5,7},{6,4},{7,5},{8,10},{9,11},{10,... | collective-permute-start | bytes 184328 | tf_op jit(solution)/shard_map/ppermute | solution.py:374
  89.6 13.2 %collective-permute-start.25 = (f16[4,40,768]{2,1,0:T(8,128)(2,1)S(1)}, f16[4,40,768]{2,1,0:T(8,128)(2,1)S(1)}, u32[]{:S(2)}, u32[]{:S(2)}) collective-permute-start(f16[4,40,768]{2,1,0:T(8,128)(2,1)S(1)} %pad_maximum_fusion), channel_id=1, source_target_pairs={{0,16},{1,9},{2,18},{3,11},{4,20},{5,13},{6,22},{7,15},{8,24},{9,1... | collective-permute-start | bytes 737288 | tf_op jit(solution)/shard_map/ppermute | solution.py:383
  101.6 6.2 %collective-permute-start.28 = (f16[4,40,768]{2,1,0:T(8,128)(2,1)S(1)}, f16[4,40,768]{2,1,0:T(8,128)(2,1)S(1)}, u32[]{:S(2)}, u32[]{:S(2)}) collective-permute-start(f16[4,40,768]{2,1,0:T(8,128)(2,1)S(1)} %pad_maximum_fusion), channel_id=1, source_target_pairs={{0,8},{1,17},{2,10},{3,19},{4,12},{5,21},{6,14},{7,23},{8,0},{9,25... | collective-permute-start | bytes 737288 | tf_op jit(solution)/shard_map/ppermute | solution.py:383
  102.8 5.7 %collective-permute-start.29 = (f16[4,40,768]{2,1,0:T(8,128)(2,1)S(1)}, f16[4,40,768]{2,1,0:T(8,128)(2,1)S(1)}, u32[]{:S(2)}, u32[]{:S(2)}) collective-permute-start(f16[4,40,768]{2,1,0:T(8,128)(2,1)S(1)} %pad_maximum_fusion), channel_id=1, source_target_pairs={{0,1},{1,0},{2,3},{3,2},{4,5},{5,4},{6,7},{7,6},{8,9},{9,8},{10,11... | collective-permute-start | bytes 737288 | tf_op jit(solution)/shard_map/ppermute | solution.py:374
  102.9 7.6 %collective-permute-start.26 = (f16[4,40,768]{2,1,0:T(8,128)(2,1)S(1)}, f16[4,40,768]{2,1,0:T(8,128)(2,1)S(1)}, u32[]{:S(2)}, u32[]{:S(2)}) collective-permute-start(f16[4,40,768]{2,1,0:T(8,128)(2,1)S(1)} %collective-permute-done.25), channel_id=1, source_target_pairs={{0,8},{1,17},{2,10},{3,19},{4,12},{5,21},{6,14},{7,23},{8,0},{9,25... | collective-permute-start | bytes 737288 | tf_op jit(solution)/shard_map/ppermute | solution.py:383
  105.0 5.4 %collective-permute-start.30 = (f16[4,40,768]{2,1,0:T(8,128)(2,1)S(1)}, f16[4,40,768]{2,1,0:T(8,128)(2,1)S(1)}, u32[]{:S(2)}, u32[]{:S(2)}) collective-permute-start(f16[4,40,768]{2,1,0:T(8,128)(2,1)S(1)} %collective-permute-done.25), channel_id=1, source_target_pairs={{0,1},{1,0},{2,3},{3,2},{4,5},{5,4},{6,7},{7,6},{8,9},{9,8},{10,11... | collective-permute-start | bytes 737288 | tf_op jit(solution)/shard_map/ppermute | solution.py:374
  (25 other events, 275.6 us)

commit v2 on v1

--- a/solution.py
+++ b/solution.py
@@ -16,6 +16,7 @@
 f16 = jnp.float16
 HIGHEST = lax.Precision.HIGHEST
 LANES = 128
+NOTE = 32
 
 
 def contract(a, b, dims, precision=None):
@@ -64,21 +65,35 @@
     return total
 
 
-def stats_body(count, step_ref, latent_ref, cot_ref, out_ref):
+def stats_body(
+    count, step_ref, latent_hbm, cot_hbm, out_ref, down_ref, up_ref, latent_ref, cot_ref, sem
+):
     row_count, channels, cols = latent_ref.shape
+    loads = []
+    for number, (source, target) in enumerate(((latent_hbm, latent_ref), (cot_hbm, cot_ref))):
+        for row in range(row_count):
+            load = pltpu.make_async_copy(source.at[row], target.at[row], sem.at[number, row])
+            load.start()
+            loads.append(load)
     member = member_matrix(channels)
     ones = jnp.ones((cols, LANES), bf16)
     tall = jnp.ones((8, cols), bf16)
     sums = jnp.zeros((channels, LANES), f32)
+    for row in range(row_count):
+        loads[row].wait()
+        sums = sums + contract(latent_ref[row], ones, ((1,), (0,)))
+    mean = contract(member, sums, ((1,), (0,)), HIGHEST) / count
     grads = jnp.zeros((8, channels), f32)
     top = jnp.zeros((channels, LANES), f32)
     for row in range(row_count):
-        sums = sums + contract(latent_ref[row], ones, ((1,), (0,)))
+        loads[row_count + row].wait()
         grads = grads + contract(tall, cot_ref[row], ((1,), (1,)))
         size = jnp.abs(cot_ref[row].astype(f32))
         for start in range(0, cols, LANES):
             top = jnp.maximum(top, size[:, start : start + LANES])
-    mean = contract(member, sums, ((1,), (0,)), HIGHEST) / count
+    for ref, row in ((down_ref, row_count - 1), (up_ref, 0)):
+        ref[0] = cot_ref[row]
+        ref[1] = latent_ref[row]
     squares = jnp.zeros((channels, LANES), f32)
     for row in range(row_count):
         centered = latent_ref[row].astype(f32) - mean[:, :1]
@@ -97,26 +112,30 @@
     return parts[0]
 
 
-def merge_body(count, total, *refs):
-    out_ref = refs[-1]
-    parts = [ref[...] for ref in refs[:-1]]
+def merge_body(count, total, parts, *refs):
+    refs, outs = refs[:parts], refs[parts:]
+    parts = [ref[...] for ref in refs]
     mean = tree_sum([part[0:1] for part in parts]) / len(parts)
     squares = tree_sum([part[1:2] + count * (part[0:1] - mean) ** 2 for part in parts])
+    if total:
+        squares = lax.rsqrt(squares / total + epsilon)
     grads = tree_sum([part[2:3] for part in parts])
     largest = functools.reduce(jnp.maximum, [part[3:4] for part in parts])
-    if total:
-        squares = lax.rsqrt(squares / total + epsilon)
+    step = parts[0][4:5]
     shape = parts[0].shape
-    out_ref[...] = rows_of(
-        *[
-            jnp.broadcast_to(row, shape)
-            for row in (mean, squares, grads, largest, parts[0][4:5])
-        ]
-    )
+    rows = (mean, squares, grads, largest, step)
+    outs[0][...] = rows_of(*[jnp.broadcast_to(row, shape) for row in rows])
+    if len(outs) > 1:
+        table_ref = outs[1]
+        channels = shape[1]
+        table_ref[...] = jnp.zeros(table_ref.shape, f32)
+        table_ref[0:1, :channels] = grads
+        table_ref[0:1, channels : channels + NOTE] = step[:, :NOTE]
+        table_ref[0:1, channels + NOTE : channels + 2 * NOTE] = largest[:, :NOTE]
 
 
 def column_values(stats_ref, gain_ref, bias_ref):
-    channels = gain_ref.shape[1]
+    channels = gain_ref.shape[0]
     shape = (8, channels)
     table = rows_of(
         jnp.broadcast_to(stats_ref[0:1], shape),
@@ -161,10 +180,10 @@
 
 def put_gradient(taps_ref, cot_ref, above_ref, below_ref):
     row_count = cot_ref.shape[0]
-    put_taps(taps_ref, 0, above_ref[...], True)
+    put_taps(taps_ref, 0, above_ref[0], True)
     for row in range(row_count):
         put_taps(taps_ref, row + 1, cot_ref[row], True)
-    put_taps(taps_ref, row_count + 1, below_ref[...], True)
+    put_taps(taps_ref, row_count + 1, below_ref[0], True)
 
 
 def weight_body(
@@ -229,7 +248,7 @@
     values = column_values(stats_ref, gain_ref, bias_ref)
     for place, ref, end in ((0, above_ref, 0), (row_count + 1, below_ref, 1)):
         keep = ends_ref[end].astype(f32)
-        put_taps(taps_ref, place, (activate(ref[...], values).astype(f32) * keep).astype(bf16), False)
+        put_taps(taps_ref, place, (activate(ref[1], values).astype(f32) * keep).astype(bf16), False)
     for row in range(row_count):
         put_taps(taps_ref, row + 1, act_ref[:, row * cols : (row + 1) * cols], False)
     for tap_row in range(3):
@@ -246,12 +265,10 @@
 
 
 def backward_body(
-    latent_ref, cot_ref, above_ref, below_ref, stats_ref, gain_ref, bias_ref, weight_ref,
-    grad_ref, sums_ref, taps_ref, flat_ref,
+    latent_ref, taps_ref, stats_ref, gain_ref, bias_ref, weight_ref, grad_ref, sums_ref, flat_ref
 ):
     row_count, channels, cols = latent_ref.shape
     values = column_values(stats_ref, gain_ref, bias_ref)
-    put_gradient(taps_ref, cot_ref, above_ref, below_ref)
     for tap_row in range(3):
         flat_ref[tap_row] = jnp.concatenate([weight_ref[tap_row, j] for j in range(3)], axis=1)
     first = jnp.zeros((channels, LANES), f32)
@@ -332,33 +349,56 @@
 
 
 def power_of_two(top, factor, spread, gain_ref, bias_ref, shape):
-    reach = spread * jnp.max(jnp.abs(gain_ref[...]), axis=1, keepdims=True) + jnp.max(
-        jnp.abs(bias_ref[...]), axis=1, keepdims=True
-    )
-    bound = jnp.maximum(jnp.max(top, axis=1, keepdims=True) * reach * factor, 1e-30)
+    gain = jnp.max(jnp.abs(gain_ref[...][None, :]), axis=1, keepdims=True)
+    bias = jnp.max(jnp.abs(bias_ref[...][None, :]), axis=1, keepdims=True)
+    reach = spread * gain + bias
+    bound = jnp.maximum(top * reach * factor, 1e-30)
     power = jnp.clip(jnp.floor(jnp.log2(30000.0 / bound)), -100.0, 100.0)
     scale = jnp.broadcast_to(jnp.exp2(power), shape)
     return rows_of(scale, 1.0 / scale)
 
 
-def scale_body(factor, spread, gain_ref, bias_ref, *refs):
-    parts, (scale_ref, steps_ref) = refs[:-2], refs[-2:]
-    top = functools.reduce(jnp.maximum, [ref[3:4] for ref in parts])
-    scale_ref[...] = power_of_two(top, factor, spread, gain_ref, bias_ref, scale_ref.shape)
-    steps_ref[...] = rows_of(*[jnp.broadcast_to(ref[4:5], steps_ref.shape) for ref in parts])
-
-
-def gather_body(sums_ref, partner_ref, *refs):
-    parts, out_ref = refs[:-1], refs[-1]
-    top = functools.reduce(jnp.maximum, [ref[3:4] for ref in parts])
-    rows = [sums_ref[0:1] + partner_ref[0:1], sums_ref[1:2] + partner_ref[1:2], top]
-    rows += [ref[2:3] for ref in parts]
+def largest_note(table, channels):
+    return jnp.max(
+        jnp.max(table[:, channels + NOTE : channels + 2 * NOTE], axis=1, keepdims=True),
+        axis=0,
+        keepdims=True,
+    )
+
+
+def spread_body(
+    known, masks, factor, spread, where_ref, gain_ref, bias_ref, mine_ref, other_ref,
+    table_ref, scale_ref, steps_ref,
+):
+    channels = gain_ref.shape[0]
+    table_ref[...] = mine_ref[...]
+    for core in range(2):
+
+        @pl.when(where_ref[0] == core)
+        def _():
+            for row in known[core]:
+                at = row ^ masks[core]
+                table_ref[at : at + 1] = other_ref[row : row + 1]
+
+    table = table_ref[...]
+    scale_ref[...] = power_of_two(
+        largest_note(table, channels), factor, spread, gain_ref, bias_ref, scale_ref.shape
+    )
+    steps_ref[...] = jnp.broadcast_to(table[:, channels : channels + 1], steps_ref.shape)
+
+
+def gather_body(images, sums_ref, partner_ref, table_ref, out_ref):
+    channels = sums_ref.shape[1]
+    table = table_ref[...]
+    rows = [sums_ref[0:1] + partner_ref[0:1], sums_ref[1:2] + partner_ref[1:2]]
+    rows += [largest_note(table, channels)]
+    rows += [table[i : i + 1, :channels] for i in range(images)]
     out_ref[...] = rows_of(*[jnp.broadcast_to(row, out_ref.shape) for row in rows])
 
 
 def total_body(factor, spread, gain_ref, bias_ref, *refs):
     parts, (total_ref, scale_ref) = refs[:-2], refs[-2:]
-    top = functools.reduce(jnp.maximum, [ref[2:3] for ref in parts])
+    top = functools.reduce(jnp.maximum, [ref[2:3, 0:1] for ref in parts])
     scale_ref[...] = power_of_two(top, factor, spread, gain_ref, bias_ref, scale_ref.shape)
     total_ref[...] = tree_sum([ref[...] for ref in parts])
 
@@ -408,8 +448,7 @@
 
     lat = latent.transpose(0, 1, 3, 2)[0]
     cot = cotangent.transpose(0, 1, 3, 2)[0]
-    gain = norm_gain.reshape(1, channels)
-    bias = norm_bias.reshape(1, channels)
+    gain, bias = norm_gain, norm_bias
     smem = pl.BlockSpec(memory_space=pltpu.SMEM)
     vmem = pl.BlockSpec(memory_space=pltpu.VMEM)
     small = jax.ShapeDtypeStruct((8, channels), f32)
@@ -421,26 +460,38 @@
     taps = pltpu.VMEM((3 * channels, (row_count + 2) * col_count), bf16)
     flat = pltpu.VMEM((3, channels, 3 * channels), bf16)
 
-    cot_above = lax.ppermute(cot[row_count - 1], "space", down)
-    cot_below = lax.ppermute(cot[0], "space", up)
-    lat_above = lax.ppermute(lat[row_count - 1], "space", down)
-    lat_below = lax.ppermute(lat[0], "space", up)
-    own = call(
+    edge = jax.ShapeDtypeStruct((2, channels, col_count), bf16)
+    anywhere = pl.BlockSpec(memory_space=pl.ANY)
+    slab = pltpu.VMEM((row_count, channels, col_count), bf16)
+    own, edge_down, edge_up = call(
         functools.partial(stats_body, local_count),
-        small,
+        (small, edge, edge),
         (timesteps, lat, cot),
-        specs=(smem, vmem, vmem),
+        specs=(smem, anywhere, anywhere),
+        scratch=(slab, slab, pltpu.SemaphoreType.DMA((2, row_count))),
         moved=2 * lat.size * 2,
         flops=positions * channels * 60,
+        limit=12 << 20,
     )
     partner = swap_space(own, 1)
-    pair = call(functools.partial(merge_body, local_count, None), small, (own, partner))
+    above = lax.ppermute(edge_down, "space", down)
+    below = lax.ppermute(edge_up, "space", up)
+    table_shape = jax.ShapeDtypeStruct((-(-image_count // 8) * 8, channels + 2 * NOTE), f32)
+    pair, table = call(
+        functools.partial(merge_body, local_count, None, 2),
+        (small, table_shape),
+        (own, partner),
+        limit=4 << 20,
+    )
     parts = [pair]
     for mask in range(1, zones):
         parts.append(swap_space(pair, 2 * mask))
     stats = call(
-        functools.partial(merge_body, 2 * local_count, total_count), small, tuple(parts)
-    )
+        functools.partial(merge_body, 2 * local_count, total_count, zones),
+        (small,),
+        tuple(parts),
+        limit=4 << 20,
+    )[0]
 
     orders = [list(range(bits)), list(range(bits))[::-1]]
 
@@ -454,44 +505,60 @@
     mine, other = rest_index(core), rest_index(1 - core)
     where = jnp.stack([core, mine, other, zone_index]).astype(jnp.int32)
     share_shape = jax.ShapeDtypeStruct((blocks // 2, zones, height, width), f32)
-    act, near, far = call(
+    taps_shape = jax.ShapeDtypeStruct((3 * channels, (row_count + 2) * col_count), bf16)
+    act, near, far, grad_taps = call(
         functools.partial(weight_body, (blocks, zones, height, width)),
-        (jax.ShapeDtypeStruct((channels, positions), bf16), share_shape, share_shape),
-        (where, lat, cot, cot_above, cot_below, stats, gain, bias),
+        (jax.ShapeDtypeStruct((channels, positions), bf16), share_shape, share_shape, taps_shape),
+        (where, lat, cot, above, below, stats, gain, bias),
         specs=(smem,) + (vmem,) * 7,
-        scratch=(taps,),
         flops=flops,
         moved=8 * lat.size,
-    )
-    everyone = [pair]
-    for mask in range(1, image_count):
-        everyone.append(swap_image(pair, (mask, mask)))
+        limit=20 << 20,
+    )
     factor, spread = float(positions * slab_count * image_count), math.sqrt(per_group)
     scales_shape = jax.ShapeDtypeStruct((8, LANES), f32)
-    scales, steps = call(
-        functools.partial(scale_body, factor, spread),
-        (scales_shape, jax.ShapeDtypeStruct((-(-image_count // 8) * 8, channels), f32)),
-        (gain, bias, *everyone),
-    )
-    scale, back = scales[0, 0], scales[1, 0]
+    steps_shape = jax.ShapeDtypeStruct((table_shape.shape[0], channels), f32)
+    known = ([0], [0])
+    scales = []
+    for step in range(bits):
+        masks = (1 << orders[0][step], 1 << orders[1][step])
+        arrived = swap_image(table, masks)
+        table, found, steps = call(
+            functools.partial(spread_body, known, masks, factor, spread),
+            (table_shape, scales_shape, steps_shape),
+            (where, gain, bias, table, arrived),
+            specs=(smem,) + (vmem,) * 4,
+            limit=4 << 20,
+        )
+        scales.append((found[0, 0], found[1, 0]))
+        known = tuple(rows + [row ^ mask for row in rows] for rows, mask in zip(known, masks))
 
     grad, sums = call(
         backward_body,
         (jax.ShapeDtypeStruct((row_count, channels, col_count), f32), small),
-        (lat, cot, cot_above, cot_below, stats, gain, bias, conv_weight),
-        scratch=(taps, flat),
+        (lat, grad_taps, stats, gain, bias, conv_weight),
+        scratch=(flat,),
         flops=flops,
         moved=8 * lat.size,
+        limit=20 << 20,
     )
     sums_partner = swap_space(sums, 1)
     message = jax.ShapeDtypeStruct((-(-(3 + image_count) // 8) * 8, channels), f32)
-    gathered = [call(gather_body, message, (sums, sums_partner, *everyone))]
+    gathered = [
+        call(
+            functools.partial(gather_body, image_count),
+            message,
+            (sums, sums_partner, table),
+            limit=4 << 20,
+        )
+    ]
     for mask in range(1, zones):
         gathered.append(swap_space(gathered[0], 2 * mask))
     totals, line_scales = call(
         functools.partial(total_body, factor, spread),
         (message, scales_shape),
         (gain, bias, *gathered),
+        limit=4 << 20,
     )
     line_scale, line_back = line_scales[0, 0], line_scales[1, 0]
 
@@ -502,6 +569,7 @@
     keeping = near[:middle] + near_in
     for step in range(bits):
         masks = (1 << orders[0][step], 1 << orders[1][step])
+        scale, back = scales[step]
         arrived = swap_image((sending * scale).astype(f16), masks)
         total = keeping + arrived.astype(f32) * back
         middle = total.shape[0] // 2
@@ -534,7 +602,6 @@
 
     def place(cells, at, before):
         table = jnp.stack(at + zone_spots).astype(jnp.int32)
-        anywhere = pl.BlockSpec(memory_space=pl.ANY)
         count = len(cells)
         return pl.pallas_call(
             functools.partial(place_body, (zones, height, width), count),
@@ -547,7 +614,7 @@
                 pltpu.SemaphoreType.DMA((count,)),
             ],
             input_output_aliases={1 + count: 0} if before else {},
-            compiler_params=pltpu.CompilerParams(vmem_limit_bytes=40 << 20),
+            compiler_params=pltpu.CompilerParams(vmem_limit_bytes=12 << 20),
             cost_estimate=pl.CostEstimate(
                 flops=0,
                 bytes_accessed=8 * count * zones * height * width,
@@ -572,15 +639,17 @@
         functools.partial(time_body, image_count),
         jax.ShapeDtypeStruct((channels, channels), f32),
         (embedding.astype(f32), totals),
+        limit=4 << 20,
     )
     block_out = call(
         conv_body,
         jax.ShapeDtypeStruct((row_count, channels, col_count), bf16),
-        (ends, act, lat, lat_above, lat_below, stats, gain, bias, conv_weight, extra),
+        (ends, act, lat, above, below, stats, gain, bias, conv_weight, extra),
         specs=(smem,) + (vmem,) * 9,
         scratch=(taps, flat),
         flops=flops,
         moved=8 * lat.size,
+        limit=20 << 20,
     )
     latent_grad = call(
         functools.partial(latent_body, total_count),
@@ -588,6 +657,7 @@
         (grad, lat, cot, stats, totals),
         flops=lat.size * 20,
         moved=10 * lat.size,
+        limit=12 << 20,
     )
 
     block_out = block_out[None].transpose(0, 1, 3, 2)

time: 118 us -> 127 us (1.076)
  starting transfers between devices: 39 us -> 32.4 us
  waiting for transfers between devices: 20.1 us -> 25.8 us
  Pallas kernels: 32.4 us -> 37.5 us
  local copies, waits for them, and re-layouts: 11.1 us -> 13.7 us
  other arithmetic: 12.5 us -> 14.6 us
    pallas_call x11 -> x12, Pallas kernels: 28.1 us -> 33.3 us  [call(): pl.pallas_call(body, out_shape=tuple(outs) if many else outs, in_specs=li...]
    unnamed x34 -> x30, local copies, waits for them, and re-layouts: 5.57 us -> 10.2 us
    ppermute x4 -> x2, starting transfers between devices: 7.81 us -> 4.54 us  [the longest x1 3.26 us: slab_program(): above = lax.ppermute(edge_down, 'space', down)]
    ppermute x8 -> x7, waiting for transfers between devices: 7.12 us -> 10.1 us  [swap_image(): return lax.ppermute(cells, ('dp', 'space'), pairs)]
    squeeze x2 -> x0, local copies, waits for them, and re-layouts: 2.95 us -> none  [the longest x1 2.06 us: slab_program(): cot_below = lax.ppermute(cot[0], 'space', up)]
    ppermute x20, waiting for transfers between devices: 13 us -> 15.7 us  [swap_space(): return lax.ppermute(cells, 'space', [(i, i ^ mask) for i in range(count)])]
    ppermute x8 -> x7, starting transfers between devices: 9.65 us -> 7.66 us  [swap_image(): return lax.ppermute(cells, ('dp', 'space'), pairs)]
    ppermute x20, starting transfers between devices: 21.5 us -> 20.1 us  [swap_space(): return lax.ppermute(cells, 'space', [(i, i ^ mask) for i in range(count)])]
  transfers between devices with their start and end apart: 32 -> 29, of which waited for: 13 -> 12; matrix products, arithmetic and copies ran while one was open for 12% -> 10% of each run, Pallas kernels for 20% -> 18%
where the time goes in v2:
time: 127 us; the launch traced here: 126 us
  Pallas kernels  37.5 us (30%)
  starting transfers between devices  32.4 us (26%)
  waiting for transfers between devices  25.8 us (20%)
  other arithmetic  14.6 us (11%)
  local copies, waits for them, and re-layouts  13.7 us (11%)
  between operations  1.89 us (1%)
    pallas_call x12, Pallas kernels, call(): pl.pallas_call(body, out_shape=tuple(outs) if many else outs, in_specs=li...  33.3 us
    ppermute x20, starting transfers between devices, swap_space(): return lax.ppermute(cells, 'space', [(i, i ^ mask) for i in range(count)])  20.1 us
    ppermute x20, waiting for transfers between devices, swap_space(): return lax.ppermute(cells, 'space', [(i, i ^ mask) for i in range(count)])  15.7 us
    unnamed x30, local copies, waits for them, and re-layouts  10.2 us
    ppermute x7, waiting for transfers between devices, swap_image(): return lax.ppermute(cells, ('dp', 'space'), pairs)  10.1 us
    ppermute x7, starting transfers between devices, swap_image(): return lax.ppermute(cells, ('dp', 'space'), pairs)  7.66 us
    mul x8, other arithmetic, place(): piece.astype(f32) * line_back  5.71 us
    pallas_call x2, Pallas kernels, place(): pl.pallas_call(functools.partial(place_body, (zones, height, width), coun...  4.25 us
  transfers between devices with their start and end apart: 29, of which 12 were waited for; matrix products, arithmetic and copies ran while one was open for 10% of the time, Pallas kernels for 18%

profile of v2, /device:TPU:0, one launch (start us, length us, event | category | flops | bytes accessed | tf_op | source)
XLA Modules:
  0.0 126.1 jit_solution(15990881311880692812)
XLA Ops:
  4.0 5.5 %shard_map.111 = (f32[8,320]{1,0:T(8,128)S(1)}, bf16[2,320,512]{2,1,0:T(8,128)(2,1)}, bf16[2,320,512]{2,1,0:T(8,128)(2,1)}) custom-call(s32[1]{0:T(128)S(6)} %copy.14.step_ref, bf16[4,320,512]{2,1,0:T(8,128)(2,1)S(1)} %bitcast.62, bf16[4,320,512]{2,1,0:T(8,128)(2,1)S(1)} %bitcast.67), custom_call_target="tpu_custom_call" | custom-call | flops 39321600 | bytes 2621440 | tf_op jit(solution)/shard_map/pallas_call | solution.py:29
  9.5 3.3 %collective-permute-start = (bf16[2,320,512]{2,1,0:T(8,128)(2,1)}, bf16[2,320,512]{2,1,0:T(8,128)(2,1)}, u32[]{:S(2)}, u32[]{:S(2)}) collective-permute-start(bf16[2,320,512]{2,1,0:T(8,128)(2,1)} %get-tuple-element.22), channel_id=1, source_target_pairs={{0,1},{1,2},{2,3},{3,4},{4,5},{5,6},{6,7},{8,9},{9,10},{10,11},{11... | collective-permute-start | bytes 1966088 | tf_op jit(solution)/shard_map/ppermute | solution.py:477
  14.1 2.5 %collective-permute-start.2 = (f32[8,320]{1,0:T(8,128)S(1)}, f32[8,320]{1,0:T(8,128)S(1)}, u32[]{:S(2)}, u32[]{:S(2)}) collective-permute-start(f32[8,320]{1,0:T(8,128)S(1)} %get-tuple-element.24.refs_0_), channel_id=1, source_target_pairs={{0,1},{1,0},{2,3},{3,2},{4,5},{5,4},{6,7},{7,6},{8,9},{9,8},{10,11... | collective-permute-start | bytes 30728 | tf_op jit(solution)/shard_map/ppermute | solution.py:414
  16.6 1.8 %collective-permute-done.2.refs_1_ = f32[8,320]{1,0:T(8,128)S(1)} collective-permute-done((f32[8,320]{1,0:T(8,128)S(1)}, f32[8,320]{1,0:T(8,128)S(1)}, u32[]{:S(2)}, u32[]{:S(2)}) %collective-permute-start.2) | collective-permute-done | bytes 10272 | tf_op jit(solution)/shard_map/ppermute | solution.py:414
  18.5 3.0 %collective-permute-start.5 = (f32[8,320]{1,0:T(8,128)S(1)}, f32[8,320]{1,0:T(8,128)S(1)}, u32[]{:S(2)}, u32[]{:S(2)}) collective-permute-start(f32[8,320]{1,0:T(8,128)S(1)} %get-tuple-element.25.refs_0_), channel_id=1, source_target_pairs={{0,6},{1,7},{2,4},{3,5},{4,2},{5,3},{6,0},{7,1},{8,14},{9,15},{10,... | collective-permute-start | bytes 30728 | tf_op jit(solution)/shard_map/ppermute | solution.py:414
  23.0 6.5 %collective-permute-done.5.refs_3_ = f32[8,320]{1,0:T(8,128)S(1)} collective-permute-done((f32[8,320]{1,0:T(8,128)S(1)}, f32[8,320]{1,0:T(8,128)S(1)}, u32[]{:S(2)}, u32[]{:S(2)}) %collective-permute-start.5) | collective-permute-done | bytes 10272 | tf_op jit(solution)/shard_map/ppermute | solution.py:414
  29.5 7.8 %shard_map.114 = (bf16[320,2048]{1,0:T(8,128)(2,1)S(1)}, f32[4,4,40,768]{3,2,1,0:T(8,128)S(1)}, f32[4,4,40,768]{3,2,1,0:T(8,128)S(1)}, bf16[960,3072]{1,0:T(8,128)(2,1)S(1)}) custom-call(s32[4]{0:T(128)S(1)} %pad_add_fusion.where_ref, bf16[4,320,512]{2,1,0:T(8,128)(2,1)S(1)} %bitcast.63, bf16[4,320,512]{2,1,0:T(8,128)(2,1)S(1)} %bitcast.68, ...), custom_call_target="tpu_custom_call" | custom-call | flops 3774873600 | bytes 5242880 | tf_op jit(solution)/shard_map/pallas_call | solution.py:29
  37.3 2.5 %copy-done.10 = bf16[960,3072]{1,0:T(8,128)(2,1)} copy-done((bf16[960,3072]{1,0:T(8,128)(2,1)}, bf16[960,3072]{1,0:T(8,128)(2,1)S(1)}, u32[]{:S(2)}) %copy-start.10) | copy-done | bytes 5898264
  43.9 1.9 %collective-permute-done.6.other_ref = f32[8,384]{1,0:T(8,128)S(1)} collective-permute-done((f32[8,384]{1,0:T(8,128)S(1)}, f32[8,384]{1,0:T(8,128)S(1)}, u32[]{:S(2)}, u32[]{:S(2)}) %collective-permute-start.6) | collective-permute-done | bytes 12320 | tf_op jit(solution)/shard_map/ppermute | solution.py:423
  49.2 3.0 %multiply_convert_fusion = f16[2,4,40,768]{3,2,1,0:T(8,128)(2,1)} fusion(f32[2,4,40,768]{3,2,1,0:T(8,128)} %collective-permute-done.13, f32[4,4,40,768]{3,2,1,0:T(8,128)} %copy-done.5, f32[]{:T(128)} %bitcast.21), kind=kLoop, calls=%fused_computation.2 | loop fusion | flops 737280 | bytes 2457604 | tf_op jit(solution)/shard_map/convert_element_type | solution.py:573
  56.4 2.7 %copy-done.11 = bf16[960,3072]{1,0:T(8,128)(2,1)S(1)} copy-done((bf16[960,3072]{1,0:T(8,128)(2,1)S(1)}, bf16[960,3072]{1,0:T(8,128)(2,1)}, u32[]{:S(2)}) %copy-start.11) | copy-done | bytes 5898264
  59.1 6.3 %shard_map.118 = (f32[4,320,512]{2,1,0:T(8,128)S(1)}, f32[8,320]{1,0:T(8,128)S(1)}) custom-call(bf16[4,320,512]{2,1,0:T(8,128)(2,1)S(1)} %bitcast.64, bf16[960,3072]{1,0:T(8,128)(2,1)S(1)} %copy-done.11, f32[8,320]{1,0:T(8,128)S(1)} %shard_map.113.stats_ref, f32[320]{0:T(512)S(1)} %copy-done.7, f32[320]{0:T(512)S(1)} %copy-done.8, ...), custom_call_target="tpu_custom_call" | custom-call | flops 3774873600 | bytes 5242880 | tf_op jit(solution)/shard_map/pallas_call | solution.py:29
  66.6 2.1 %collective-permute-start.10 = (f32[8,320]{1,0:T(8,128)S(1)}, f32[8,320]{1,0:T(8,128)S(1)}, u32[]{:S(2)}, u32[]{:S(2)}) collective-permute-start(f32[8,320]{1,0:T(8,128)S(1)} %shard_map.119.refs_0_), channel_id=1, source_target_pairs={{0,4},{1,5},{2,6},{3,7},{4,0},{5,1},{6,2},{7,3},{8,12},{9,13},{10,... | collective-permute-start | bytes 30728 | tf_op jit(solution)/shard_map/ppermute | solution.py:414
  68.8 2.2 %collective-permute-start.9 = (f32[8,320]{1,0:T(8,128)S(1)}, f32[8,320]{1,0:T(8,128)S(1)}, u32[]{:S(2)}, u32[]{:S(2)}) collective-permute-start(f32[8,320]{1,0:T(8,128)S(1)} %shard_map.119.refs_0_), channel_id=1, source_target_pairs={{0,2},{1,3},{2,0},{3,1},{4,6},{5,7},{6,4},{7,5},{8,10},{9,11},{10,... | collective-permute-start | bytes 30728 | tf_op jit(solution)/shard_map/ppermute | solution.py:414
  71.0 2.0 %multiply_add_fusion = f32[2,4,40,768]{3,2,1,0:T(8,128)S(1)} fusion(f16[2,4,40,768]{3,2,1,0:T(8,128)(2,1)S(1)} %collective-permute-done.14, f32[2,4,40,768]{3,2,1,0:T(8,128)} %collective-permute-done.12, f32[4,4,40,768]{3,2,1,0:T(8,128)S(1)} %copy-done.6, f32[]{:T(128)} %bitcast.22), kind=kLoop, calls=%fused_computation.1 | loop fusion | flops 983040 | bytes 3440644 | tf_op jit(solution)/shard_map/add | solution.py:574
  75.2 4.9 %collective-permute-done.15 = f16[1,4,40,768]{3,2,1,0:T(8,128)(2,1)S(1)} collective-permute-done((f16[1,4,40,768]{3,2,1,0:T(8,128)(2,1)S(1)}, f16[1,4,40,768]{3,2,1,0:T(8,128)(2,1)S(1)}, u32[]{:S(2)}, u32[]{:S(2)}) %collective-permute-start.15) | collective-permute-done | bytes 245792 | tf_op jit(solution)/shard_map/ppermute | solution.py:423
  83.0 2.0 %collective-permute-start.17 = (f16[40,768]{1,0:T(8,128)(2,1)S(1)}, f16[40,768]{1,0:T(8,128)(2,1)S(1)}, u32[]{:S(2)}, u32[]{:S(2)}) collective-permute-start(f16[40,768]{1,0:T(8,128)(2,1)S(1)} %get-tuple-element.44), channel_id=1, source_target_pairs={{0,4},{1,5},{2,6},{3,7},{4,0},{5,1},{6,2},{7,3},{8,12},{9,13},{10,... | collective-permute-start | bytes 184328 | tf_op jit(solution)/shard_map/ppermute | solution.py:414
  90.6 2.1 %collective-permute-start.21 = (f16[40,768]{1,0:T(8,128)(2,1)S(1)}, f16[40,768]{1,0:T(8,128)(2,1)S(1)}, u32[]{:S(2)}, u32[]{:S(2)}) collective-permute-start(f16[40,768]{1,0:T(8,128)(2,1)S(1)} %fusion.8), channel_id=1, source_target_pairs={{0,6},{1,7},{2,4},{3,5},{4,2},{5,3},{6,0},{7,1},{8,14},{9,15},{10,... | collective-permute-start | bytes 184328 | tf_op jit(solution)/shard_map/ppermute | solution.py:414
  92.7 2.4 %collective-permute-start.19 = (f16[40,768]{1,0:T(8,128)(2,1)S(1)}, f16[40,768]{1,0:T(8,128)(2,1)S(1)}, u32[]{:S(2)}, u32[]{:S(2)}) collective-permute-start(f16[40,768]{1,0:T(8,128)(2,1)S(1)} %fusion.8), channel_id=1, source_target_pairs={{0,2},{1,3},{2,0},{3,1},{4,6},{5,7},{6,4},{7,5},{8,10},{9,11},{10,... | collective-permute-start | bytes 184328 | tf_op jit(solution)/shard_map/ppermute | solution.py:414
  98.7 7.7 %shard_map.117 = bf16[4,320,512]{2,1,0:T(8,128)(2,1)} custom-call(s32[2]{0:T(128)S(1)} %add_convert_fusion.ends_ref, bf16[320,2048]{1,0:T(8,128)(2,1)S(1)} %copy-done.13, bf16[4,320,512]{2,1,0:T(8,128)(2,1)S(1)} %bitcast.65, bf16[2,320,512]{2,1,0:T(8,128)(2,1)} %collective-permute-done.above_ref, bf16[2,320,512]{2,1,0:T(8,128)(2,1)} %collective-permute-done.1.below_ref, ...), custom_call_target="tpu_custom_call" | custom-call | flops 3774873600 | bytes 5242880 | tf_op jit(solution)/shard_map/pallas_call | solution.py:29
  107.5 2.5 %shard_map.121 = bf16[4,320,512]{2,1,0:T(8,128)(2,1)} custom-call(f32[4,320,512]{2,1,0:T(8,128)S(1)} %get-tuple-element.31.grad_ref, bf16[4,320,512]{2,1,0:T(8,128)(2,1)S(1)} %bitcast.66, bf16[4,320,512]{2,1,0:T(8,128)(2,1)S(1)} %bitcast.69, f32[8,320]{1,0:T(8,128)S(1)} %shard_map.113.stats_ref, f32[8,320]{1,0:T(8,128)S(1)} %get-tuple-element.34.sums_ref.total_ref), custom_call_target="tpu_custom_call" | custom-call | flops 13107200 | bytes 6553600 | tf_op jit(solution)/shard_map/pallas_call | solution.py:29
  114.1 2.1 %collective-permute-done.25 = f16[4,40,768]{2,1,0:T(8,128)(2,1)S(1)} collective-permute-done((f16[4,40,768]{2,1,0:T(8,128)(2,1)S(1)}, f16[4,40,768]{2,1,0:T(8,128)(2,1)S(1)}, u32[]{:S(2)}, u32[]{:S(2)}) %collective-permute-start.25) | collective-permute-done | bytes 245792 | tf_op jit(solution)/shard_map/ppermute | solution.py:423
  120.3 2.5 %shard_map.122.refs_2_ = f32[9,320,320]{2,1,0:T(8,128)} custom-call(s32[10]{0:T(128)S(1)} %stack.108.places_ref, f32[4,40,768]{2,1,0:T(8,128)S(1)} %convert_multiply_fusion.5.refs_0_, f32[4,40,768]{2,1,0:T(8,128)S(1)} %convert_multiply_fusion.4.refs_1_, f32[4,40,768]{2,1,0:T(8,128)S(1)} %convert_multiply_fusion.3.refs_2_, ...), custom_call_target="tpu_custom_call" | custom-call | bytes 5898240 | tf_op jit(solution)/shard_map/pallas_call | solution.py:606
  124.2 1.7 %shard_map.123 = f32[9,320,320]{2,1,0:T(8,128)} custom-call(s32[6]{0:T(128)S(1)} %stack.96.places_ref, f32[4,40,768]{2,1,0:T(8,128)S(1)} %convert_multiply_fusion.7.refs_0_, f32[4,40,768]{2,1,0:T(8,128)S(1)} %convert_multiply_fusion.6.refs_1_, f32[9,320,320]{2,1,0:T(8,128)} %shard_map.122.refs_2_), custom_call_target="tpu_custom_call", output_to_operand_aliasing={{}: (3, {})} | custom-call | bytes 1966080 | tf_op jit(solution)/shard_map/pallas_call | solution.py:606
  (107 shorter events, 43.4 us)
Async XLA Ops:
  9.5 20.0 %collective-permute-start = (bf16[2,320,512]{2,1,0:T(8,128)(2,1)}, bf16[2,320,512]{2,1,0:T(8,128)(2,1)}, u32[]{:S(2)}, u32[]{:S(2)}) collective-permute-start(bf16[2,320,512]{2,1,0:T(8,128)(2,1)} %get-tuple-element.22), channel_id=1, source_target_pairs={{0,1},{1,2},{2,3},{3,4},{4,5},{5,6},{6,7},{8,9},{9,10},{10,11},{11... | collective-permute-start | bytes 1966088 | tf_op jit(solution)/shard_map/ppermute | solution.py:477
  12.8 16.7 %collective-permute-start.1 = (bf16[2,320,512]{2,1,0:T(8,128)(2,1)}, bf16[2,320,512]{2,1,0:T(8,128)(2,1)}, u32[]{:S(2)}, u32[]{:S(2)}) collective-permute-start(bf16[2,320,512]{2,1,0:T(8,128)(2,1)} %get-tuple-element.23), channel_id=1, source_target_pairs={{1,0},{2,1},{3,2},{4,3},{5,4},{6,5},{7,6},{9,8},{10,9},{11,10},{12... | collective-permute-start | bytes 1966088 | tf_op jit(solution)/shard_map/ppermute | solution.py:478
  18.5 10.9 %collective-permute-start.5 = (f32[8,320]{1,0:T(8,128)S(1)}, f32[8,320]{1,0:T(8,128)S(1)}, u32[]{:S(2)}, u32[]{:S(2)}) collective-permute-start(f32[8,320]{1,0:T(8,128)S(1)} %get-tuple-element.25.refs_0_), channel_id=1, source_target_pairs={{0,6},{1,7},{2,4},{3,5},{4,2},{5,3},{6,0},{7,1},{8,14},{9,15},{10,... | collective-permute-start | bytes 30728 | tf_op jit(solution)/shard_map/ppermute | solution.py:414
  21.5 7.9 %collective-permute-start.4 = (f32[8,320]{1,0:T(8,128)S(1)}, f32[8,320]{1,0:T(8,128)S(1)}, u32[]{:S(2)}, u32[]{:S(2)}) collective-permute-start(f32[8,320]{1,0:T(8,128)S(1)} %get-tuple-element.25.refs_0_), channel_id=1, source_target_pairs={{0,4},{1,5},{2,6},{3,7},{4,0},{5,1},{6,2},{7,3},{8,12},{9,13},{10,... | collective-permute-start | bytes 30728 | tf_op jit(solution)/shard_map/ppermute | solution.py:414
  21.6 7.9 %collective-permute-start.3 = (f32[8,320]{1,0:T(8,128)S(1)}, f32[8,320]{1,0:T(8,128)S(1)}, u32[]{:S(2)}, u32[]{:S(2)}) collective-permute-start(f32[8,320]{1,0:T(8,128)S(1)} %get-tuple-element.25.refs_0_), channel_id=1, source_target_pairs={{0,2},{1,3},{2,0},{3,1},{4,6},{5,7},{6,4},{7,5},{8,10},{9,11},{10,... | collective-permute-start | bytes 30728 | tf_op jit(solution)/shard_map/ppermute | solution.py:414
  42.2 7.0 %collective-permute-start.13 = (f32[2,4,40,768]{3,2,1,0:T(8,128)}, f32[2,4,40,768]{3,2,1,0:T(8,128)}, u32[]{:S(2)}, u32[]{:S(2)}) collective-permute-start(f32[2,4,40,768]{3,2,1,0:T(8,128)} %get-tuple-element.41), channel_id=1, source_target_pairs={{0,1},{1,0},{2,3},{3,2},{4,5},{5,4},{6,7},{7,6},{8,9},{9,8},{10,11... | collective-permute-start | bytes 2949128 | tf_op jit(solution)/shard_map/ppermute | solution.py:414
  43.6 27.4 %collective-permute-start.12 = (f32[2,4,40,768]{3,2,1,0:T(8,128)}, f32[2,4,40,768]{3,2,1,0:T(8,128)}, u32[]{:S(2)}, u32[]{:S(2)}) collective-permute-start(f32[2,4,40,768]{3,2,1,0:T(8,128)} %get-tuple-element.40), channel_id=1, source_target_pairs={{0,1},{1,0},{2,3},{3,2},{4,5},{5,4},{6,7},{7,6},{8,9},{9,8},{10,11... | collective-permute-start | bytes 2949128 | tf_op jit(solution)/shard_map/ppermute | solution.py:414
  47.1 6.8 %collective-permute-start.7 = (f32[8,384]{1,0:T(8,128)S(1)}, f32[8,384]{1,0:T(8,128)S(1)}, u32[]{:S(2)}, u32[]{:S(2)}) collective-permute-start(f32[8,384]{1,0:T(8,128)S(1)} %get-tuple-element.28.mine_ref), channel_id=1, source_target_pairs={{0,16},{1,9},{2,18},{3,11},{4,20},{5,13},{6,22},{7,15},{8,24},{9,1... | collective-permute-start | bytes 36872 | tf_op jit(solution)/shard_map/ppermute | solution.py:423
  52.1 18.9 %collective-permute-start.14 = (f16[2,4,40,768]{3,2,1,0:T(8,128)(2,1)}, f16[2,4,40,768]{3,2,1,0:T(8,128)(2,1)S(1)}, u32[]{:S(2)}, u32[]{:S(2)}) collective-permute-start(f16[2,4,40,768]{3,2,1,0:T(8,128)(2,1)} %multiply_convert_fusion), channel_id=1, source_target_pairs={{0,8},{1,17},{2,10},{3,19},{4,12},{5,21},{6,14},{7,23},{8,0},{9,25... | collective-permute-start | bytes 1474568 | tf_op jit(solution)/shard_map/ppermute | solution.py:423
  66.6 7.8 %collective-permute-start.11 = (f32[8,320]{1,0:T(8,128)S(1)}, f32[8,320]{1,0:T(8,128)S(1)}, u32[]{:S(2)}, u32[]{:S(2)}) collective-permute-start(f32[8,320]{1,0:T(8,128)S(1)} %shard_map.119.refs_0_), channel_id=1, source_target_pairs={{0,6},{1,7},{2,4},{3,5},{4,2},{5,3},{6,0},{7,1},{8,14},{9,15},{10,... | collective-permute-start | bytes 30728 | tf_op jit(solution)/shard_map/ppermute | solution.py:414
  66.6 7.8 %collective-permute-start.10 = (f32[8,320]{1,0:T(8,128)S(1)}, f32[8,320]{1,0:T(8,128)S(1)}, u32[]{:S(2)}, u32[]{:S(2)}) collective-permute-start(f32[8,320]{1,0:T(8,128)S(1)} %shard_map.119.refs_0_), channel_id=1, source_target_pairs={{0,4},{1,5},{2,6},{3,7},{4,0},{5,1},{6,2},{7,3},{8,12},{9,13},{10,... | collective-permute-start | bytes 30728 | tf_op jit(solution)/shard_map/ppermute | solution.py:414
  68.8 5.7 %collective-permute-start.9 = (f32[8,320]{1,0:T(8,128)S(1)}, f32[8,320]{1,0:T(8,128)S(1)}, u32[]{:S(2)}, u32[]{:S(2)}) collective-permute-start(f32[8,320]{1,0:T(8,128)S(1)} %shard_map.119.refs_0_), channel_id=1, source_target_pairs={{0,2},{1,3},{2,0},{3,1},{4,6},{5,7},{6,4},{7,5},{8,10},{9,11},{10,... | collective-permute-start | bytes 30728 | tf_op jit(solution)/shard_map/ppermute | solution.py:414
  73.8 6.3 %collective-permute-start.15 = (f16[1,4,40,768]{3,2,1,0:T(8,128)(2,1)S(1)}, f16[1,4,40,768]{3,2,1,0:T(8,128)(2,1)S(1)}, u32[]{:S(2)}, u32[]{:S(2)}) collective-permute-start(f16[1,4,40,768]{3,2,1,0:T(8,128)(2,1)S(1)} %fusion), channel_id=1, source_target_pairs={{0,16},{1,9},{2,18},{3,11},{4,20},{5,13},{6,22},{7,15},{8,24},{9,1... | collective-permute-start | bytes 737288 | tf_op jit(solution)/shard_map/ppermute | solution.py:423
  81.5 5.1 %collective-permute-start.16 = (f16[40,768]{1,0:T(8,128)(2,1)S(1)}, f16[40,768]{1,0:T(8,128)(2,1)S(1)}, u32[]{:S(2)}, u32[]{:S(2)}) collective-permute-start(f16[40,768]{1,0:T(8,128)(2,1)S(1)} %get-tuple-element.42), channel_id=1, source_target_pairs={{0,2},{1,3},{2,0},{3,1},{4,6},{5,7},{6,4},{7,5},{8,10},{9,11},{10,... | collective-permute-start | bytes 184328 | tf_op jit(solution)/shard_map/ppermute | solution.py:414
  81.6 6.2 %collective-permute-start.18 = (f16[40,768]{1,0:T(8,128)(2,1)S(1)}, f16[40,768]{1,0:T(8,128)(2,1)S(1)}, u32[]{:S(2)}, u32[]{:S(2)}) collective-permute-start(f16[40,768]{1,0:T(8,128)(2,1)S(1)} %get-tuple-element.43), channel_id=1, source_target_pairs={{0,6},{1,7},{2,4},{3,5},{4,2},{5,3},{6,0},{7,1},{8,14},{9,15},{10,... | collective-permute-start | bytes 184328 | tf_op jit(solution)/shard_map/ppermute | solution.py:414
  83.0 6.2 %collective-permute-start.17 = (f16[40,768]{1,0:T(8,128)(2,1)S(1)}, f16[40,768]{1,0:T(8,128)(2,1)S(1)}, u32[]{:S(2)}, u32[]{:S(2)}) collective-permute-start(f16[40,768]{1,0:T(8,128)(2,1)S(1)} %get-tuple-element.44), channel_id=1, source_target_pairs={{0,4},{1,5},{2,6},{3,7},{4,0},{5,1},{6,2},{7,3},{8,12},{9,13},{10,... | collective-permute-start | bytes 184328 | tf_op jit(solution)/shard_map/ppermute | solution.py:414
  90.6 6.1 %collective-permute-start.21 = (f16[40,768]{1,0:T(8,128)(2,1)S(1)}, f16[40,768]{1,0:T(8,128)(2,1)S(1)}, u32[]{:S(2)}, u32[]{:S(2)}) collective-permute-start(f16[40,768]{1,0:T(8,128)(2,1)S(1)} %fusion.8), channel_id=1, source_target_pairs={{0,6},{1,7},{2,4},{3,5},{4,2},{5,3},{6,0},{7,1},{8,14},{9,15},{10,... | collective-permute-start | bytes 184328 | tf_op jit(solution)/shard_map/ppermute | solution.py:414
  92.7 5.3 %collective-permute-start.20 = (f16[40,768]{1,0:T(8,128)(2,1)S(1)}, f16[40,768]{1,0:T(8,128)(2,1)S(1)}, u32[]{:S(2)}, u32[]{:S(2)}) collective-permute-start(f16[40,768]{1,0:T(8,128)(2,1)S(1)} %fusion.8), channel_id=1, source_target_pairs={{0,4},{1,5},{2,6},{3,7},{4,0},{5,1},{6,2},{7,3},{8,12},{9,13},{10,... | collective-permute-start | bytes 184328 | tf_op jit(solution)/shard_map/ppermute | solution.py:414
  92.7 5.3 %collective-permute-start.19 = (f16[40,768]{1,0:T(8,128)(2,1)S(1)}, f16[40,768]{1,0:T(8,128)(2,1)S(1)}, u32[]{:S(2)}, u32[]{:S(2)}) collective-permute-start(f16[40,768]{1,0:T(8,128)(2,1)S(1)} %fusion.8), channel_id=1, source_target_pairs={{0,2},{1,3},{2,0},{3,1},{4,6},{5,7},{6,4},{7,5},{8,10},{9,11},{10,... | collective-permute-start | bytes 184328 | tf_op jit(solution)/shard_map/ppermute | solution.py:414
  98.1 13.3 %collective-permute-start.22 = (f16[4,40,768]{2,1,0:T(8,128)(2,1)S(1)}, f16[4,40,768]{2,1,0:T(8,128)(2,1)S(1)}, u32[]{:S(2)}, u32[]{:S(2)}) collective-permute-start(f16[4,40,768]{2,1,0:T(8,128)(2,1)S(1)} %pad_maximum_fusion), channel_id=1, source_target_pairs={{0,16},{1,9},{2,18},{3,11},{4,20},{5,13},{6,22},{7,15},{8,24},{9,1... | collective-permute-start | bytes 737288 | tf_op jit(solution)/shard_map/ppermute | solution.py:423
  110.0 6.2 %collective-permute-start.25 = (f16[4,40,768]{2,1,0:T(8,128)(2,1)S(1)}, f16[4,40,768]{2,1,0:T(8,128)(2,1)S(1)}, u32[]{:S(2)}, u32[]{:S(2)}) collective-permute-start(f16[4,40,768]{2,1,0:T(8,128)(2,1)S(1)} %pad_maximum_fusion), channel_id=1, source_target_pairs={{0,8},{1,17},{2,10},{3,19},{4,12},{5,21},{6,14},{7,23},{8,0},{9,25... | collective-permute-start | bytes 737288 | tf_op jit(solution)/shard_map/ppermute | solution.py:423
  111.3 5.6 %collective-permute-start.26 = (f16[4,40,768]{2,1,0:T(8,128)(2,1)S(1)}, f16[4,40,768]{2,1,0:T(8,128)(2,1)S(1)}, u32[]{:S(2)}, u32[]{:S(2)}) collective-permute-start(f16[4,40,768]{2,1,0:T(8,128)(2,1)S(1)} %pad_maximum_fusion), channel_id=1, source_target_pairs={{0,1},{1,0},{2,3},{3,2},{4,5},{5,4},{6,7},{7,6},{8,9},{9,8},{10,11... | collective-permute-start | bytes 737288 | tf_op jit(solution)/shard_map/ppermute | solution.py:414
  111.4 8.2 %collective-permute-start.27 = (f16[4,40,768]{2,1,0:T(8,128)(2,1)S(1)}, f16[4,40,768]{2,1,0:T(8,128)(2,1)S(1)}, u32[]{:S(2)}, u32[]{:S(2)}) collective-permute-start(f16[4,40,768]{2,1,0:T(8,128)(2,1)S(1)} %collective-permute-done.22), channel_id=1, source_target_pairs={{0,1},{1,0},{2,3},{3,2},{4,5},{5,4},{6,7},{7,6},{8,9},{9,8},{10,11... | collective-permute-start | bytes 737288 | tf_op jit(solution)/shard_map/ppermute | solution.py:414
  111.9 7.0 %collective-permute-start.23 = (f16[4,40,768]{2,1,0:T(8,128)(2,1)S(1)}, f16[4,40,768]{2,1,0:T(8,128)(2,1)S(1)}, u32[]{:S(2)}, u32[]{:S(2)}) collective-permute-start(f16[4,40,768]{2,1,0:T(8,128)(2,1)S(1)} %collective-permute-done.22), channel_id=1, source_target_pairs={{0,8},{1,17},{2,10},{3,19},{4,12},{5,21},{6,14},{7,23},{8,0},{9,25... | collective-permute-start | bytes 737288 | tf_op jit(solution)/shard_map/ppermute | solution.py:423
  (20 other events, 273.4 us)

commit v3 on v2

--- a/solution.py
+++ b/solution.py
@@ -23,14 +23,16 @@
     return lax.dot_general(a, b, (dims, ((), ())), preferred_element_type=f32, precision=precision)
 
 
-def call(body, outs, args, specs=None, scratch=(), flops=0, moved=0, limit=40 << 20):
+def call(
+    body, outs, args, specs=None, out_specs=None, scratch=(), flops=0, moved=0, limit=40 << 20
+):
     vmem = pl.BlockSpec(memory_space=pltpu.VMEM)
     many = isinstance(outs, (list, tuple))
     return pl.pallas_call(
         body,
         out_shape=tuple(outs) if many else outs,
         in_specs=list(specs) if specs else [vmem] * len(args),
-        out_specs=tuple([vmem] * len(outs)) if many else vmem,
+        out_specs=out_specs or (tuple([vmem] * len(outs)) if many else vmem),
         scratch_shapes=list(scratch),
         compiler_params=pltpu.CompilerParams(vmem_limit_bytes=limit),
         cost_estimate=pl.CostEstimate(flops=flops, bytes_accessed=moved, transcendentals=0),
@@ -65,35 +67,21 @@
     return total
 
 
-def stats_body(
-    count, step_ref, latent_hbm, cot_hbm, out_ref, down_ref, up_ref, latent_ref, cot_ref, sem
-):
+def stats_body(count, step_ref, latent_ref, cot_ref, out_ref):
     row_count, channels, cols = latent_ref.shape
-    loads = []
-    for number, (source, target) in enumerate(((latent_hbm, latent_ref), (cot_hbm, cot_ref))):
-        for row in range(row_count):
-            load = pltpu.make_async_copy(source.at[row], target.at[row], sem.at[number, row])
-            load.start()
-            loads.append(load)
     member = member_matrix(channels)
     ones = jnp.ones((cols, LANES), bf16)
     tall = jnp.ones((8, cols), bf16)
     sums = jnp.zeros((channels, LANES), f32)
-    for row in range(row_count):
-        loads[row].wait()
-        sums = sums + contract(latent_ref[row], ones, ((1,), (0,)))
-    mean = contract(member, sums, ((1,), (0,)), HIGHEST) / count
     grads = jnp.zeros((8, channels), f32)
     top = jnp.zeros((channels, LANES), f32)
     for row in range(row_count):
-        loads[row_count + row].wait()
+        sums = sums + contract(latent_ref[row], ones, ((1,), (0,)))
         grads = grads + contract(tall, cot_ref[row], ((1,), (1,)))
         size = jnp.abs(cot_ref[row].astype(f32))
         for start in range(0, cols, LANES):
             top = jnp.maximum(top, size[:, start : start + LANES])
-    for ref, row in ((down_ref, row_count - 1), (up_ref, 0)):
-        ref[0] = cot_ref[row]
-        ref[1] = latent_ref[row]
+    mean = contract(member, sums, ((1,), (0,)), HIGHEST) / count
     squares = jnp.zeros((channels, LANES), f32)
     for row in range(row_count):
         centered = latent_ref[row].astype(f32) - mean[:, :1]
@@ -178,7 +166,7 @@
         )
 
 
-def put_gradient(taps_ref, cot_ref, above_ref, below_ref):
+def taps_body(cot_ref, above_ref, below_ref, taps_ref):
     row_count = cot_ref.shape[0]
     put_taps(taps_ref, 0, above_ref[0], True)
     for row in range(row_count):
@@ -187,8 +175,8 @@
 
 
 def weight_body(
-    shape, where_ref, latent_ref, cot_ref, above_ref, below_ref, stats_ref, gain_ref, bias_ref,
-    act_ref, near_ref, far_ref, taps_ref,
+    shape, where_ref, latent_ref, taps_ref, stats_ref, gain_ref, bias_ref,
+    act_out, near_ref, far_ref, act_ref, sem,
 ):
     blocks, zones, height, width = shape
     row_count, channels, cols = latent_ref.shape
@@ -196,7 +184,8 @@
     values = column_values(stats_ref, gain_ref, bias_ref)
     for row in range(row_count):
         act_ref[:, row * cols : (row + 1) * cols] = activate(latent_ref[row], values)
-    put_gradient(taps_ref, cot_ref, above_ref, below_ref)
+    kept = pltpu.make_async_copy(act_ref, act_out, sem)
+    kept.start()
     tap_width = zones * width // 3
 
     def store(ref, place, found, block, tap_row):
@@ -239,6 +228,8 @@
                 for rest in range(blocks // 2):
                     store(far_ref, other ^ rest, found, half * blocks // 2 + rest, tap_row)
 
+    kept.wait()
+
 
 def conv_body(
     ends_ref, act_ref, latent_ref, above_ref, below_ref, stats_ref, gain_ref, bias_ref,
@@ -265,12 +256,14 @@
 
 
 def backward_body(
-    latent_ref, taps_ref, stats_ref, gain_ref, bias_ref, weight_ref, grad_ref, sums_ref, flat_ref
+    latent_ref, taps_ref, stats_ref, gain_ref, bias_ref, weight_ref, grad_out, sums_ref, flat_ref,
+    grad_ref, sem,
 ):
     row_count, channels, cols = latent_ref.shape
     values = column_values(stats_ref, gain_ref, bias_ref)
     for tap_row in range(3):
         flat_ref[tap_row] = jnp.concatenate([weight_ref[tap_row, j] for j in range(3)], axis=1)
+    kept = []
     first = jnp.zeros((channels, LANES), f32)
     second = jnp.zeros((channels, LANES), f32)
     for row in range(row_count):
@@ -283,12 +276,16 @@
         normed, shifted, sigmoid = normalized(latent_ref[row], values)
         grad = total * sigmoid * (1.0 + shifted * (1.0 - sigmoid)) * values[2]
         grad_ref[row] = grad
+        kept.append(pltpu.make_async_copy(grad_ref.at[row], grad_out.at[row], sem.at[row]))
+        kept[row].start()
         first = first + fold_lanes(grad)
         second = second + fold_lanes(grad * normed)
     member = member_matrix(channels)
     first = contract(member, first, ((1,), (0,)), HIGHEST)
     second = contract(member, second, ((1,), (0,)), HIGHEST)
     sums_ref[...] = rows_of(lane_form(first), lane_form(second))
+    for copy in kept:
+        copy.wait()
 
 
 def latent_body(total, grad_ref, latent_ref, cot_ref, stats_ref, sums_ref, out_ref):
@@ -451,6 +448,7 @@
     gain, bias = norm_gain, norm_bias
     smem = pl.BlockSpec(memory_space=pltpu.SMEM)
     vmem = pl.BlockSpec(memory_space=pltpu.VMEM)
+    anywhere = pl.BlockSpec(memory_space=pl.ANY)
     small = jax.ShapeDtypeStruct((8, channels), f32)
 
     down = [(i, i + 1) for i in range(slab_count - 1)]
@@ -460,22 +458,18 @@
     taps = pltpu.VMEM((3 * channels, (row_count + 2) * col_count), bf16)
     flat = pltpu.VMEM((3, channels, 3 * channels), bf16)
 
-    edge = jax.ShapeDtypeStruct((2, channels, col_count), bf16)
-    anywhere = pl.BlockSpec(memory_space=pl.ANY)
-    slab = pltpu.VMEM((row_count, channels, col_count), bf16)
-    own, edge_down, edge_up = call(
+    above = lax.ppermute(jnp.stack([cot[row_count - 1], lat[row_count - 1]]), "space", down)
+    below = lax.ppermute(jnp.stack([cot[0], lat[0]]), "space", up)
+    own = call(
         functools.partial(stats_body, local_count),
-        (small, edge, edge),
+        small,
         (timesteps, lat, cot),
-        specs=(smem, anywhere, anywhere),
-        scratch=(slab, slab, pltpu.SemaphoreType.DMA((2, row_count))),
+        specs=(smem, vmem, vmem),
         moved=2 * lat.size * 2,
         flops=positions * channels * 60,
         limit=12 << 20,
     )
     partner = swap_space(own, 1)
-    above = lax.ppermute(edge_down, "space", down)
-    below = lax.ppermute(edge_up, "space", up)
     table_shape = jax.ShapeDtypeStruct((-(-image_count // 8) * 8, channels + 2 * NOTE), f32)
     pair, table = call(
         functools.partial(merge_body, local_count, None, 2),
@@ -506,11 +500,18 @@
     where = jnp.stack([core, mine, other, zone_index]).astype(jnp.int32)
     share_shape = jax.ShapeDtypeStruct((blocks // 2, zones, height, width), f32)
     taps_shape = jax.ShapeDtypeStruct((3 * channels, (row_count + 2) * col_count), bf16)
-    act, near, far, grad_taps = call(
+    hbm = pl.BlockSpec(memory_space=pltpu.HBM)
+    grad_taps = call(
+        taps_body, taps_shape, (cot, above, below), moved=12 * lat.size, limit=12 << 20
+    )
+    act_shape = jax.ShapeDtypeStruct((channels, positions), bf16)
+    act, near, far = call(
         functools.partial(weight_body, (blocks, zones, height, width)),
-        (jax.ShapeDtypeStruct((channels, positions), bf16), share_shape, share_shape, taps_shape),
-        (where, lat, cot, above, below, stats, gain, bias),
-        specs=(smem,) + (vmem,) * 7,
+        (act_shape, share_shape, share_shape),
+        (where, lat, grad_taps, stats, gain, bias),
+        specs=(smem,) + (vmem,) * 5,
+        out_specs=(hbm, vmem, vmem),
+        scratch=(pltpu.VMEM(act_shape.shape, bf16), pltpu.SemaphoreType.DMA(())),
         flops=flops,
         moved=8 * lat.size,
         limit=20 << 20,
@@ -537,7 +538,12 @@
         backward_body,
         (jax.ShapeDtypeStruct((row_count, channels, col_count), f32), small),
         (lat, grad_taps, stats, gain, bias, conv_weight),
-        scratch=(flat,),
+        out_specs=(hbm, vmem),
+        scratch=(
+            flat,
+            pltpu.VMEM((row_count, channels, col_count), f32),
+            pltpu.SemaphoreType.DMA((row_count,)),
+        ),
         flops=flops,
         moved=8 * lat.size,
         limit=20 << 20,
@@ -571,15 +577,19 @@
         masks = (1 << orders[0][step], 1 << orders[1][step])
         scale, back = scales[step]
         arrived = swap_image((sending * scale).astype(f16), masks)
-        total = keeping + arrived.astype(f32) * back
-        middle = total.shape[0] // 2
-        sending, keeping = total[middle:], total[:middle]
-    total = total[0] if bits else keeping[0]
-    share = total[0]
-    arrivals = []
+        middle = keeping.shape[0] // 2
+
+        def joined(first, last):
+            return keeping[first:last] + arrived[first:last].astype(f32) * back
+
+        if middle:
+            sending, keeping = joined(middle, 2 * middle), joined(0, middle)
+    sent = []
     for mask in range(1, zones):
-        arrivals.append(swap_space((total[mask] * line_scale).astype(f16), 2 * mask))
-    for arrived in arrivals:
+        block = keeping[0, mask] + arrived[0, mask].astype(f32) * back
+        sent.append(swap_space((block * line_scale).astype(f16), 2 * mask))
+    share = keeping[0, 0] + arrived[0, 0].astype(f32) * back
+    for arrived in sent:
         share = share + arrived.astype(f32) * line_back
     share = (share * line_scale).astype(f16)
     collected = [share]

time: 127 us -> 130 us (1.024)
  other arithmetic: 14.6 us -> 19 us
  waiting for transfers between devices: 25.8 us -> 22.7 us
  starting transfers between devices: 32.4 us -> 33.7 us
    ppermute x20, waiting for transfers between devices: 15.7 us -> 12.7 us  [swap_space(): return lax.ppermute(cells, 'space', [(i, i ^ mask) for i in range(count)])]
    convert_element_type x2, other arithmetic: 3.79 us -> 6.68 us  [slab_program(): arrived = swap_image((sending * scale).astype(f16), masks)]
    add x2 -> x0, other arithmetic: 2.66 us -> none  [slab_program(): total = keeping + arrived.astype(f32) * back]
    ppermute x20, starting transfers between devices: 20.1 us -> 22.1 us  [swap_space(): return lax.ppermute(cells, 'space', [(i, i ^ mask) for i in range(count)])]
    another operation x1 -> x3, other arithmetic: 0.05 us -> 1.84 us  [the longest x1 0.9 us: slab_program(): jnp.stack([cot[row_count - 1], lat[row_count - 1]])]
    unnamed x30 -> x48, local copies, waits for them, and re-layouts: 10.2 us -> 8.47 us
    slice x1 -> x2, local copies, waits for them, and re-layouts: 1.62 us -> 2.99 us  [the longest x1 1.59 us: slab_program(): far_in = swap_space(far[middle:], 1)]
    mul x0 -> x1, other arithmetic: none -> 1.34 us  [slab_program(): sent.append(swap_space((block * line_scale).astype(f16), 2 * mask))]
  transfers between devices with their start and end apart: 29 -> 29, of which waited for: 12 -> 14; matrix products, arithmetic and copies ran while one was open for 10% -> 13% of each run, Pallas kernels for 18% -> 21%
where the time goes in v3:
time: 130 us
  Pallas kernels  37.6 us (29%)
  starting transfers between devices  33.7 us (26%)
  waiting for transfers between devices  22.7 us (17%)
  other arithmetic  19 us (15%)
  local copies, waits for them, and re-layouts  14.5 us (11%)
  between operations  1.92 us (1%)
    pallas_call x13, Pallas kernels, call(): pl.pallas_call(body, out_shape=tuple(outs) if many else outs, in_specs=li...  33.4 us
    ppermute x20, starting transfers between devices, swap_space(): return lax.ppermute(cells, 'space', [(i, i ^ mask) for i in range(count)])  22.1 us
    ppermute x20, waiting for transfers between devices, swap_space(): return lax.ppermute(cells, 'space', [(i, i ^ mask) for i in range(count)])  12.7 us
    ppermute x7, waiting for transfers between devices, swap_image(): return lax.ppermute(cells, ('dp', 'space'), pairs)  10 us
    unnamed x48, local copies, waits for them, and re-layouts  8.47 us
    ppermute x7, starting transfers between devices, swap_image(): return lax.ppermute(cells, ('dp', 'space'), pairs)  7.72 us
    convert_element_type x2, other arithmetic, slab_program(): arrived = swap_image((sending * scale).astype(f16), masks)  6.68 us
    mul x8, other arithmetic, place(): piece.astype(f32) * line_back  5.75 us
  transfers between devices with their start and end apart: 29, of which 14 were waited for; matrix products, arithmetic and copies ran while one was open for 13% of the time, Pallas kernels for 21%

profile of v3, /device:TPU:0, one launch (start us, length us, event | category | flops | bytes accessed | tf_op | source)
XLA Modules:
  0.0 129.6 jit_solution(16594067556786413696)
XLA Ops:
  3.0 2.6 %collective-permute-start = (bf16[2,320,512]{2,1,0:T(8,128)(2,1)}, bf16[2,320,512]{2,1,0:T(8,128)(2,1)S(1)}, u32[]{:S(2)}, u32[]{:S(2)}) collective-permute-start(bf16[2,320,512]{2,1,0:T(8,128)(2,1)} %pad_maximum_fusion), channel_id=1, source_target_pairs={{0,1},{1,2},{2,3},{3,4},{4,5},{5,6},{6,7},{8,9},{9,10},{10,11},{11... | collective-permute-start | bytes 1966088 | tf_op jit(solution)/shard_map/ppermute | solution.py:461
  8.4 2.7 %shard_map.112.refs_0_ = f32[8,320]{1,0:T(8,128)S(1)} custom-call(s32[1]{0:T(128)S(6)} %copy.14.step_ref, bf16[4,320,512]{2,1,0:T(8,128)(2,1)S(1)} %bitcast.75, bf16[4,320,512]{2,1,0:T(8,128)(2,1)S(1)} %bitcast.71), custom_call_target="tpu_custom_call" | custom-call | flops 39321600 | bytes 2621440 | tf_op jit(solution)/shard_map/pallas_call | solution.py:31
  11.1 3.3 %collective-permute-start.2 = (f32[8,320]{1,0:T(8,128)S(1)}, f32[8,320]{1,0:T(8,128)S(1)}, u32[]{:S(2)}, u32[]{:S(2)}) collective-permute-start(f32[8,320]{1,0:T(8,128)S(1)} %shard_map.112.refs_0_), channel_id=1, source_target_pairs={{0,1},{1,0},{2,3},{3,2},{4,5},{5,4},{6,7},{7,6},{8,9},{9,8},{10,11... | collective-permute-start | bytes 30728 | tf_op jit(solution)/shard_map/ppermute | solution.py:411
  16.6 2.0 %collective-permute-start.3 = (f32[8,320]{1,0:T(8,128)S(1)}, f32[8,320]{1,0:T(8,128)S(1)}, u32[]{:S(2)}, u32[]{:S(2)}) collective-permute-start(f32[8,320]{1,0:T(8,128)S(1)} %get-tuple-element.18.refs_0_), channel_id=1, source_target_pairs={{0,2},{1,3},{2,0},{3,1},{4,6},{5,7},{6,4},{7,5},{8,10},{9,11},{10,... | collective-permute-start | bytes 30728 | tf_op jit(solution)/shard_map/ppermute | solution.py:411
  18.6 2.6 %collective-permute-start.4 = (f32[8,320]{1,0:T(8,128)S(1)}, f32[8,320]{1,0:T(8,128)S(1)}, u32[]{:S(2)}, u32[]{:S(2)}) collective-permute-start(f32[8,320]{1,0:T(8,128)S(1)} %get-tuple-element.18.refs_0_), channel_id=1, source_target_pairs={{0,4},{1,5},{2,6},{3,7},{4,0},{5,1},{6,2},{7,3},{8,12},{9,13},{10,... | collective-permute-start | bytes 30728 | tf_op jit(solution)/shard_map/ppermute | solution.py:411
  23.2 3.5 %collective-permute-done.5.refs_3_ = f32[8,320]{1,0:T(8,128)S(1)} collective-permute-done((f32[8,320]{1,0:T(8,128)S(1)}, f32[8,320]{1,0:T(8,128)S(1)}, u32[]{:S(2)}, u32[]{:S(2)}) %collective-permute-start.5) | collective-permute-done | bytes 10272 | tf_op jit(solution)/shard_map/ppermute | solution.py:411
  26.7 2.5 %shard_map.111.taps_ref = bf16[960,3072]{1,0:T(8,128)(2,1)S(1)} custom-call(bf16[4,320,512]{2,1,0:T(8,128)(2,1)S(1)} %bitcast.72, bf16[2,320,512]{2,1,0:T(8,128)(2,1)S(1)} %collective-permute-done.above_ref, bf16[2,320,512]{2,1,0:T(8,128)(2,1)} %collective-permute-done.1.below_ref), custom_call_target="tpu_custom_call" | custom-call | bytes 7864320 | tf_op jit(solution)/shard_map/pallas_call | solution.py:31
  29.3 6.6 %shard_map.115 = (bf16[320,2048]{1,0:T(8,128)(2,1)S(1)}, f32[4,4,40,768]{3,2,1,0:T(8,128)S(1)}, f32[4,4,40,768]{3,2,1,0:T(8,128)S(1)}) custom-call(s32[4]{0:T(128)S(1)} %pad_add_fusion.where_ref, bf16[4,320,512]{2,1,0:T(8,128)(2,1)S(1)} %bitcast.76, bf16[960,3072]{1,0:T(8,128)(2,1)S(1)} %shard_map.111.taps_ref, f32[8,320]{1,0:T(8,128)S(1)} %shard_map.114.stats_ref, ...), custom_call_target="tpu_custom_call" | custom-call | flops 3774873600 | bytes 5242880 | tf_op jit(solution)/shard_map/pallas_call | solution.py:31
  40.8 1.8 %collective-permute-done.6.other_ref = f32[8,384]{1,0:T(8,128)} collective-permute-done((f32[8,384]{1,0:T(8,128)S(1)}, f32[8,384]{1,0:T(8,128)}, u32[]{:S(2)}, u32[]{:S(2)}) %collective-permute-start.6) | collective-permute-done | bytes 12320 | tf_op jit(solution)/shard_map/ppermute | solution.py:420
  47.5 4.1 %multiply_convert_fusion = (f16[2,4,40,768]{3,2,1,0:T(8,128)(2,1)}, f32[2,4,40,768]{3,2,1,0:T(8,128)}) fusion(f32[2,4,40,768]{3,2,1,0:T(8,128)} %collective-permute-done.13, f32[4,4,40,768]{3,2,1,0:T(8,128)} %copy-done.5, f32[]{:T(128)} %bitcast.25, f32[2,4,40,768]{3,2,1,0:T(8,128)} %collective-permute-done.12), kind=kLoop, calls=%fused_computation.1 | loop fusion | flops 983040 | bytes 5406724 | tf_op jit(solution)/shard_map/convert_element_type | solution.py:579
  56.6 2.7 %copy-done.4 = bf16[960,3072]{1,0:T(8,128)(2,1)S(1)} copy-done((bf16[960,3072]{1,0:T(8,128)(2,1)S(1)}, bf16[960,3072]{1,0:T(8,128)(2,1)}, u32[]{:S(2)}) %copy-start.4) | copy-done | bytes 5898264
  60.9 7.8 %shard_map.119 = (f32[4,320,512]{2,1,0:T(8,128)S(1)}, f32[8,320]{1,0:T(8,128)S(1)}) custom-call(bf16[4,320,512]{2,1,0:T(8,128)(2,1)S(1)} %bitcast.77, bf16[960,3072]{1,0:T(8,128)(2,1)S(1)} %copy-done.4, f32[8,320]{1,0:T(8,128)S(1)} %shard_map.114.stats_ref, f32[320]{0:T(512)S(1)} %copy-done.6, f32[320]{0:T(512)S(1)} %copy-done.7, ...), custom_call_target="tpu_custom_call" | custom-call | flops 3774873600 | bytes 5242880 | tf_op jit(solution)/shard_map/pallas_call | solution.py:31
  70.8 3.7 %collective-permute-start.11 = (f32[8,320]{1,0:T(8,128)S(1)}, f32[8,320]{1,0:T(8,128)S(1)}, u32[]{:S(2)}, u32[]{:S(2)}) collective-permute-start(f32[8,320]{1,0:T(8,128)S(1)} %shard_map.120.refs_0_), channel_id=1, source_target_pairs={{0,6},{1,7},{2,4},{3,5},{4,2},{5,3},{6,0},{7,1},{8,14},{9,15},{10,... | collective-permute-start | bytes 30728 | tf_op jit(solution)/shard_map/ppermute | solution.py:411
  74.5 2.6 %fusion.1 = (f16[1,4,40,768]{3,2,1,0:T(8,128)(2,1)S(1)}, f32[1,4,40,768]{3,2,1,0:T(8,128)S(1)}) fusion(f32[2,4,40,768]{3,2,1,0:T(8,128)S(1)} %copy-done.21, f16[2,4,40,768]{3,2,1,0:T(8,128)(2,1)} %collective-permute-done.14, f32[]{:T(128)} %bitcast.27, f32[]{:T(128)} %bitcast.26), kind=kLoop, calls=%fused_computation.7 | loop fusion | flops 983040 | bytes 2211848 | tf_op jit(solution)/shard_map/convert_element_type | solution.py:579
  78.5 4.9 %collective-permute-done.15 = f16[1,4,40,768]{3,2,1,0:T(8,128)(2,1)S(1)} collective-permute-done((f16[1,4,40,768]{3,2,1,0:T(8,128)(2,1)S(1)}, f16[1,4,40,768]{3,2,1,0:T(8,128)(2,1)S(1)}, u32[]{:S(2)}, u32[]{:S(2)}) %collective-permute-start.15) | collective-permute-done | bytes 245792 | tf_op jit(solution)/shard_map/ppermute | solution.py:420
  85.4 3.7 %collective-permute-start.16 = (f16[40,768]{1,0:T(8,128)(2,1)S(1)}, f16[40,768]{1,0:T(8,128)(2,1)S(1)}, u32[]{:S(2)}, u32[]{:S(2)}) collective-permute-start(f16[40,768]{1,0:T(8,128)(2,1)S(1)} %get-tuple-element.42), channel_id=1, source_target_pairs={{0,2},{1,3},{2,0},{3,1},{4,6},{5,7},{6,4},{7,5},{8,10},{9,11},{10,... | collective-permute-start | bytes 184328 | tf_op jit(solution)/shard_map/ppermute | solution.py:411
  91.4 2.0 %fusion.13 = f16[40,768]{1,0:T(8,128)(2,1)S(1)} fusion(f32[1,4,40,768]{3,2,1,0:T(8,128)S(1)} %get-tuple-element.37, f16[40,768]{1,0:T(8,128)(2,1)S(1)} %collective-permute-done.18, f16[40,768]{1,0:T(8,128)(2,1)S(1)} %collective-permute-done.17, f16[40,768]{1,0:T(8,128)(2,1)S(1)} %collective-permute-done.16, ...), kind=kLoop, calls=%fused_computation.37 | loop fusion | flops 430080 | bytes 430092 | tf_op jit(solution)/shard_map/convert_element_type | solution.py:594
  93.4 2.3 %collective-permute-start.21 = (f16[40,768]{1,0:T(8,128)(2,1)S(1)}, f16[40,768]{1,0:T(8,128)(2,1)S(1)}, u32[]{:S(2)}, u32[]{:S(2)}) collective-permute-start(f16[40,768]{1,0:T(8,128)(2,1)S(1)} %fusion.13), channel_id=1, source_target_pairs={{0,6},{1,7},{2,4},{3,5},{4,2},{5,3},{6,0},{7,1},{8,14},{9,15},{10,... | collective-permute-start | bytes 184328 | tf_op jit(solution)/shard_map/ppermute | solution.py:411
  98.0 1.9 %collective-permute-done.21 = f16[40,768]{1,0:T(8,128)(2,1)S(1)} collective-permute-done((f16[40,768]{1,0:T(8,128)(2,1)S(1)}, f16[40,768]{1,0:T(8,128)(2,1)S(1)}, u32[]{:S(2)}, u32[]{:S(2)}) %collective-permute-start.21) | collective-permute-done | bytes 61472 | tf_op jit(solution)/shard_map/ppermute | solution.py:411
  102.4 7.5 %shard_map.118 = bf16[4,320,512]{2,1,0:T(8,128)(2,1)} custom-call(s32[2]{0:T(128)S(1)} %copy-done.18, bf16[320,2048]{1,0:T(8,128)(2,1)S(1)} %copy-done.20, bf16[4,320,512]{2,1,0:T(8,128)(2,1)S(1)} %bitcast.78, bf16[2,320,512]{2,1,0:T(8,128)(2,1)S(1)} %collective-permute-done.above_ref, bf16[2,320,512]{2,1,0:T(8,128)(2,1)} %collective-permute-done.1.below_ref, ...), custom_call_target="tpu_custom_call" | custom-call | flops 3774873600 | bytes 5242880 | tf_op jit(solution)/shard_map/pallas_call | solution.py:31
  111.1 2.2 %shard_map.122 = bf16[4,320,512]{2,1,0:T(8,128)(2,1)} custom-call(f32[4,320,512]{2,1,0:T(8,128)S(1)} %get-tuple-element.23.grad_ref, bf16[4,320,512]{2,1,0:T(8,128)(2,1)S(1)} %bitcast.79, bf16[4,320,512]{2,1,0:T(8,128)(2,1)S(1)} %bitcast.73, f32[8,320]{1,0:T(8,128)S(1)} %shard_map.114.stats_ref, f32[8,320]{1,0:T(8,128)S(1)} %get-tuple-element.26.sums_ref.total_ref), custom_call_target="tpu_custom_call" | custom-call | flops 13107200 | bytes 6553600 | tf_op jit(solution)/shard_map/pallas_call | solution.py:31
  117.3 2.3 %collective-permute-done.25 = f16[4,40,768]{2,1,0:T(8,128)(2,1)S(1)} collective-permute-done((f16[4,40,768]{2,1,0:T(8,128)(2,1)S(1)}, f16[4,40,768]{2,1,0:T(8,128)(2,1)S(1)}, u32[]{:S(2)}, u32[]{:S(2)}) %collective-permute-start.25) | collective-permute-done | bytes 245792 | tf_op jit(solution)/shard_map/ppermute | solution.py:420
  123.7 2.5 %shard_map.123.refs_2_ = f32[9,320,320]{2,1,0:T(8,128)} custom-call(s32[10]{0:T(128)S(1)} %copy-done.16, f32[4,40,768]{2,1,0:T(8,128)S(1)} %convert_multiply_fusion.5.refs_0_, f32[4,40,768]{2,1,0:T(8,128)S(1)} %convert_multiply_fusion.4.refs_1_, f32[4,40,768]{2,1,0:T(8,128)S(1)} %convert_multiply_fusion.3.refs_2_, ...), custom_call_target="tpu_custom_call" | custom-call | bytes 5898240 | tf_op jit(solution)/shard_map/pallas_call | solution.py:616
  127.7 1.7 %shard_map.124 = f32[9,320,320]{2,1,0:T(8,128)} custom-call(s32[6]{0:T(128)S(1)} %copy-done.15, f32[4,40,768]{2,1,0:T(8,128)S(1)} %convert_multiply_fusion.7.refs_0_, f32[4,40,768]{2,1,0:T(8,128)S(1)} %convert_multiply_fusion.6.refs_1_, f32[9,320,320]{2,1,0:T(8,128)} %shard_map.123.refs_2_), custom_call_target="tpu_custom_call", output_to_operand_aliasing={{}: (3, {})} | custom-call | bytes 1966080 | tf_op jit(solution)/shard_map/pallas_call | solution.py:616
  (127 shorter events, 48.2 us)
Async XLA Ops:
  3.0 23.7 %collective-permute-start = (bf16[2,320,512]{2,1,0:T(8,128)(2,1)}, bf16[2,320,512]{2,1,0:T(8,128)(2,1)S(1)}, u32[]{:S(2)}, u32[]{:S(2)}) collective-permute-start(bf16[2,320,512]{2,1,0:T(8,128)(2,1)} %pad_maximum_fusion), channel_id=1, source_target_pairs={{0,1},{1,2},{2,3},{3,4},{4,5},{5,6},{6,7},{8,9},{9,10},{10,11},{11... | collective-permute-start | bytes 1966088 | tf_op jit(solution)/shard_map/ppermute | solution.py:461
  6.4 20.3 %collective-permute-start.1 = (bf16[2,320,512]{2,1,0:T(8,128)(2,1)}, bf16[2,320,512]{2,1,0:T(8,128)(2,1)}, u32[]{:S(2)}, u32[]{:S(2)}) collective-permute-start(bf16[2,320,512]{2,1,0:T(8,128)(2,1)} %pad_maximum_fusion.1), channel_id=1, source_target_pairs={{1,0},{2,1},{3,2},{4,3},{5,4},{6,5},{7,6},{9,8},{10,9},{11,10},{12... | collective-permute-start | bytes 1966088 | tf_op jit(solution)/shard_map/ppermute | solution.py:462
  16.6 5.0 %collective-permute-start.3 = (f32[8,320]{1,0:T(8,128)S(1)}, f32[8,320]{1,0:T(8,128)S(1)}, u32[]{:S(2)}, u32[]{:S(2)}) collective-permute-start(f32[8,320]{1,0:T(8,128)S(1)} %get-tuple-element.18.refs_0_), channel_id=1, source_target_pairs={{0,2},{1,3},{2,0},{3,1},{4,6},{5,7},{6,4},{7,5},{8,10},{9,11},{10,... | collective-permute-start | bytes 30728 | tf_op jit(solution)/shard_map/ppermute | solution.py:411
  21.2 5.5 %collective-permute-start.5 = (f32[8,320]{1,0:T(8,128)S(1)}, f32[8,320]{1,0:T(8,128)S(1)}, u32[]{:S(2)}, u32[]{:S(2)}) collective-permute-start(f32[8,320]{1,0:T(8,128)S(1)} %get-tuple-element.18.refs_0_), channel_id=1, source_target_pairs={{0,6},{1,7},{2,4},{3,5},{4,2},{5,3},{6,0},{7,1},{8,14},{9,15},{10,... | collective-permute-start | bytes 30728 | tf_op jit(solution)/shard_map/ppermute | solution.py:411
  38.3 9.2 %collective-permute-start.13 = (f32[2,4,40,768]{3,2,1,0:T(8,128)}, f32[2,4,40,768]{3,2,1,0:T(8,128)}, u32[]{:S(2)}, u32[]{:S(2)}) collective-permute-start(f32[2,4,40,768]{3,2,1,0:T(8,128)} %get-tuple-element.34), channel_id=1, source_target_pairs={{0,1},{1,0},{2,3},{3,2},{4,5},{5,4},{6,7},{7,6},{8,9},{9,8},{10,11... | collective-permute-start | bytes 2949128 | tf_op jit(solution)/shard_map/ppermute | solution.py:411
  38.3 9.2 %collective-permute-start.12 = (f32[2,4,40,768]{3,2,1,0:T(8,128)}, f32[2,4,40,768]{3,2,1,0:T(8,128)}, u32[]{:S(2)}, u32[]{:S(2)}) collective-permute-start(f32[2,4,40,768]{3,2,1,0:T(8,128)} %get-tuple-element.35), channel_id=1, source_target_pairs={{0,1},{1,0},{2,3},{3,2},{4,5},{5,4},{6,7},{7,6},{8,9},{9,8},{10,11... | collective-permute-start | bytes 2949128 | tf_op jit(solution)/shard_map/ppermute | solution.py:411
  45.4 9.5 %collective-permute-start.7 = (f32[8,384]{1,0:T(8,128)S(1)}, f32[8,384]{1,0:T(8,128)}, u32[]{:S(2)}, u32[]{:S(2)}) collective-permute-start(f32[8,384]{1,0:T(8,128)S(1)} %get-tuple-element.21.mine_ref), channel_id=1, source_target_pairs={{0,16},{1,9},{2,18},{3,11},{4,20},{5,13},{6,22},{7,15},{8,24},{9,1... | collective-permute-start | bytes 36872 | tf_op jit(solution)/shard_map/ppermute | solution.py:420
  51.5 22.9 %collective-permute-start.14 = (f16[2,4,40,768]{3,2,1,0:T(8,128)(2,1)}, f16[2,4,40,768]{3,2,1,0:T(8,128)(2,1)}, u32[]{:S(2)}, u32[]{:S(2)}) collective-permute-start(f16[2,4,40,768]{3,2,1,0:T(8,128)(2,1)} %get-tuple-element.32), channel_id=1, source_target_pairs={{0,8},{1,17},{2,10},{3,19},{4,12},{5,21},{6,14},{7,23},{8,0},{9,25... | collective-permute-start | bytes 1474568 | tf_op jit(solution)/shard_map/ppermute | solution.py:420
  70.1 7.6 %collective-permute-start.9 = (f32[8,320]{1,0:T(8,128)S(1)}, f32[8,320]{1,0:T(8,128)S(1)}, u32[]{:S(2)}, u32[]{:S(2)}) collective-permute-start(f32[8,320]{1,0:T(8,128)S(1)} %shard_map.120.refs_0_), channel_id=1, source_target_pairs={{0,2},{1,3},{2,0},{3,1},{4,6},{5,7},{6,4},{7,5},{8,10},{9,11},{10,... | collective-permute-start | bytes 30728 | tf_op jit(solution)/shard_map/ppermute | solution.py:411
  70.1 7.6 %collective-permute-start.10 = (f32[8,320]{1,0:T(8,128)S(1)}, f32[8,320]{1,0:T(8,128)S(1)}, u32[]{:S(2)}, u32[]{:S(2)}) collective-permute-start(f32[8,320]{1,0:T(8,128)S(1)} %shard_map.120.refs_0_), channel_id=1, source_target_pairs={{0,4},{1,5},{2,6},{3,7},{4,0},{5,1},{6,2},{7,3},{8,12},{9,13},{10,... | collective-permute-start | bytes 30728 | tf_op jit(solution)/shard_map/ppermute | solution.py:411
  70.8 7.0 %collective-permute-start.11 = (f32[8,320]{1,0:T(8,128)S(1)}, f32[8,320]{1,0:T(8,128)S(1)}, u32[]{:S(2)}, u32[]{:S(2)}) collective-permute-start(f32[8,320]{1,0:T(8,128)S(1)} %shard_map.120.refs_0_), channel_id=1, source_target_pairs={{0,6},{1,7},{2,4},{3,5},{4,2},{5,3},{6,0},{7,1},{8,14},{9,15},{10,... | collective-permute-start | bytes 30728 | tf_op jit(solution)/shard_map/ppermute | solution.py:411
  77.1 6.3 %collective-permute-start.15 = (f16[1,4,40,768]{3,2,1,0:T(8,128)(2,1)S(1)}, f16[1,4,40,768]{3,2,1,0:T(8,128)(2,1)S(1)}, u32[]{:S(2)}, u32[]{:S(2)}) collective-permute-start(f16[1,4,40,768]{3,2,1,0:T(8,128)(2,1)S(1)} %get-tuple-element.36), channel_id=1, source_target_pairs={{0,16},{1,9},{2,18},{3,11},{4,20},{5,13},{6,22},{7,15},{8,24},{9,1... | collective-permute-start | bytes 737288 | tf_op jit(solution)/shard_map/ppermute | solution.py:420
  84.7 6.1 %collective-permute-start.18 = (f16[40,768]{1,0:T(8,128)(2,1)S(1)}, f16[40,768]{1,0:T(8,128)(2,1)S(1)}, u32[]{:S(2)}, u32[]{:S(2)}) collective-permute-start(f16[40,768]{1,0:T(8,128)(2,1)S(1)} %get-tuple-element.43), channel_id=1, source_target_pairs={{0,6},{1,7},{2,4},{3,5},{4,2},{5,3},{6,0},{7,1},{8,14},{9,15},{10,... | collective-permute-start | bytes 184328 | tf_op jit(solution)/shard_map/ppermute | solution.py:411
  84.9 5.9 %collective-permute-start.17 = (f16[40,768]{1,0:T(8,128)(2,1)S(1)}, f16[40,768]{1,0:T(8,128)(2,1)S(1)}, u32[]{:S(2)}, u32[]{:S(2)}) collective-permute-start(f16[40,768]{1,0:T(8,128)(2,1)S(1)} %get-tuple-element.44), channel_id=1, source_target_pairs={{0,4},{1,5},{2,6},{3,7},{4,0},{5,1},{6,2},{7,3},{8,12},{9,13},{10,... | collective-permute-start | bytes 184328 | tf_op jit(solution)/shard_map/ppermute | solution.py:411
  85.4 6.0 %collective-permute-start.16 = (f16[40,768]{1,0:T(8,128)(2,1)S(1)}, f16[40,768]{1,0:T(8,128)(2,1)S(1)}, u32[]{:S(2)}, u32[]{:S(2)}) collective-permute-start(f16[40,768]{1,0:T(8,128)(2,1)S(1)} %get-tuple-element.42), channel_id=1, source_target_pairs={{0,2},{1,3},{2,0},{3,1},{4,6},{5,7},{6,4},{7,5},{8,10},{9,11},{10,... | collective-permute-start | bytes 184328 | tf_op jit(solution)/shard_map/ppermute | solution.py:411
  93.4 6.4 %collective-permute-start.21 = (f16[40,768]{1,0:T(8,128)(2,1)S(1)}, f16[40,768]{1,0:T(8,128)(2,1)S(1)}, u32[]{:S(2)}, u32[]{:S(2)}) collective-permute-start(f16[40,768]{1,0:T(8,128)(2,1)S(1)} %fusion.13), channel_id=1, source_target_pairs={{0,6},{1,7},{2,4},{3,5},{4,2},{5,3},{6,0},{7,1},{8,14},{9,15},{10,... | collective-permute-start | bytes 184328 | tf_op jit(solution)/shard_map/ppermute | solution.py:411
  95.8 5.5 %collective-permute-start.20 = (f16[40,768]{1,0:T(8,128)(2,1)S(1)}, f16[40,768]{1,0:T(8,128)(2,1)S(1)}, u32[]{:S(2)}, u32[]{:S(2)}) collective-permute-start(f16[40,768]{1,0:T(8,128)(2,1)S(1)} %fusion.13), channel_id=1, source_target_pairs={{0,4},{1,5},{2,6},{3,7},{4,0},{5,1},{6,2},{7,3},{8,12},{9,13},{10,... | collective-permute-start | bytes 184328 | tf_op jit(solution)/shard_map/ppermute | solution.py:411
  96.9 4.9 %collective-permute-start.19 = (f16[40,768]{1,0:T(8,128)(2,1)S(1)}, f16[40,768]{1,0:T(8,128)(2,1)S(1)}, u32[]{:S(2)}, u32[]{:S(2)}) collective-permute-start(f16[40,768]{1,0:T(8,128)(2,1)S(1)} %fusion.13), channel_id=1, source_target_pairs={{0,2},{1,3},{2,0},{3,1},{4,6},{5,7},{6,4},{7,5},{8,10},{9,11},{10,... | collective-permute-start | bytes 184328 | tf_op jit(solution)/shard_map/ppermute | solution.py:411
  101.8 12.9 %collective-permute-start.22 = (f16[4,40,768]{2,1,0:T(8,128)(2,1)S(1)}, f16[4,40,768]{2,1,0:T(8,128)(2,1)S(1)}, u32[]{:S(2)}, u32[]{:S(2)}) collective-permute-start(f16[4,40,768]{2,1,0:T(8,128)(2,1)S(1)} %pad_maximum_fusion.2), channel_id=1, source_target_pairs={{0,16},{1,9},{2,18},{3,11},{4,20},{5,13},{6,22},{7,15},{8,24},{9,1... | collective-permute-start | bytes 737288 | tf_op jit(solution)/shard_map/ppermute | solution.py:420
  113.4 6.2 %collective-permute-start.25 = (f16[4,40,768]{2,1,0:T(8,128)(2,1)S(1)}, f16[4,40,768]{2,1,0:T(8,128)(2,1)S(1)}, u32[]{:S(2)}, u32[]{:S(2)}) collective-permute-start(f16[4,40,768]{2,1,0:T(8,128)(2,1)S(1)} %pad_maximum_fusion.2), channel_id=1, source_target_pairs={{0,8},{1,17},{2,10},{3,19},{4,12},{5,21},{6,14},{7,23},{8,0},{9,25... | collective-permute-start | bytes 737288 | tf_op jit(solution)/shard_map/ppermute | solution.py:420
  114.7 5.7 %collective-permute-start.26 = (f16[4,40,768]{2,1,0:T(8,128)(2,1)S(1)}, f16[4,40,768]{2,1,0:T(8,128)(2,1)S(1)}, u32[]{:S(2)}, u32[]{:S(2)}) collective-permute-start(f16[4,40,768]{2,1,0:T(8,128)(2,1)S(1)} %pad_maximum_fusion.2), channel_id=1, source_target_pairs={{0,1},{1,0},{2,3},{3,2},{4,5},{5,4},{6,7},{7,6},{8,9},{9,8},{10,11... | collective-permute-start | bytes 737288 | tf_op jit(solution)/shard_map/ppermute | solution.py:411
  114.8 7.4 %collective-permute-start.23 = (f16[4,40,768]{2,1,0:T(8,128)(2,1)S(1)}, f16[4,40,768]{2,1,0:T(8,128)(2,1)S(1)}, u32[]{:S(2)}, u32[]{:S(2)}) collective-permute-start(f16[4,40,768]{2,1,0:T(8,128)(2,1)S(1)} %collective-permute-done.22), channel_id=1, source_target_pairs={{0,8},{1,17},{2,10},{3,19},{4,12},{5,21},{6,14},{7,23},{8,0},{9,25... | collective-permute-start | bytes 737288 | tf_op jit(solution)/shard_map/ppermute | solution.py:420
  117.1 5.2 %collective-permute-start.27 = (f16[4,40,768]{2,1,0:T(8,128)(2,1)S(1)}, f16[4,40,768]{2,1,0:T(8,128)(2,1)S(1)}, u32[]{:S(2)}, u32[]{:S(2)}) collective-permute-start(f16[4,40,768]{2,1,0:T(8,128)(2,1)S(1)} %collective-permute-done.22), channel_id=1, source_target_pairs={{0,1},{1,0},{2,3},{3,2},{4,5},{5,4},{6,7},{7,6},{8,9},{9,8},{10,11... | collective-permute-start | bytes 737288 | tf_op jit(solution)/shard_map/ppermute | solution.py:411
  122.2 4.7 %collective-permute-start.24 = (f16[4,40,768]{2,1,0:T(8,128)(2,1)S(1)}, f16[4,40,768]{2,1,0:T(8,128)(2,1)S(1)}, u32[]{:S(2)}, u32[]{:S(2)}) collective-permute-start(f16[4,40,768]{2,1,0:T(8,128)(2,1)S(1)} %collective-permute-done.23), channel_id=1, source_target_pairs={{0,1},{1,0},{2,3},{3,2},{4,5},{5,4},{6,7},{7,6},{8,9},{9,8},{10,11... | collective-permute-start | bytes 737288 | tf_op jit(solution)/shard_map/ppermute | solution.py:411
  (29 other events, 283.5 us)

commit v4 on v2

--- a/solution.py
+++ b/solution.py
@@ -178,25 +178,29 @@
         )
 
 
-def put_gradient(taps_ref, cot_ref, above_ref, below_ref):
-    row_count = cot_ref.shape[0]
-    put_taps(taps_ref, 0, above_ref[0], True)
-    for row in range(row_count):
-        put_taps(taps_ref, row + 1, cot_ref[row], True)
-    put_taps(taps_ref, row_count + 1, below_ref[0], True)
-
-
-def weight_body(
-    shape, where_ref, latent_ref, cot_ref, above_ref, below_ref, stats_ref, gain_ref, bias_ref,
-    act_ref, near_ref, far_ref, taps_ref,
-):
-    blocks, zones, height, width = shape
-    row_count, channels, cols = latent_ref.shape
-    core, mine, other, zone_index = [where_ref[i] for i in range(4)]
+def taps_body(cot_ref, taps_ref):
+    for row in range(cot_ref.shape[0]):
+        put_taps(taps_ref, row, cot_ref[row], True)
+
+
+def middle_body(latent_ref, taps_ref, stats_ref, gain_ref, bias_ref, act_ref, found_ref):
+    row_count, _, cols = latent_ref.shape
     values = column_values(stats_ref, gain_ref, bias_ref)
     for row in range(row_count):
         act_ref[:, row * cols : (row + 1) * cols] = activate(latent_ref[row], values)
-    put_gradient(taps_ref, cot_ref, above_ref, below_ref)
+    found_ref[...] = contract(act_ref[...], taps_ref[...], ((1,), (1,)))
+
+
+def weight_body(
+    shape, cols, where_ref, act_ref, taps_ref, above_ref, below_ref, middle_ref,
+    near_ref, low_ref, high_ref, edge_ref,
+):
+    blocks, zones, height, width = shape
+    channels, positions = act_ref.shape
+    core, mine, other, zone_index = [where_ref[i] for i in range(4)]
+    quarter = blocks // 4
+    put_taps(edge_ref, 0, above_ref[0], True)
+    put_taps(edge_ref, 1, below_ref[0], True)
     tap_width = zones * width // 3
 
     def store(ref, place, found, block, tap_row):
@@ -222,11 +226,16 @@
             if size < height and used:
                 ref[place, at, size:, left : left + used] = jnp.zeros((height - size, used), f32)
 
-    for tap_row in range(3):
-        start = (2 - tap_row) * cols
-        found = contract(
-            act_ref[...], taps_ref[:, start : start + row_count * cols], ((1,), (1,))
-        )
+    for tap_row in (1, 0, 2):
+        if tap_row == 1:
+            found = middle_ref
+        else:
+            inner = slice(0, positions - cols) if tap_row == 0 else slice(cols, positions)
+            shifted = slice(cols, positions) if tap_row == 0 else slice(0, positions - cols)
+            outer = slice(positions - cols, positions) if tap_row == 0 else slice(0, cols)
+            edge = slice(cols, 2 * cols) if tap_row == 0 else slice(0, cols)
+            found = contract(act_ref[:, inner], taps_ref[:, shifted], ((1,), (1,)))
+            found = found + contract(act_ref[:, outer], edge_ref[:, edge], ((1,), (1,)))
         for half in range(2):
 
             @pl.when(core == half)
@@ -234,15 +243,19 @@
                 for rest in range(blocks // 2):
                     store(near_ref, mine ^ rest, found, half * blocks // 2 + rest, tap_row)
 
-            @pl.when(core != half)
-            def _():
-                for rest in range(blocks // 2):
-                    store(far_ref, other ^ rest, found, half * blocks // 2 + rest, tap_row)
+            for top in range(2):
+
+                @pl.when((core != half) & (other // quarter == top))
+                def _():
+                    for rest in range(blocks // 2):
+                        ref = high_ref if rest // quarter != top else low_ref
+                        at = (other ^ rest) % quarter
+                        store(ref, at, found, half * blocks // 2 + rest, tap_row)
 
 
 def conv_body(
-    ends_ref, act_ref, latent_ref, above_ref, below_ref, stats_ref, gain_ref, bias_ref,
-    weight_ref, extra_ref, out_ref, taps_ref, flat_ref,
+    ends_ref, latent_ref, above_ref, below_ref, stats_ref, gain_ref, bias_ref, weight_ref,
+    extra_ref, out_ref, taps_ref, flat_ref,
 ):
     row_count, channels, cols = latent_ref.shape
     values = column_values(stats_ref, gain_ref, bias_ref)
@@ -250,7 +263,7 @@
         keep = ends_ref[end].astype(f32)
         put_taps(taps_ref, place, (activate(ref[1], values).astype(f32) * keep).astype(bf16), False)
     for row in range(row_count):
-        put_taps(taps_ref, row + 1, act_ref[:, row * cols : (row + 1) * cols], False)
+        put_taps(taps_ref, row + 1, activate(latent_ref[row], values), False)
     for tap_row in range(3):
         flat_ref[tap_row] = weight_ref[tap_row].reshape(3 * channels, channels).T
     extra = jnp.broadcast_to(extra_ref[...], (8, channels)).T[:, :1]
@@ -265,7 +278,8 @@
 
 
 def backward_body(
-    latent_ref, taps_ref, stats_ref, gain_ref, bias_ref, weight_ref, grad_ref, sums_ref, flat_ref
+    latent_ref, taps_ref, edge_ref, stats_ref, gain_ref, bias_ref, weight_ref,
+    grad_ref, sums_ref, flat_ref,
 ):
     row_count, channels, cols = latent_ref.shape
     values = column_values(stats_ref, gain_ref, bias_ref)
@@ -276,10 +290,13 @@
     for row in range(row_count):
         total = jnp.zeros((channels, cols), f32)
         for tap_row in range(3):
-            start = (row + 2 - tap_row) * cols
-            total = total + contract(
-                flat_ref[tap_row], taps_ref[:, start : start + cols], ((1,), (0,))
-            )
+            source = row + 1 - tap_row
+            if 0 <= source < row_count:
+                piece = taps_ref[:, source * cols : (source + 1) * cols]
+            else:
+                start = cols if source > 0 else 0
+                piece = edge_ref[:, start : start + cols]
+            total = total + contract(flat_ref[tap_row], piece, ((1,), (0,)))
         normed, shifted, sigmoid = normalized(latent_ref[row], values)
         grad = total * sigmoid * (1.0 + shifted * (1.0 - sigmoid)) * values[2]
         grad_ref[row] = grad
@@ -471,7 +488,7 @@
         scratch=(slab, slab, pltpu.SemaphoreType.DMA((2, row_count))),
         moved=2 * lat.size * 2,
         flops=positions * channels * 60,
-        limit=12 << 20,
+        limit=None,
     )
     partner = swap_space(own, 1)
     above = lax.ppermute(edge_down, "space", down)
@@ -504,16 +521,34 @@
 
     mine, other = rest_index(core), rest_index(1 - core)
     where = jnp.stack([core, mine, other, zone_index]).astype(jnp.int32)
+    part_shape = jax.ShapeDtypeStruct((blocks // 4, zones, height, width), f32)
     share_shape = jax.ShapeDtypeStruct((blocks // 2, zones, height, width), f32)
-    taps_shape = jax.ShapeDtypeStruct((3 * channels, (row_count + 2) * col_count), bf16)
-    act, near, far, grad_taps = call(
-        functools.partial(weight_body, (blocks, zones, height, width)),
-        (jax.ShapeDtypeStruct((channels, positions), bf16), share_shape, share_shape, taps_shape),
-        (where, lat, cot, above, below, stats, gain, bias),
-        specs=(smem,) + (vmem,) * 7,
+    taps_shape = jax.ShapeDtypeStruct((3 * channels, positions), bf16)
+    grad_taps = call(taps_body, taps_shape, (cot,), moved=10 * lat.size, limit=6 << 20)
+    act, middle_rows = call(
+        middle_body,
+        (
+            jax.ShapeDtypeStruct((channels, positions), bf16),
+            jax.ShapeDtypeStruct((channels, 3 * channels), f32),
+        ),
+        (lat, grad_taps, stats, gain, bias),
+        flops=flops // 3,
+        moved=8 * lat.size,
+        limit=8 << 20,
+    )
+    near, far_low, far_high, edge_taps = call(
+        functools.partial(weight_body, (blocks, zones, height, width), col_count),
+        (
+            share_shape,
+            part_shape,
+            part_shape,
+            jax.ShapeDtypeStruct((3 * channels, 2 * col_count), bf16),
+        ),
+        (where, act, grad_taps, above, below, middle_rows),
+        specs=(smem,) + (vmem,) * 5,
         flops=flops,
         moved=8 * lat.size,
-        limit=20 << 20,
+        limit=12 << 20,
     )
     factor, spread = float(positions * slab_count * image_count), math.sqrt(per_group)
     scales_shape = jax.ShapeDtypeStruct((8, LANES), f32)
@@ -536,11 +571,11 @@
     grad, sums = call(
         backward_body,
         (jax.ShapeDtypeStruct((row_count, channels, col_count), f32), small),
-        (lat, grad_taps, stats, gain, bias, conv_weight),
+        (lat, grad_taps, edge_taps, stats, gain, bias, conv_weight),
         scratch=(flat,),
         flops=flops,
         moved=8 * lat.size,
-        limit=20 << 20,
+        limit=8 << 20,
     )
     sums_partner = swap_space(sums, 1)
     message = jax.ShapeDtypeStruct((-(-(3 + image_count) // 8) * 8, channels), f32)
@@ -563,8 +598,8 @@
     line_scale, line_back = line_scales[0, 0], line_scales[1, 0]
 
     middle = blocks // 4
-    far_in = swap_space(far[middle:], 1)
-    near_in = swap_space(far[:middle], 1)
+    far_in = swap_space(far_high, 1)
+    near_in = swap_space(far_low, 1)
     sending = near[middle:] + far_in
     keeping = near[:middle] + near_in
     for step in range(bits):
@@ -644,12 +679,12 @@
     block_out = call(
         conv_body,
         jax.ShapeDtypeStruct((row_count, channels, col_count), bf16),
-        (ends, act, lat, above, below, stats, gain, bias, conv_weight, extra),
-        specs=(smem,) + (vmem,) * 9,
+        (ends, lat, above, below, stats, gain, bias, conv_weight, extra),
+        specs=(smem,) + (vmem,) * 8,
         scratch=(taps, flat),
         flops=flops,
         moved=8 * lat.size,
-        limit=20 << 20,
+        limit=14 << 20,
     )
     latent_grad = call(
         functools.partial(latent_body, total_count),

time: 127 us -> 129 us (1.016)
  waiting for transfers between devices: 25.8 us -> 29.1 us
  local copies, waits for them, and re-layouts: 13.7 us -> 10.5 us
  Pallas kernels: 37.5 us -> 39.7 us
    ppermute x7, waiting for transfers between devices: 10.1 us -> 13.7 us  [swap_image(): return lax.ppermute(cells, ('dp', 'space'), pairs)]
    pallas_call x12 -> x14, Pallas kernels: 33.3 us -> 35.4 us  [call(): pl.pallas_call(body, out_shape=tuple(outs) if many else outs, in_specs=li...]
    slice x1 -> x0, local copies, waits for them, and re-layouts: 1.62 us -> none  [slab_program(): near_in = swap_space(far[:middle], 1)]
    unnamed x30, local copies, waits for them, and re-layouts: 10.2 us -> 8.65 us
  transfers between devices with their start and end apart: 29 -> 29, of which waited for: 12 -> 13; matrix products, arithmetic and copies ran while one was open for 10% -> 10% of each run, Pallas kernels for 18% -> 20%
where the time goes in v4:
time: 129 us; the launch traced here: 128 us
  Pallas kernels  39.7 us (31%)
  starting transfers between devices  32.4 us (25%)
  waiting for transfers between devices  29.1 us (23%)
  other arithmetic  14.7 us (11%)
  local copies, waits for them, and re-layouts  10.5 us (8%)
  between operations  1.95 us (2%)
    pallas_call x14, Pallas kernels, call(): pl.pallas_call(body, out_shape=tuple(outs) if many else outs, in_specs=li...  35.4 us
    ppermute x20, starting transfers between devices, swap_space(): return lax.ppermute(cells, 'space', [(i, i ^ mask) for i in range(count)])  20.1 us
    ppermute x20, waiting for transfers between devices, swap_space(): return lax.ppermute(cells, 'space', [(i, i ^ mask) for i in range(count)])  15.4 us
    ppermute x7, waiting for transfers between devices, swap_image(): return lax.ppermute(cells, ('dp', 'space'), pairs)  13.7 us
    unnamed x30, local copies, waits for them, and re-layouts  8.65 us
    ppermute x7, starting transfers between devices, swap_image(): return lax.ppermute(cells, ('dp', 'space'), pairs)  7.72 us
    mul x8, other arithmetic, place(): piece.astype(f32) * line_back  5.69 us
    pallas_call x2, Pallas kernels, place(): pl.pallas_call(functools.partial(place_body, (zones, height, width), coun...  4.25 us
  transfers between devices with their start and end apart: 29, of which 13 were waited for; matrix products, arithmetic and copies ran while one was open for 10% of the time, Pallas kernels for 20%

profile of v4, /device:TPU:0, one launch (start us, length us, event | category | flops | bytes accessed | tf_op | source)
XLA Modules:
  0.0 128.5 jit_solution(489895314479242920)
XLA Ops:
  1.4 5.7 %shard_map.111 = (f32[8,320]{1,0:T(8,128)}, bf16[2,320,512]{2,1,0:T(8,128)(2,1)}, bf16[2,320,512]{2,1,0:T(8,128)(2,1)}) custom-call(s32[1]{0:T(128)S(6)} %copy.14.step_ref, bf16[4,320,512]{2,1,0:T(8,128)(2,1)} %bitcast.62, bf16[4,320,512]{2,1,0:T(8,128)(2,1)} %bitcast.67), custom_call_target="tpu_custom_call" | custom-call | flops 39321600 | bytes 2621440 | tf_op jit(solution)/shard_map/pallas_call | solution.py:29
  7.1 3.3 %collective-permute-start = (bf16[2,320,512]{2,1,0:T(8,128)(2,1)}, bf16[2,320,512]{2,1,0:T(8,128)(2,1)}, u32[]{:S(2)}, u32[]{:S(2)}) collective-permute-start(bf16[2,320,512]{2,1,0:T(8,128)(2,1)} %get-tuple-element.24), channel_id=1, source_target_pairs={{0,1},{1,2},{2,3},{3,4},{4,5},{5,6},{6,7},{8,9},{9,10},{10,11},{11... | collective-permute-start | bytes 1966088 | tf_op jit(solution)/shard_map/ppermute | solution.py:494
  11.6 2.5 %collective-permute-start.2 = (f32[8,320]{1,0:T(8,128)}, f32[8,320]{1,0:T(8,128)S(1)}, u32[]{:S(2)}, u32[]{:S(2)}) collective-permute-start(f32[8,320]{1,0:T(8,128)} %get-tuple-element.26.refs_0_), channel_id=1, source_target_pairs={{0,1},{1,0},{2,3},{3,2},{4,5},{5,4},{6,7},{7,6},{8,9},{9,8},{10,11... | collective-permute-start | bytes 30728 | tf_op jit(solution)/shard_map/ppermute | solution.py:431
  18.4 2.2 %collective-permute-start.4 = (f32[8,320]{1,0:T(8,128)S(1)}, f32[8,320]{1,0:T(8,128)S(1)}, u32[]{:S(2)}, u32[]{:S(2)}) collective-permute-start(f32[8,320]{1,0:T(8,128)S(1)} %get-tuple-element.27.refs_0_), channel_id=1, source_target_pairs={{0,4},{1,5},{2,6},{3,7},{4,0},{5,1},{6,2},{7,3},{8,12},{9,13},{10,... | collective-permute-start | bytes 30728 | tf_op jit(solution)/shard_map/ppermute | solution.py:431
  22.3 2.7 %collective-permute-done.3.refs_1_ = f32[8,320]{1,0:T(8,128)S(1)} collective-permute-done((f32[8,320]{1,0:T(8,128)S(1)}, f32[8,320]{1,0:T(8,128)S(1)}, u32[]{:S(2)}, u32[]{:S(2)}) %collective-permute-start.3) | collective-permute-done | bytes 10272 | tf_op jit(solution)/shard_map/ppermute | solution.py:431
  27.3 1.9 %shard_map.118 = (bf16[320,2048]{1,0:T(8,128)(2,1)S(1)}, f32[320,960]{1,0:T(8,128)S(1)}) custom-call(bf16[4,320,512]{2,1,0:T(8,128)(2,1)S(1)} %bitcast.63, bf16[960,2048]{1,0:T(8,128)(2,1)S(1)} %shard_map.117.taps_ref, f32[8,320]{1,0:T(8,128)S(1)} %shard_map.113.stats_ref, f32[320]{0:T(512)S(1)} %copy-done.7, f32[320]{0:T(512)S(1)} %copy-done.8), custom_call_target="tpu_custom_call" | custom-call | flops 1258291200 | bytes 5242880 | tf_op jit(solution)/shard_map/pallas_call | solution.py:29
  29.3 6.6 %shard_map.119 = (f32[4,4,40,768]{3,2,1,0:T(8,128)S(1)}, f32[2,4,40,768]{3,2,1,0:T(8,128)}, f32[2,4,40,768]{3,2,1,0:T(8,128)}, bf16[960,1024]{1,0:T(8,128)(2,1)S(1)}) custom-call(s32[4]{0:T(128)S(1)} %pad_add_fusion.where_ref, bf16[320,2048]{1,0:T(8,128)(2,1)S(1)} %get-tuple-element.31.act_ref, bf16[960,2048]{1,0:T(8,128)(2,1)S(1)} %shard_map.117.taps_ref, ...), custom_call_target="tpu_custom_call" | custom-call | flops 3774873600 | bytes 5242880 | tf_op jit(solution)/shard_map/pallas_call | solution.py:29
  40.2 1.9 %collective-permute-done.6.other_ref = f32[8,384]{1,0:T(8,128)S(1)} collective-permute-done((f32[8,384]{1,0:T(8,128)S(1)}, f32[8,384]{1,0:T(8,128)S(1)}, u32[]{:S(2)}, u32[]{:S(2)}) %collective-permute-start.6) | collective-permute-done | bytes 12320 | tf_op jit(solution)/shard_map/ppermute | solution.py:440
  45.5 3.0 %multiply_convert_fusion = f16[2,4,40,768]{3,2,1,0:T(8,128)(2,1)} fusion(f32[2,4,40,768]{3,2,1,0:T(8,128)} %collective-permute-done.13, f32[4,4,40,768]{3,2,1,0:T(8,128)} %copy-done.5, f32[]{:T(128)} %bitcast.21), kind=kLoop, calls=%fused_computation.2 | loop fusion | flops 737280 | bytes 2457604 | tf_op jit(solution)/shard_map/convert_element_type | solution.py:608
  51.1 2.1 %copy-done.2 = bf16[960,2048]{1,0:T(8,128)(2,1)S(1)} copy-done((bf16[960,2048]{1,0:T(8,128)(2,1)S(1)}, bf16[960,2048]{1,0:T(8,128)(2,1)}, u32[]{:S(2)}) %copy-start.2) | copy-done | bytes 3932184
  56.4 6.3 %shard_map.120 = (f32[4,320,512]{2,1,0:T(8,128)S(1)}, f32[8,320]{1,0:T(8,128)S(1)}) custom-call(bf16[4,320,512]{2,1,0:T(8,128)(2,1)S(1)} %bitcast.64, bf16[960,2048]{1,0:T(8,128)(2,1)S(1)} %copy-done.2, bf16[960,1024]{1,0:T(8,128)(2,1)S(1)} %copy-done.13, f32[8,320]{1,0:T(8,128)S(1)} %shard_map.113.stats_ref, f32[320]{0:T(512)S(1)} %copy-done.7, ...), custom_call_target="tpu_custom_call" | custom-call | flops 3774873600 | bytes 5242880 | tf_op jit(solution)/shard_map/pallas_call | solution.py:29
  64.3 2.5 %collective-permute-start.11 = (f32[8,320]{1,0:T(8,128)S(1)}, f32[8,320]{1,0:T(8,128)S(1)}, u32[]{:S(2)}, u32[]{:S(2)}) collective-permute-start(f32[8,320]{1,0:T(8,128)S(1)} %shard_map.121.refs_0_), channel_id=1, source_target_pairs={{0,6},{1,7},{2,4},{3,5},{4,2},{5,3},{6,0},{7,1},{8,14},{9,15},{10,... | collective-permute-start | bytes 30728 | tf_op jit(solution)/shard_map/ppermute | solution.py:431
  67.5 2.0 %multiply_add_fusion = f32[2,4,40,768]{3,2,1,0:T(8,128)S(1)} fusion(f16[2,4,40,768]{3,2,1,0:T(8,128)(2,1)S(1)} %collective-permute-done.14, f32[2,4,40,768]{3,2,1,0:T(8,128)} %collective-permute-done.12, f32[4,4,40,768]{3,2,1,0:T(8,128)S(1)} %copy-done.6, f32[]{:T(128)} %bitcast.22), kind=kLoop, calls=%fused_computation.1 | loop fusion | flops 983040 | bytes 3440644 | tf_op jit(solution)/shard_map/add | solution.py:609
  71.8 4.9 %collective-permute-done.15 = f16[1,4,40,768]{3,2,1,0:T(8,128)(2,1)S(1)} collective-permute-done((f16[1,4,40,768]{3,2,1,0:T(8,128)(2,1)S(1)}, f16[1,4,40,768]{3,2,1,0:T(8,128)(2,1)S(1)}, u32[]{:S(2)}, u32[]{:S(2)}) %collective-permute-start.15) | collective-permute-done | bytes 245792 | tf_op jit(solution)/shard_map/ppermute | solution.py:440
  79.6 2.9 %collective-permute-start.18 = (f16[40,768]{1,0:T(8,128)(2,1)S(1)}, f16[40,768]{1,0:T(8,128)(2,1)S(1)}, u32[]{:S(2)}, u32[]{:S(2)}) collective-permute-start(f16[40,768]{1,0:T(8,128)(2,1)S(1)} %get-tuple-element.45), channel_id=1, source_target_pairs={{0,6},{1,7},{2,4},{3,5},{4,2},{5,3},{6,0},{7,1},{8,14},{9,15},{10,... | collective-permute-start | bytes 184328 | tf_op jit(solution)/shard_map/ppermute | solution.py:431
  83.4 2.5 %collective-permute-done.17 = f16[40,768]{1,0:T(8,128)(2,1)S(1)} collective-permute-done((f16[40,768]{1,0:T(8,128)(2,1)S(1)}, f16[40,768]{1,0:T(8,128)(2,1)S(1)}, u32[]{:S(2)}, u32[]{:S(2)}) %collective-permute-start.17) | collective-permute-done | bytes 61472 | tf_op jit(solution)/shard_map/ppermute | solution.py:431
  88.5 2.0 %collective-permute-start.20 = (f16[40,768]{1,0:T(8,128)(2,1)S(1)}, f16[40,768]{1,0:T(8,128)(2,1)S(1)}, u32[]{:S(2)}, u32[]{:S(2)}) collective-permute-start(f16[40,768]{1,0:T(8,128)(2,1)S(1)} %fusion.8), channel_id=1, source_target_pairs={{0,4},{1,5},{2,6},{3,7},{4,0},{5,1},{6,2},{7,3},{8,12},{9,13},{10,... | collective-permute-start | bytes 184328 | tf_op jit(solution)/shard_map/ppermute | solution.py:431
  91.8 2.5 %collective-permute-done.20 = f16[40,768]{1,0:T(8,128)(2,1)S(1)} collective-permute-done((f16[40,768]{1,0:T(8,128)(2,1)S(1)}, f16[40,768]{1,0:T(8,128)(2,1)S(1)}, u32[]{:S(2)}, u32[]{:S(2)}) %collective-permute-start.20) | collective-permute-done | bytes 61472 | tf_op jit(solution)/shard_map/ppermute | solution.py:431
  94.3 2.2 %collective-permute-done.21 = f16[40,768]{1,0:T(8,128)(2,1)S(1)} collective-permute-done((f16[40,768]{1,0:T(8,128)(2,1)S(1)}, f16[40,768]{1,0:T(8,128)(2,1)S(1)}, u32[]{:S(2)}, u32[]{:S(2)}) %collective-permute-start.21) | collective-permute-done | bytes 61472 | tf_op jit(solution)/shard_map/ppermute | solution.py:431
  97.2 7.9 %shard_map.116 = bf16[4,320,512]{2,1,0:T(8,128)(2,1)} custom-call(s32[2]{0:T(128)S(1)} %add_convert_fusion.ends_ref, bf16[4,320,512]{2,1,0:T(8,128)(2,1)S(1)} %bitcast.65, bf16[2,320,512]{2,1,0:T(8,128)(2,1)} %collective-permute-done.above_ref, bf16[2,320,512]{2,1,0:T(8,128)(2,1)} %collective-permute-done.1.below_ref, f32[8,320]{1,0:T(8,128)S(1)} %shard_map.113.stats_ref, ...), custom_call_target="tpu_custom_call" | custom-call | flops 3774873600 | bytes 5242880 | tf_op jit(solution)/shard_map/pallas_call | solution.py:29
  106.5 2.3 %shard_map.123 = bf16[4,320,512]{2,1,0:T(8,128)(2,1)} custom-call(f32[4,320,512]{2,1,0:T(8,128)S(1)} %get-tuple-element.34.grad_ref, bf16[4,320,512]{2,1,0:T(8,128)(2,1)S(1)} %bitcast.66, bf16[4,320,512]{2,1,0:T(8,128)(2,1)S(1)} %bitcast.69, f32[8,320]{1,0:T(8,128)S(1)} %shard_map.113.stats_ref, f32[8,320]{1,0:T(8,128)S(1)} %get-tuple-element.37.sums_ref.total_ref), custom_call_target="tpu_custom_call" | custom-call | flops 13107200 | bytes 6553600 | tf_op jit(solution)/shard_map/pallas_call | solution.py:29
  111.3 3.6 %collective-permute-done.22 = f16[4,40,768]{2,1,0:T(8,128)(2,1)S(1)} collective-permute-done((f16[4,40,768]{2,1,0:T(8,128)(2,1)S(1)}, f16[4,40,768]{2,1,0:T(8,128)(2,1)S(1)}, u32[]{:S(2)}, u32[]{:S(2)}) %collective-permute-start.22) | collective-permute-done | bytes 245792 | tf_op jit(solution)/shard_map/ppermute | solution.py:440
  117.9 3.2 %collective-permute-done.23 = f16[4,40,768]{2,1,0:T(8,128)(2,1)S(1)} collective-permute-done((f16[4,40,768]{2,1,0:T(8,128)(2,1)S(1)}, f16[4,40,768]{2,1,0:T(8,128)(2,1)S(1)}, u32[]{:S(2)}, u32[]{:S(2)}) %collective-permute-start.23) | collective-permute-done | bytes 245792 | tf_op jit(solution)/shard_map/ppermute | solution.py:440
  122.6 2.5 %shard_map.124.refs_2_ = f32[9,320,320]{2,1,0:T(8,128)} custom-call(s32[10]{0:T(128)S(1)} %stack.108.places_ref, f32[4,40,768]{2,1,0:T(8,128)S(1)} %convert_multiply_fusion.5.refs_0_, f32[4,40,768]{2,1,0:T(8,128)S(1)} %convert_multiply_fusion.4.refs_1_, f32[4,40,768]{2,1,0:T(8,128)S(1)} %convert_multiply_fusion.3.refs_2_, ...), custom_call_target="tpu_custom_call" | custom-call | bytes 5898240 | tf_op jit(solution)/shard_map/pallas_call | solution.py:641
  (108 shorter events, 47.3 us)
Async XLA Ops:
  7.1 22.2 %collective-permute-start = (bf16[2,320,512]{2,1,0:T(8,128)(2,1)}, bf16[2,320,512]{2,1,0:T(8,128)(2,1)}, u32[]{:S(2)}, u32[]{:S(2)}) collective-permute-start(bf16[2,320,512]{2,1,0:T(8,128)(2,1)} %get-tuple-element.24), channel_id=1, source_target_pairs={{0,1},{1,2},{2,3},{3,4},{4,5},{5,6},{6,7},{8,9},{9,10},{10,11},{11... | collective-permute-start | bytes 1966088 | tf_op jit(solution)/shard_map/ppermute | solution.py:494
  10.3 19.0 %collective-permute-start.1 = (bf16[2,320,512]{2,1,0:T(8,128)(2,1)}, bf16[2,320,512]{2,1,0:T(8,128)(2,1)}, u32[]{:S(2)}, u32[]{:S(2)}) collective-permute-start(bf16[2,320,512]{2,1,0:T(8,128)(2,1)} %get-tuple-element.25), channel_id=1, source_target_pairs={{1,0},{2,1},{3,2},{4,3},{5,4},{6,5},{7,6},{9,8},{10,9},{11,10},{12... | collective-permute-start | bytes 1966088 | tf_op jit(solution)/shard_map/ppermute | solution.py:495
  16.8 8.2 %collective-permute-start.3 = (f32[8,320]{1,0:T(8,128)S(1)}, f32[8,320]{1,0:T(8,128)S(1)}, u32[]{:S(2)}, u32[]{:S(2)}) collective-permute-start(f32[8,320]{1,0:T(8,128)S(1)} %get-tuple-element.27.refs_0_), channel_id=1, source_target_pairs={{0,2},{1,3},{2,0},{3,1},{4,6},{5,7},{6,4},{7,5},{8,10},{9,11},{10,... | collective-permute-start | bytes 30728 | tf_op jit(solution)/shard_map/ppermute | solution.py:431
  18.4 7.8 %collective-permute-start.4 = (f32[8,320]{1,0:T(8,128)S(1)}, f32[8,320]{1,0:T(8,128)S(1)}, u32[]{:S(2)}, u32[]{:S(2)}) collective-permute-start(f32[8,320]{1,0:T(8,128)S(1)} %get-tuple-element.27.refs_0_), channel_id=1, source_target_pairs={{0,4},{1,5},{2,6},{3,7},{4,0},{5,1},{6,2},{7,3},{8,12},{9,13},{10,... | collective-permute-start | bytes 30728 | tf_op jit(solution)/shard_map/ppermute | solution.py:431
  20.6 6.7 %collective-permute-start.5 = (f32[8,320]{1,0:T(8,128)S(1)}, f32[8,320]{1,0:T(8,128)S(1)}, u32[]{:S(2)}, u32[]{:S(2)}) collective-permute-start(f32[8,320]{1,0:T(8,128)S(1)} %get-tuple-element.27.refs_0_), channel_id=1, source_target_pairs={{0,6},{1,7},{2,4},{3,5},{4,2},{5,3},{6,0},{7,1},{8,14},{9,15},{10,... | collective-permute-start | bytes 30728 | tf_op jit(solution)/shard_map/ppermute | solution.py:431
  38.5 7.0 %collective-permute-start.13 = (f32[2,4,40,768]{3,2,1,0:T(8,128)}, f32[2,4,40,768]{3,2,1,0:T(8,128)}, u32[]{:S(2)}, u32[]{:S(2)}) collective-permute-start(f32[2,4,40,768]{3,2,1,0:T(8,128)} %get-tuple-element.40), channel_id=1, source_target_pairs={{0,1},{1,0},{2,3},{3,2},{4,5},{5,4},{6,7},{7,6},{8,9},{9,8},{10,11... | collective-permute-start | bytes 2949128 | tf_op jit(solution)/shard_map/ppermute | solution.py:431
  40.0 27.5 %collective-permute-start.12 = (f32[2,4,40,768]{3,2,1,0:T(8,128)}, f32[2,4,40,768]{3,2,1,0:T(8,128)}, u32[]{:S(2)}, u32[]{:S(2)}) collective-permute-start(f32[2,4,40,768]{3,2,1,0:T(8,128)} %get-tuple-element.39), channel_id=1, source_target_pairs={{0,1},{1,0},{2,3},{3,2},{4,5},{5,4},{6,7},{7,6},{8,9},{9,8},{10,11... | collective-permute-start | bytes 2949128 | tf_op jit(solution)/shard_map/ppermute | solution.py:431
  43.4 6.8 %collective-permute-start.7 = (f32[8,384]{1,0:T(8,128)S(1)}, f32[8,384]{1,0:T(8,128)S(1)}, u32[]{:S(2)}, u32[]{:S(2)}) collective-permute-start(f32[8,384]{1,0:T(8,128)S(1)} %get-tuple-element.29.mine_ref), channel_id=1, source_target_pairs={{0,16},{1,9},{2,18},{3,11},{4,20},{5,13},{6,22},{7,15},{8,24},{9,1... | collective-permute-start | bytes 36872 | tf_op jit(solution)/shard_map/ppermute | solution.py:440
  48.5 19.0 %collective-permute-start.14 = (f16[2,4,40,768]{3,2,1,0:T(8,128)(2,1)}, f16[2,4,40,768]{3,2,1,0:T(8,128)(2,1)S(1)}, u32[]{:S(2)}, u32[]{:S(2)}) collective-permute-start(f16[2,4,40,768]{3,2,1,0:T(8,128)(2,1)} %multiply_convert_fusion), channel_id=1, source_target_pairs={{0,8},{1,17},{2,10},{3,19},{4,12},{5,21},{6,14},{7,23},{8,0},{9,25... | collective-permute-start | bytes 1474568 | tf_op jit(solution)/shard_map/ppermute | solution.py:440
  64.0 7.0 %collective-permute-start.10 = (f32[8,320]{1,0:T(8,128)S(1)}, f32[8,320]{1,0:T(8,128)S(1)}, u32[]{:S(2)}, u32[]{:S(2)}) collective-permute-start(f32[8,320]{1,0:T(8,128)S(1)} %shard_map.121.refs_0_), channel_id=1, source_target_pairs={{0,4},{1,5},{2,6},{3,7},{4,0},{5,1},{6,2},{7,3},{8,12},{9,13},{10,... | collective-permute-start | bytes 30728 | tf_op jit(solution)/shard_map/ppermute | solution.py:431
  64.3 6.7 %collective-permute-start.11 = (f32[8,320]{1,0:T(8,128)S(1)}, f32[8,320]{1,0:T(8,128)S(1)}, u32[]{:S(2)}, u32[]{:S(2)}) collective-permute-start(f32[8,320]{1,0:T(8,128)S(1)} %shard_map.121.refs_0_), channel_id=1, source_target_pairs={{0,6},{1,7},{2,4},{3,5},{4,2},{5,3},{6,0},{7,1},{8,14},{9,15},{10,... | collective-permute-start | bytes 30728 | tf_op jit(solution)/shard_map/ppermute | solution.py:431
  70.4 6.3 %collective-permute-start.15 = (f16[1,4,40,768]{3,2,1,0:T(8,128)(2,1)S(1)}, f16[1,4,40,768]{3,2,1,0:T(8,128)(2,1)S(1)}, u32[]{:S(2)}, u32[]{:S(2)}) collective-permute-start(f16[1,4,40,768]{3,2,1,0:T(8,128)(2,1)S(1)} %fusion), channel_id=1, source_target_pairs={{0,16},{1,9},{2,18},{3,11},{4,20},{5,13},{6,22},{7,15},{8,24},{9,1... | collective-permute-start | bytes 737288 | tf_op jit(solution)/shard_map/ppermute | solution.py:440
  78.1 5.4 %collective-permute-start.16 = (f16[40,768]{1,0:T(8,128)(2,1)S(1)}, f16[40,768]{1,0:T(8,128)(2,1)S(1)}, u32[]{:S(2)}, u32[]{:S(2)}) collective-permute-start(f16[40,768]{1,0:T(8,128)(2,1)S(1)} %get-tuple-element.44), channel_id=1, source_target_pairs={{0,2},{1,3},{2,0},{3,1},{4,6},{5,7},{6,4},{7,5},{8,10},{9,11},{10,... | collective-permute-start | bytes 184328 | tf_op jit(solution)/shard_map/ppermute | solution.py:431
  79.4 6.4 %collective-permute-start.17 = (f16[40,768]{1,0:T(8,128)(2,1)S(1)}, f16[40,768]{1,0:T(8,128)(2,1)S(1)}, u32[]{:S(2)}, u32[]{:S(2)}) collective-permute-start(f16[40,768]{1,0:T(8,128)(2,1)S(1)} %get-tuple-element.46), channel_id=1, source_target_pairs={{0,4},{1,5},{2,6},{3,7},{4,0},{5,1},{6,2},{7,3},{8,12},{9,13},{10,... | collective-permute-start | bytes 184328 | tf_op jit(solution)/shard_map/ppermute | solution.py:431
  79.6 6.3 %collective-permute-start.18 = (f16[40,768]{1,0:T(8,128)(2,1)S(1)}, f16[40,768]{1,0:T(8,128)(2,1)S(1)}, u32[]{:S(2)}, u32[]{:S(2)}) collective-permute-start(f16[40,768]{1,0:T(8,128)(2,1)S(1)} %get-tuple-element.45), channel_id=1, source_target_pairs={{0,6},{1,7},{2,4},{3,5},{4,2},{5,3},{6,0},{7,1},{8,14},{9,15},{10,... | collective-permute-start | bytes 184328 | tf_op jit(solution)/shard_map/ppermute | solution.py:431
  88.5 5.8 %collective-permute-start.20 = (f16[40,768]{1,0:T(8,128)(2,1)S(1)}, f16[40,768]{1,0:T(8,128)(2,1)S(1)}, u32[]{:S(2)}, u32[]{:S(2)}) collective-permute-start(f16[40,768]{1,0:T(8,128)(2,1)S(1)} %fusion.8), channel_id=1, source_target_pairs={{0,4},{1,5},{2,6},{3,7},{4,0},{5,1},{6,2},{7,3},{8,12},{9,13},{10,... | collective-permute-start | bytes 184328 | tf_op jit(solution)/shard_map/ppermute | solution.py:431
  90.5 6.0 %collective-permute-start.21 = (f16[40,768]{1,0:T(8,128)(2,1)S(1)}, f16[40,768]{1,0:T(8,128)(2,1)S(1)}, u32[]{:S(2)}, u32[]{:S(2)}) collective-permute-start(f16[40,768]{1,0:T(8,128)(2,1)S(1)} %fusion.8), channel_id=1, source_target_pairs={{0,6},{1,7},{2,4},{3,5},{4,2},{5,3},{6,0},{7,1},{8,14},{9,15},{10,... | collective-permute-start | bytes 184328 | tf_op jit(solution)/shard_map/ppermute | solution.py:431
  96.6 13.4 %collective-permute-start.25 = (f16[4,40,768]{2,1,0:T(8,128)(2,1)S(1)}, f16[4,40,768]{2,1,0:T(8,128)(2,1)S(1)}, u32[]{:S(2)}, u32[]{:S(2)}) collective-permute-start(f16[4,40,768]{2,1,0:T(8,128)(2,1)S(1)} %pad_maximum_fusion), channel_id=1, source_target_pairs={{0,8},{1,17},{2,10},{3,19},{4,12},{5,21},{6,14},{7,23},{8,0},{9,25... | collective-permute-start | bytes 737288 | tf_op jit(solution)/shard_map/ppermute | solution.py:440
  108.8 6.2 %collective-permute-start.22 = (f16[4,40,768]{2,1,0:T(8,128)(2,1)S(1)}, f16[4,40,768]{2,1,0:T(8,128)(2,1)S(1)}, u32[]{:S(2)}, u32[]{:S(2)}) collective-permute-start(f16[4,40,768]{2,1,0:T(8,128)(2,1)S(1)} %pad_maximum_fusion), channel_id=1, source_target_pairs={{0,16},{1,9},{2,18},{3,11},{4,20},{5,13},{6,22},{7,15},{8,24},{9,1... | collective-permute-start | bytes 737288 | tf_op jit(solution)/shard_map/ppermute | solution.py:440
  109.3 7.9 %collective-permute-start.26 = (f16[4,40,768]{2,1,0:T(8,128)(2,1)S(1)}, f16[4,40,768]{2,1,0:T(8,128)(2,1)S(1)}, u32[]{:S(2)}, u32[]{:S(2)}) collective-permute-start(f16[4,40,768]{2,1,0:T(8,128)(2,1)S(1)} %pad_maximum_fusion), channel_id=1, source_target_pairs={{0,1},{1,0},{2,3},{3,2},{4,5},{5,4},{6,7},{7,6},{8,9},{9,8},{10,11... | collective-permute-start | bytes 737288 | tf_op jit(solution)/shard_map/ppermute | solution.py:431
  110.0 11.1 %collective-permute-start.28 = (f16[4,40,768]{2,1,0:T(8,128)(2,1)S(1)}, f16[4,40,768]{2,1,0:T(8,128)(2,1)S(1)}, u32[]{:S(2)}, u32[]{:S(2)}) collective-permute-start(f16[4,40,768]{2,1,0:T(8,128)(2,1)S(1)} %collective-permute-done.25), channel_id=1, source_target_pairs={{0,1},{1,0},{2,3},{3,2},{4,5},{5,4},{6,7},{7,6},{8,9},{9,8},{10,11... | collective-permute-start | bytes 737288 | tf_op jit(solution)/shard_map/ppermute | solution.py:431
  115.0 6.9 %collective-permute-start.27 = (f16[4,40,768]{2,1,0:T(8,128)(2,1)S(1)}, f16[4,40,768]{2,1,0:T(8,128)(2,1)S(1)}, u32[]{:S(2)}, u32[]{:S(2)}) collective-permute-start(f16[4,40,768]{2,1,0:T(8,128)(2,1)S(1)} %collective-permute-done.22), channel_id=1, source_target_pairs={{0,1},{1,0},{2,3},{3,2},{4,5},{5,4},{6,7},{7,6},{8,9},{9,8},{10,11... | collective-permute-start | bytes 737288 | tf_op jit(solution)/shard_map/ppermute | solution.py:431
  115.0 6.2 %collective-permute-start.23 = (f16[4,40,768]{2,1,0:T(8,128)(2,1)S(1)}, f16[4,40,768]{2,1,0:T(8,128)(2,1)S(1)}, u32[]{:S(2)}, u32[]{:S(2)}) collective-permute-start(f16[4,40,768]{2,1,0:T(8,128)(2,1)S(1)} %collective-permute-done.22), channel_id=1, source_target_pairs={{0,8},{1,17},{2,10},{3,19},{4,12},{5,21},{6,14},{7,23},{8,0},{9,25... | collective-permute-start | bytes 737288 | tf_op jit(solution)/shard_map/ppermute | solution.py:440
  121.2 4.7 %collective-permute-start.24 = (f16[4,40,768]{2,1,0:T(8,128)(2,1)S(1)}, f16[4,40,768]{2,1,0:T(8,128)(2,1)S(1)}, u32[]{:S(2)}, u32[]{:S(2)}) collective-permute-start(f16[4,40,768]{2,1,0:T(8,128)(2,1)S(1)} %collective-permute-done.23), channel_id=1, source_target_pairs={{0,1},{1,0},{2,3},{3,2},{4,5},{5,4},{6,7},{7,6},{8,9},{9,8},{10,11... | collective-permute-start | bytes 737288 | tf_op jit(solution)/shard_map/ppermute | solution.py:431
  (20 other events, 206.4 us)

commit v5 on v4

--- a/solution.py
+++ b/solution.py
@@ -65,9 +65,7 @@
     return total
 
 
-def stats_body(
-    count, step_ref, latent_hbm, cot_hbm, out_ref, down_ref, up_ref, latent_ref, cot_ref, sem
-):
+def stats_body(count, step_ref, latent_hbm, cot_hbm, out_ref, latent_ref, cot_ref, sem):
     row_count, channels, cols = latent_ref.shape
     loads = []
     for number, (source, target) in enumerate(((latent_hbm, latent_ref), (cot_hbm, cot_ref))):
@@ -77,33 +75,25 @@
             loads.append(load)
     member = member_matrix(channels)
     ones = jnp.ones((cols, LANES), bf16)
-    tall = jnp.ones((8, cols), bf16)
     sums = jnp.zeros((channels, LANES), f32)
     for row in range(row_count):
         loads[row].wait()
         sums = sums + contract(latent_ref[row], ones, ((1,), (0,)))
     mean = contract(member, sums, ((1,), (0,)), HIGHEST) / count
-    grads = jnp.zeros((8, channels), f32)
-    top = jnp.zeros((channels, LANES), f32)
-    for row in range(row_count):
-        loads[row_count + row].wait()
-        grads = grads + contract(tall, cot_ref[row], ((1,), (1,)))
-        size = jnp.abs(cot_ref[row].astype(f32))
-        for start in range(0, cols, LANES):
-            top = jnp.maximum(top, size[:, start : start + LANES])
-    for ref, row in ((down_ref, row_count - 1), (up_ref, 0)):
-        ref[0] = cot_ref[row]
-        ref[1] = latent_ref[row]
     squares = jnp.zeros((channels, LANES), f32)
     for row in range(row_count):
         centered = latent_ref[row].astype(f32) - mean[:, :1]
         squares = squares + fold_lanes(centered * centered)
     grouped = contract(member, squares, ((1,), (0,)), HIGHEST)
+    top = jnp.zeros((channels, LANES), bf16)
+    for row in range(row_count):
+        loads[row_count + row].wait()
+        size = jnp.abs(cot_ref[row])
+        for start in range(0, cols, LANES):
+            top = jnp.maximum(top, size[:, start : start + LANES])
     step = jnp.full((8, channels), step_ref[0].astype(f32))
-    largest = jnp.broadcast_to(jnp.max(top), (8, channels))
-    out_ref[...] = rows_of(
-        lane_form(mean) * (1.0 / LANES), lane_form(grouped), grads, largest, step
-    )
+    largest = jnp.broadcast_to(jnp.max(top.astype(f32)), (8, channels))
+    out_ref[...] = rows_of(lane_form(mean) * (1.0 / LANES), lane_form(grouped), largest, step)
 
 
 def tree_sum(parts):
@@ -112,26 +102,15 @@
     return parts[0]
 
 
-def merge_body(count, total, parts, *refs):
-    refs, outs = refs[:parts], refs[parts:]
-    parts = [ref[...] for ref in refs]
+def merge_body(count, total, *refs):
+    parts, out_ref = [ref[...] for ref in refs[:-1]], refs[-1]
     mean = tree_sum([part[0:1] for part in parts]) / len(parts)
     squares = tree_sum([part[1:2] + count * (part[0:1] - mean) ** 2 for part in parts])
     if total:
         squares = lax.rsqrt(squares / total + epsilon)
-    grads = tree_sum([part[2:3] for part in parts])
-    largest = functools.reduce(jnp.maximum, [part[3:4] for part in parts])
-    step = parts[0][4:5]
-    shape = parts[0].shape
-    rows = (mean, squares, grads, largest, step)
-    outs[0][...] = rows_of(*[jnp.broadcast_to(row, shape) for row in rows])
-    if len(outs) > 1:
-        table_ref = outs[1]
-        channels = shape[1]
-        table_ref[...] = jnp.zeros(table_ref.shape, f32)
-        table_ref[0:1, :channels] = grads
-        table_ref[0:1, channels : channels + NOTE] = step[:, :NOTE]
-        table_ref[0:1, channels + NOTE : channels + 2 * NOTE] = largest[:, :NOTE]
+    largest = functools.reduce(jnp.maximum, [part[2:3] for part in parts])
+    rows = (mean, squares, largest, parts[0][3:4])
+    out_ref[...] = rows_of(*[jnp.broadcast_to(row, out_ref.shape) for row in rows])
 
 
 def column_values(stats_ref, gain_ref, bias_ref):
@@ -178,13 +157,24 @@
         )
 
 
-def taps_body(cot_ref, taps_ref):
-    for row in range(cot_ref.shape[0]):
+def taps_body(cot_ref, taps_ref, sums_ref):
+    row_count, channels, cols = cot_ref.shape
+    tall = jnp.ones((8, cols), bf16)
+    sums = jnp.zeros((8, channels), f32)
+    for row in range(row_count):
         put_taps(taps_ref, row, cot_ref[row], True)
-
-
-def middle_body(latent_ref, taps_ref, stats_ref, gain_ref, bias_ref, act_ref, found_ref):
-    row_count, _, cols = latent_ref.shape
+        sums = sums + contract(tall, cot_ref[row], ((1,), (1,)))
+    sums_ref[...] = sums
+
+
+def middle_body(
+    latent_ref, taps_ref, stats_ref, gain_ref, bias_ref, sums_ref, act_ref, found_ref, table_ref
+):
+    row_count, channels, cols = latent_ref.shape
+    table_ref[...] = jnp.zeros(table_ref.shape, f32)
+    table_ref[0:1, :channels] = sums_ref[0:1]
+    table_ref[0:1, channels : channels + NOTE] = stats_ref[3:4, :NOTE]
+    table_ref[0:1, channels + NOTE : channels + 2 * NOTE] = stats_ref[2:3, :NOTE]
     values = column_values(stats_ref, gain_ref, bias_ref)
     for row in range(row_count):
         act_ref[:, row * cols : (row + 1) * cols] = activate(latent_ref[row], values)
@@ -199,8 +189,8 @@
     channels, positions = act_ref.shape
     core, mine, other, zone_index = [where_ref[i] for i in range(4)]
     quarter = blocks // 4
-    put_taps(edge_ref, 0, above_ref[0], True)
-    put_taps(edge_ref, 1, below_ref[0], True)
+    put_taps(edge_ref, 0, above_ref[...], True)
+    put_taps(edge_ref, 1, below_ref[...], True)
     tap_width = zones * width // 3
 
     def store(ref, place, found, block, tap_row):
@@ -261,7 +251,7 @@
     values = column_values(stats_ref, gain_ref, bias_ref)
     for place, ref, end in ((0, above_ref, 0), (row_count + 1, below_ref, 1)):
         keep = ends_ref[end].astype(f32)
-        put_taps(taps_ref, place, (activate(ref[1], values).astype(f32) * keep).astype(bf16), False)
+        put_taps(taps_ref, place, (activate(ref[...], values).astype(f32) * keep).astype(bf16), False)
     for row in range(row_count):
         put_taps(taps_ref, row + 1, activate(latent_ref[row], values), False)
     for tap_row in range(3):
@@ -404,25 +394,20 @@
     steps_ref[...] = jnp.broadcast_to(table[:, channels : channels + 1], steps_ref.shape)
 
 
-def gather_body(images, sums_ref, partner_ref, table_ref, out_ref):
+def gather_body(images, sums_ref, table_ref, out_ref):
     channels = sums_ref.shape[1]
-    table = table_ref[...]
-    rows = [sums_ref[0:1] + partner_ref[0:1], sums_ref[1:2] + partner_ref[1:2]]
-    rows += [largest_note(table, channels)]
-    rows += [table[i : i + 1, :channels] for i in range(images)]
+    rows = [sums_ref[0:1], sums_ref[1:2]]
+    rows += [table_ref[i : i + 1, :channels] for i in range(images)]
     out_ref[...] = rows_of(*[jnp.broadcast_to(row, out_ref.shape) for row in rows])
 
 
-def total_body(factor, spread, gain_ref, bias_ref, *refs):
-    parts, (total_ref, scale_ref) = refs[:-2], refs[-2:]
-    top = functools.reduce(jnp.maximum, [ref[2:3, 0:1] for ref in parts])
-    scale_ref[...] = power_of_two(top, factor, spread, gain_ref, bias_ref, scale_ref.shape)
-    total_ref[...] = tree_sum([ref[...] for ref in parts])
+def total_body(*refs):
+    refs[-1][...] = tree_sum([ref[...] for ref in refs[:-1]])
 
 
 def time_body(count, embed_ref, total_ref, out_ref):
     columns = embed_ref[...].T
-    terms = [columns[:, i : i + 1] * total_ref[3 + i : 4 + i] for i in range(count)]
+    terms = [columns[:, i : i + 1] * total_ref[2 + i : 3 + i] for i in range(count)]
     out_ref[...] = tree_sum(terms)
 
 
@@ -468,6 +453,7 @@
     gain, bias = norm_gain, norm_bias
     smem = pl.BlockSpec(memory_space=pltpu.SMEM)
     vmem = pl.BlockSpec(memory_space=pltpu.VMEM)
+    anywhere = pl.BlockSpec(memory_space=pl.ANY)
     small = jax.ShapeDtypeStruct((8, channels), f32)
 
     down = [(i, i + 1) for i in range(slab_count - 1)]
@@ -477,38 +463,34 @@
     taps = pltpu.VMEM((3 * channels, (row_count + 2) * col_count), bf16)
     flat = pltpu.VMEM((3, channels, 3 * channels), bf16)
 
-    edge = jax.ShapeDtypeStruct((2, channels, col_count), bf16)
-    anywhere = pl.BlockSpec(memory_space=pl.ANY)
     slab = pltpu.VMEM((row_count, channels, col_count), bf16)
-    own, edge_down, edge_up = call(
+    own = call(
         functools.partial(stats_body, local_count),
-        (small, edge, edge),
+        small,
         (timesteps, lat, cot),
         specs=(smem, anywhere, anywhere),
         scratch=(slab, slab, pltpu.SemaphoreType.DMA((2, row_count))),
         moved=2 * lat.size * 2,
         flops=positions * channels * 60,
-        limit=None,
+        limit=63 << 20,
     )
     partner = swap_space(own, 1)
-    above = lax.ppermute(edge_down, "space", down)
-    below = lax.ppermute(edge_up, "space", up)
-    table_shape = jax.ShapeDtypeStruct((-(-image_count // 8) * 8, channels + 2 * NOTE), f32)
-    pair, table = call(
-        functools.partial(merge_body, local_count, None, 2),
-        (small, table_shape),
-        (own, partner),
-        limit=4 << 20,
+    pair = call(
+        functools.partial(merge_body, local_count, None), small, (own, partner), limit=4 << 20
     )
     parts = [pair]
     for mask in range(1, zones):
         parts.append(swap_space(pair, 2 * mask))
+    above = lax.ppermute(cot[row_count - 1], "space", down)
+    below = lax.ppermute(cot[0], "space", up)
+    lat_above = lax.ppermute(lat[row_count - 1], "space", down)
+    lat_below = lax.ppermute(lat[0], "space", up)
     stats = call(
-        functools.partial(merge_body, 2 * local_count, total_count, zones),
-        (small,),
+        functools.partial(merge_body, 2 * local_count, total_count),
+        small,
         tuple(parts),
         limit=4 << 20,
-    )[0]
+    )
 
     orders = [list(range(bits)), list(range(bits))[::-1]]
 
@@ -524,14 +506,18 @@
     part_shape = jax.ShapeDtypeStruct((blocks // 4, zones, height, width), f32)
     share_shape = jax.ShapeDtypeStruct((blocks // 2, zones, height, width), f32)
     taps_shape = jax.ShapeDtypeStruct((3 * channels, positions), bf16)
-    grad_taps = call(taps_body, taps_shape, (cot,), moved=10 * lat.size, limit=6 << 20)
-    act, middle_rows = call(
+    grad_taps, col_sums = call(
+        taps_body, (taps_shape, small), (cot,), moved=10 * lat.size, limit=6 << 20
+    )
+    table_shape = jax.ShapeDtypeStruct((-(-image_count // 8) * 8, channels + 2 * NOTE), f32)
+    act, middle_rows, table = call(
         middle_body,
         (
             jax.ShapeDtypeStruct((channels, positions), bf16),
             jax.ShapeDtypeStruct((channels, 3 * channels), f32),
+            table_shape,
         ),
-        (lat, grad_taps, stats, gain, bias),
+        (lat, grad_taps, stats, gain, bias, col_sums),
         flops=flops // 3,
         moved=8 * lat.size,
         limit=8 << 20,
@@ -577,25 +563,15 @@
         moved=8 * lat.size,
         limit=8 << 20,
     )
-    sums_partner = swap_space(sums, 1)
-    message = jax.ShapeDtypeStruct((-(-(3 + image_count) // 8) * 8, channels), f32)
-    gathered = [
-        call(
-            functools.partial(gather_body, image_count),
-            message,
-            (sums, sums_partner, table),
-            limit=4 << 20,
-        )
-    ]
+    message = jax.ShapeDtypeStruct((-(-(2 + image_count) // 8) * 8, channels), f32)
+    gathered = call(
+        functools.partial(gather_body, image_count), message, (sums, table), limit=4 << 20
+    )
+    gathered = [gathered + swap_space(gathered, 1)]
     for mask in range(1, zones):
         gathered.append(swap_space(gathered[0], 2 * mask))
-    totals, line_scales = call(
-        functools.partial(total_body, factor, spread),
-        (message, scales_shape),
-        (gain, bias, *gathered),
-        limit=4 << 20,
-    )
-    line_scale, line_back = line_scales[0, 0], line_scales[1, 0]
+    totals = call(total_body, message, tuple(gathered), limit=4 << 20)
+    line_scale, line_back = scales[-1]
 
     middle = blocks // 4
     far_in = swap_space(far_high, 1)
@@ -679,7 +655,7 @@
     block_out = call(
         conv_body,
         jax.ShapeDtypeStruct((row_count, channels, col_count), bf16),
-        (ends, lat, above, below, stats, gain, bias, conv_weight, extra),
+        (ends, lat, lat_above, lat_below, stats, gain, bias, conv_weight, extra),
         specs=(smem,) + (vmem,) * 8,
         scratch=(taps, flat),
         flops=flops,

time: 129 us -> 119 us (0.922)
  waiting for transfers between devices: 29.1 us -> 15.8 us
  starting transfers between devices: 32.4 us -> 40.2 us
  local copies, waits for them, and re-layouts: 10.5 us -> 7.78 us
  Pallas kernels: 39.7 us -> 37.6 us
    ppermute x20, waiting for transfers between devices: 15.4 us -> 3.87 us  [swap_space(): return lax.ppermute(cells, 'space', [(i, i ^ mask) for i in range(count)])]
    unnamed x30 -> x26, local copies, waits for them, and re-layouts: 8.65 us -> 3.63 us
    ppermute x2 -> x4, starting transfers between devices: 4.54 us -> 8.66 us  [the longest x1 3.05 us: slab_program(): lat_above = lax.ppermute(lat[row_count - 1], 'space', down)]
    squeeze x0 -> x2, local copies, waits for them, and re-layouts: none -> 2.86 us  [the longest x1 1.99 us: slab_program(): below = lax.ppermute(cot[0], 'space', up)]
    pallas_call x14, Pallas kernels: 35.4 us -> 33.4 us  [call(): pl.pallas_call(body, out_shape=tuple(outs) if many else outs, in_specs=li...]
    ppermute x7, starting transfers between devices: 7.72 us -> 9.78 us  [swap_image(): return lax.ppermute(cells, ('dp', 'space'), pairs)]
    ppermute x7, waiting for transfers between devices: 13.7 us -> 12 us  [swap_image(): return lax.ppermute(cells, ('dp', 'space'), pairs)]
    ppermute x20, starting transfers between devices: 20.1 us -> 21.8 us  [swap_space(): return lax.ppermute(cells, 'space', [(i, i ^ mask) for i in range(count)])]
  transfers between devices with their start and end apart: 29 -> 31, of which waited for: 13 -> 9; matrix products, arithmetic and copies ran while one was open for 10% -> 14% of each run, Pallas kernels for 20% -> 25%
where the time goes in v5:
time: 119 us; the launch traced here: 118 us
  starting transfers between devices  40.2 us (34%)
  Pallas kernels  37.6 us (32%)
  waiting for transfers between devices  15.8 us (13%)
  other arithmetic  14.7 us (12%)
  local copies, waits for them, and re-layouts  7.78 us (7%)
  between operations  1.92 us (2%)
    pallas_call x14, Pallas kernels, call(): pl.pallas_call(body, out_shape=tuple(outs) if many else outs, in_specs=li...  33.4 us
    ppermute x20, starting transfers between devices, swap_space(): return lax.ppermute(cells, 'space', [(i, i ^ mask) for i in range(count)])  21.8 us
    ppermute x7, waiting for transfers between devices, swap_image(): return lax.ppermute(cells, ('dp', 'space'), pairs)  12 us
    ppermute x7, starting transfers between devices, swap_image(): return lax.ppermute(cells, ('dp', 'space'), pairs)  9.78 us
    mul x8, other arithmetic, place(): piece.astype(f32) * line_back  5.39 us
    pallas_call x2, Pallas kernels, place(): pl.pallas_call(functools.partial(place_body, (zones, height, width), coun...  4.25 us
    ppermute x20, waiting for transfers between devices, swap_space(): return lax.ppermute(cells, 'space', [(i, i ^ mask) for i in range(count)])  3.87 us
    unnamed x26, local copies, waits for them, and re-layouts  3.63 us
  transfers between devices with their start and end apart: 31, of which 9 were waited for; matrix products, arithmetic and copies ran while one was open for 14% of the time, Pallas kernels for 25%

profile of v5, /device:TPU:0, one launch (start us, length us, event | category | flops | bytes accessed | tf_op | source)
XLA Modules:
  0.0 118.3 jit_solution(13901083523170981115)
XLA Ops:
  0.6 2.0 %slice_bitcast_fusion = (bf16[320,512]{1,0:T(8,128)(2,1)}, bf16[320,512]{1,0:T(8,128)(2,1)}) fusion(bf16[1,4,320,512]{3,2,1,0:T(8,128)(2,1)} %bitcast.68), kind=kLoop, calls=%fused_computation.14 | loop fusion | bytes 1310720 | tf_op jit(solution)/shard_map/squeeze | solution.py:485
  3.9 3.0 %collective-permute-start.8 = (bf16[320,512]{1,0:T(8,128)(2,1)}, bf16[320,512]{1,0:T(8,128)(2,1)S(1)}, u32[]{:S(2)}, u32[]{:S(2)}) collective-permute-start(bf16[320,512]{1,0:T(8,128)(2,1)} %get-tuple-element.37), channel_id=1, source_target_pairs={{0,1},{1,2},{2,3},{3,4},{4,5},{5,6},{6,7},{8,9},{9,10},{10,11},{11... | collective-permute-start | bytes 983048 | tf_op jit(solution)/shard_map/ppermute | solution.py:484
  7.7 5.1 %shard_map.111.refs_0_ = f32[8,320]{1,0:T(8,128)} custom-call(s32[1]{0:T(128)S(6)} %copy.14.step_ref, bf16[4,320,512]{2,1,0:T(8,128)(2,1)} %bitcast.72, bf16[4,320,512]{2,1,0:T(8,128)(2,1)} %bitcast.69), custom_call_target="tpu_custom_call" | custom-call | flops 39321600 | bytes 2621440 | tf_op jit(solution)/shard_map/pallas_call | solution.py:29
  12.8 2.7 %collective-permute-start.2 = (f32[8,320]{1,0:T(8,128)}, f32[8,320]{1,0:T(8,128)S(1)}, u32[]{:S(2)}, u32[]{:S(2)}) collective-permute-start(f32[8,320]{1,0:T(8,128)} %shard_map.111.refs_0_), channel_id=1, source_target_pairs={{0,1},{1,0},{2,3},{3,2},{4,5},{5,4},{6,7},{7,6},{8,9},{9,8},{10,11... | collective-permute-start | bytes 30728 | tf_op jit(solution)/shard_map/ppermute | solution.py:416
  17.3 2.8 %collective-permute-start.5 = (f32[8,320]{1,0:T(8,128)S(1)}, f32[8,320]{1,0:T(8,128)S(1)}, u32[]{:S(2)}, u32[]{:S(2)}) collective-permute-start(f32[8,320]{1,0:T(8,128)S(1)} %shard_map.112.refs_0_), channel_id=1, source_target_pairs={{0,6},{1,7},{2,4},{3,5},{4,2},{5,3},{6,0},{7,1},{8,14},{9,15},{10,... | collective-permute-start | bytes 30728 | tf_op jit(solution)/shard_map/ppermute | solution.py:416
  24.8 2.0 %shard_map.115 = (bf16[320,2048]{1,0:T(8,128)(2,1)S(1)}, f32[320,960]{1,0:T(8,128)S(1)}, f32[8,384]{1,0:T(8,128)S(1)}) custom-call(bf16[4,320,512]{2,1,0:T(8,128)(2,1)S(1)} %bitcast.73, bf16[960,2048]{1,0:T(8,128)(2,1)S(1)} %get-tuple-element.20.taps_ref, f32[8,320]{1,0:T(8,128)S(1)} %shard_map.113.stats_ref, f32[320]{0:T(512)S(1)} %copy-done.7, ...), custom_call_target="tpu_custom_call" | custom-call | flops 1258291200 | bytes 5242880 | tf_op jit(solution)/shard_map/pallas_call | solution.py:29
  26.9 5.8 %shard_map.119 = (f32[4,4,40,768]{3,2,1,0:T(8,128)}, f32[2,4,40,768]{3,2,1,0:T(8,128)S(1)}, f32[2,4,40,768]{3,2,1,0:T(8,128)S(1)}, bf16[960,1024]{1,0:T(8,128)(2,1)S(1)}) custom-call(s32[4]{0:T(128)S(1)} %pad_add_fusion.where_ref, bf16[320,2048]{1,0:T(8,128)(2,1)S(1)} %get-tuple-element.25.act_ref, bf16[960,2048]{1,0:T(8,128)(2,1)S(1)} %get-tuple-element.20.taps_ref, ...), custom_call_target="tpu_custom_call" | custom-call | flops 3774873600 | bytes 5242880 | tf_op jit(solution)/shard_map/pallas_call | solution.py:29
  34.2 2.2 %collective-permute-done.6.other_ref = f32[8,384]{1,0:T(8,128)S(1)} collective-permute-done((f32[8,384]{1,0:T(8,128)S(1)}, f32[8,384]{1,0:T(8,128)S(1)}, u32[]{:S(2)}, u32[]{:S(2)}) %collective-permute-start.6) | collective-permute-done | bytes 12320 | tf_op jit(solution)/shard_map/ppermute | solution.py:425
  38.2 2.8 %multiply_convert_fusion = f16[2,4,40,768]{3,2,1,0:T(8,128)(2,1)} fusion(f32[2,4,40,768]{3,2,1,0:T(8,128)S(1)} %collective-permute-done.15, f32[4,4,40,768]{3,2,1,0:T(8,128)} %get-tuple-element.31, f32[]{:T(128)} %bitcast.25), kind=kLoop, calls=%fused_computation.2 | loop fusion | flops 737280 | bytes 2457604 | tf_op jit(solution)/shard_map/convert_element_type | solution.py:584
  44.6 3.0 %collective-permute-start = (bf16[320,512]{1,0:T(8,128)(2,1)}, bf16[320,512]{1,0:T(8,128)(2,1)S(1)}, u32[]{:S(2)}, u32[]{:S(2)}) collective-permute-start(bf16[320,512]{1,0:T(8,128)(2,1)} %get-tuple-element.39), channel_id=1, source_target_pairs={{0,1},{1,2},{2,3},{3,4},{4,5},{5,6},{6,7},{8,9},{9,10},{10,11},{11... | collective-permute-start | bytes 983048 | tf_op jit(solution)/shard_map/ppermute | solution.py:486
  49.5 1.9 %collective-permute-done.7.other_ref = f32[8,384]{1,0:T(8,128)S(1)} collective-permute-done((f32[8,384]{1,0:T(8,128)S(1)}, f32[8,384]{1,0:T(8,128)S(1)}, u32[]{:S(2)}, u32[]{:S(2)}) %collective-permute-start.7) | collective-permute-done | bytes 12320 | tf_op jit(solution)/shard_map/ppermute | solution.py:425
  52.9 2.7 %multiply_add_fusion = f32[2,4,40,768]{3,2,1,0:T(8,128)S(1)} fusion(f16[2,4,40,768]{3,2,1,0:T(8,128)(2,1)} %collective-permute-done.16, f32[2,4,40,768]{3,2,1,0:T(8,128)} %collective-permute-done.14, f32[4,4,40,768]{3,2,1,0:T(8,128)} %get-tuple-element.31, f32[]{:T(128)} %bitcast.26), kind=kLoop, calls=%fused_computation.1 | loop fusion | flops 983040 | bytes 3440644 | tf_op jit(solution)/shard_map/add | solution.py:585
  58.3 4.4 %collective-permute-done.17 = f16[1,4,40,768]{3,2,1,0:T(8,128)(2,1)S(1)} collective-permute-done((f16[1,4,40,768]{3,2,1,0:T(8,128)(2,1)S(1)}, f16[1,4,40,768]{3,2,1,0:T(8,128)(2,1)S(1)}, u32[]{:S(2)}, u32[]{:S(2)}) %collective-permute-start.17) | collective-permute-done | bytes 245792 | tf_op jit(solution)/shard_map/ppermute | solution.py:425
  65.5 2.1 %collective-permute-start.20 = (f16[40,768]{1,0:T(8,128)(2,1)S(1)}, f16[40,768]{1,0:T(8,128)(2,1)S(1)}, u32[]{:S(2)}, u32[]{:S(2)}) collective-permute-start(f16[40,768]{1,0:T(8,128)(2,1)S(1)} %get-tuple-element.41), channel_id=1, source_target_pairs={{0,6},{1,7},{2,4},{3,5},{4,2},{5,3},{6,0},{7,1},{8,14},{9,15},{10,... | collective-permute-start | bytes 184328 | tf_op jit(solution)/shard_map/ppermute | solution.py:416
  69.2 6.3 %shard_map.120 = (f32[4,320,512]{2,1,0:T(8,128)S(1)}, f32[8,320]{1,0:T(8,128)S(1)}) custom-call(bf16[4,320,512]{2,1,0:T(8,128)(2,1)S(1)} %bitcast.75, bf16[960,2048]{1,0:T(8,128)(2,1)S(1)} %copy-done.5, bf16[960,1024]{1,0:T(8,128)(2,1)S(1)} %copy-done.11, f32[8,320]{1,0:T(8,128)S(1)} %shard_map.113.stats_ref, f32[320]{0:T(512)S(1)} %copy-done.7, ...), custom_call_target="tpu_custom_call" | custom-call | flops 3774873600 | bytes 5242880 | tf_op jit(solution)/shard_map/pallas_call | solution.py:29
  76.9 2.9 %collective-permute-start.23 = (f16[40,768]{1,0:T(8,128)(2,1)S(1)}, f16[40,768]{1,0:T(8,128)(2,1)S(1)}, u32[]{:S(2)}, u32[]{:S(2)}) collective-permute-start(f16[40,768]{1,0:T(8,128)(2,1)S(1)} %fusion.8), channel_id=1, source_target_pairs={{0,6},{1,7},{2,4},{3,5},{4,2},{5,3},{6,0},{7,1},{8,14},{9,15},{10,... | collective-permute-start | bytes 184328 | tf_op jit(solution)/shard_map/ppermute | solution.py:416
  81.5 1.8 %collective-permute-done.23 = f16[40,768]{1,0:T(8,128)(2,1)S(1)} collective-permute-done((f16[40,768]{1,0:T(8,128)(2,1)S(1)}, f16[40,768]{1,0:T(8,128)(2,1)S(1)}, u32[]{:S(2)}, u32[]{:S(2)}) %collective-permute-start.23) | collective-permute-done | bytes 61472 | tf_op jit(solution)/shard_map/ppermute | solution.py:416
  83.3 3.3 %collective-permute-start.13 = (f32[8,320]{1,0:T(8,128)S(1)}, f32[8,320]{1,0:T(8,128)S(1)}, u32[]{:S(2)}, u32[]{:S(2)}) collective-permute-start(f32[8,320]{1,0:T(8,128)S(1)} %add.69.refs_0_), channel_id=1, source_target_pairs={{0,6},{1,7},{2,4},{3,5},{4,2},{5,3},{6,0},{7,1},{8,14},{9,15},{10,... | collective-permute-start | bytes 30728 | tf_op jit(solution)/shard_map/ppermute | solution.py:416
  87.9 1.8 %collective-permute-start.11 = (f32[8,320]{1,0:T(8,128)S(1)}, f32[8,320]{1,0:T(8,128)S(1)}, u32[]{:S(2)}, u32[]{:S(2)}) collective-permute-start(f32[8,320]{1,0:T(8,128)S(1)} %add.69.refs_0_), channel_id=1, source_target_pairs={{0,2},{1,3},{2,0},{3,1},{4,6},{5,7},{6,4},{7,5},{8,10},{9,11},{10,... | collective-permute-start | bytes 30728 | tf_op jit(solution)/shard_map/ppermute | solution.py:416
  91.4 7.2 %shard_map.118 = bf16[4,320,512]{2,1,0:T(8,128)(2,1)} custom-call(s32[2]{0:T(128)S(1)} %add_convert_fusion.ends_ref, bf16[4,320,512]{2,1,0:T(8,128)(2,1)S(1)} %bitcast.76, bf16[320,512]{1,0:T(8,128)(2,1)S(1)} %collective-permute-done.above_ref, bf16[320,512]{1,0:T(8,128)(2,1)S(1)} %collective-permute-done.1.below_ref, f32[8,320]{1,0:T(8,128)S(1)} %shard_map.113.stats_ref, ...), custom_call_target="tpu_custom_call" | custom-call | flops 3774873600 | bytes 5242880 | tf_op jit(solution)/shard_map/pallas_call | solution.py:29
  100.0 2.3 %shard_map.123 = bf16[4,320,512]{2,1,0:T(8,128)(2,1)} custom-call(f32[4,320,512]{2,1,0:T(8,128)S(1)} %get-tuple-element.28.grad_ref, bf16[4,320,512]{2,1,0:T(8,128)(2,1)S(1)} %bitcast.77, bf16[4,320,512]{2,1,0:T(8,128)(2,1)S(1)} %bitcast.71, f32[8,320]{1,0:T(8,128)S(1)} %shard_map.113.stats_ref, f32[8,320]{1,0:T(8,128)S(1)} %shard_map.122.sums_ref.total_ref), custom_call_target="tpu_custom_call" | custom-call | flops 13107200 | bytes 6553600 | tf_op jit(solution)/shard_map/pallas_call | solution.py:29
  106.3 2.2 %collective-permute-done.27 = f16[4,40,768]{2,1,0:T(8,128)(2,1)S(1)} collective-permute-done((f16[4,40,768]{2,1,0:T(8,128)(2,1)S(1)}, f16[4,40,768]{2,1,0:T(8,128)(2,1)S(1)}, u32[]{:S(2)}, u32[]{:S(2)}) %collective-permute-start.27) | collective-permute-done | bytes 245792 | tf_op jit(solution)/shard_map/ppermute | solution.py:425
  112.5 2.5 %shard_map.124.refs_2_ = f32[9,320,320]{2,1,0:T(8,128)} custom-call(s32[10]{0:T(128)S(1)} %stack.108.places_ref, f32[4,40,768]{2,1,0:T(8,128)S(1)} %convert_multiply_fusion.5.refs_0_, f32[4,40,768]{2,1,0:T(8,128)S(1)} %convert_multiply_fusion.4.refs_1_, f32[4,40,768]{2,1,0:T(8,128)S(1)} %convert_multiply_fusion.3.refs_2_, ...), custom_call_target="tpu_custom_call" | custom-call | bytes 5898240 | tf_op jit(solution)/shard_map/pallas_call | solution.py:617
  116.4 1.7 %shard_map.125 = f32[9,320,320]{2,1,0:T(8,128)} custom-call(s32[6]{0:T(128)S(1)} %stack.96.places_ref, f32[4,40,768]{2,1,0:T(8,128)S(1)} %convert_multiply_fusion.7.refs_0_, f32[4,40,768]{2,1,0:T(8,128)S(1)} %convert_multiply_fusion.6.refs_1_, f32[9,320,320]{2,1,0:T(8,128)} %shard_map.124.refs_2_), custom_call_target="tpu_custom_call", output_to_operand_aliasing={{}: (3, {})} | custom-call | bytes 1966080 | tf_op jit(solution)/shard_map/pallas_call | solution.py:617
  (110 shorter events, 41.8 us)
Async XLA Ops:
  2.6 24.2 %collective-permute-start.9 = (bf16[320,512]{1,0:T(8,128)(2,1)}, bf16[320,512]{1,0:T(8,128)(2,1)S(1)}, u32[]{:S(2)}, u32[]{:S(2)}) collective-permute-start(bf16[320,512]{1,0:T(8,128)(2,1)} %get-tuple-element.36), channel_id=1, source_target_pairs={{1,0},{2,1},{3,2},{4,3},{5,4},{6,5},{7,6},{9,8},{10,9},{11,10},{12... | collective-permute-start | bytes 983048 | tf_op jit(solution)/shard_map/ppermute | solution.py:485
  3.9 22.9 %collective-permute-start.8 = (bf16[320,512]{1,0:T(8,128)(2,1)}, bf16[320,512]{1,0:T(8,128)(2,1)S(1)}, u32[]{:S(2)}, u32[]{:S(2)}) collective-permute-start(bf16[320,512]{1,0:T(8,128)(2,1)} %get-tuple-element.37), channel_id=1, source_target_pairs={{0,1},{1,2},{2,3},{3,4},{4,5},{5,6},{6,7},{8,9},{9,10},{10,11},{11... | collective-permute-start | bytes 983048 | tf_op jit(solution)/shard_map/ppermute | solution.py:484
  17.3 6.9 %collective-permute-start.5 = (f32[8,320]{1,0:T(8,128)S(1)}, f32[8,320]{1,0:T(8,128)S(1)}, u32[]{:S(2)}, u32[]{:S(2)}) collective-permute-start(f32[8,320]{1,0:T(8,128)S(1)} %shard_map.112.refs_0_), channel_id=1, source_target_pairs={{0,6},{1,7},{2,4},{3,5},{4,2},{5,3},{6,0},{7,1},{8,14},{9,15},{10,... | collective-permute-start | bytes 30728 | tf_op jit(solution)/shard_map/ppermute | solution.py:416
  32.7 5.5 %collective-permute-start.15 = (f32[2,4,40,768]{3,2,1,0:T(8,128)S(1)}, f32[2,4,40,768]{3,2,1,0:T(8,128)S(1)}, u32[]{:S(2)}, u32[]{:S(2)}) collective-permute-start(f32[2,4,40,768]{3,2,1,0:T(8,128)S(1)} %get-tuple-element.33), channel_id=1, source_target_pairs={{0,1},{1,0},{2,3},{3,2},{4,5},{5,4},{6,7},{7,6},{8,9},{9,8},{10,11... | collective-permute-start | bytes 2949128 | tf_op jit(solution)/shard_map/ppermute | solution.py:416
  37.6 15.2 %collective-permute-start.14 = (f32[2,4,40,768]{3,2,1,0:T(8,128)S(1)}, f32[2,4,40,768]{3,2,1,0:T(8,128)}, u32[]{:S(2)}, u32[]{:S(2)}) collective-permute-start(f32[2,4,40,768]{3,2,1,0:T(8,128)S(1)} %get-tuple-element.32), channel_id=1, source_target_pairs={{0,1},{1,0},{2,3},{3,2},{4,5},{5,4},{6,7},{7,6},{8,9},{9,8},{10,11... | collective-permute-start | bytes 2949128 | tf_op jit(solution)/shard_map/ppermute | solution.py:416
  40.9 12.0 %collective-permute-start.16 = (f16[2,4,40,768]{3,2,1,0:T(8,128)(2,1)}, f16[2,4,40,768]{3,2,1,0:T(8,128)(2,1)}, u32[]{:S(2)}, u32[]{:S(2)}) collective-permute-start(f16[2,4,40,768]{3,2,1,0:T(8,128)(2,1)} %multiply_convert_fusion), channel_id=1, source_target_pairs={{0,8},{1,17},{2,10},{3,19},{4,12},{5,21},{6,14},{7,23},{8,0},{9,25... | collective-permute-start | bytes 1474568 | tf_op jit(solution)/shard_map/ppermute | solution.py:425
  43.3 46.5 %collective-permute-start.1 = (bf16[320,512]{1,0:T(8,128)(2,1)}, bf16[320,512]{1,0:T(8,128)(2,1)S(1)}, u32[]{:S(2)}, u32[]{:S(2)}) collective-permute-start(bf16[320,512]{1,0:T(8,128)(2,1)} %get-tuple-element.38), channel_id=1, source_target_pairs={{1,0},{2,1},{3,2},{4,3},{5,4},{6,5},{7,6},{9,8},{10,9},{11,10},{12... | collective-permute-start | bytes 983048 | tf_op jit(solution)/shard_map/ppermute | solution.py:487
  44.6 46.8 %collective-permute-start = (bf16[320,512]{1,0:T(8,128)(2,1)}, bf16[320,512]{1,0:T(8,128)(2,1)S(1)}, u32[]{:S(2)}, u32[]{:S(2)}) collective-permute-start(bf16[320,512]{1,0:T(8,128)(2,1)} %get-tuple-element.39), channel_id=1, source_target_pairs={{0,1},{1,2},{2,3},{3,4},{4,5},{5,6},{6,7},{8,9},{9,10},{10,11},{11... | collective-permute-start | bytes 983048 | tf_op jit(solution)/shard_map/ppermute | solution.py:486
  56.4 6.3 %collective-permute-start.17 = (f16[1,4,40,768]{3,2,1,0:T(8,128)(2,1)S(1)}, f16[1,4,40,768]{3,2,1,0:T(8,128)(2,1)S(1)}, u32[]{:S(2)}, u32[]{:S(2)}) collective-permute-start(f16[1,4,40,768]{3,2,1,0:T(8,128)(2,1)S(1)} %fusion), channel_id=1, source_target_pairs={{0,16},{1,9},{2,18},{3,11},{4,20},{5,13},{6,22},{7,15},{8,24},{9,1... | collective-permute-start | bytes 737288 | tf_op jit(solution)/shard_map/ppermute | solution.py:425
  64.1 11.4 %collective-permute-start.18 = (f16[40,768]{1,0:T(8,128)(2,1)S(1)}, f16[40,768]{1,0:T(8,128)(2,1)S(1)}, u32[]{:S(2)}, u32[]{:S(2)}) collective-permute-start(f16[40,768]{1,0:T(8,128)(2,1)S(1)} %get-tuple-element.40), channel_id=1, source_target_pairs={{0,2},{1,3},{2,0},{3,1},{4,6},{5,7},{6,4},{7,5},{8,10},{9,11},{10,... | collective-permute-start | bytes 184328 | tf_op jit(solution)/shard_map/ppermute | solution.py:416
  65.5 10.1 %collective-permute-start.20 = (f16[40,768]{1,0:T(8,128)(2,1)S(1)}, f16[40,768]{1,0:T(8,128)(2,1)S(1)}, u32[]{:S(2)}, u32[]{:S(2)}) collective-permute-start(f16[40,768]{1,0:T(8,128)(2,1)S(1)} %get-tuple-element.41), channel_id=1, source_target_pairs={{0,6},{1,7},{2,4},{3,5},{4,2},{5,3},{6,0},{7,1},{8,14},{9,15},{10,... | collective-permute-start | bytes 184328 | tf_op jit(solution)/shard_map/ppermute | solution.py:416
  67.6 8.0 %collective-permute-start.19 = (f16[40,768]{1,0:T(8,128)(2,1)S(1)}, f16[40,768]{1,0:T(8,128)(2,1)S(1)}, u32[]{:S(2)}, u32[]{:S(2)}) collective-permute-start(f16[40,768]{1,0:T(8,128)(2,1)S(1)} %get-tuple-element.42), channel_id=1, source_target_pairs={{0,4},{1,5},{2,6},{3,7},{4,0},{5,1},{6,2},{7,3},{8,12},{9,13},{10,... | collective-permute-start | bytes 184328 | tf_op jit(solution)/shard_map/ppermute | solution.py:416
  75.5 5.2 %collective-permute-start.10 = (f32[8,320]{1,0:T(8,128)S(1)}, f32[8,320]{1,0:T(8,128)S(1)}, u32[]{:S(2)}, u32[]{:S(2)}) collective-permute-start(f32[8,320]{1,0:T(8,128)S(1)} %shard_map.121), channel_id=1, source_target_pairs={{0,1},{1,0},{2,3},{3,2},{4,5},{5,4},{6,7},{7,6},{8,9},{9,8},{10,11... | collective-permute-start | bytes 30728 | tf_op jit(solution)/shard_map/ppermute | solution.py:416
  76.9 6.4 %collective-permute-start.23 = (f16[40,768]{1,0:T(8,128)(2,1)S(1)}, f16[40,768]{1,0:T(8,128)(2,1)S(1)}, u32[]{:S(2)}, u32[]{:S(2)}) collective-permute-start(f16[40,768]{1,0:T(8,128)(2,1)S(1)} %fusion.8), channel_id=1, source_target_pairs={{0,6},{1,7},{2,4},{3,5},{4,2},{5,3},{6,0},{7,1},{8,14},{9,15},{10,... | collective-permute-start | bytes 184328 | tf_op jit(solution)/shard_map/ppermute | solution.py:416
  79.8 7.2 %collective-permute-start.22 = (f16[40,768]{1,0:T(8,128)(2,1)S(1)}, f16[40,768]{1,0:T(8,128)(2,1)S(1)}, u32[]{:S(2)}, u32[]{:S(2)}) collective-permute-start(f16[40,768]{1,0:T(8,128)(2,1)S(1)} %fusion.8), channel_id=1, source_target_pairs={{0,4},{1,5},{2,6},{3,7},{4,0},{5,1},{6,2},{7,3},{8,12},{9,13},{10,... | collective-permute-start | bytes 184328 | tf_op jit(solution)/shard_map/ppermute | solution.py:416
  80.7 7.2 %collective-permute-start.21 = (f16[40,768]{1,0:T(8,128)(2,1)S(1)}, f16[40,768]{1,0:T(8,128)(2,1)S(1)}, u32[]{:S(2)}, u32[]{:S(2)}) collective-permute-start(f16[40,768]{1,0:T(8,128)(2,1)S(1)} %fusion.8), channel_id=1, source_target_pairs={{0,2},{1,3},{2,0},{3,1},{4,6},{5,7},{6,4},{7,5},{8,10},{9,11},{10,... | collective-permute-start | bytes 184328 | tf_op jit(solution)/shard_map/ppermute | solution.py:416
  83.3 15.3 %collective-permute-start.13 = (f32[8,320]{1,0:T(8,128)S(1)}, f32[8,320]{1,0:T(8,128)S(1)}, u32[]{:S(2)}, u32[]{:S(2)}) collective-permute-start(f32[8,320]{1,0:T(8,128)S(1)} %add.69.refs_0_), channel_id=1, source_target_pairs={{0,6},{1,7},{2,4},{3,5},{4,2},{5,3},{6,0},{7,1},{8,14},{9,15},{10,... | collective-permute-start | bytes 30728 | tf_op jit(solution)/shard_map/ppermute | solution.py:416
  87.0 11.6 %collective-permute-start.12 = (f32[8,320]{1,0:T(8,128)S(1)}, f32[8,320]{1,0:T(8,128)S(1)}, u32[]{:S(2)}, u32[]{:S(2)}) collective-permute-start(f32[8,320]{1,0:T(8,128)S(1)} %add.69.refs_0_), channel_id=1, source_target_pairs={{0,4},{1,5},{2,6},{3,7},{4,0},{5,1},{6,2},{7,3},{8,12},{9,13},{10,... | collective-permute-start | bytes 30728 | tf_op jit(solution)/shard_map/ppermute | solution.py:416
  87.9 10.7 %collective-permute-start.11 = (f32[8,320]{1,0:T(8,128)S(1)}, f32[8,320]{1,0:T(8,128)S(1)}, u32[]{:S(2)}, u32[]{:S(2)}) collective-permute-start(f32[8,320]{1,0:T(8,128)S(1)} %add.69.refs_0_), channel_id=1, source_target_pairs={{0,2},{1,3},{2,0},{3,1},{4,6},{5,7},{6,4},{7,5},{8,10},{9,11},{10,... | collective-permute-start | bytes 30728 | tf_op jit(solution)/shard_map/ppermute | solution.py:416
  89.8 13.8 %collective-permute-start.24 = (f16[4,40,768]{2,1,0:T(8,128)(2,1)S(1)}, f16[4,40,768]{2,1,0:T(8,128)(2,1)S(1)}, u32[]{:S(2)}, u32[]{:S(2)}) collective-permute-start(f16[4,40,768]{2,1,0:T(8,128)(2,1)S(1)} %pad_maximum_fusion), channel_id=1, source_target_pairs={{0,16},{1,9},{2,18},{3,11},{4,20},{5,13},{6,22},{7,15},{8,24},{9,1... | collective-permute-start | bytes 737288 | tf_op jit(solution)/shard_map/ppermute | solution.py:425
  102.3 6.2 %collective-permute-start.27 = (f16[4,40,768]{2,1,0:T(8,128)(2,1)S(1)}, f16[4,40,768]{2,1,0:T(8,128)(2,1)S(1)}, u32[]{:S(2)}, u32[]{:S(2)}) collective-permute-start(f16[4,40,768]{2,1,0:T(8,128)(2,1)S(1)} %pad_maximum_fusion), channel_id=1, source_target_pairs={{0,8},{1,17},{2,10},{3,19},{4,12},{5,21},{6,14},{7,23},{8,0},{9,25... | collective-permute-start | bytes 737288 | tf_op jit(solution)/shard_map/ppermute | solution.py:425
  103.5 5.6 %collective-permute-start.28 = (f16[4,40,768]{2,1,0:T(8,128)(2,1)S(1)}, f16[4,40,768]{2,1,0:T(8,128)(2,1)S(1)}, u32[]{:S(2)}, u32[]{:S(2)}) collective-permute-start(f16[4,40,768]{2,1,0:T(8,128)(2,1)S(1)} %pad_maximum_fusion), channel_id=1, source_target_pairs={{0,1},{1,0},{2,3},{3,2},{4,5},{5,4},{6,7},{7,6},{8,9},{9,8},{10,11... | collective-permute-start | bytes 737288 | tf_op jit(solution)/shard_map/ppermute | solution.py:416
  103.6 8.2 %collective-permute-start.29 = (f16[4,40,768]{2,1,0:T(8,128)(2,1)S(1)}, f16[4,40,768]{2,1,0:T(8,128)(2,1)S(1)}, u32[]{:S(2)}, u32[]{:S(2)}) collective-permute-start(f16[4,40,768]{2,1,0:T(8,128)(2,1)S(1)} %collective-permute-done.24), channel_id=1, source_target_pairs={{0,1},{1,0},{2,3},{3,2},{4,5},{5,4},{6,7},{7,6},{8,9},{9,8},{10,11... | collective-permute-start | bytes 737288 | tf_op jit(solution)/shard_map/ppermute | solution.py:416
  104.1 7.0 %collective-permute-start.25 = (f16[4,40,768]{2,1,0:T(8,128)(2,1)S(1)}, f16[4,40,768]{2,1,0:T(8,128)(2,1)S(1)}, u32[]{:S(2)}, u32[]{:S(2)}) collective-permute-start(f16[4,40,768]{2,1,0:T(8,128)(2,1)S(1)} %collective-permute-done.24), channel_id=1, source_target_pairs={{0,8},{1,17},{2,10},{3,19},{4,12},{5,21},{6,14},{7,23},{8,0},{9,25... | collective-permute-start | bytes 737288 | tf_op jit(solution)/shard_map/ppermute | solution.py:425
  (20 other events, 181.2 us)

commit v6 on v5

--- a/solution.py
+++ b/solution.py
@@ -168,13 +168,16 @@
 
 
 def middle_body(
-    latent_ref, taps_ref, stats_ref, gain_ref, bias_ref, sums_ref, act_ref, found_ref, table_ref
+    factor, spread, latent_ref, taps_ref, stats_ref, gain_ref, bias_ref, sums_ref, act_ref, found_ref, table_ref
 ):
     row_count, channels, cols = latent_ref.shape
     table_ref[...] = jnp.zeros(table_ref.shape, f32)
     table_ref[0:1, :channels] = sums_ref[0:1]
     table_ref[0:1, channels : channels + NOTE] = stats_ref[3:4, :NOTE]
-    table_ref[0:1, channels + NOTE : channels + 2 * NOTE] = stats_ref[2:3, :NOTE]
+    gain = jnp.max(jnp.abs(gain_ref[...][None, :]), axis=1, keepdims=True)
+    bias = jnp.max(jnp.abs(bias_ref[...][None, :]), axis=1, keepdims=True)
+    bound = stats_ref[2:3] * ((spread * gain + bias) * factor)
+    table_ref[0:1, channels + NOTE : channels + 2 * NOTE] = bound[:, :NOTE]
     values = column_values(stats_ref, gain_ref, bias_ref)
     for row in range(row_count):
         act_ref[:, row * cols : (row + 1) * cols] = activate(latent_ref[row], values)
@@ -244,13 +247,13 @@
 
 
 def conv_body(
-    ends_ref, latent_ref, above_ref, below_ref, stats_ref, gain_ref, bias_ref, weight_ref,
+    where_ref, latent_ref, above_ref, below_ref, stats_ref, gain_ref, bias_ref, weight_ref,
     extra_ref, out_ref, taps_ref, flat_ref,
 ):
     row_count, channels, cols = latent_ref.shape
     values = column_values(stats_ref, gain_ref, bias_ref)
-    for place, ref, end in ((0, above_ref, 0), (row_count + 1, below_ref, 1)):
-        keep = ends_ref[end].astype(f32)
+    for place, ref, end in ((0, above_ref, 4), (row_count + 1, below_ref, 5)):
+        keep = where_ref[end].astype(f32)
         put_taps(taps_ref, place, (activate(ref[...], values).astype(f32) * keep).astype(bf16), False)
     for row in range(row_count):
         put_taps(taps_ref, row + 1, activate(latent_ref[row], values), False)
@@ -315,16 +318,22 @@
         out_ref[row] = (cot_ref[row].astype(f32) + change).astype(bf16)
 
 
-def place_body(shape, count, places_ref, *refs):
+def place_body(shape, half_blocks, pieces, where_ref, *refs):
     zones, height, width = shape
+    count = len(pieces)
     cells = refs[:count]
+    core, mine, other, zone_index = [where_ref[i] for i in range(4)]
+    spots = [
+        (1 - core) * half_blocks + (other ^ rest) if crossed else core * half_blocks + (mine ^ rest)
+        for crossed, rest in pieces
+    ]
     out_ref, flat_ref, rows_ref, sem = refs[-4:]
     channels = out_ref.shape[1]
     tap_width = zones * width // 3
     whole, part = channels // height, channels % height
 
     def copies(index, act):
-        block = places_ref[index]
+        block = spots[index]
 
         def copy(size):
             return pltpu.make_async_copy(
@@ -345,7 +354,7 @@
 
     for index in range(count):
         for zone in range(zones):
-            left = pl.multiple_of(places_ref[count + zone] * width, LANES)
+            left = pl.multiple_of((zone_index ^ zone) * width, LANES)
             flat_ref[index, :, pl.ds(left, width)] = cells[index][zone]
         for tap in range(9):
             left = (tap // 3) * tap_width + (tap % 3) * channels
@@ -355,29 +364,10 @@
         copies(index, lambda copy: copy.wait())
 
 
-def power_of_two(top, factor, spread, gain_ref, bias_ref, shape):
-    gain = jnp.max(jnp.abs(gain_ref[...][None, :]), axis=1, keepdims=True)
-    bias = jnp.max(jnp.abs(bias_ref[...][None, :]), axis=1, keepdims=True)
-    reach = spread * gain + bias
-    bound = jnp.maximum(top * reach * factor, 1e-30)
-    power = jnp.clip(jnp.floor(jnp.log2(30000.0 / bound)), -100.0, 100.0)
-    scale = jnp.broadcast_to(jnp.exp2(power), shape)
-    return rows_of(scale, 1.0 / scale)
-
-
-def largest_note(table, channels):
-    return jnp.max(
-        jnp.max(table[:, channels + NOTE : channels + 2 * NOTE], axis=1, keepdims=True),
-        axis=0,
-        keepdims=True,
-    )
-
-
 def spread_body(
-    known, masks, factor, spread, where_ref, gain_ref, bias_ref, mine_ref, other_ref,
-    table_ref, scale_ref, steps_ref,
+    known, masks, where_ref, mine_ref, other_ref, table_ref, scale_ref, back_ref, steps_ref
 ):
-    channels = gain_ref.shape[0]
+    channels = steps_ref.shape[1]
     table_ref[...] = mine_ref[...]
     for core in range(2):
 
@@ -388,9 +378,11 @@
                 table_ref[at : at + 1] = other_ref[row : row + 1]
 
     table = table_ref[...]
-    scale_ref[...] = power_of_two(
-        largest_note(table, channels), factor, spread, gain_ref, bias_ref, scale_ref.shape
-    )
+    bound = jnp.max(table[:, channels + NOTE : channels + NOTE + 1], axis=0, keepdims=True)
+    power = jnp.floor(jnp.log2(30000.0 / jnp.maximum(bound, 1e-30)))
+    power = jnp.clip(power, -100.0, 100.0)
+    scale_ref[...] = jnp.exp2(power)
+    back_ref[...] = 1.0 / jnp.exp2(power)
     steps_ref[...] = jnp.broadcast_to(table[:, channels : channels + 1], steps_ref.shape)
 
 
@@ -502,7 +494,9 @@
         return index
 
     mine, other = rest_index(core), rest_index(1 - core)
-    where = jnp.stack([core, mine, other, zone_index]).astype(jnp.int32)
+    inside = [slab_index > 0, slab_index < slab_count - 1]
+    where = jnp.stack([core, mine, other, zone_index] + [x.astype(core.dtype) for x in inside])
+    where = where.astype(jnp.int32)
     part_shape = jax.ShapeDtypeStruct((blocks // 4, zones, height, width), f32)
     share_shape = jax.ShapeDtypeStruct((blocks // 2, zones, height, width), f32)
     taps_shape = jax.ShapeDtypeStruct((3 * channels, positions), bf16)
@@ -510,8 +504,9 @@
         taps_body, (taps_shape, small), (cot,), moved=10 * lat.size, limit=6 << 20
     )
     table_shape = jax.ShapeDtypeStruct((-(-image_count // 8) * 8, channels + 2 * NOTE), f32)
+    factor, spread = float(positions * slab_count * image_count), math.sqrt(per_group)
     act, middle_rows, table = call(
-        middle_body,
+        functools.partial(middle_body, factor, spread),
         (
             jax.ShapeDtypeStruct((channels, positions), bf16),
             jax.ShapeDtypeStruct((channels, 3 * channels), f32),
@@ -536,22 +531,21 @@
         moved=8 * lat.size,
         limit=12 << 20,
     )
-    factor, spread = float(positions * slab_count * image_count), math.sqrt(per_group)
-    scales_shape = jax.ShapeDtypeStruct((8, LANES), f32)
+    unit = jax.ShapeDtypeStruct((1, 1), f32)
     steps_shape = jax.ShapeDtypeStruct((table_shape.shape[0], channels), f32)
     known = ([0], [0])
     scales = []
     for step in range(bits):
         masks = (1 << orders[0][step], 1 << orders[1][step])
         arrived = swap_image(table, masks)
-        table, found, steps = call(
-            functools.partial(spread_body, known, masks, factor, spread),
-            (table_shape, scales_shape, steps_shape),
-            (where, gain, bias, table, arrived),
-            specs=(smem,) + (vmem,) * 4,
+        table, scale, back, steps = call(
+            functools.partial(spread_body, known, masks),
+            (table_shape, unit, unit, steps_shape),
+            (where, table, arrived),
+            specs=(smem,) + (vmem,) * 2,
             limit=4 << 20,
         )
-        scales.append((found[0, 0], found[1, 0]))
+        scales.append((scale[0, 0], back[0, 0]))
         known = tuple(rows + [row ^ mask for row in rows] for rows, mask in zip(known, masks))
 
     grad, sums = call(
@@ -576,22 +570,27 @@
     middle = blocks // 4
     far_in = swap_space(far_high, 1)
     near_in = swap_space(far_low, 1)
-    sending = near[middle:] + far_in
+    sent = ((near[middle:] + far_in) * scales[0][0]).astype(f16)
+    near, near_in, _ = lax.optimization_barrier((near, near_in, sent))
     keeping = near[:middle] + near_in
     for step in range(bits):
         masks = (1 << orders[0][step], 1 << orders[1][step])
-        scale, back = scales[step]
-        arrived = swap_image((sending * scale).astype(f16), masks)
-        total = keeping + arrived.astype(f32) * back
-        middle = total.shape[0] // 2
-        sending, keeping = total[middle:], total[:middle]
-    total = total[0] if bits else keeping[0]
-    share = total[0]
-    arrivals = []
+        arrived = swap_image(sent, masks)
+        back = scales[step][1]
+        middle = keeping.shape[0] // 2
+        if middle:
+            total = keeping[middle:] + arrived[middle:].astype(f32) * back
+            sent = (total * scales[step + 1][0]).astype(f16)
+            keeping, arrived, _ = lax.optimization_barrier((keeping, arrived, sent))
+            keeping = keeping[:middle] + arrived[:middle].astype(f32) * back
+    sent = []
     for mask in range(1, zones):
-        arrivals.append(swap_space((total[mask] * line_scale).astype(f16), 2 * mask))
-    for arrived in arrivals:
-        share = share + arrived.astype(f32) * line_back
+        total = keeping[0, mask] + arrived[0, mask].astype(f32) * back
+        sent.append((total * line_scale).astype(f16))
+    keeping, arrived, *_ = lax.optimization_barrier((keeping, arrived, *sent))
+    share = keeping[0, 0] + arrived[0, 0].astype(f32) * back
+    for mask in range(1, zones):
+        share = share + swap_space(sent[mask - 1], 2 * mask).astype(f32) * line_back
     share = (share * line_scale).astype(f16)
     collected = [share]
     for mask in range(1, zones):
@@ -607,15 +606,16 @@
     for piece in pieces:
         crossed.append(swap_space(piece, 1))
     half_blocks = blocks // 2
-    spots = [core * half_blocks + (mine ^ rest) for rest in range(half_blocks)]
-    cross_spots = [(1 - core) * half_blocks + (other ^ rest) for rest in range(half_blocks)]
-    zone_spots = [zone_index ^ mask for mask in range(zones)]
-
-    def place(cells, at, before):
-        table = jnp.stack(at + zone_spots).astype(jnp.int32)
-        count = len(cells)
+    numbers = list(range(half_blocks))
+
+    def place(chosen, before):
+        count = len(chosen)
+        cells = []
+        for is_crossed, rest in chosen:
+            piece = crossed[rest] if is_crossed else pieces[rest]
+            cells.append(piece.astype(f32) * line_back)
         return pl.pallas_call(
-            functools.partial(place_body, (zones, height, width), count),
+            functools.partial(place_body, (zones, height, width), half_blocks, chosen),
             out_shape=jax.ShapeDtypeStruct((9, channels, channels), f32),
             in_specs=[smem] + [vmem] * count + [anywhere] * len(before),
             out_specs=anywhere,
@@ -631,12 +631,11 @@
                 bytes_accessed=8 * count * zones * height * width,
                 transcendentals=0,
             ),
-        )(table, *[piece.astype(f32) * line_back for piece in cells], *before)
-
-    weight_grad = place(
-        pieces[:-1] + crossed[:-1], spots[:-1] + cross_spots[:-1], ()
-    )
-    weight_grad = place(pieces[-1:] + crossed[-1:], spots[-1:] + cross_spots[-1:], (weight_grad,))
+        )(where, *cells, *before)
+
+    early = [(side, rest) for side in (False, True) for rest in numbers[:-1]]
+    weight_grad = place(early, ())
+    weight_grad = place([(False, numbers[-1]), (True, numbers[-1])], (weight_grad,))
     weight_grad = weight_grad.reshape(3, 3, channels, channels)
 
     half_count = channels // 2
@@ -645,7 +644,6 @@
     embedding = jnp.concatenate([jnp.cos(angles), jnp.sin(angles)], axis=1).astype(bf16)
     time_bias = jnp.dot(embedding[:1], time_weight, preferred_element_type=f32)
     extra = time_bias + conv_bias.reshape(1, channels)
-    ends = jnp.stack([slab_index > 0, slab_index < slab_count - 1]).astype(jnp.int32)
     time_grad = call(
         functools.partial(time_body, image_count),
         jax.ShapeDtypeStruct((channels, channels), f32),
@@ -655,7 +653,7 @@
     block_out = call(
         conv_body,
         jax.ShapeDtypeStruct((row_count, channels, col_count), bf16),
-        (ends, lat, lat_above, lat_below, stats, gain, bias, conv_weight, extra),
+        (where, lat, lat_above, lat_below, stats, gain, bias, conv_weight, extra),
         specs=(smem,) + (vmem,) * 8,
         scratch=(taps, flat),
         flops=flops,

time: 119 us -> 121 us (1.017)
  waiting for transfers between devices: 15.8 us -> 22.2 us
  other arithmetic: 14.7 us -> 11.2 us
    ppermute x7, waiting for transfers between devices: 12 us -> 16.8 us  [swap_image(): return lax.ppermute(cells, ('dp', 'space'), pairs)]
    add x2, other arithmetic: 3.36 us -> 0.83 us  [the longest x1 0.72 us: slab_program(): keeping = keeping[:middle] + arrived[:middle].astype(f32) * back]
    unnamed x26 -> x24, local copies, waits for them, and re-layouts: 3.63 us -> 6.15 us
    convert_element_type x4 -> x2, other arithmetic: 4.33 us -> 2.18 us  [the longest x1 1.4 us: slab_program(): sent = (total * scales[step + 1][0]).astype(f16)]
    ppermute x20, waiting for transfers between devices: 3.87 us -> 5.33 us  [swap_space(): return lax.ppermute(cells, 'space', [(i, i ^ mask) for i in range(count)])]
    mul x8 -> x9, other arithmetic: 5.39 us -> 6.64 us  [the longest x8 5.29 us: place(): cells.append(piece.astype(f32) * line_back)]
  transfers between devices with their start and end apart: 31 -> 31, of which waited for: 9 -> 9; matrix products, arithmetic and copies ran while one was open for 14% -> 9% of each run, Pallas kernels for 25% -> 26%
where the time goes in v6:
time: 121 us; the launch traced here: 120 us
  starting transfers between devices  39.5 us (33%)
  Pallas kernels  37 us (31%)
  waiting for transfers between devices  22.2 us (18%)
  other arithmetic  11.2 us (9%)
  local copies, waits for them, and re-layouts  8.27 us (7%)
  between operations  1.91 us (2%)
    pallas_call x14, Pallas kernels, call(): pl.pallas_call(body, out_shape=tuple(outs) if many else outs, in_specs=li...  32.8 us
    ppermute x20, starting transfers between devices, swap_space(): return lax.ppermute(cells, 'space', [(i, i ^ mask) for i in range(count)])  22.8 us
    ppermute x7, waiting for transfers between devices, swap_image(): return lax.ppermute(cells, ('dp', 'space'), pairs)  16.8 us
    ppermute x7, starting transfers between devices, swap_image(): return lax.ppermute(cells, ('dp', 'space'), pairs)  9.39 us
    unnamed x24, local copies, waits for them, and re-layouts  6.15 us
    ppermute x20, waiting for transfers between devices, swap_space(): return lax.ppermute(cells, 'space', [(i, i ^ mask) for i in range(count)])  5.33 us
    mul x8, other arithmetic, place(): cells.append(piece.astype(f32) * line_back)  5.29 us
    pallas_call x2, Pallas kernels, place(): pl.pallas_call(functools.partial(place_body, (zones, height, width), half...  4.25 us
  transfers between devices with their start and end apart: 31, of which 9 were waited for; matrix products, arithmetic and copies ran while one was open for 9% of the time, Pallas kernels for 26%

profile of v6, /device:TPU:0, one launch (start us, length us, event | category | flops | bytes accessed | tf_op | source)
XLA Modules:
  0.0 120.3 jit_solution(2127786064982181818)
XLA Ops:
  0.6 2.0 %slice_bitcast_fusion = (bf16[320,512]{1,0:T(8,128)(2,1)}, bf16[320,512]{1,0:T(8,128)(2,1)}) fusion(bf16[1,4,320,512]{3,2,1,0:T(8,128)(2,1)} %bitcast.55), kind=kLoop, calls=%fused_computation.15 | loop fusion | bytes 1310720 | tf_op jit(solution)/shard_map/squeeze | solution.py:477
  2.6 2.4 %collective-permute-start.8 = (bf16[320,512]{1,0:T(8,128)(2,1)}, bf16[320,512]{1,0:T(8,128)(2,1)S(1)}, u32[]{:S(2)}, u32[]{:S(2)}) collective-permute-start(bf16[320,512]{1,0:T(8,128)(2,1)} %get-tuple-element.53), channel_id=1, source_target_pairs={{0,1},{1,2},{2,3},{3,4},{4,5},{5,6},{6,7},{8,9},{9,10},{10,11},{11... | collective-permute-start | bytes 983048 | tf_op jit(solution)/shard_map/ppermute | solution.py:476
  7.0 5.1 %shard_map.111.refs_0_ = f32[8,320]{1,0:T(8,128)} custom-call(s32[1]{0:T(128)S(6)} %copy.14.step_ref, bf16[4,320,512]{2,1,0:T(8,128)(2,1)} %bitcast.59, bf16[4,320,512]{2,1,0:T(8,128)(2,1)} %bitcast.56), custom_call_target="tpu_custom_call" | custom-call | flops 39321600 | bytes 2621440 | tf_op jit(solution)/shard_map/pallas_call | solution.py:29
  12.2 3.4 %collective-permute-start.2 = (f32[8,320]{1,0:T(8,128)}, f32[8,320]{1,0:T(8,128)S(1)}, u32[]{:S(2)}, u32[]{:S(2)}) collective-permute-start(f32[8,320]{1,0:T(8,128)} %shard_map.111.refs_0_), channel_id=1, source_target_pairs={{0,1},{1,0},{2,3},{3,2},{4,5},{5,4},{6,7},{7,6},{8,9},{9,8},{10,11... | collective-permute-start | bytes 30728 | tf_op jit(solution)/shard_map/ppermute | solution.py:408
  17.3 2.0 %collective-permute-start.3 = (f32[8,320]{1,0:T(8,128)S(1)}, f32[8,320]{1,0:T(8,128)S(1)}, u32[]{:S(2)}, u32[]{:S(2)}) collective-permute-start(f32[8,320]{1,0:T(8,128)S(1)} %shard_map.112.refs_0_), channel_id=1, source_target_pairs={{0,2},{1,3},{2,0},{3,1},{4,6},{5,7},{6,4},{7,5},{8,10},{9,11},{10,... | collective-permute-start | bytes 30728 | tf_op jit(solution)/shard_map/ppermute | solution.py:408
  19.3 2.6 %collective-permute-start.4 = (f32[8,320]{1,0:T(8,128)S(1)}, f32[8,320]{1,0:T(8,128)S(1)}, u32[]{:S(2)}, u32[]{:S(2)}) collective-permute-start(f32[8,320]{1,0:T(8,128)S(1)} %shard_map.112.refs_0_), channel_id=1, source_target_pairs={{0,4},{1,5},{2,6},{3,7},{4,0},{5,1},{6,2},{7,3},{8,12},{9,13},{10,... | collective-permute-start | bytes 30728 | tf_op jit(solution)/shard_map/ppermute | solution.py:408
  24.3 1.9 %copy-done.4 = bf16[960,2048]{1,0:T(8,128)(2,1)} copy-done((bf16[960,2048]{1,0:T(8,128)(2,1)}, bf16[960,2048]{1,0:T(8,128)(2,1)S(1)}, u32[]{:S(2)}) %copy-start.4) | copy-done | bytes 3932184
  27.5 2.1 %copy-done.5 = bf16[960,2048]{1,0:T(8,128)(2,1)S(1)} copy-done((bf16[960,2048]{1,0:T(8,128)(2,1)S(1)}, bf16[960,2048]{1,0:T(8,128)(2,1)}, u32[]{:S(2)}) %copy-start.5) | copy-done | bytes 3932184
  29.6 2.0 %shard_map.115 = (bf16[320,2048]{1,0:T(8,128)(2,1)S(1)}, f32[320,960]{1,0:T(8,128)S(1)}, f32[8,384]{1,0:T(8,128)S(1)}) custom-call(bf16[4,320,512]{2,1,0:T(8,128)(2,1)S(1)} %bitcast.60, bf16[960,2048]{1,0:T(8,128)(2,1)S(1)} %copy-done.5, f32[8,320]{1,0:T(8,128)S(1)} %shard_map.113.stats_ref, f32[320]{0:T(512)S(1)} %copy-done.8, f32[320]{0:T(512)S(1)} %copy-done.9, ...), custom_call_target="tpu_custom_call" | custom-call | flops 1258291200 | bytes 5242880 | tf_op jit(solution)/shard_map/pallas_call | solution.py:29
  31.7 4.5 %shard_map.119 = (f32[4,4,40,768]{3,2,1,0:T(8,128)S(1)}, f32[2,4,40,768]{3,2,1,0:T(8,128)S(1)}, f32[2,4,40,768]{3,2,1,0:T(8,128)S(1)}, bf16[960,1024]{1,0:T(8,128)(2,1)S(1)}) custom-call(s32[6]{0:T(128)S(1)} %stack.50.where_ref, bf16[320,2048]{1,0:T(8,128)(2,1)S(1)} %get-tuple-element.33.act_ref, bf16[960,2048]{1,0:T(8,128)(2,1)S(1)} %copy-done.6, ...), custom_call_target="tpu_custom_call" | custom-call | flops 3774873600 | bytes 5242880 | tf_op jit(solution)/shard_map/pallas_call | solution.py:29
  38.1 2.3 %collective-permute-start = (bf16[320,512]{1,0:T(8,128)(2,1)S(1)}, bf16[320,512]{1,0:T(8,128)(2,1)S(1)}, u32[]{:S(2)}, u32[]{:S(2)}) collective-permute-start(bf16[320,512]{1,0:T(8,128)(2,1)S(1)} %get-tuple-element.55), channel_id=1, source_target_pairs={{0,1},{1,2},{2,3},{3,4},{4,5},{5,6},{6,7},{8,9},{9,10},{10,11},{11... | collective-permute-start | bytes 983048 | tf_op jit(solution)/shard_map/ppermute | solution.py:478
  44.5 2.2 %collective-permute-done.7.other_ref = f32[8,384]{1,0:T(8,128)S(1)} collective-permute-done((f32[8,384]{1,0:T(8,128)S(1)}, f32[8,384]{1,0:T(8,128)S(1)}, u32[]{:S(2)}, u32[]{:S(2)}) %collective-permute-start.7) | collective-permute-done | bytes 12320 | tf_op jit(solution)/shard_map/ppermute | solution.py:417
  50.5 7.2 %collective-permute-done.16 = f16[2,4,40,768]{3,2,1,0:T(8,128)(2,1)S(1)} collective-permute-done((f16[2,4,40,768]{3,2,1,0:T(8,128)(2,1)S(1)}, f16[2,4,40,768]{3,2,1,0:T(8,128)(2,1)S(1)}, u32[]{:S(2)}, u32[]{:S(2)}) %collective-permute-start.16) | collective-permute-done | bytes 491552 | tf_op jit(solution)/shard_map/ppermute | solution.py:417
  61.4 4.0 %collective-permute-done.17 = f16[1,4,40,768]{3,2,1,0:T(8,128)(2,1)S(1)} collective-permute-done((f16[1,4,40,768]{3,2,1,0:T(8,128)(2,1)S(1)}, f16[1,4,40,768]{3,2,1,0:T(8,128)(2,1)S(1)}, u32[]{:S(2)}, u32[]{:S(2)}) %collective-permute-start.17) | collective-permute-done | bytes 245792 | tf_op jit(solution)/shard_map/ppermute | solution.py:417
  66.7 4.8 %collective-permute-start.20 = (f16[40,768]{1,0:T(8,128)(2,1)S(1)}, f16[40,768]{1,0:T(8,128)(2,1)S(1)}, u32[]{:S(2)}, u32[]{:S(2)}) collective-permute-start(f16[40,768]{1,0:T(8,128)(2,1)S(1)} %get-tuple-element.57), channel_id=1, source_target_pairs={{0,6},{1,7},{2,4},{3,5},{4,2},{5,3},{6,0},{7,1},{8,14},{9,15},{10,... | collective-permute-start | bytes 184328 | tf_op jit(solution)/shard_map/ppermute | solution.py:408
  72.2 6.4 %shard_map.120 = (f32[4,320,512]{2,1,0:T(8,128)S(1)}, f32[8,320]{1,0:T(8,128)S(1)}) custom-call(bf16[4,320,512]{2,1,0:T(8,128)(2,1)S(1)} %bitcast.62, bf16[960,2048]{1,0:T(8,128)(2,1)S(1)} %copy-done.6, bf16[960,1024]{1,0:T(8,128)(2,1)S(1)} %get-tuple-element.35.edge_ref, f32[8,320]{1,0:T(8,128)S(1)} %shard_map.113.stats_ref, f32[320]{0:T(512)S(1)} %copy-done.8, ...), custom_call_target="tpu_custom_call" | custom-call | flops 3774873600 | bytes 5242880 | tf_op jit(solution)/shard_map/pallas_call | solution.py:29
  80.1 3.8 %collective-permute-start.23 = (f16[40,768]{1,0:T(8,128)(2,1)S(1)}, f16[40,768]{1,0:T(8,128)(2,1)S(1)}, u32[]{:S(2)}, u32[]{:S(2)}) collective-permute-start(f16[40,768]{1,0:T(8,128)(2,1)S(1)} %fusion.11), channel_id=1, source_target_pairs={{0,6},{1,7},{2,4},{3,5},{4,2},{5,3},{6,0},{7,1},{8,14},{9,15},{10,... | collective-permute-start | bytes 184328 | tf_op jit(solution)/shard_map/ppermute | solution.py:408
  84.6 2.3 %collective-permute-done.23 = f16[40,768]{1,0:T(8,128)(2,1)S(1)} collective-permute-done((f16[40,768]{1,0:T(8,128)(2,1)S(1)}, f16[40,768]{1,0:T(8,128)(2,1)S(1)}, u32[]{:S(2)}, u32[]{:S(2)}) %collective-permute-start.23) | collective-permute-done | bytes 61472 | tf_op jit(solution)/shard_map/ppermute | solution.py:408
  89.4 1.8 %collective-permute-start.12 = (f32[8,320]{1,0:T(8,128)S(1)}, f32[8,320]{1,0:T(8,128)S(1)}, u32[]{:S(2)}, u32[]{:S(2)}) collective-permute-start(f32[8,320]{1,0:T(8,128)S(1)} %add.63.refs_0_), channel_id=1, source_target_pairs={{0,4},{1,5},{2,6},{3,7},{4,0},{5,1},{6,2},{7,3},{8,12},{9,13},{10,... | collective-permute-start | bytes 30728 | tf_op jit(solution)/shard_map/ppermute | solution.py:408
  93.4 7.4 %shard_map.118 = bf16[4,320,512]{2,1,0:T(8,128)(2,1)} custom-call(s32[6]{0:T(128)S(1)} %stack.50.where_ref, bf16[4,320,512]{2,1,0:T(8,128)(2,1)S(1)} %bitcast.63, bf16[320,512]{1,0:T(8,128)(2,1)S(1)} %collective-permute-done.above_ref, bf16[320,512]{1,0:T(8,128)(2,1)S(1)} %collective-permute-done.1.below_ref, f32[8,320]{1,0:T(8,128)S(1)} %shard_map.113.stats_ref, ...), custom_call_target="tpu_custom_call" | custom-call | flops 3774873600 | bytes 5242880 | tf_op jit(solution)/shard_map/pallas_call | solution.py:29
  102.0 2.3 %shard_map.123 = bf16[4,320,512]{2,1,0:T(8,128)(2,1)} custom-call(f32[4,320,512]{2,1,0:T(8,128)S(1)} %get-tuple-element.36.grad_ref, bf16[4,320,512]{2,1,0:T(8,128)(2,1)S(1)} %bitcast.64, bf16[4,320,512]{2,1,0:T(8,128)(2,1)S(1)} %bitcast.58, f32[8,320]{1,0:T(8,128)S(1)} %shard_map.113.stats_ref, f32[8,320]{1,0:T(8,128)S(1)} %shard_map.122.sums_ref.total_ref), custom_call_target="tpu_custom_call" | custom-call | flops 13107200 | bytes 6553600 | tf_op jit(solution)/shard_map/pallas_call | solution.py:29
  108.2 2.3 %collective-permute-done.27 = f16[4,40,768]{2,1,0:T(8,128)(2,1)S(1)} collective-permute-done((f16[4,40,768]{2,1,0:T(8,128)(2,1)S(1)}, f16[4,40,768]{2,1,0:T(8,128)(2,1)S(1)}, u32[]{:S(2)}, u32[]{:S(2)}) %collective-permute-start.27) | collective-permute-done | bytes 245792 | tf_op jit(solution)/shard_map/ppermute | solution.py:417
  114.5 2.5 %shard_map.124.refs_2_ = f32[9,320,320]{2,1,0:T(8,128)} custom-call(s32[6]{0:T(128)S(1)} %stack.50.where_ref, f32[4,40,768]{2,1,0:T(8,128)S(1)} %convert_multiply_fusion.5.refs_0_, f32[4,40,768]{2,1,0:T(8,128)S(1)} %convert_multiply_fusion.4.refs_1_, f32[4,40,768]{2,1,0:T(8,128)S(1)} %convert_multiply_fusion.3.refs_2_, ...), custom_call_target="tpu_custom_call" | custom-call | bytes 5898240 | tf_op jit(solution)/shard_map/pallas_call | solution.py:617
  118.4 1.7 %shard_map.125 = f32[9,320,320]{2,1,0:T(8,128)} custom-call(s32[6]{0:T(128)S(1)} %stack.50.where_ref, f32[4,40,768]{2,1,0:T(8,128)S(1)} %convert_multiply_fusion.7.refs_0_, f32[4,40,768]{2,1,0:T(8,128)S(1)} %convert_multiply_fusion.6.refs_1_, f32[9,320,320]{2,1,0:T(8,128)} %shard_map.124.refs_2_), custom_call_target="tpu_custom_call", output_to_operand_aliasing={{}: (3, {})} | custom-call | bytes 1966080 | tf_op jit(solution)/shard_map/pallas_call | solution.py:617
  (103 shorter events, 39.4 us)
Async XLA Ops:
  2.6 29.0 %collective-permute-start.8 = (bf16[320,512]{1,0:T(8,128)(2,1)}, bf16[320,512]{1,0:T(8,128)(2,1)S(1)}, u32[]{:S(2)}, u32[]{:S(2)}) collective-permute-start(bf16[320,512]{1,0:T(8,128)(2,1)} %get-tuple-element.53), channel_id=1, source_target_pairs={{0,1},{1,2},{2,3},{3,4},{4,5},{5,6},{6,7},{8,9},{9,10},{10,11},{11... | collective-permute-start | bytes 983048 | tf_op jit(solution)/shard_map/ppermute | solution.py:476
  5.0 26.6 %collective-permute-start.9 = (bf16[320,512]{1,0:T(8,128)(2,1)}, bf16[320,512]{1,0:T(8,128)(2,1)S(1)}, u32[]{:S(2)}, u32[]{:S(2)}) collective-permute-start(bf16[320,512]{1,0:T(8,128)(2,1)} %get-tuple-element.52), channel_id=1, source_target_pairs={{1,0},{2,1},{3,2},{4,3},{5,4},{6,5},{7,6},{9,8},{10,9},{11,10},{12... | collective-permute-start | bytes 983048 | tf_op jit(solution)/shard_map/ppermute | solution.py:477
  17.3 9.0 %collective-permute-start.3 = (f32[8,320]{1,0:T(8,128)S(1)}, f32[8,320]{1,0:T(8,128)S(1)}, u32[]{:S(2)}, u32[]{:S(2)}) collective-permute-start(f32[8,320]{1,0:T(8,128)S(1)} %shard_map.112.refs_0_), channel_id=1, source_target_pairs={{0,2},{1,3},{2,0},{3,1},{4,6},{5,7},{6,4},{7,5},{8,10},{9,11},{10,... | collective-permute-start | bytes 30728 | tf_op jit(solution)/shard_map/ppermute | solution.py:408
  19.3 6.9 %collective-permute-start.4 = (f32[8,320]{1,0:T(8,128)S(1)}, f32[8,320]{1,0:T(8,128)S(1)}, u32[]{:S(2)}, u32[]{:S(2)}) collective-permute-start(f32[8,320]{1,0:T(8,128)S(1)} %shard_map.112.refs_0_), channel_id=1, source_target_pairs={{0,4},{1,5},{2,6},{3,7},{4,0},{5,1},{6,2},{7,3},{8,12},{9,13},{10,... | collective-permute-start | bytes 30728 | tf_op jit(solution)/shard_map/ppermute | solution.py:408
  21.9 5.5 %collective-permute-start.5 = (f32[8,320]{1,0:T(8,128)S(1)}, f32[8,320]{1,0:T(8,128)S(1)}, u32[]{:S(2)}, u32[]{:S(2)}) collective-permute-start(f32[8,320]{1,0:T(8,128)S(1)} %shard_map.112.refs_0_), channel_id=1, source_target_pairs={{0,6},{1,7},{2,4},{3,5},{4,2},{5,3},{6,0},{7,1},{8,14},{9,15},{10,... | collective-permute-start | bytes 30728 | tf_op jit(solution)/shard_map/ppermute | solution.py:408
  36.2 11.8 %collective-permute-start.15 = (f32[2,4,40,768]{3,2,1,0:T(8,128)S(1)}, f32[2,4,40,768]{3,2,1,0:T(8,128)S(1)}, u32[]{:S(2)}, u32[]{:S(2)}) collective-permute-start(f32[2,4,40,768]{3,2,1,0:T(8,128)S(1)} %get-tuple-element.41), channel_id=1, source_target_pairs={{0,1},{1,0},{2,3},{3,2},{4,5},{5,4},{6,7},{7,6},{8,9},{9,8},{10,11... | collective-permute-start | bytes 2949128 | tf_op jit(solution)/shard_map/ppermute | solution.py:408
  37.9 12.5 %collective-permute-start.14 = (f32[2,4,40,768]{3,2,1,0:T(8,128)S(1)}, f32[2,4,40,768]{3,2,1,0:T(8,128)S(1)}, u32[]{:S(2)}, u32[]{:S(2)}) collective-permute-start(f32[2,4,40,768]{3,2,1,0:T(8,128)S(1)} %get-tuple-element.40), channel_id=1, source_target_pairs={{0,1},{1,0},{2,3},{3,2},{4,5},{5,4},{6,7},{7,6},{8,9},{9,8},{10,11... | collective-permute-start | bytes 2949128 | tf_op jit(solution)/shard_map/ppermute | solution.py:408
  38.1 53.9 %collective-permute-start = (bf16[320,512]{1,0:T(8,128)(2,1)S(1)}, bf16[320,512]{1,0:T(8,128)(2,1)S(1)}, u32[]{:S(2)}, u32[]{:S(2)}) collective-permute-start(bf16[320,512]{1,0:T(8,128)(2,1)S(1)} %get-tuple-element.55), channel_id=1, source_target_pairs={{0,1},{1,2},{2,3},{3,4},{4,5},{5,6},{6,7},{8,9},{9,10},{10,11},{11... | collective-permute-start | bytes 983048 | tf_op jit(solution)/shard_map/ppermute | solution.py:478
  40.4 53.0 %collective-permute-start.1 = (bf16[320,512]{1,0:T(8,128)(2,1)S(1)}, bf16[320,512]{1,0:T(8,128)(2,1)S(1)}, u32[]{:S(2)}, u32[]{:S(2)}) collective-permute-start(bf16[320,512]{1,0:T(8,128)(2,1)S(1)} %get-tuple-element.54), channel_id=1, source_target_pairs={{1,0},{2,1},{3,2},{4,3},{5,4},{6,5},{7,6},{9,8},{10,9},{11,10},{12... | collective-permute-start | bytes 983048 | tf_op jit(solution)/shard_map/ppermute | solution.py:479
  48.8 8.9 %collective-permute-start.16 = (f16[2,4,40,768]{3,2,1,0:T(8,128)(2,1)S(1)}, f16[2,4,40,768]{3,2,1,0:T(8,128)(2,1)S(1)}, u32[]{:S(2)}, u32[]{:S(2)}) collective-permute-start(f16[2,4,40,768]{3,2,1,0:T(8,128)(2,1)S(1)} %multiply_convert_fusion), channel_id=1, source_target_pairs={{0,8},{1,17},{2,10},{3,19},{4,12},{5,21},{6,14},{7,23},{8,0},{9,25... | collective-permute-start | bytes 1474568 | tf_op jit(solution)/shard_map/ppermute | solution.py:417
  59.1 6.3 %collective-permute-start.17 = (f16[1,4,40,768]{3,2,1,0:T(8,128)(2,1)S(1)}, f16[1,4,40,768]{3,2,1,0:T(8,128)(2,1)S(1)}, u32[]{:S(2)}, u32[]{:S(2)}) collective-permute-start(f16[1,4,40,768]{3,2,1,0:T(8,128)(2,1)S(1)} %fusion.1), channel_id=1, source_target_pairs={{0,16},{1,9},{2,18},{3,11},{4,20},{5,13},{6,22},{7,15},{8,24},{9,1... | collective-permute-start | bytes 737288 | tf_op jit(solution)/shard_map/ppermute | solution.py:417
  66.7 11.9 %collective-permute-start.20 = (f16[40,768]{1,0:T(8,128)(2,1)S(1)}, f16[40,768]{1,0:T(8,128)(2,1)S(1)}, u32[]{:S(2)}, u32[]{:S(2)}) collective-permute-start(f16[40,768]{1,0:T(8,128)(2,1)S(1)} %get-tuple-element.57), channel_id=1, source_target_pairs={{0,6},{1,7},{2,4},{3,5},{4,2},{5,3},{6,0},{7,1},{8,14},{9,15},{10,... | collective-permute-start | bytes 184328 | tf_op jit(solution)/shard_map/ppermute | solution.py:408
  71.5 7.2 %collective-permute-start.19 = (f16[40,768]{1,0:T(8,128)(2,1)S(1)}, f16[40,768]{1,0:T(8,128)(2,1)S(1)}, u32[]{:S(2)}, u32[]{:S(2)}) collective-permute-start(f16[40,768]{1,0:T(8,128)(2,1)S(1)} %get-tuple-element.58), channel_id=1, source_target_pairs={{0,4},{1,5},{2,6},{3,7},{4,0},{5,1},{6,2},{7,3},{8,12},{9,13},{10,... | collective-permute-start | bytes 184328 | tf_op jit(solution)/shard_map/ppermute | solution.py:408
  71.5 7.2 %collective-permute-start.18 = (f16[40,768]{1,0:T(8,128)(2,1)S(1)}, f16[40,768]{1,0:T(8,128)(2,1)S(1)}, u32[]{:S(2)}, u32[]{:S(2)}) collective-permute-start(f16[40,768]{1,0:T(8,128)(2,1)S(1)} %get-tuple-element.56), channel_id=1, source_target_pairs={{0,2},{1,3},{2,0},{3,1},{4,6},{5,7},{6,4},{7,5},{8,10},{9,11},{10,... | collective-permute-start | bytes 184328 | tf_op jit(solution)/shard_map/ppermute | solution.py:408
  80.1 6.8 %collective-permute-start.23 = (f16[40,768]{1,0:T(8,128)(2,1)S(1)}, f16[40,768]{1,0:T(8,128)(2,1)S(1)}, u32[]{:S(2)}, u32[]{:S(2)}) collective-permute-start(f16[40,768]{1,0:T(8,128)(2,1)S(1)} %fusion.11), channel_id=1, source_target_pairs={{0,6},{1,7},{2,4},{3,5},{4,2},{5,3},{6,0},{7,1},{8,14},{9,15},{10,... | collective-permute-start | bytes 184328 | tf_op jit(solution)/shard_map/ppermute | solution.py:408
  83.9 5.5 %collective-permute-start.22 = (f16[40,768]{1,0:T(8,128)(2,1)S(1)}, f16[40,768]{1,0:T(8,128)(2,1)S(1)}, u32[]{:S(2)}, u32[]{:S(2)}) collective-permute-start(f16[40,768]{1,0:T(8,128)(2,1)S(1)} %fusion.11), channel_id=1, source_target_pairs={{0,4},{1,5},{2,6},{3,7},{4,0},{5,1},{6,2},{7,3},{8,12},{9,13},{10,... | collective-permute-start | bytes 184328 | tf_op jit(solution)/shard_map/ppermute | solution.py:408
  83.9 7.3 %collective-permute-start.21 = (f16[40,768]{1,0:T(8,128)(2,1)S(1)}, f16[40,768]{1,0:T(8,128)(2,1)S(1)}, u32[]{:S(2)}, u32[]{:S(2)}) collective-permute-start(f16[40,768]{1,0:T(8,128)(2,1)S(1)} %fusion.11), channel_id=1, source_target_pairs={{0,2},{1,3},{2,0},{3,1},{4,6},{5,7},{6,4},{7,5},{8,10},{9,11},{10,... | collective-permute-start | bytes 184328 | tf_op jit(solution)/shard_map/ppermute | solution.py:408
  86.9 13.9 %collective-permute-start.11 = (f32[8,320]{1,0:T(8,128)S(1)}, f32[8,320]{1,0:T(8,128)S(1)}, u32[]{:S(2)}, u32[]{:S(2)}) collective-permute-start(f32[8,320]{1,0:T(8,128)S(1)} %add.63.refs_0_), channel_id=1, source_target_pairs={{0,2},{1,3},{2,0},{3,1},{4,6},{5,7},{6,4},{7,5},{8,10},{9,11},{10,... | collective-permute-start | bytes 30728 | tf_op jit(solution)/shard_map/ppermute | solution.py:408
  89.4 11.4 %collective-permute-start.12 = (f32[8,320]{1,0:T(8,128)S(1)}, f32[8,320]{1,0:T(8,128)S(1)}, u32[]{:S(2)}, u32[]{:S(2)}) collective-permute-start(f32[8,320]{1,0:T(8,128)S(1)} %add.63.refs_0_), channel_id=1, source_target_pairs={{0,4},{1,5},{2,6},{3,7},{4,0},{5,1},{6,2},{7,3},{8,12},{9,13},{10,... | collective-permute-start | bytes 30728 | tf_op jit(solution)/shard_map/ppermute | solution.py:408
  91.2 9.6 %collective-permute-start.13 = (f32[8,320]{1,0:T(8,128)S(1)}, f32[8,320]{1,0:T(8,128)S(1)}, u32[]{:S(2)}, u32[]{:S(2)}) collective-permute-start(f32[8,320]{1,0:T(8,128)S(1)} %add.63.refs_0_), channel_id=1, source_target_pairs={{0,6},{1,7},{2,4},{3,5},{4,2},{5,3},{6,0},{7,1},{8,14},{9,15},{10,... | collective-permute-start | bytes 30728 | tf_op jit(solution)/shard_map/ppermute | solution.py:408
  92.0 13.8 %collective-permute-start.24 = (f16[4,40,768]{2,1,0:T(8,128)(2,1)S(1)}, f16[4,40,768]{2,1,0:T(8,128)(2,1)S(1)}, u32[]{:S(2)}, u32[]{:S(2)}) collective-permute-start(f16[4,40,768]{2,1,0:T(8,128)(2,1)S(1)} %pad_maximum_fusion), channel_id=1, source_target_pairs={{0,16},{1,9},{2,18},{3,11},{4,20},{5,13},{6,22},{7,15},{8,24},{9,1... | collective-permute-start | bytes 737288 | tf_op jit(solution)/shard_map/ppermute | solution.py:417
  104.3 6.2 %collective-permute-start.27 = (f16[4,40,768]{2,1,0:T(8,128)(2,1)S(1)}, f16[4,40,768]{2,1,0:T(8,128)(2,1)S(1)}, u32[]{:S(2)}, u32[]{:S(2)}) collective-permute-start(f16[4,40,768]{2,1,0:T(8,128)(2,1)S(1)} %pad_maximum_fusion), channel_id=1, source_target_pairs={{0,8},{1,17},{2,10},{3,19},{4,12},{5,21},{6,14},{7,23},{8,0},{9,25... | collective-permute-start | bytes 737288 | tf_op jit(solution)/shard_map/ppermute | solution.py:417
  105.6 5.6 %collective-permute-start.28 = (f16[4,40,768]{2,1,0:T(8,128)(2,1)S(1)}, f16[4,40,768]{2,1,0:T(8,128)(2,1)S(1)}, u32[]{:S(2)}, u32[]{:S(2)}) collective-permute-start(f16[4,40,768]{2,1,0:T(8,128)(2,1)S(1)} %pad_maximum_fusion), channel_id=1, source_target_pairs={{0,1},{1,0},{2,3},{3,2},{4,5},{5,4},{6,7},{7,6},{8,9},{9,8},{10,11... | collective-permute-start | bytes 737288 | tf_op jit(solution)/shard_map/ppermute | solution.py:408
  105.7 7.4 %collective-permute-start.25 = (f16[4,40,768]{2,1,0:T(8,128)(2,1)S(1)}, f16[4,40,768]{2,1,0:T(8,128)(2,1)S(1)}, u32[]{:S(2)}, u32[]{:S(2)}) collective-permute-start(f16[4,40,768]{2,1,0:T(8,128)(2,1)S(1)} %collective-permute-done.24), channel_id=1, source_target_pairs={{0,8},{1,17},{2,10},{3,19},{4,12},{5,21},{6,14},{7,23},{8,0},{9,25... | collective-permute-start | bytes 737288 | tf_op jit(solution)/shard_map/ppermute | solution.py:417
  (19 other events, 178.0 us)

commit v7 on v6

--- a/solution.py
+++ b/solution.py
@@ -379,10 +379,9 @@
 
     table = table_ref[...]
     bound = jnp.max(table[:, channels + NOTE : channels + NOTE + 1], axis=0, keepdims=True)
-    power = jnp.floor(jnp.log2(30000.0 / jnp.maximum(bound, 1e-30)))
-    power = jnp.clip(power, -100.0, 100.0)
-    scale_ref[...] = jnp.exp2(power)
-    back_ref[...] = 1.0 / jnp.exp2(power)
+    bound = jnp.maximum(bound, 1e-25) * (1.0 / 30000.0)
+    back_ref[...] = bound
+    scale_ref[...] = 1.0 / bound
     steps_ref[...] = jnp.broadcast_to(table[:, channels : channels + 1], steps_ref.shape)
 
 

time: 121 us -> 121 us (level)
  no operation moved by 1% of the time
where the time goes in v7:
time: 121 us; the launch traced here: 120 us
  starting transfers between devices  39.5 us (33%)
  Pallas kernels  37 us (31%)
  waiting for transfers between devices  22.2 us (18%)
  other arithmetic  11.2 us (9%)
  local copies, waits for them, and re-layouts  8.27 us (7%)
  between operations  1.91 us (2%)
    pallas_call x14, Pallas kernels, call(): pl.pallas_call(body, out_shape=tuple(outs) if many else outs, in_specs=li...  32.7 us
    ppermute x20, starting transfers between devices, swap_space(): return lax.ppermute(cells, 'space', [(i, i ^ mask) for i in range(count)])  22.8 us
    ppermute x7, waiting for transfers between devices, swap_image(): return lax.ppermute(cells, ('dp', 'space'), pairs)  16.8 us
    ppermute x7, starting transfers between devices, swap_image(): return lax.ppermute(cells, ('dp', 'space'), pairs)  9.39 us
    unnamed x24, local copies, waits for them, and re-layouts  6.15 us
    ppermute x20, waiting for transfers between devices, swap_space(): return lax.ppermute(cells, 'space', [(i, i ^ mask) for i in range(count)])  5.33 us
    mul x8, other arithmetic, place(): cells.append(piece.astype(f32) * line_back)  5.29 us
    pallas_call x2, Pallas kernels, place(): pl.pallas_call(functools.partial(place_body, (zones, height, width), half...  4.25 us
  transfers between devices with their start and end apart: 31, of which 9 were waited for; matrix products, arithmetic and copies ran while one was open for 9% of the time, Pallas kernels for 26%

profile of v7, /device:TPU:0, one launch (start us, length us, event | category | flops | bytes accessed | tf_op | source)
XLA Modules:
  0.0 120.2 jit_solution(7668562969902631309)
XLA Ops:
  0.6 2.0 %slice_bitcast_fusion = (bf16[320,512]{1,0:T(8,128)(2,1)}, bf16[320,512]{1,0:T(8,128)(2,1)}) fusion(bf16[1,4,320,512]{3,2,1,0:T(8,128)(2,1)} %bitcast.55), kind=kLoop, calls=%fused_computation.15 | loop fusion | bytes 1310720 | tf_op jit(solution)/shard_map/squeeze | solution.py:476
  2.6 2.4 %collective-permute-start.8 = (bf16[320,512]{1,0:T(8,128)(2,1)}, bf16[320,512]{1,0:T(8,128)(2,1)S(1)}, u32[]{:S(2)}, u32[]{:S(2)}) collective-permute-start(bf16[320,512]{1,0:T(8,128)(2,1)} %get-tuple-element.53), channel_id=1, source_target_pairs={{0,1},{1,2},{2,3},{3,4},{4,5},{5,6},{6,7},{8,9},{9,10},{10,11},{11... | collective-permute-start | bytes 983048 | tf_op jit(solution)/shard_map/ppermute | solution.py:475
  7.0 5.1 %shard_map.111.refs_0_ = f32[8,320]{1,0:T(8,128)} custom-call(s32[1]{0:T(128)S(6)} %copy.14.step_ref, bf16[4,320,512]{2,1,0:T(8,128)(2,1)} %bitcast.59, bf16[4,320,512]{2,1,0:T(8,128)(2,1)} %bitcast.56), custom_call_target="tpu_custom_call" | custom-call | flops 39321600 | bytes 2621440 | tf_op jit(solution)/shard_map/pallas_call | solution.py:29
  12.2 3.4 %collective-permute-start.2 = (f32[8,320]{1,0:T(8,128)}, f32[8,320]{1,0:T(8,128)S(1)}, u32[]{:S(2)}, u32[]{:S(2)}) collective-permute-start(f32[8,320]{1,0:T(8,128)} %shard_map.111.refs_0_), channel_id=1, source_target_pairs={{0,1},{1,0},{2,3},{3,2},{4,5},{5,4},{6,7},{7,6},{8,9},{9,8},{10,11... | collective-permute-start | bytes 30728 | tf_op jit(solution)/shard_map/ppermute | solution.py:407
  17.3 2.0 %collective-permute-start.3 = (f32[8,320]{1,0:T(8,128)S(1)}, f32[8,320]{1,0:T(8,128)S(1)}, u32[]{:S(2)}, u32[]{:S(2)}) collective-permute-start(f32[8,320]{1,0:T(8,128)S(1)} %shard_map.112.refs_0_), channel_id=1, source_target_pairs={{0,2},{1,3},{2,0},{3,1},{4,6},{5,7},{6,4},{7,5},{8,10},{9,11},{10,... | collective-permute-start | bytes 30728 | tf_op jit(solution)/shard_map/ppermute | solution.py:407
  19.3 2.6 %collective-permute-start.4 = (f32[8,320]{1,0:T(8,128)S(1)}, f32[8,320]{1,0:T(8,128)S(1)}, u32[]{:S(2)}, u32[]{:S(2)}) collective-permute-start(f32[8,320]{1,0:T(8,128)S(1)} %shard_map.112.refs_0_), channel_id=1, source_target_pairs={{0,4},{1,5},{2,6},{3,7},{4,0},{5,1},{6,2},{7,3},{8,12},{9,13},{10,... | collective-permute-start | bytes 30728 | tf_op jit(solution)/shard_map/ppermute | solution.py:407
  24.3 1.9 %copy-done.4 = bf16[960,2048]{1,0:T(8,128)(2,1)} copy-done((bf16[960,2048]{1,0:T(8,128)(2,1)}, bf16[960,2048]{1,0:T(8,128)(2,1)S(1)}, u32[]{:S(2)}) %copy-start.4) | copy-done | bytes 3932184
  27.5 2.1 %copy-done.5 = bf16[960,2048]{1,0:T(8,128)(2,1)S(1)} copy-done((bf16[960,2048]{1,0:T(8,128)(2,1)S(1)}, bf16[960,2048]{1,0:T(8,128)(2,1)}, u32[]{:S(2)}) %copy-start.5) | copy-done | bytes 3932184
  29.6 2.0 %shard_map.115 = (bf16[320,2048]{1,0:T(8,128)(2,1)S(1)}, f32[320,960]{1,0:T(8,128)S(1)}, f32[8,384]{1,0:T(8,128)S(1)}) custom-call(bf16[4,320,512]{2,1,0:T(8,128)(2,1)S(1)} %bitcast.60, bf16[960,2048]{1,0:T(8,128)(2,1)S(1)} %copy-done.5, f32[8,320]{1,0:T(8,128)S(1)} %shard_map.113.stats_ref, f32[320]{0:T(512)S(1)} %copy-done.8, f32[320]{0:T(512)S(1)} %copy-done.9, ...), custom_call_target="tpu_custom_call" | custom-call | flops 1258291200 | bytes 5242880 | tf_op jit(solution)/shard_map/pallas_call | solution.py:29
  31.7 4.5 %shard_map.119 = (f32[4,4,40,768]{3,2,1,0:T(8,128)S(1)}, f32[2,4,40,768]{3,2,1,0:T(8,128)S(1)}, f32[2,4,40,768]{3,2,1,0:T(8,128)S(1)}, bf16[960,1024]{1,0:T(8,128)(2,1)S(1)}) custom-call(s32[6]{0:T(128)S(1)} %stack.50.where_ref, bf16[320,2048]{1,0:T(8,128)(2,1)S(1)} %get-tuple-element.33.act_ref, bf16[960,2048]{1,0:T(8,128)(2,1)S(1)} %copy-done.6, ...), custom_call_target="tpu_custom_call" | custom-call | flops 3774873600 | bytes 5242880 | tf_op jit(solution)/shard_map/pallas_call | solution.py:29
  38.1 2.3 %collective-permute-start = (bf16[320,512]{1,0:T(8,128)(2,1)S(1)}, bf16[320,512]{1,0:T(8,128)(2,1)S(1)}, u32[]{:S(2)}, u32[]{:S(2)}) collective-permute-start(bf16[320,512]{1,0:T(8,128)(2,1)S(1)} %get-tuple-element.55), channel_id=1, source_target_pairs={{0,1},{1,2},{2,3},{3,4},{4,5},{5,6},{6,7},{8,9},{9,10},{10,11},{11... | collective-permute-start | bytes 983048 | tf_op jit(solution)/shard_map/ppermute | solution.py:477
  44.4 2.2 %collective-permute-done.7.other_ref = f32[8,384]{1,0:T(8,128)S(1)} collective-permute-done((f32[8,384]{1,0:T(8,128)S(1)}, f32[8,384]{1,0:T(8,128)S(1)}, u32[]{:S(2)}, u32[]{:S(2)}) %collective-permute-start.7) | collective-permute-done | bytes 12320 | tf_op jit(solution)/shard_map/ppermute | solution.py:416
  50.5 7.2 %collective-permute-done.16 = f16[2,4,40,768]{3,2,1,0:T(8,128)(2,1)S(1)} collective-permute-done((f16[2,4,40,768]{3,2,1,0:T(8,128)(2,1)S(1)}, f16[2,4,40,768]{3,2,1,0:T(8,128)(2,1)S(1)}, u32[]{:S(2)}, u32[]{:S(2)}) %collective-permute-start.16) | collective-permute-done | bytes 491552 | tf_op jit(solution)/shard_map/ppermute | solution.py:416
  61.4 4.0 %collective-permute-done.17 = f16[1,4,40,768]{3,2,1,0:T(8,128)(2,1)S(1)} collective-permute-done((f16[1,4,40,768]{3,2,1,0:T(8,128)(2,1)S(1)}, f16[1,4,40,768]{3,2,1,0:T(8,128)(2,1)S(1)}, u32[]{:S(2)}, u32[]{:S(2)}) %collective-permute-start.17) | collective-permute-done | bytes 245792 | tf_op jit(solution)/shard_map/ppermute | solution.py:416
  66.7 4.8 %collective-permute-start.20 = (f16[40,768]{1,0:T(8,128)(2,1)S(1)}, f16[40,768]{1,0:T(8,128)(2,1)S(1)}, u32[]{:S(2)}, u32[]{:S(2)}) collective-permute-start(f16[40,768]{1,0:T(8,128)(2,1)S(1)} %get-tuple-element.57), channel_id=1, source_target_pairs={{0,6},{1,7},{2,4},{3,5},{4,2},{5,3},{6,0},{7,1},{8,14},{9,15},{10,... | collective-permute-start | bytes 184328 | tf_op jit(solution)/shard_map/ppermute | solution.py:407
  72.1 6.4 %shard_map.120 = (f32[4,320,512]{2,1,0:T(8,128)S(1)}, f32[8,320]{1,0:T(8,128)S(1)}) custom-call(bf16[4,320,512]{2,1,0:T(8,128)(2,1)S(1)} %bitcast.62, bf16[960,2048]{1,0:T(8,128)(2,1)S(1)} %copy-done.6, bf16[960,1024]{1,0:T(8,128)(2,1)S(1)} %get-tuple-element.35.edge_ref, f32[8,320]{1,0:T(8,128)S(1)} %shard_map.113.stats_ref, f32[320]{0:T(512)S(1)} %copy-done.8, ...), custom_call_target="tpu_custom_call" | custom-call | flops 3774873600 | bytes 5242880 | tf_op jit(solution)/shard_map/pallas_call | solution.py:29
  80.0 3.8 %collective-permute-start.23 = (f16[40,768]{1,0:T(8,128)(2,1)S(1)}, f16[40,768]{1,0:T(8,128)(2,1)S(1)}, u32[]{:S(2)}, u32[]{:S(2)}) collective-permute-start(f16[40,768]{1,0:T(8,128)(2,1)S(1)} %fusion.11), channel_id=1, source_target_pairs={{0,6},{1,7},{2,4},{3,5},{4,2},{5,3},{6,0},{7,1},{8,14},{9,15},{10,... | collective-permute-start | bytes 184328 | tf_op jit(solution)/shard_map/ppermute | solution.py:407
  84.6 2.3 %collective-permute-done.23 = f16[40,768]{1,0:T(8,128)(2,1)S(1)} collective-permute-done((f16[40,768]{1,0:T(8,128)(2,1)S(1)}, f16[40,768]{1,0:T(8,128)(2,1)S(1)}, u32[]{:S(2)}, u32[]{:S(2)}) %collective-permute-start.23) | collective-permute-done | bytes 61472 | tf_op jit(solution)/shard_map/ppermute | solution.py:407
  89.3 1.8 %collective-permute-start.12 = (f32[8,320]{1,0:T(8,128)S(1)}, f32[8,320]{1,0:T(8,128)S(1)}, u32[]{:S(2)}, u32[]{:S(2)}) collective-permute-start(f32[8,320]{1,0:T(8,128)S(1)} %add.63.refs_0_), channel_id=1, source_target_pairs={{0,4},{1,5},{2,6},{3,7},{4,0},{5,1},{6,2},{7,3},{8,12},{9,13},{10,... | collective-permute-start | bytes 30728 | tf_op jit(solution)/shard_map/ppermute | solution.py:407
  93.3 7.4 %shard_map.118 = bf16[4,320,512]{2,1,0:T(8,128)(2,1)} custom-call(s32[6]{0:T(128)S(1)} %stack.50.where_ref, bf16[4,320,512]{2,1,0:T(8,128)(2,1)S(1)} %bitcast.63, bf16[320,512]{1,0:T(8,128)(2,1)S(1)} %collective-permute-done.above_ref, bf16[320,512]{1,0:T(8,128)(2,1)S(1)} %collective-permute-done.1.below_ref, f32[8,320]{1,0:T(8,128)S(1)} %shard_map.113.stats_ref, ...), custom_call_target="tpu_custom_call" | custom-call | flops 3774873600 | bytes 5242880 | tf_op jit(solution)/shard_map/pallas_call | solution.py:29
  102.0 2.3 %shard_map.123 = bf16[4,320,512]{2,1,0:T(8,128)(2,1)} custom-call(f32[4,320,512]{2,1,0:T(8,128)S(1)} %get-tuple-element.36.grad_ref, bf16[4,320,512]{2,1,0:T(8,128)(2,1)S(1)} %bitcast.64, bf16[4,320,512]{2,1,0:T(8,128)(2,1)S(1)} %bitcast.58, f32[8,320]{1,0:T(8,128)S(1)} %shard_map.113.stats_ref, f32[8,320]{1,0:T(8,128)S(1)} %shard_map.122.sums_ref.total_ref), custom_call_target="tpu_custom_call" | custom-call | flops 13107200 | bytes 6553600 | tf_op jit(solution)/shard_map/pallas_call | solution.py:29
  108.2 2.3 %collective-permute-done.27 = f16[4,40,768]{2,1,0:T(8,128)(2,1)S(1)} collective-permute-done((f16[4,40,768]{2,1,0:T(8,128)(2,1)S(1)}, f16[4,40,768]{2,1,0:T(8,128)(2,1)S(1)}, u32[]{:S(2)}, u32[]{:S(2)}) %collective-permute-start.27) | collective-permute-done | bytes 245792 | tf_op jit(solution)/shard_map/ppermute | solution.py:416
  114.4 2.5 %shard_map.124.refs_2_ = f32[9,320,320]{2,1,0:T(8,128)} custom-call(s32[6]{0:T(128)S(1)} %stack.50.where_ref, f32[4,40,768]{2,1,0:T(8,128)S(1)} %convert_multiply_fusion.5.refs_0_, f32[4,40,768]{2,1,0:T(8,128)S(1)} %convert_multiply_fusion.4.refs_1_, f32[4,40,768]{2,1,0:T(8,128)S(1)} %convert_multiply_fusion.3.refs_2_, ...), custom_call_target="tpu_custom_call" | custom-call | bytes 5898240 | tf_op jit(solution)/shard_map/pallas_call | solution.py:616
  118.3 1.7 %shard_map.125 = f32[9,320,320]{2,1,0:T(8,128)} custom-call(s32[6]{0:T(128)S(1)} %stack.50.where_ref, f32[4,40,768]{2,1,0:T(8,128)S(1)} %convert_multiply_fusion.7.refs_0_, f32[4,40,768]{2,1,0:T(8,128)S(1)} %convert_multiply_fusion.6.refs_1_, f32[9,320,320]{2,1,0:T(8,128)} %shard_map.124.refs_2_), custom_call_target="tpu_custom_call", output_to_operand_aliasing={{}: (3, {})} | custom-call | bytes 1966080 | tf_op jit(solution)/shard_map/pallas_call | solution.py:616
  (103 shorter events, 39.3 us)
Async XLA Ops:
  2.6 29.0 %collective-permute-start.8 = (bf16[320,512]{1,0:T(8,128)(2,1)}, bf16[320,512]{1,0:T(8,128)(2,1)S(1)}, u32[]{:S(2)}, u32[]{:S(2)}) collective-permute-start(bf16[320,512]{1,0:T(8,128)(2,1)} %get-tuple-element.53), channel_id=1, source_target_pairs={{0,1},{1,2},{2,3},{3,4},{4,5},{5,6},{6,7},{8,9},{9,10},{10,11},{11... | collective-permute-start | bytes 983048 | tf_op jit(solution)/shard_map/ppermute | solution.py:475
  5.0 26.6 %collective-permute-start.9 = (bf16[320,512]{1,0:T(8,128)(2,1)}, bf16[320,512]{1,0:T(8,128)(2,1)S(1)}, u32[]{:S(2)}, u32[]{:S(2)}) collective-permute-start(bf16[320,512]{1,0:T(8,128)(2,1)} %get-tuple-element.52), channel_id=1, source_target_pairs={{1,0},{2,1},{3,2},{4,3},{5,4},{6,5},{7,6},{9,8},{10,9},{11,10},{12... | collective-permute-start | bytes 983048 | tf_op jit(solution)/shard_map/ppermute | solution.py:476
  17.3 9.0 %collective-permute-start.3 = (f32[8,320]{1,0:T(8,128)S(1)}, f32[8,320]{1,0:T(8,128)S(1)}, u32[]{:S(2)}, u32[]{:S(2)}) collective-permute-start(f32[8,320]{1,0:T(8,128)S(1)} %shard_map.112.refs_0_), channel_id=1, source_target_pairs={{0,2},{1,3},{2,0},{3,1},{4,6},{5,7},{6,4},{7,5},{8,10},{9,11},{10,... | collective-permute-start | bytes 30728 | tf_op jit(solution)/shard_map/ppermute | solution.py:407
  19.3 6.9 %collective-permute-start.4 = (f32[8,320]{1,0:T(8,128)S(1)}, f32[8,320]{1,0:T(8,128)S(1)}, u32[]{:S(2)}, u32[]{:S(2)}) collective-permute-start(f32[8,320]{1,0:T(8,128)S(1)} %shard_map.112.refs_0_), channel_id=1, source_target_pairs={{0,4},{1,5},{2,6},{3,7},{4,0},{5,1},{6,2},{7,3},{8,12},{9,13},{10,... | collective-permute-start | bytes 30728 | tf_op jit(solution)/shard_map/ppermute | solution.py:407
  21.9 5.5 %collective-permute-start.5 = (f32[8,320]{1,0:T(8,128)S(1)}, f32[8,320]{1,0:T(8,128)S(1)}, u32[]{:S(2)}, u32[]{:S(2)}) collective-permute-start(f32[8,320]{1,0:T(8,128)S(1)} %shard_map.112.refs_0_), channel_id=1, source_target_pairs={{0,6},{1,7},{2,4},{3,5},{4,2},{5,3},{6,0},{7,1},{8,14},{9,15},{10,... | collective-permute-start | bytes 30728 | tf_op jit(solution)/shard_map/ppermute | solution.py:407
  36.2 11.8 %collective-permute-start.15 = (f32[2,4,40,768]{3,2,1,0:T(8,128)S(1)}, f32[2,4,40,768]{3,2,1,0:T(8,128)S(1)}, u32[]{:S(2)}, u32[]{:S(2)}) collective-permute-start(f32[2,4,40,768]{3,2,1,0:T(8,128)S(1)} %get-tuple-element.41), channel_id=1, source_target_pairs={{0,1},{1,0},{2,3},{3,2},{4,5},{5,4},{6,7},{7,6},{8,9},{9,8},{10,11... | collective-permute-start | bytes 2949128 | tf_op jit(solution)/shard_map/ppermute | solution.py:407
  37.9 12.5 %collective-permute-start.14 = (f32[2,4,40,768]{3,2,1,0:T(8,128)S(1)}, f32[2,4,40,768]{3,2,1,0:T(8,128)S(1)}, u32[]{:S(2)}, u32[]{:S(2)}) collective-permute-start(f32[2,4,40,768]{3,2,1,0:T(8,128)S(1)} %get-tuple-element.40), channel_id=1, source_target_pairs={{0,1},{1,0},{2,3},{3,2},{4,5},{5,4},{6,7},{7,6},{8,9},{9,8},{10,11... | collective-permute-start | bytes 2949128 | tf_op jit(solution)/shard_map/ppermute | solution.py:407
  38.1 53.8 %collective-permute-start = (bf16[320,512]{1,0:T(8,128)(2,1)S(1)}, bf16[320,512]{1,0:T(8,128)(2,1)S(1)}, u32[]{:S(2)}, u32[]{:S(2)}) collective-permute-start(bf16[320,512]{1,0:T(8,128)(2,1)S(1)} %get-tuple-element.55), channel_id=1, source_target_pairs={{0,1},{1,2},{2,3},{3,4},{4,5},{5,6},{6,7},{8,9},{9,10},{10,11},{11... | collective-permute-start | bytes 983048 | tf_op jit(solution)/shard_map/ppermute | solution.py:477
  40.4 53.0 %collective-permute-start.1 = (bf16[320,512]{1,0:T(8,128)(2,1)S(1)}, bf16[320,512]{1,0:T(8,128)(2,1)S(1)}, u32[]{:S(2)}, u32[]{:S(2)}) collective-permute-start(bf16[320,512]{1,0:T(8,128)(2,1)S(1)} %get-tuple-element.54), channel_id=1, source_target_pairs={{1,0},{2,1},{3,2},{4,3},{5,4},{6,5},{7,6},{9,8},{10,9},{11,10},{12... | collective-permute-start | bytes 983048 | tf_op jit(solution)/shard_map/ppermute | solution.py:478
  48.8 8.9 %collective-permute-start.16 = (f16[2,4,40,768]{3,2,1,0:T(8,128)(2,1)S(1)}, f16[2,4,40,768]{3,2,1,0:T(8,128)(2,1)S(1)}, u32[]{:S(2)}, u32[]{:S(2)}) collective-permute-start(f16[2,4,40,768]{3,2,1,0:T(8,128)(2,1)S(1)} %multiply_convert_fusion), channel_id=1, source_target_pairs={{0,8},{1,17},{2,10},{3,19},{4,12},{5,21},{6,14},{7,23},{8,0},{9,25... | collective-permute-start | bytes 1474568 | tf_op jit(solution)/shard_map/ppermute | solution.py:416
  59.1 6.3 %collective-permute-start.17 = (f16[1,4,40,768]{3,2,1,0:T(8,128)(2,1)S(1)}, f16[1,4,40,768]{3,2,1,0:T(8,128)(2,1)S(1)}, u32[]{:S(2)}, u32[]{:S(2)}) collective-permute-start(f16[1,4,40,768]{3,2,1,0:T(8,128)(2,1)S(1)} %fusion.1), channel_id=1, source_target_pairs={{0,16},{1,9},{2,18},{3,11},{4,20},{5,13},{6,22},{7,15},{8,24},{9,1... | collective-permute-start | bytes 737288 | tf_op jit(solution)/shard_map/ppermute | solution.py:416
  66.7 11.9 %collective-permute-start.20 = (f16[40,768]{1,0:T(8,128)(2,1)S(1)}, f16[40,768]{1,0:T(8,128)(2,1)S(1)}, u32[]{:S(2)}, u32[]{:S(2)}) collective-permute-start(f16[40,768]{1,0:T(8,128)(2,1)S(1)} %get-tuple-element.57), channel_id=1, source_target_pairs={{0,6},{1,7},{2,4},{3,5},{4,2},{5,3},{6,0},{7,1},{8,14},{9,15},{10,... | collective-permute-start | bytes 184328 | tf_op jit(solution)/shard_map/ppermute | solution.py:407
  71.5 7.2 %collective-permute-start.19 = (f16[40,768]{1,0:T(8,128)(2,1)S(1)}, f16[40,768]{1,0:T(8,128)(2,1)S(1)}, u32[]{:S(2)}, u32[]{:S(2)}) collective-permute-start(f16[40,768]{1,0:T(8,128)(2,1)S(1)} %get-tuple-element.58), channel_id=1, source_target_pairs={{0,4},{1,5},{2,6},{3,7},{4,0},{5,1},{6,2},{7,3},{8,12},{9,13},{10,... | collective-permute-start | bytes 184328 | tf_op jit(solution)/shard_map/ppermute | solution.py:407
  71.5 7.2 %collective-permute-start.18 = (f16[40,768]{1,0:T(8,128)(2,1)S(1)}, f16[40,768]{1,0:T(8,128)(2,1)S(1)}, u32[]{:S(2)}, u32[]{:S(2)}) collective-permute-start(f16[40,768]{1,0:T(8,128)(2,1)S(1)} %get-tuple-element.56), channel_id=1, source_target_pairs={{0,2},{1,3},{2,0},{3,1},{4,6},{5,7},{6,4},{7,5},{8,10},{9,11},{10,... | collective-permute-start | bytes 184328 | tf_op jit(solution)/shard_map/ppermute | solution.py:407
  80.0 6.8 %collective-permute-start.23 = (f16[40,768]{1,0:T(8,128)(2,1)S(1)}, f16[40,768]{1,0:T(8,128)(2,1)S(1)}, u32[]{:S(2)}, u32[]{:S(2)}) collective-permute-start(f16[40,768]{1,0:T(8,128)(2,1)S(1)} %fusion.11), channel_id=1, source_target_pairs={{0,6},{1,7},{2,4},{3,5},{4,2},{5,3},{6,0},{7,1},{8,14},{9,15},{10,... | collective-permute-start | bytes 184328 | tf_op jit(solution)/shard_map/ppermute | solution.py:407
  83.8 5.5 %collective-permute-start.22 = (f16[40,768]{1,0:T(8,128)(2,1)S(1)}, f16[40,768]{1,0:T(8,128)(2,1)S(1)}, u32[]{:S(2)}, u32[]{:S(2)}) collective-permute-start(f16[40,768]{1,0:T(8,128)(2,1)S(1)} %fusion.11), channel_id=1, source_target_pairs={{0,4},{1,5},{2,6},{3,7},{4,0},{5,1},{6,2},{7,3},{8,12},{9,13},{10,... | collective-permute-start | bytes 184328 | tf_op jit(solution)/shard_map/ppermute | solution.py:407
  83.8 7.3 %collective-permute-start.21 = (f16[40,768]{1,0:T(8,128)(2,1)S(1)}, f16[40,768]{1,0:T(8,128)(2,1)S(1)}, u32[]{:S(2)}, u32[]{:S(2)}) collective-permute-start(f16[40,768]{1,0:T(8,128)(2,1)S(1)} %fusion.11), channel_id=1, source_target_pairs={{0,2},{1,3},{2,0},{3,1},{4,6},{5,7},{6,4},{7,5},{8,10},{9,11},{10,... | collective-permute-start | bytes 184328 | tf_op jit(solution)/shard_map/ppermute | solution.py:407
  86.9 13.9 %collective-permute-start.11 = (f32[8,320]{1,0:T(8,128)S(1)}, f32[8,320]{1,0:T(8,128)S(1)}, u32[]{:S(2)}, u32[]{:S(2)}) collective-permute-start(f32[8,320]{1,0:T(8,128)S(1)} %add.63.refs_0_), channel_id=1, source_target_pairs={{0,2},{1,3},{2,0},{3,1},{4,6},{5,7},{6,4},{7,5},{8,10},{9,11},{10,... | collective-permute-start | bytes 30728 | tf_op jit(solution)/shard_map/ppermute | solution.py:407
  89.3 11.4 %collective-permute-start.12 = (f32[8,320]{1,0:T(8,128)S(1)}, f32[8,320]{1,0:T(8,128)S(1)}, u32[]{:S(2)}, u32[]{:S(2)}) collective-permute-start(f32[8,320]{1,0:T(8,128)S(1)} %add.63.refs_0_), channel_id=1, source_target_pairs={{0,4},{1,5},{2,6},{3,7},{4,0},{5,1},{6,2},{7,3},{8,12},{9,13},{10,... | collective-permute-start | bytes 30728 | tf_op jit(solution)/shard_map/ppermute | solution.py:407
  91.2 9.6 %collective-permute-start.13 = (f32[8,320]{1,0:T(8,128)S(1)}, f32[8,320]{1,0:T(8,128)S(1)}, u32[]{:S(2)}, u32[]{:S(2)}) collective-permute-start(f32[8,320]{1,0:T(8,128)S(1)} %add.63.refs_0_), channel_id=1, source_target_pairs={{0,6},{1,7},{2,4},{3,5},{4,2},{5,3},{6,0},{7,1},{8,14},{9,15},{10,... | collective-permute-start | bytes 30728 | tf_op jit(solution)/shard_map/ppermute | solution.py:407
  91.9 13.8 %collective-permute-start.24 = (f16[4,40,768]{2,1,0:T(8,128)(2,1)S(1)}, f16[4,40,768]{2,1,0:T(8,128)(2,1)S(1)}, u32[]{:S(2)}, u32[]{:S(2)}) collective-permute-start(f16[4,40,768]{2,1,0:T(8,128)(2,1)S(1)} %pad_maximum_fusion), channel_id=1, source_target_pairs={{0,16},{1,9},{2,18},{3,11},{4,20},{5,13},{6,22},{7,15},{8,24},{9,1... | collective-permute-start | bytes 737288 | tf_op jit(solution)/shard_map/ppermute | solution.py:416
  104.3 6.2 %collective-permute-start.27 = (f16[4,40,768]{2,1,0:T(8,128)(2,1)S(1)}, f16[4,40,768]{2,1,0:T(8,128)(2,1)S(1)}, u32[]{:S(2)}, u32[]{:S(2)}) collective-permute-start(f16[4,40,768]{2,1,0:T(8,128)(2,1)S(1)} %pad_maximum_fusion), channel_id=1, source_target_pairs={{0,8},{1,17},{2,10},{3,19},{4,12},{5,21},{6,14},{7,23},{8,0},{9,25... | collective-permute-start | bytes 737288 | tf_op jit(solution)/shard_map/ppermute | solution.py:416
  105.6 5.6 %collective-permute-start.28 = (f16[4,40,768]{2,1,0:T(8,128)(2,1)S(1)}, f16[4,40,768]{2,1,0:T(8,128)(2,1)S(1)}, u32[]{:S(2)}, u32[]{:S(2)}) collective-permute-start(f16[4,40,768]{2,1,0:T(8,128)(2,1)S(1)} %pad_maximum_fusion), channel_id=1, source_target_pairs={{0,1},{1,0},{2,3},{3,2},{4,5},{5,4},{6,7},{7,6},{8,9},{9,8},{10,11... | collective-permute-start | bytes 737288 | tf_op jit(solution)/shard_map/ppermute | solution.py:407
  105.7 7.4 %collective-permute-start.25 = (f16[4,40,768]{2,1,0:T(8,128)(2,1)S(1)}, f16[4,40,768]{2,1,0:T(8,128)(2,1)S(1)}, u32[]{:S(2)}, u32[]{:S(2)}) collective-permute-start(f16[4,40,768]{2,1,0:T(8,128)(2,1)S(1)} %collective-permute-done.24), channel_id=1, source_target_pairs={{0,8},{1,17},{2,10},{3,19},{4,12},{5,21},{6,14},{7,23},{8,0},{9,25... | collective-permute-start | bytes 737288 | tf_op jit(solution)/shard_map/ppermute | solution.py:416
  (19 other events, 177.9 us)

commit v8 on v7

--- a/solution.py
+++ b/solution.py
@@ -21,6 +21,20 @@
 
 def contract(a, b, dims, precision=None):
     return lax.dot_general(a, b, (dims, ((), ())), preferred_element_type=f32, precision=precision)
+
+
+def spot(bits):
+    image, slab = lax.axis_index("dp"), lax.axis_index("space")
+    core = lax.rem(slab, 2)
+
+    def index(which):
+        found = 0
+        for step in range(bits):
+            shift = jnp.where(which == 0, step, bits - 1 - step)
+            found = found * 2 + (lax.shift_right_logical(image, shift) & 1)
+        return found
+
+    return core, index(core), index(1 - core), lax.shift_right_logical(slab, 1)
 
 
 def call(body, outs, args, specs=None, scratch=(), flops=0, moved=0, limit=40 << 20):
@@ -65,7 +79,7 @@
     return total
 
 
-def stats_body(count, step_ref, latent_hbm, cot_hbm, out_ref, latent_ref, cot_ref, sem):
+def stats_body(count, latent_hbm, cot_hbm, out_ref, latent_ref, cot_ref, sem):
     row_count, channels, cols = latent_ref.shape
     loads = []
     for number, (source, target) in enumerate(((latent_hbm, latent_ref), (cot_hbm, cot_ref))):
@@ -91,9 +105,8 @@
         size = jnp.abs(cot_ref[row])
         for start in range(0, cols, LANES):
             top = jnp.maximum(top, size[:, start : start + LANES])
-    step = jnp.full((8, channels), step_ref[0].astype(f32))
     largest = jnp.broadcast_to(jnp.max(top.astype(f32)), (8, channels))
-    out_ref[...] = rows_of(lane_form(mean) * (1.0 / LANES), lane_form(grouped), largest, step)
+    out_ref[...] = rows_of(lane_form(mean) * (1.0 / LANES), lane_form(grouped), largest)
 
 
 def tree_sum(parts):
@@ -109,7 +122,7 @@
     if total:
         squares = lax.rsqrt(squares / total + epsilon)
     largest = functools.reduce(jnp.maximum, [part[2:3] for part in parts])
-    rows = (mean, squares, largest, parts[0][3:4])
+    rows = (mean, squares, largest)
     out_ref[...] = rows_of(*[jnp.broadcast_to(row, out_ref.shape) for row in rows])
 
 
@@ -151,10 +164,9 @@
     wide = cells.astype(f32)
     after, before = shifted_cols(wide)
     order = (after, cells, before) if flip else (before, cells, after)
+    start = place * cols if isinstance(place, int) else pl.multiple_of(place * cols, LANES)
     for tap, piece in enumerate(order):
-        buffer_ref[tap * channels : (tap + 1) * channels, place * cols : (place + 1) * cols] = (
-            piece.astype(bf16)
-        )
+        buffer_ref[tap * channels : (tap + 1) * channels, pl.ds(start, cols)] = piece.astype(bf16)
 
 
 def taps_body(cot_ref, taps_ref, sums_ref):
@@ -168,12 +180,13 @@
 
 
 def middle_body(
-    factor, spread, latent_ref, taps_ref, stats_ref, gain_ref, bias_ref, sums_ref, act_ref, found_ref, table_ref
+    factor, spread, latent_ref, taps_ref, stats_ref, gain_ref, bias_ref, sums_ref, step_ref,
+    act_ref, found_ref, table_ref,
 ):
     row_count, channels, cols = latent_ref.shape
     table_ref[...] = jnp.zeros(table_ref.shape, f32)
     table_ref[0:1, :channels] = sums_ref[0:1]
-    table_ref[0:1, channels : channels + NOTE] = stats_ref[3:4, :NOTE]
+    table_ref[0:1, channels : channels + NOTE] = jnp.broadcast_to(step_ref[...], (1, NOTE))
     gain = jnp.max(jnp.abs(gain_ref[...][None, :]), axis=1, keepdims=True)
     bias = jnp.max(jnp.abs(bias_ref[...][None, :]), axis=1, keepdims=True)
     bound = stats_ref[2:3] * ((spread * gain + bias) * factor)
@@ -185,15 +198,15 @@
 
 
 def weight_body(
-    shape, cols, where_ref, act_ref, taps_ref, above_ref, below_ref, middle_ref,
+    shape, cols, act_ref, taps_ref, outer_ref, inner_ref, middle_ref,
     near_ref, low_ref, high_ref, edge_ref,
 ):
     blocks, zones, height, width = shape
     channels, positions = act_ref.shape
-    core, mine, other, zone_index = [where_ref[i] for i in range(4)]
+    core, mine, other, zone_index = spot((blocks // 2).bit_length() - 1)
     quarter = blocks // 4
-    put_taps(edge_ref, 0, above_ref[...], True)
-    put_taps(edge_ref, 1, below_ref[...], True)
+    put_taps(edge_ref, core, outer_ref[...], True)
+    put_taps(edge_ref, 1 - core, inner_ref[...], True)
     tap_width = zones * width // 3
 
     def store(ref, place, found, block, tap_row):
@@ -247,14 +260,17 @@
 
 
 def conv_body(
-    where_ref, latent_ref, above_ref, below_ref, stats_ref, gain_ref, bias_ref, weight_ref,
+    latent_ref, outer_ref, inner_ref, stats_ref, gain_ref, bias_ref, weight_ref,
     extra_ref, out_ref, taps_ref, flat_ref,
 ):
     row_count, channels, cols = latent_ref.shape
     values = column_values(stats_ref, gain_ref, bias_ref)
-    for place, ref, end in ((0, above_ref, 4), (row_count + 1, below_ref, 5)):
-        keep = where_ref[end].astype(f32)
-        put_taps(taps_ref, place, (activate(ref[...], values).astype(f32) * keep).astype(bf16), False)
+    slab, last = lax.axis_index("space"), lax.axis_size("space") - 1
+    core = lax.rem(slab, 2)
+    keep = jnp.where((slab == 0) | (slab == last), 0.0, 1.0).astype(f32)
+    outer = (activate(outer_ref[...], values).astype(f32) * keep).astype(bf16)
+    put_taps(taps_ref, core * (row_count + 1), outer, False)
+    put_taps(taps_ref, (1 - core) * (row_count + 1), activate(inner_ref[...], values), False)
     for row in range(row_count):
         put_taps(taps_ref, row + 1, activate(latent_ref[row], values), False)
     for tap_row in range(3):
@@ -318,11 +334,11 @@
         out_ref[row] = (cot_ref[row].astype(f32) + change).astype(bf16)
 
 
-def place_body(shape, half_blocks, pieces, where_ref, *refs):
+def place_body(shape, half_blocks, pieces, *refs):
     zones, height, width = shape
     count = len(pieces)
     cells = refs[:count]
-    core, mine, other, zone_index = [where_ref[i] for i in range(4)]
+    core, mine, other, zone_index = spot(half_blocks.bit_length() - 1)
     spots = [
         (1 - core) * half_blocks + (other ^ rest) if crossed else core * half_blocks + (mine ^ rest)
         for crossed, rest in pieces
@@ -365,13 +381,13 @@
 
 
 def spread_body(
-    known, masks, where_ref, mine_ref, other_ref, table_ref, scale_ref, back_ref, steps_ref
+    known, masks, mine_ref, other_ref, table_ref, scale_ref, back_ref, steps_ref
 ):
     channels = steps_ref.shape[1]
     table_ref[...] = mine_ref[...]
     for core in range(2):
 
-        @pl.when(where_ref[0] == core)
+        @pl.when(lax.rem(lax.axis_index("space"), 2) == core)
         def _():
             for row in known[core]:
                 at = row ^ masks[core]
@@ -434,21 +450,15 @@
     total_count = local_count * slab_count
     positions = row_count * col_count
 
-    image_index = lax.axis_index("dp")
     slab_index = lax.axis_index("space")
     core = slab_index % 2
-    zone_index = slab_index // 2
 
     lat = latent.transpose(0, 1, 3, 2)[0]
     cot = cotangent.transpose(0, 1, 3, 2)[0]
     gain, bias = norm_gain, norm_bias
-    smem = pl.BlockSpec(memory_space=pltpu.SMEM)
     vmem = pl.BlockSpec(memory_space=pltpu.VMEM)
     anywhere = pl.BlockSpec(memory_space=pl.ANY)
     small = jax.ShapeDtypeStruct((8, channels), f32)
-
-    down = [(i, i + 1) for i in range(slab_count - 1)]
-    up = [(i + 1, i) for i in range(slab_count - 1)]
 
     flops = 2 * positions * channels * channels * 9
     taps = pltpu.VMEM((3 * channels, (row_count + 2) * col_count), bf16)
@@ -458,8 +468,8 @@
     own = call(
         functools.partial(stats_body, local_count),
         small,
-        (timesteps, lat, cot),
-        specs=(smem, anywhere, anywhere),
+        (lat, cot),
+        specs=(anywhere, anywhere),
         scratch=(slab, slab, pltpu.SemaphoreType.DMA((2, row_count))),
         moved=2 * lat.size * 2,
         flops=positions * channels * 60,
@@ -472,10 +482,17 @@
     parts = [pair]
     for mask in range(1, zones):
         parts.append(swap_space(pair, 2 * mask))
-    above = lax.ppermute(cot[row_count - 1], "space", down)
-    below = lax.ppermute(cot[0], "space", up)
-    lat_above = lax.ppermute(lat[row_count - 1], "space", down)
-    lat_below = lax.ppermute(lat[0], "space", up)
+    far_row = jnp.where(core == 0, 0, row_count - 1)
+    between = [(i, i - 1 if i % 2 == 0 else i + 1) for i in range(1, slab_count - 1)]
+
+    def edges(cells):
+        outward = lax.dynamic_index_in_dim(cells, far_row, 0, keepdims=False)
+        inward = lax.dynamic_index_in_dim(cells, row_count - 1 - far_row, 0, keepdims=False)
+        outer = lax.ppermute(outward, "space", between)
+        return outer, swap_space(inward, 1)
+
+    outer, inner = edges(cot)
+    lat_outer, lat_inner = edges(lat)
     stats = call(
         functools.partial(merge_body, 2 * local_count, total_count),
         small,
@@ -485,17 +502,6 @@
 
     orders = [list(range(bits)), list(range(bits))[::-1]]
 
-    def rest_index(which):
-        index = 0
-        for step in range(bits):
-            shift = jnp.where(which == 0, orders[0][step], orders[1][step])
-            index = index * 2 + ((image_index >> shift) & 1)
-        return index
-
-    mine, other = rest_index(core), rest_index(1 - core)
-    inside = [slab_index > 0, slab_index < slab_count - 1]
-    where = jnp.stack([core, mine, other, zone_index] + [x.astype(core.dtype) for x in inside])
-    where = where.astype(jnp.int32)
     part_shape = jax.ShapeDtypeStruct((blocks // 4, zones, height, width), f32)
     share_shape = jax.ShapeDtypeStruct((blocks // 2, zones, height, width), f32)
     taps_shape = jax.ShapeDtypeStruct((3 * channels, positions), bf16)
@@ -511,7 +517,7 @@
             jax.ShapeDtypeStruct((channels, 3 * channels), f32),
             table_shape,
         ),
-        (lat, grad_taps, stats, gain, bias, col_sums),
+        (lat, grad_taps, stats, gain, bias, col_sums, timesteps.astype(f32).reshape(1, 1)),
         flops=flops // 3,
         moved=8 * lat.size,
         limit=8 << 20,
@@ -524,8 +530,7 @@
             part_shape,
             jax.ShapeDtypeStruct((3 * channels, 2 * col_count), bf16),
         ),
-        (where, act, grad_taps, above, below, middle_rows),
-        specs=(smem,) + (vmem,) * 5,
+        (act, grad_taps, outer, inner, middle_rows),
         flops=flops,
         moved=8 * lat.size,
         limit=12 << 20,
@@ -540,8 +545,7 @@
         table, scale, back, steps = call(
             functools.partial(spread_body, known, masks),
             (table_shape, unit, unit, steps_shape),
-            (where, table, arrived),
-            specs=(smem,) + (vmem,) * 2,
+            (table, arrived),
             limit=4 << 20,
         )
         scales.append((scale[0, 0], back[0, 0]))
@@ -616,21 +620,21 @@
         return pl.pallas_call(
             functools.partial(place_body, (zones, height, width), half_blocks, chosen),
             out_shape=jax.ShapeDtypeStruct((9, channels, channels), f32),
-            in_specs=[smem] + [vmem] * count + [anywhere] * len(before),
+            in_specs=[vmem] * count + [anywhere] * len(before),
             out_specs=anywhere,
             scratch_shapes=[
                 pltpu.VMEM((count, height, zones * width), f32),
                 pltpu.VMEM((count, 9, height, channels), f32),
                 pltpu.SemaphoreType.DMA((count,)),
             ],
-            input_output_aliases={1 + count: 0} if before else {},
+            input_output_aliases={count: 0} if before else {},
             compiler_params=pltpu.CompilerParams(vmem_limit_bytes=12 << 20),
             cost_estimate=pl.CostEstimate(
                 flops=0,
                 bytes_accessed=8 * count * zones * height * width,
                 transcendentals=0,
             ),
-        )(where, *cells, *before)
+        )(*cells, *before)
 
     early = [(side, rest) for side in (False, True) for rest in numbers[:-1]]
     weight_grad = place(early, ())
@@ -652,8 +656,7 @@
     block_out = call(
         conv_body,
         jax.ShapeDtypeStruct((row_count, channels, col_count), bf16),
-        (where, lat, lat_above, lat_below, stats, gain, bias, conv_weight, extra),
-        specs=(smem,) + (vmem,) * 8,
+        (lat, lat_outer, lat_inner, stats, gain, bias, conv_weight, extra),
         scratch=(taps, flat),
         flops=flops,
         moved=8 * lat.size,

time: 121 us -> 109 us (0.901)
  starting transfers between devices: 39.5 us -> 33.8 us
  local copies, waits for them, and re-layouts: 8.27 us -> 4.1 us
  Pallas kernels: 37 us -> 34 us
    ppermute x4 -> x2, starting transfers between devices: 7.24 us -> 1.35 us  [edges(): outer = lax.ppermute(outward, 'space', between)]
    unnamed x24 -> x18, local copies, waits for them, and re-layouts: 6.15 us -> 2.06 us
    pallas_call x14, Pallas kernels: 32.7 us -> 30.8 us  [call(): pl.pallas_call(body, out_shape=tuple(outs) if many else outs, in_specs=li...]
    ppermute x20 -> x22, waiting for transfers between devices: 5.33 us -> 6.5 us  [swap_space(): return lax.ppermute(cells, 'space', [(i, i ^ mask) for i in range(count)])]
    ppermute x20 -> x22, starting transfers between devices: 22.8 us -> 22.7 us  [swap_space(): return lax.ppermute(cells, 'space', [(i, i ^ mask) for i in range(count)])]
  transfers between devices with their start and end apart: 31 -> 31, of which waited for: 9 -> 9; matrix products, arithmetic and copies ran while one was open for 9% -> 10% of each run, Pallas kernels for 26% -> 27%
where the time goes in v8:
time: 109 us
  Pallas kernels  34 us (31%)
  starting transfers between devices  33.8 us (31%)
  waiting for transfers between devices  23.4 us (21%)
  other arithmetic  11.3 us (10%)
  local copies, waits for them, and re-layouts  4.1 us (4%)
  between operations  1.88 us (2%)
    pallas_call x14, Pallas kernels, call(): pl.pallas_call(body, out_shape=tuple(outs) if many else outs, in_specs=li...  30.8 us
    ppermute x22, starting transfers between devices, swap_space(): return lax.ppermute(cells, 'space', [(i, i ^ mask) for i in range(count)])  22.7 us
    ppermute x7, waiting for transfers between devices, swap_image(): return lax.ppermute(cells, ('dp', 'space'), pairs)  16.9 us
    ppermute x7, starting transfers between devices, swap_image(): return lax.ppermute(cells, ('dp', 'space'), pairs)  9.73 us
    ppermute x22, waiting for transfers between devices, swap_space(): return lax.ppermute(cells, 'space', [(i, i ^ mask) for i in range(count)])  6.5 us
    mul x8, other arithmetic, place(): cells.append(piece.astype(f32) * line_back)  5.36 us
    pallas_call x2, Pallas kernels, place(): pl.pallas_call(functools.partial(place_body, (zones, height, width), half...  3.19 us
  transfers between devices with their start and end apart: 31, of which 9 were waited for; matrix products, arithmetic and copies ran while one was open for 10% of the time, Pallas kernels for 27%

profile of v8, /device:TPU:0, one launch (start us, length us, event | category | flops | bytes accessed | tf_op | source)
XLA Modules:
  0.0 108.6 jit_solution(1766526447992887727)
XLA Ops:
  0.7 2.0 %dynamic-slice_bitcast_fusion = (bf16[320,512]{1,0:T(8,128)(2,1)}, bf16[320,512]{1,0:T(8,128)(2,1)}) fusion(bf16[1,4,512,320]{2,3,1,0:T(8,128)(2,1)} %param.15, s32[]{:T(128)S(6)} %select_n.20, s32[]{:T(128)S(6)} %select_n.19), kind=kLoop, calls=%fused_computation.15 | loop fusion | bytes 1310728 | tf_op jit(solution)/shard_map/jit(dynamic_index_in_dim)/squeeze | solution.py:490
  3.3 4.5 %collective-permute-start.9 = (bf16[320,512]{1,0:T(8,128)(2,1)}, bf16[320,512]{1,0:T(8,128)(2,1)S(1)}, u32[]{:S(2)}, u32[]{:S(2)}) collective-permute-start(bf16[320,512]{1,0:T(8,128)(2,1)} %get-tuple-element.52), channel_id=1, source_target_pairs={{0,1},{1,0},{2,3},{3,2},{4,5},{5,4},{6,7},{7,6},{8,9},{9,8},{10,11... | collective-permute-start | bytes 983048 | tf_op jit(solution)/shard_map/ppermute | solution.py:423
  7.8 5.2 %shard_map.111.refs_0_ = f32[8,320]{1,0:T(8,128)} custom-call(bf16[4,320,512]{2,1,0:T(8,128)(2,1)} %bitcast.61, bf16[4,320,512]{2,1,0:T(8,128)(2,1)} %bitcast.58), custom_call_target="tpu_custom_call" | custom-call | flops 39321600 | bytes 2621440 | tf_op jit(solution)/shard_map/pallas_call | solution.py:43
  15.1 1.6 %collective-permute-start.3 = (f32[8,320]{1,0:T(8,128)S(1)}, f32[8,320]{1,0:T(8,128)S(1)}, u32[]{:S(2)}, u32[]{:S(2)}) collective-permute-start(f32[8,320]{1,0:T(8,128)S(1)} %shard_map.112.refs_0_), channel_id=1, source_target_pairs={{0,2},{1,3},{2,0},{3,1},{4,6},{5,7},{6,4},{7,5},{8,10},{9,11},{10,... | collective-permute-start | bytes 30728 | tf_op jit(solution)/shard_map/ppermute | solution.py:423
  17.9 1.7 %collective-permute-start.5 = (f32[8,320]{1,0:T(8,128)S(1)}, f32[8,320]{1,0:T(8,128)S(1)}, u32[]{:S(2)}, u32[]{:S(2)}) collective-permute-start(f32[8,320]{1,0:T(8,128)S(1)} %shard_map.112.refs_0_), channel_id=1, source_target_pairs={{0,6},{1,7},{2,4},{3,5},{4,2},{5,3},{6,0},{7,1},{8,14},{9,15},{10,... | collective-permute-start | bytes 30728 | tf_op jit(solution)/shard_map/ppermute | solution.py:423
  23.4 2.1 %shard_map.115 = (bf16[320,2048]{1,0:T(8,128)(2,1)S(1)}, f32[320,960]{1,0:T(8,128)S(1)}, f32[8,384]{1,0:T(8,128)S(1)}) custom-call(bf16[4,320,512]{2,1,0:T(8,128)(2,1)S(1)} %bitcast.62, bf16[960,2048]{1,0:T(8,128)(2,1)S(1)} %get-tuple-element.28.taps_ref, f32[8,320]{1,0:T(8,128)S(1)} %shard_map.113.stats_ref, f32[320]{0:T(512)S(1)} %copy-done.5, ...), custom_call_target="tpu_custom_call" | custom-call | flops 1258291200 | bytes 5242880 | tf_op jit(solution)/shard_map/pallas_call | solution.py:43
  25.5 4.0 %shard_map.119 = (f32[4,4,40,768]{3,2,1,0:T(8,128)S(1)}, f32[2,4,40,768]{3,2,1,0:T(8,128)S(1)}, f32[2,4,40,768]{3,2,1,0:T(8,128)S(1)}, bf16[960,1024]{1,0:T(8,128)(2,1)S(1)}) custom-call(bf16[320,2048]{1,0:T(8,128)(2,1)S(1)} %get-tuple-element.33.act_ref, bf16[960,2048]{1,0:T(8,128)(2,1)S(1)} %get-tuple-element.28.taps_ref, ...), custom_call_target="tpu_custom_call" | custom-call | flops 3774873600 | bytes 5242880 | tf_op jit(solution)/shard_map/pallas_call | solution.py:43
  32.3 1.6 %collective-permute-start.1 = (bf16[320,512]{1,0:T(8,128)(2,1)S(1)}, bf16[320,512]{1,0:T(8,128)(2,1)S(1)}, u32[]{:S(2)}, u32[]{:S(2)}) collective-permute-start(bf16[320,512]{1,0:T(8,128)(2,1)S(1)} %get-tuple-element.54), channel_id=1, source_target_pairs={{0,1},{1,0},{2,3},{3,2},{4,5},{5,4},{6,7},{7,6},{8,9},{9,8},{10,11... | collective-permute-start | bytes 983048 | tf_op jit(solution)/shard_map/ppermute | solution.py:423
  36.1 2.2 %collective-permute-done.7.other_ref = f32[8,384]{1,0:T(8,128)S(1)} collective-permute-done((f32[8,384]{1,0:T(8,128)S(1)}, f32[8,384]{1,0:T(8,128)S(1)}, u32[]{:S(2)}, u32[]{:S(2)}) %collective-permute-start.7) | collective-permute-done | bytes 12320 | tf_op jit(solution)/shard_map/ppermute | solution.py:432
  41.6 7.0 %collective-permute-done.16 = f16[2,4,40,768]{3,2,1,0:T(8,128)(2,1)S(1)} collective-permute-done((f16[2,4,40,768]{3,2,1,0:T(8,128)(2,1)S(1)}, f16[2,4,40,768]{3,2,1,0:T(8,128)(2,1)S(1)}, u32[]{:S(2)}, u32[]{:S(2)}) %collective-permute-start.16) | collective-permute-done | bytes 491552 | tf_op jit(solution)/shard_map/ppermute | solution.py:432
  50.0 1.6 %collective-permute-start.17 = (f16[1,4,40,768]{3,2,1,0:T(8,128)(2,1)S(1)}, f16[1,4,40,768]{3,2,1,0:T(8,128)(2,1)S(1)}, u32[]{:S(2)}, u32[]{:S(2)}) collective-permute-start(f16[1,4,40,768]{3,2,1,0:T(8,128)(2,1)S(1)} %fusion.1), channel_id=1, source_target_pairs={{0,16},{1,9},{2,18},{3,11},{4,20},{5,13},{6,22},{7,15},{8,24},{9,1... | collective-permute-start | bytes 737288 | tf_op jit(solution)/shard_map/ppermute | solution.py:432
  52.3 4.0 %collective-permute-done.17 = f16[1,4,40,768]{3,2,1,0:T(8,128)(2,1)S(1)} collective-permute-done((f16[1,4,40,768]{3,2,1,0:T(8,128)(2,1)S(1)}, f16[1,4,40,768]{3,2,1,0:T(8,128)(2,1)S(1)}, u32[]{:S(2)}, u32[]{:S(2)}) %collective-permute-start.17) | collective-permute-done | bytes 245792 | tf_op jit(solution)/shard_map/ppermute | solution.py:432
  57.6 1.7 %collective-permute-start.20 = (f16[40,768]{1,0:T(8,128)(2,1)S(1)}, f16[40,768]{1,0:T(8,128)(2,1)S(1)}, u32[]{:S(2)}, u32[]{:S(2)}) collective-permute-start(f16[40,768]{1,0:T(8,128)(2,1)S(1)} %get-tuple-element.57), channel_id=1, source_target_pairs={{0,6},{1,7},{2,4},{3,5},{4,2},{5,3},{6,0},{7,1},{8,14},{9,15},{10,... | collective-permute-start | bytes 184328 | tf_op jit(solution)/shard_map/ppermute | solution.py:423
  62.1 6.4 %shard_map.120 = (f32[4,320,512]{2,1,0:T(8,128)S(1)}, f32[8,320]{1,0:T(8,128)S(1)}) custom-call(bf16[4,320,512]{2,1,0:T(8,128)(2,1)S(1)} %bitcast.63, bf16[960,2048]{1,0:T(8,128)(2,1)S(1)} %get-tuple-element.28.taps_ref, bf16[960,1024]{1,0:T(8,128)(2,1)S(1)} %get-tuple-element.35.edge_ref, f32[8,320]{1,0:T(8,128)S(1)} %shard_map.113.stats_ref, ...), custom_call_target="tpu_custom_call" | custom-call | flops 3774873600 | bytes 5242880 | tf_op jit(solution)/shard_map/pallas_call | solution.py:43
  70.0 1.7 %collective-permute-start.23 = (f16[40,768]{1,0:T(8,128)(2,1)S(1)}, f16[40,768]{1,0:T(8,128)(2,1)S(1)}, u32[]{:S(2)}, u32[]{:S(2)}) collective-permute-start(f16[40,768]{1,0:T(8,128)(2,1)S(1)} %fusion.11), channel_id=1, source_target_pairs={{0,6},{1,7},{2,4},{3,5},{4,2},{5,3},{6,0},{7,1},{8,14},{9,15},{10,... | collective-permute-start | bytes 184328 | tf_op jit(solution)/shard_map/ppermute | solution.py:423
  72.0 2.4 %collective-permute-start.21 = (f16[40,768]{1,0:T(8,128)(2,1)S(1)}, f16[40,768]{1,0:T(8,128)(2,1)S(1)}, u32[]{:S(2)}, u32[]{:S(2)}) collective-permute-start(f16[40,768]{1,0:T(8,128)(2,1)S(1)} %fusion.11), channel_id=1, source_target_pairs={{0,2},{1,3},{2,0},{3,1},{4,6},{5,7},{6,4},{7,5},{8,10},{9,11},{10,... | collective-permute-start | bytes 184328 | tf_op jit(solution)/shard_map/ppermute | solution.py:423
  74.5 2.3 %collective-permute-done.23 = f16[40,768]{1,0:T(8,128)(2,1)S(1)} collective-permute-done((f16[40,768]{1,0:T(8,128)(2,1)S(1)}, f16[40,768]{1,0:T(8,128)(2,1)S(1)}, u32[]{:S(2)}, u32[]{:S(2)}) %collective-permute-start.23) | collective-permute-done | bytes 61472 | tf_op jit(solution)/shard_map/ppermute | solution.py:423
  76.8 2.0 %collective-permute-done.22 = f16[40,768]{1,0:T(8,128)(2,1)S(1)} collective-permute-done((f16[40,768]{1,0:T(8,128)(2,1)S(1)}, f16[40,768]{1,0:T(8,128)(2,1)S(1)}, u32[]{:S(2)}, u32[]{:S(2)}) %collective-permute-start.22) | collective-permute-done | bytes 61472 | tf_op jit(solution)/shard_map/ppermute | solution.py:423
  79.0 2.2 %collective-permute-start.13 = (f32[8,320]{1,0:T(8,128)S(1)}, f32[8,320]{1,0:T(8,128)S(1)}, u32[]{:S(2)}, u32[]{:S(2)}) collective-permute-start(f32[8,320]{1,0:T(8,128)S(1)} %add.63.refs_0_), channel_id=1, source_target_pairs={{0,6},{1,7},{2,4},{3,5},{4,2},{5,3},{6,0},{7,1},{8,14},{9,15},{10,... | collective-permute-start | bytes 30728 | tf_op jit(solution)/shard_map/ppermute | solution.py:423
  81.3 1.6 %collective-permute-start.24 = (f16[4,40,768]{2,1,0:T(8,128)(2,1)S(1)}, f16[4,40,768]{2,1,0:T(8,128)(2,1)S(1)}, u32[]{:S(2)}, u32[]{:S(2)}) collective-permute-start(f16[4,40,768]{2,1,0:T(8,128)(2,1)S(1)} %pad_maximum_fusion), channel_id=1, source_target_pairs={{0,16},{1,9},{2,18},{3,11},{4,20},{5,13},{6,22},{7,15},{8,24},{9,1... | collective-permute-start | bytes 737288 | tf_op jit(solution)/shard_map/ppermute | solution.py:432
  82.9 7.3 %shard_map.118 = bf16[4,320,512]{2,1,0:T(8,128)(2,1)} custom-call(bf16[4,320,512]{2,1,0:T(8,128)(2,1)S(1)} %bitcast.64, bf16[320,512]{1,0:T(8,128)(2,1)S(1)} %collective-permute-done.outer_ref, bf16[320,512]{1,0:T(8,128)(2,1)S(1)} %collective-permute-done.1.inner_ref, f32[8,320]{1,0:T(8,128)S(1)} %shard_map.113.stats_ref, f32[320]{0:T(512)S(1)} %copy-done.5, ...), custom_call_target="tpu_custom_call" | custom-call | flops 3774873600 | bytes 5242880 | tf_op jit(solution)/shard_map/pallas_call | solution.py:43
  91.4 2.3 %shard_map.123 = bf16[4,320,512]{2,1,0:T(8,128)(2,1)} custom-call(f32[4,320,512]{2,1,0:T(8,128)S(1)} %get-tuple-element.36.grad_ref, bf16[4,320,512]{2,1,0:T(8,128)(2,1)S(1)} %bitcast.65, bf16[4,320,512]{2,1,0:T(8,128)(2,1)S(1)} %bitcast.60, f32[8,320]{1,0:T(8,128)S(1)} %shard_map.113.stats_ref, f32[8,320]{1,0:T(8,128)S(1)} %shard_map.122.sums_ref.total_ref), custom_call_target="tpu_custom_call" | custom-call | flops 13107200 | bytes 6553600 | tf_op jit(solution)/shard_map/pallas_call | solution.py:43
  97.4 2.6 %collective-permute-done.27 = f16[4,40,768]{2,1,0:T(8,128)(2,1)S(1)} collective-permute-done((f16[4,40,768]{2,1,0:T(8,128)(2,1)S(1)}, f16[4,40,768]{2,1,0:T(8,128)(2,1)S(1)}, u32[]{:S(2)}, u32[]{:S(2)}) %collective-permute-start.27) | collective-permute-done | bytes 245792 | tf_op jit(solution)/shard_map/ppermute | solution.py:432
  103.9 2.0 %shard_map.124.refs_2_ = f32[9,320,320]{2,1,0:T(8,128)} custom-call(f32[4,40,768]{2,1,0:T(8,128)S(1)} %convert_multiply_fusion.5.refs_0_, f32[4,40,768]{2,1,0:T(8,128)S(1)} %convert_multiply_fusion.4.refs_1_, f32[4,40,768]{2,1,0:T(8,128)S(1)} %convert_multiply_fusion.3.refs_2_, f32[4,40,768]{2,1,0:T(8,128)S(1)} %convert_multiply_fusion.2.refs_3_, ...), custom_call_target="tpu_custom_call" | custom-call | bytes 5898240 | tf_op jit(solution)/shard_map/pallas_call | solution.py:620
  (96 shorter events, 35.0 us)
Async XLA Ops:
  2.7 22.9 %collective-permute-start.8 = (bf16[320,512]{1,0:T(8,128)(2,1)}, bf16[320,512]{1,0:T(8,128)(2,1)S(1)}, u32[]{:S(2)}, u32[]{:S(2)}) collective-permute-start(bf16[320,512]{1,0:T(8,128)(2,1)} %get-tuple-element.53), channel_id=1, source_target_pairs={{1,2},{2,1},{3,4},{4,3},{5,6},{6,5},{9,10},{10,9},{11,12},{12,11},... | collective-permute-start | bytes 983048 | tf_op jit(solution)/shard_map/ppermute | solution.py:491
  3.3 22.2 %collective-permute-start.9 = (bf16[320,512]{1,0:T(8,128)(2,1)}, bf16[320,512]{1,0:T(8,128)(2,1)S(1)}, u32[]{:S(2)}, u32[]{:S(2)}) collective-permute-start(bf16[320,512]{1,0:T(8,128)(2,1)} %get-tuple-element.52), channel_id=1, source_target_pairs={{0,1},{1,0},{2,3},{3,2},{4,5},{5,4},{6,7},{7,6},{8,9},{9,8},{10,11... | collective-permute-start | bytes 983048 | tf_op jit(solution)/shard_map/ppermute | solution.py:423
  15.1 7.5 %collective-permute-start.3 = (f32[8,320]{1,0:T(8,128)S(1)}, f32[8,320]{1,0:T(8,128)S(1)}, u32[]{:S(2)}, u32[]{:S(2)}) collective-permute-start(f32[8,320]{1,0:T(8,128)S(1)} %shard_map.112.refs_0_), channel_id=1, source_target_pairs={{0,2},{1,3},{2,0},{3,1},{4,6},{5,7},{6,4},{7,5},{8,10},{9,11},{10,... | collective-permute-start | bytes 30728 | tf_op jit(solution)/shard_map/ppermute | solution.py:423
  16.8 5.8 %collective-permute-start.4 = (f32[8,320]{1,0:T(8,128)S(1)}, f32[8,320]{1,0:T(8,128)S(1)}, u32[]{:S(2)}, u32[]{:S(2)}) collective-permute-start(f32[8,320]{1,0:T(8,128)S(1)} %shard_map.112.refs_0_), channel_id=1, source_target_pairs={{0,4},{1,5},{2,6},{3,7},{4,0},{5,1},{6,2},{7,3},{8,12},{9,13},{10,... | collective-permute-start | bytes 30728 | tf_op jit(solution)/shard_map/ppermute | solution.py:423
  17.9 5.5 %collective-permute-start.5 = (f32[8,320]{1,0:T(8,128)S(1)}, f32[8,320]{1,0:T(8,128)S(1)}, u32[]{:S(2)}, u32[]{:S(2)}) collective-permute-start(f32[8,320]{1,0:T(8,128)S(1)} %shard_map.112.refs_0_), channel_id=1, source_target_pairs={{0,6},{1,7},{2,4},{3,5},{4,2},{5,3},{6,0},{7,1},{8,14},{9,15},{10,... | collective-permute-start | bytes 30728 | tf_op jit(solution)/shard_map/ppermute | solution.py:423
  29.5 9.4 %collective-permute-start.15 = (f32[2,4,40,768]{3,2,1,0:T(8,128)S(1)}, f32[2,4,40,768]{3,2,1,0:T(8,128)S(1)}, u32[]{:S(2)}, u32[]{:S(2)}) collective-permute-start(f32[2,4,40,768]{3,2,1,0:T(8,128)S(1)} %get-tuple-element.41), channel_id=1, source_target_pairs={{0,1},{1,0},{2,3},{3,2},{4,5},{5,4},{6,7},{7,6},{8,9},{9,8},{10,11... | collective-permute-start | bytes 2949128 | tf_op jit(solution)/shard_map/ppermute | solution.py:423
  29.6 11.9 %collective-permute-start.14 = (f32[2,4,40,768]{3,2,1,0:T(8,128)S(1)}, f32[2,4,40,768]{3,2,1,0:T(8,128)S(1)}, u32[]{:S(2)}, u32[]{:S(2)}) collective-permute-start(f32[2,4,40,768]{3,2,1,0:T(8,128)S(1)} %get-tuple-element.40), channel_id=1, source_target_pairs={{0,1},{1,0},{2,3},{3,2},{4,5},{5,4},{6,7},{7,6},{8,9},{9,8},{10,11... | collective-permute-start | bytes 2949128 | tf_op jit(solution)/shard_map/ppermute | solution.py:423
  31.6 49.7 %collective-permute-start = (bf16[320,512]{1,0:T(8,128)(2,1)S(1)}, bf16[320,512]{1,0:T(8,128)(2,1)S(1)}, u32[]{:S(2)}, u32[]{:S(2)}) collective-permute-start(bf16[320,512]{1,0:T(8,128)(2,1)S(1)} %get-tuple-element.55), channel_id=1, source_target_pairs={{1,2},{2,1},{3,4},{4,3},{5,6},{6,5},{9,10},{10,9},{11,12},{12,11},... | collective-permute-start | bytes 983048 | tf_op jit(solution)/shard_map/ppermute | solution.py:491
  32.3 50.6 %collective-permute-start.1 = (bf16[320,512]{1,0:T(8,128)(2,1)S(1)}, bf16[320,512]{1,0:T(8,128)(2,1)S(1)}, u32[]{:S(2)}, u32[]{:S(2)}) collective-permute-start(bf16[320,512]{1,0:T(8,128)(2,1)S(1)} %get-tuple-element.54), channel_id=1, source_target_pairs={{0,1},{1,0},{2,3},{3,2},{4,5},{5,4},{6,7},{7,6},{8,9},{9,8},{10,11... | collective-permute-start | bytes 983048 | tf_op jit(solution)/shard_map/ppermute | solution.py:423
  39.7 8.9 %collective-permute-start.16 = (f16[2,4,40,768]{3,2,1,0:T(8,128)(2,1)S(1)}, f16[2,4,40,768]{3,2,1,0:T(8,128)(2,1)S(1)}, u32[]{:S(2)}, u32[]{:S(2)}) collective-permute-start(f16[2,4,40,768]{3,2,1,0:T(8,128)(2,1)S(1)} %multiply_convert_fusion), channel_id=1, source_target_pairs={{0,8},{1,17},{2,10},{3,19},{4,12},{5,21},{6,14},{7,23},{8,0},{9,25... | collective-permute-start | bytes 1474568 | tf_op jit(solution)/shard_map/ppermute | solution.py:432
  50.0 6.3 %collective-permute-start.17 = (f16[1,4,40,768]{3,2,1,0:T(8,128)(2,1)S(1)}, f16[1,4,40,768]{3,2,1,0:T(8,128)(2,1)S(1)}, u32[]{:S(2)}, u32[]{:S(2)}) collective-permute-start(f16[1,4,40,768]{3,2,1,0:T(8,128)(2,1)S(1)} %fusion.1), channel_id=1, source_target_pairs={{0,16},{1,9},{2,18},{3,11},{4,20},{5,13},{6,22},{7,15},{8,24},{9,1... | collective-permute-start | bytes 737288 | tf_op jit(solution)/shard_map/ppermute | solution.py:432
  57.6 10.9 %collective-permute-start.20 = (f16[40,768]{1,0:T(8,128)(2,1)S(1)}, f16[40,768]{1,0:T(8,128)(2,1)S(1)}, u32[]{:S(2)}, u32[]{:S(2)}) collective-permute-start(f16[40,768]{1,0:T(8,128)(2,1)S(1)} %get-tuple-element.57), channel_id=1, source_target_pairs={{0,6},{1,7},{2,4},{3,5},{4,2},{5,3},{6,0},{7,1},{8,14},{9,15},{10,... | collective-permute-start | bytes 184328 | tf_op jit(solution)/shard_map/ppermute | solution.py:423
  59.3 9.3 %collective-permute-start.19 = (f16[40,768]{1,0:T(8,128)(2,1)S(1)}, f16[40,768]{1,0:T(8,128)(2,1)S(1)}, u32[]{:S(2)}, u32[]{:S(2)}) collective-permute-start(f16[40,768]{1,0:T(8,128)(2,1)S(1)} %get-tuple-element.58), channel_id=1, source_target_pairs={{0,4},{1,5},{2,6},{3,7},{4,0},{5,1},{6,2},{7,3},{8,12},{9,13},{10,... | collective-permute-start | bytes 184328 | tf_op jit(solution)/shard_map/ppermute | solution.py:423
  60.5 8.1 %collective-permute-start.18 = (f16[40,768]{1,0:T(8,128)(2,1)S(1)}, f16[40,768]{1,0:T(8,128)(2,1)S(1)}, u32[]{:S(2)}, u32[]{:S(2)}) collective-permute-start(f16[40,768]{1,0:T(8,128)(2,1)S(1)} %get-tuple-element.56), channel_id=1, source_target_pairs={{0,2},{1,3},{2,0},{3,1},{4,6},{5,7},{6,4},{7,5},{8,10},{9,11},{10,... | collective-permute-start | bytes 184328 | tf_op jit(solution)/shard_map/ppermute | solution.py:423
  70.0 6.8 %collective-permute-start.23 = (f16[40,768]{1,0:T(8,128)(2,1)S(1)}, f16[40,768]{1,0:T(8,128)(2,1)S(1)}, u32[]{:S(2)}, u32[]{:S(2)}) collective-permute-start(f16[40,768]{1,0:T(8,128)(2,1)S(1)} %fusion.11), channel_id=1, source_target_pairs={{0,6},{1,7},{2,4},{3,5},{4,2},{5,3},{6,0},{7,1},{8,14},{9,15},{10,... | collective-permute-start | bytes 184328 | tf_op jit(solution)/shard_map/ppermute | solution.py:423
  71.7 7.2 %collective-permute-start.22 = (f16[40,768]{1,0:T(8,128)(2,1)S(1)}, f16[40,768]{1,0:T(8,128)(2,1)S(1)}, u32[]{:S(2)}, u32[]{:S(2)}) collective-permute-start(f16[40,768]{1,0:T(8,128)(2,1)S(1)} %fusion.11), channel_id=1, source_target_pairs={{0,4},{1,5},{2,6},{3,7},{4,0},{5,1},{6,2},{7,3},{8,12},{9,13},{10,... | collective-permute-start | bytes 184328 | tf_op jit(solution)/shard_map/ppermute | solution.py:423
  72.0 7.0 %collective-permute-start.21 = (f16[40,768]{1,0:T(8,128)(2,1)S(1)}, f16[40,768]{1,0:T(8,128)(2,1)S(1)}, u32[]{:S(2)}, u32[]{:S(2)}) collective-permute-start(f16[40,768]{1,0:T(8,128)(2,1)S(1)} %fusion.11), channel_id=1, source_target_pairs={{0,2},{1,3},{2,0},{3,1},{4,6},{5,7},{6,4},{7,5},{8,10},{9,11},{10,... | collective-permute-start | bytes 184328 | tf_op jit(solution)/shard_map/ppermute | solution.py:423
  76.8 13.4 %collective-permute-start.11 = (f32[8,320]{1,0:T(8,128)S(1)}, f32[8,320]{1,0:T(8,128)S(1)}, u32[]{:S(2)}, u32[]{:S(2)}) collective-permute-start(f32[8,320]{1,0:T(8,128)S(1)} %add.63.refs_0_), channel_id=1, source_target_pairs={{0,2},{1,3},{2,0},{3,1},{4,6},{5,7},{6,4},{7,5},{8,10},{9,11},{10,... | collective-permute-start | bytes 30728 | tf_op jit(solution)/shard_map/ppermute | solution.py:423
  78.9 11.3 %collective-permute-start.12 = (f32[8,320]{1,0:T(8,128)S(1)}, f32[8,320]{1,0:T(8,128)S(1)}, u32[]{:S(2)}, u32[]{:S(2)}) collective-permute-start(f32[8,320]{1,0:T(8,128)S(1)} %add.63.refs_0_), channel_id=1, source_target_pairs={{0,4},{1,5},{2,6},{3,7},{4,0},{5,1},{6,2},{7,3},{8,12},{9,13},{10,... | collective-permute-start | bytes 30728 | tf_op jit(solution)/shard_map/ppermute | solution.py:423
  79.0 11.2 %collective-permute-start.13 = (f32[8,320]{1,0:T(8,128)S(1)}, f32[8,320]{1,0:T(8,128)S(1)}, u32[]{:S(2)}, u32[]{:S(2)}) collective-permute-start(f32[8,320]{1,0:T(8,128)S(1)} %add.63.refs_0_), channel_id=1, source_target_pairs={{0,6},{1,7},{2,4},{3,5},{4,2},{5,3},{6,0},{7,1},{8,14},{9,15},{10,... | collective-permute-start | bytes 30728 | tf_op jit(solution)/shard_map/ppermute | solution.py:423
  81.3 14.5 %collective-permute-start.24 = (f16[4,40,768]{2,1,0:T(8,128)(2,1)S(1)}, f16[4,40,768]{2,1,0:T(8,128)(2,1)S(1)}, u32[]{:S(2)}, u32[]{:S(2)}) collective-permute-start(f16[4,40,768]{2,1,0:T(8,128)(2,1)S(1)} %pad_maximum_fusion), channel_id=1, source_target_pairs={{0,16},{1,9},{2,18},{3,11},{4,20},{5,13},{6,22},{7,15},{8,24},{9,1... | collective-permute-start | bytes 737288 | tf_op jit(solution)/shard_map/ppermute | solution.py:432
  93.7 6.2 %collective-permute-start.27 = (f16[4,40,768]{2,1,0:T(8,128)(2,1)S(1)}, f16[4,40,768]{2,1,0:T(8,128)(2,1)S(1)}, u32[]{:S(2)}, u32[]{:S(2)}) collective-permute-start(f16[4,40,768]{2,1,0:T(8,128)(2,1)S(1)} %pad_maximum_fusion), channel_id=1, source_target_pairs={{0,8},{1,17},{2,10},{3,19},{4,12},{5,21},{6,14},{7,23},{8,0},{9,25... | collective-permute-start | bytes 737288 | tf_op jit(solution)/shard_map/ppermute | solution.py:432
  95.9 6.6 %collective-permute-start.25 = (f16[4,40,768]{2,1,0:T(8,128)(2,1)S(1)}, f16[4,40,768]{2,1,0:T(8,128)(2,1)S(1)}, u32[]{:S(2)}, u32[]{:S(2)}) collective-permute-start(f16[4,40,768]{2,1,0:T(8,128)(2,1)S(1)} %collective-permute-done.24), channel_id=1, source_target_pairs={{0,8},{1,17},{2,10},{3,19},{4,12},{5,21},{6,14},{7,23},{8,0},{9,25... | collective-permute-start | bytes 737288 | tf_op jit(solution)/shard_map/ppermute | solution.py:432
  97.3 5.3 %collective-permute-start.29 = (f16[4,40,768]{2,1,0:T(8,128)(2,1)S(1)}, f16[4,40,768]{2,1,0:T(8,128)(2,1)S(1)}, u32[]{:S(2)}, u32[]{:S(2)}) collective-permute-start(f16[4,40,768]{2,1,0:T(8,128)(2,1)S(1)} %collective-permute-done.24), channel_id=1, source_target_pairs={{0,1},{1,0},{2,3},{3,2},{4,5},{5,4},{6,7},{7,6},{8,9},{9,8},{10,11... | collective-permute-start | bytes 737288 | tf_op jit(solution)/shard_map/ppermute | solution.py:423
  (16 other events, 142.2 us)

commit v9 on v8

--- a/solution.py
+++ b/solution.py
@@ -14,7 +14,6 @@
 f32 = jnp.float32
 bf16 = jnp.bfloat16
 f16 = jnp.float16
-HIGHEST = lax.Precision.HIGHEST
 LANES = 128
 NOTE = 32
 
@@ -51,17 +50,37 @@
     )(*args)
 
 
-def member_matrix(channels):
+def group_sums(*columns):
+    channels = columns[0].shape[0]
     per_group = channels // GROUPS
     row = lax.broadcasted_iota(jnp.int32, (channels, channels), 0).astype(f32)
     col = lax.broadcasted_iota(jnp.int32, (channels, channels), 1).astype(f32)
     same = jnp.floor((row + 0.5) / per_group) == jnp.floor((col + 0.5) / per_group)
-    return jnp.where(same, 1.0, 0.0).astype(f32)
-
-
-def lane_form(cells):
-    ones = jnp.ones((8, cells.shape[1]), f32)
-    return contract(ones, cells, ((1,), (1,)), HIGHEST)
+    member = jnp.where(same, 1.0, 0.0).astype(bf16)
+    lane = lax.broadcasted_iota(jnp.int32, (channels, LANES), 1)
+    cells = jnp.zeros((channels, LANES), f32)
+    for number, column in enumerate(columns):
+        rest = column
+        for part in range(3):
+            taken = rest.astype(bf16).astype(f32)
+            cells = jnp.where(lane == 3 * number + part, taken, cells)
+            rest = rest - taken
+    found = contract(member, cells.astype(bf16), ((1,), (0,)))
+    pick = [found[:, i : i + 1] for i in range(3 * len(columns))]
+    return [pick[3 * i] + pick[3 * i + 1] + pick[3 * i + 2] for i in range(len(columns))]
+
+
+def as_rows(*columns):
+    channels = columns[0].shape[0]
+    lane = lax.broadcasted_iota(jnp.int32, (channels, LANES), 1)
+    cells = jnp.zeros((channels, LANES), f32)
+    for number, column in enumerate(columns):
+        cells = jnp.where(lane == number, column, cells)
+    return cells.T[:8]
+
+
+def lane_sum(cells):
+    return jnp.sum(cells, axis=1, keepdims=True)
 
 
 def rows_of(*rows):
@@ -87,26 +106,25 @@
             load = pltpu.make_async_copy(source.at[row], target.at[row], sem.at[number, row])
             load.start()
             loads.append(load)
-    member = member_matrix(channels)
     ones = jnp.ones((cols, LANES), bf16)
     sums = jnp.zeros((channels, LANES), f32)
     for row in range(row_count):
         loads[row].wait()
         sums = sums + contract(latent_ref[row], ones, ((1,), (0,)))
-    mean = contract(member, sums, ((1,), (0,)), HIGHEST) / count
+    mean = group_sums(sums[:, :1])[0] / count
     squares = jnp.zeros((channels, LANES), f32)
     for row in range(row_count):
-        centered = latent_ref[row].astype(f32) - mean[:, :1]
+        centered = latent_ref[row].astype(f32) - mean
         squares = squares + fold_lanes(centered * centered)
-    grouped = contract(member, squares, ((1,), (0,)), HIGHEST)
+    grouped = group_sums(lane_sum(squares))[0]
     top = jnp.zeros((channels, LANES), bf16)
     for row in range(row_count):
         loads[row_count + row].wait()
         size = jnp.abs(cot_ref[row])
         for start in range(0, cols, LANES):
             top = jnp.maximum(top, size[:, start : start + LANES])
-    largest = jnp.broadcast_to(jnp.max(top.astype(f32)), (8, channels))
-    out_ref[...] = rows_of(lane_form(mean) * (1.0 / LANES), lane_form(grouped), largest)
+    largest = jnp.max(top.astype(f32), axis=(0, 1), keepdims=True)
+    out_ref[...] = as_rows(mean, grouped, jnp.broadcast_to(largest, mean.shape))
 
 
 def tree_sum(parts):
@@ -260,7 +278,7 @@
 
 
 def conv_body(
-    latent_ref, outer_ref, inner_ref, stats_ref, gain_ref, bias_ref, weight_ref,
+    act_ref, latent_ref, outer_ref, inner_ref, stats_ref, gain_ref, bias_ref, weight_ref,
     extra_ref, out_ref, taps_ref, flat_ref,
 ):
     row_count, channels, cols = latent_ref.shape
@@ -272,7 +290,7 @@
     put_taps(taps_ref, core * (row_count + 1), outer, False)
     put_taps(taps_ref, (1 - core) * (row_count + 1), activate(inner_ref[...], values), False)
     for row in range(row_count):
-        put_taps(taps_ref, row + 1, activate(latent_ref[row], values), False)
+        put_taps(taps_ref, row + 1, act_ref[:, row * cols : (row + 1) * cols], False)
     for tap_row in range(3):
         flat_ref[tap_row] = weight_ref[tap_row].reshape(3 * channels, channels).T
     extra = jnp.broadcast_to(extra_ref[...], (8, channels)).T[:, :1]
@@ -311,10 +329,7 @@
         grad_ref[row] = grad
         first = first + fold_lanes(grad)
         second = second + fold_lanes(grad * normed)
-    member = member_matrix(channels)
-    first = contract(member, first, ((1,), (0,)), HIGHEST)
-    second = contract(member, second, ((1,), (0,)), HIGHEST)
-    sums_ref[...] = rows_of(lane_form(first), lane_form(second))
+    sums_ref[...] = as_rows(*group_sums(lane_sum(first), lane_sum(second)))
 
 
 def latent_body(total, grad_ref, latent_ref, cot_ref, stats_ref, sums_ref, out_ref):
@@ -473,7 +488,7 @@
         scratch=(slab, slab, pltpu.SemaphoreType.DMA((2, row_count))),
         moved=2 * lat.size * 2,
         flops=positions * channels * 60,
-        limit=63 << 20,
+        limit=60 << 20,
     )
     partner = swap_space(own, 1)
     pair = call(
@@ -656,7 +671,7 @@
     block_out = call(
         conv_body,
         jax.ShapeDtypeStruct((row_count, channels, col_count), bf16),
-        (lat, lat_outer, lat_inner, stats, gain, bias, conv_weight, extra),
+        (act, lat, lat_outer, lat_inner, stats, gain, bias, conv_weight, extra),
         scratch=(taps, flat),
         flops=flops,
         moved=8 * lat.size,

time: 109 us -> 106 us (0.972)
  Pallas kernels: 34 us -> 31.9 us
  waiting for transfers between devices: 23.4 us -> 25 us
  local copies, waits for them, and re-layouts: 4.1 us -> 2.75 us
    pallas_call x14, Pallas kernels: 30.8 us -> 28.7 us  [call(): pl.pallas_call(body, out_shape=tuple(outs) if many else outs, in_specs=li...]
    unnamed x18 -> x16, local copies, waits for them, and re-layouts: 2.06 us -> 0.74 us
    ppermute x22, waiting for transfers between devices: 6.5 us -> 7.8 us  [swap_space(): return lax.ppermute(cells, 'space', [(i, i ^ mask) for i in range(count)])]
  transfers between devices with their start and end apart: 31 -> 31, of which waited for: 9 -> 10; matrix products, arithmetic and copies ran while one was open for 10% -> 10% of each run, Pallas kernels for 27% -> 25%
where the time goes in v9:
time: 106 us
  starting transfers between devices  33.8 us (32%)
  Pallas kernels  31.9 us (30%)
  waiting for transfers between devices  25 us (24%)
  other arithmetic  10.4 us (10%)
  local copies, waits for them, and re-layouts  2.75 us (3%)
  between operations  1.88 us (2%)
    pallas_call x14, Pallas kernels, call(): pl.pallas_call(body, out_shape=tuple(outs) if many else outs, in_specs=li...  28.7 us
    ppermute x22, starting transfers between devices, swap_space(): return lax.ppermute(cells, 'space', [(i, i ^ mask) for i in range(count)])  22.7 us
    ppermute x7, waiting for transfers between devices, swap_image(): return lax.ppermute(cells, ('dp', 'space'), pairs)  17.2 us
    ppermute x7, starting transfers between devices, swap_image(): return lax.ppermute(cells, ('dp', 'space'), pairs)  9.73 us
    ppermute x22, waiting for transfers between devices, swap_space(): return lax.ppermute(cells, 'space', [(i, i ^ mask) for i in range(count)])  7.8 us
    mul x8, other arithmetic, place(): cells.append(piece.astype(f32) * line_back)  4.68 us
    pallas_call x2, Pallas kernels, place(): pl.pallas_call(functools.partial(place_body, (zones, height, width), half...  3.19 us
  transfers between devices with their start and end apart: 31, of which 10 were waited for; matrix products, arithmetic and copies ran while one was open for 10% of the time, Pallas kernels for 25%

profile of v9, /device:TPU:0, one launch (start us, length us, event | category | flops | bytes accessed | tf_op | source)
XLA Modules:
  0.0 106.0 jit_solution(7858902926976662286)
XLA Ops:
  0.7 2.0 %dynamic-slice_bitcast_fusion = (bf16[320,512]{1,0:T(8,128)(2,1)S(1)}, bf16[320,512]{1,0:T(8,128)(2,1)}) fusion(bf16[1,4,512,320]{2,3,1,0:T(8,128)(2,1)} %param.15, s32[]{:T(128)S(6)} %select_n.20, s32[]{:T(128)S(6)} %select_n.19), kind=kLoop, calls=%fused_computation.15 | loop fusion | bytes 1310728 | tf_op jit(solution)/shard_map/jit(dynamic_index_in_dim)/squeeze | solution.py:505
  3.3 4.5 %collective-permute-start.9 = (bf16[320,512]{1,0:T(8,128)(2,1)S(1)}, bf16[320,512]{1,0:T(8,128)(2,1)S(1)}, u32[]{:S(2)}, u32[]{:S(2)}) collective-permute-start(bf16[320,512]{1,0:T(8,128)(2,1)S(1)} %get-tuple-element.52), channel_id=1, source_target_pairs={{0,1},{1,0},{2,3},{3,2},{4,5},{5,4},{6,7},{7,6},{8,9},{9,8},{10,11... | collective-permute-start | bytes 983048 | tf_op jit(solution)/shard_map/ppermute | solution.py:438
  7.8 4.4 %shard_map.112.refs_0_ = f32[8,320]{1,0:T(8,128)} custom-call(bf16[4,320,512]{2,1,0:T(8,128)(2,1)} %bitcast.61, bf16[4,320,512]{2,1,0:T(8,128)(2,1)} %bitcast.58), custom_call_target="tpu_custom_call" | custom-call | flops 39321600 | bytes 2621440 | tf_op jit(solution)/shard_map/pallas_call | solution.py:42
  14.3 1.6 %collective-permute-start.1 = (f32[8,320]{1,0:T(8,128)S(1)}, f32[8,320]{1,0:T(8,128)S(1)}, u32[]{:S(2)}, u32[]{:S(2)}) collective-permute-start(f32[8,320]{1,0:T(8,128)S(1)} %shard_map.113.refs_0_), channel_id=1, source_target_pairs={{0,2},{1,3},{2,0},{3,1},{4,6},{5,7},{6,4},{7,5},{8,10},{9,11},{10,... | collective-permute-start | bytes 30728 | tf_op jit(solution)/shard_map/ppermute | solution.py:438
  17.1 1.7 %collective-permute-start.3 = (f32[8,320]{1,0:T(8,128)S(1)}, f32[8,320]{1,0:T(8,128)S(1)}, u32[]{:S(2)}, u32[]{:S(2)}) collective-permute-start(f32[8,320]{1,0:T(8,128)S(1)} %shard_map.113.refs_0_), channel_id=1, source_target_pairs={{0,6},{1,7},{2,4},{3,5},{4,2},{5,3},{6,0},{7,1},{8,14},{9,15},{10,... | collective-permute-start | bytes 30728 | tf_op jit(solution)/shard_map/ppermute | solution.py:438
  20.6 2.0 %collective-permute-done.3.refs_3_ = f32[8,320]{1,0:T(8,128)S(1)} collective-permute-done((f32[8,320]{1,0:T(8,128)S(1)}, f32[8,320]{1,0:T(8,128)S(1)}, u32[]{:S(2)}, u32[]{:S(2)}) %collective-permute-start.3) | collective-permute-done | bytes 10272 | tf_op jit(solution)/shard_map/ppermute | solution.py:438
  22.6 2.1 %shard_map.115 = (bf16[320,2048]{1,0:T(8,128)(2,1)S(1)}, f32[320,960]{1,0:T(8,128)S(1)}, f32[8,384]{1,0:T(8,128)S(1)}) custom-call(bf16[4,320,512]{2,1,0:T(8,128)(2,1)S(1)} %bitcast.62, bf16[960,2048]{1,0:T(8,128)(2,1)S(1)} %get-tuple-element.28.taps_ref, f32[8,320]{1,0:T(8,128)S(1)} %shard_map.114.stats_ref, f32[320]{0:T(512)S(1)} %copy-done.4, ...), custom_call_target="tpu_custom_call" | custom-call | flops 1258291200 | bytes 5242880 | tf_op jit(solution)/shard_map/pallas_call | solution.py:42
  24.7 4.0 %shard_map.119 = (f32[4,4,40,768]{3,2,1,0:T(8,128)S(1)}, f32[2,4,40,768]{3,2,1,0:T(8,128)S(1)}, f32[2,4,40,768]{3,2,1,0:T(8,128)S(1)}, bf16[960,1024]{1,0:T(8,128)(2,1)S(1)}) custom-call(bf16[320,2048]{1,0:T(8,128)(2,1)S(1)} %get-tuple-element.30.act_ref, bf16[960,2048]{1,0:T(8,128)(2,1)S(1)} %get-tuple-element.28.taps_ref, ...), custom_call_target="tpu_custom_call" | custom-call | flops 3774873600 | bytes 5242880 | tf_op jit(solution)/shard_map/pallas_call | solution.py:42
  35.3 2.2 %collective-permute-done.7.other_ref = f32[8,384]{1,0:T(8,128)S(1)} collective-permute-done((f32[8,384]{1,0:T(8,128)S(1)}, f32[8,384]{1,0:T(8,128)S(1)}, u32[]{:S(2)}, u32[]{:S(2)}) %collective-permute-start.7) | collective-permute-done | bytes 12320 | tf_op jit(solution)/shard_map/ppermute | solution.py:447
  40.7 7.0 %collective-permute-done.16 = f16[2,4,40,768]{3,2,1,0:T(8,128)(2,1)S(1)} collective-permute-done((f16[2,4,40,768]{3,2,1,0:T(8,128)(2,1)S(1)}, f16[2,4,40,768]{3,2,1,0:T(8,128)(2,1)S(1)}, u32[]{:S(2)}, u32[]{:S(2)}) %collective-permute-start.16) | collective-permute-done | bytes 491552 | tf_op jit(solution)/shard_map/ppermute | solution.py:447
  51.4 4.0 %collective-permute-done.17 = f16[1,4,40,768]{3,2,1,0:T(8,128)(2,1)S(1)} collective-permute-done((f16[1,4,40,768]{3,2,1,0:T(8,128)(2,1)S(1)}, f16[1,4,40,768]{3,2,1,0:T(8,128)(2,1)S(1)}, u32[]{:S(2)}, u32[]{:S(2)}) %collective-permute-start.17) | collective-permute-done | bytes 245792 | tf_op jit(solution)/shard_map/ppermute | solution.py:447
  56.7 1.7 %collective-permute-start.20 = (f16[40,768]{1,0:T(8,128)(2,1)S(1)}, f16[40,768]{1,0:T(8,128)(2,1)S(1)}, u32[]{:S(2)}, u32[]{:S(2)}) collective-permute-start(f16[40,768]{1,0:T(8,128)(2,1)S(1)} %get-tuple-element.57), channel_id=1, source_target_pairs={{0,6},{1,7},{2,4},{3,5},{4,2},{5,3},{6,0},{7,1},{8,14},{9,15},{10,... | collective-permute-start | bytes 184328 | tf_op jit(solution)/shard_map/ppermute | solution.py:438
  59.4 1.7 %collective-permute-start.18 = (f16[40,768]{1,0:T(8,128)(2,1)S(1)}, f16[40,768]{1,0:T(8,128)(2,1)S(1)}, u32[]{:S(2)}, u32[]{:S(2)}) collective-permute-start(f16[40,768]{1,0:T(8,128)(2,1)S(1)} %get-tuple-element.56), channel_id=1, source_target_pairs={{0,2},{1,3},{2,0},{3,1},{4,6},{5,7},{6,4},{7,5},{8,10},{9,11},{10,... | collective-permute-start | bytes 184328 | tf_op jit(solution)/shard_map/ppermute | solution.py:438
  61.1 5.5 %shard_map.120 = (f32[4,320,512]{2,1,0:T(8,128)S(1)}, f32[8,320]{1,0:T(8,128)S(1)}) custom-call(bf16[4,320,512]{2,1,0:T(8,128)(2,1)S(1)} %bitcast.63, bf16[960,2048]{1,0:T(8,128)(2,1)S(1)} %get-tuple-element.28.taps_ref, bf16[960,1024]{1,0:T(8,128)(2,1)S(1)} %get-tuple-element.35.edge_ref, f32[8,320]{1,0:T(8,128)S(1)} %shard_map.114.stats_ref, ...), custom_call_target="tpu_custom_call" | custom-call | flops 3774873600 | bytes 5242880 | tf_op jit(solution)/shard_map/pallas_call | solution.py:42
  68.1 1.7 %collective-permute-start.23 = (f16[40,768]{1,0:T(8,128)(2,1)S(1)}, f16[40,768]{1,0:T(8,128)(2,1)S(1)}, u32[]{:S(2)}, u32[]{:S(2)}) collective-permute-start(f16[40,768]{1,0:T(8,128)(2,1)S(1)} %fusion.11), channel_id=1, source_target_pairs={{0,6},{1,7},{2,4},{3,5},{4,2},{5,3},{6,0},{7,1},{8,14},{9,15},{10,... | collective-permute-start | bytes 184328 | tf_op jit(solution)/shard_map/ppermute | solution.py:438
  69.9 2.6 %collective-permute-start.21 = (f16[40,768]{1,0:T(8,128)(2,1)S(1)}, f16[40,768]{1,0:T(8,128)(2,1)S(1)}, u32[]{:S(2)}, u32[]{:S(2)}) collective-permute-start(f16[40,768]{1,0:T(8,128)(2,1)S(1)} %fusion.11), channel_id=1, source_target_pairs={{0,2},{1,3},{2,0},{3,1},{4,6},{5,7},{6,4},{7,5},{8,10},{9,11},{10,... | collective-permute-start | bytes 184328 | tf_op jit(solution)/shard_map/ppermute | solution.py:438
  72.6 2.3 %collective-permute-done.23 = f16[40,768]{1,0:T(8,128)(2,1)S(1)} collective-permute-done((f16[40,768]{1,0:T(8,128)(2,1)S(1)}, f16[40,768]{1,0:T(8,128)(2,1)S(1)}, u32[]{:S(2)}, u32[]{:S(2)}) %collective-permute-start.23) | collective-permute-done | bytes 61472 | tf_op jit(solution)/shard_map/ppermute | solution.py:438
  74.9 2.0 %collective-permute-done.22 = f16[40,768]{1,0:T(8,128)(2,1)S(1)} collective-permute-done((f16[40,768]{1,0:T(8,128)(2,1)S(1)}, f16[40,768]{1,0:T(8,128)(2,1)S(1)}, u32[]{:S(2)}, u32[]{:S(2)}) %collective-permute-start.22) | collective-permute-done | bytes 61472 | tf_op jit(solution)/shard_map/ppermute | solution.py:438
  77.1 2.2 %collective-permute-start.13 = (f32[8,320]{1,0:T(8,128)S(1)}, f32[8,320]{1,0:T(8,128)S(1)}, u32[]{:S(2)}, u32[]{:S(2)}) collective-permute-start(f32[8,320]{1,0:T(8,128)S(1)} %add.63.refs_0_), channel_id=1, source_target_pairs={{0,6},{1,7},{2,4},{3,5},{4,2},{5,3},{6,0},{7,1},{8,14},{9,15},{10,... | collective-permute-start | bytes 30728 | tf_op jit(solution)/shard_map/ppermute | solution.py:438
  79.4 1.6 %collective-permute-start.24 = (f16[4,40,768]{2,1,0:T(8,128)(2,1)S(1)}, f16[4,40,768]{2,1,0:T(8,128)(2,1)S(1)}, u32[]{:S(2)}, u32[]{:S(2)}) collective-permute-start(f16[4,40,768]{2,1,0:T(8,128)(2,1)S(1)} %pad_maximum_fusion), channel_id=1, source_target_pairs={{0,16},{1,9},{2,18},{3,11},{4,20},{5,13},{6,22},{7,15},{8,24},{9,1... | collective-permute-start | bytes 737288 | tf_op jit(solution)/shard_map/ppermute | solution.py:447
  81.0 6.7 %shard_map.118 = bf16[4,320,512]{2,1,0:T(8,128)(2,1)} custom-call(bf16[320,2048]{1,0:T(8,128)(2,1)S(1)} %get-tuple-element.30.act_ref, bf16[4,320,512]{2,1,0:T(8,128)(2,1)S(1)} %bitcast.64, bf16[320,512]{1,0:T(8,128)(2,1)S(1)} %collective-permute-done.4.outer_ref, bf16[320,512]{1,0:T(8,128)(2,1)S(1)} %collective-permute-done.5.inner_ref, ...), custom_call_target="tpu_custom_call" | custom-call | flops 3774873600 | bytes 5242880 | tf_op jit(solution)/shard_map/pallas_call | solution.py:42
  88.9 2.5 %shard_map.123 = bf16[4,320,512]{2,1,0:T(8,128)(2,1)} custom-call(f32[4,320,512]{2,1,0:T(8,128)S(1)} %get-tuple-element.36.grad_ref, bf16[4,320,512]{2,1,0:T(8,128)(2,1)S(1)} %bitcast.65, bf16[4,320,512]{2,1,0:T(8,128)(2,1)S(1)} %bitcast.60, f32[8,320]{1,0:T(8,128)S(1)} %shard_map.114.stats_ref, f32[8,320]{1,0:T(8,128)S(1)} %shard_map.122.sums_ref.total_ref), custom_call_target="tpu_custom_call" | custom-call | flops 13107200 | bytes 6553600 | tf_op jit(solution)/shard_map/pallas_call | solution.py:42
  94.9 2.7 %collective-permute-done.27 = f16[4,40,768]{2,1,0:T(8,128)(2,1)S(1)} collective-permute-done((f16[4,40,768]{2,1,0:T(8,128)(2,1)S(1)}, f16[4,40,768]{2,1,0:T(8,128)(2,1)S(1)}, u32[]{:S(2)}, u32[]{:S(2)}) %collective-permute-start.27) | collective-permute-done | bytes 245792 | tf_op jit(solution)/shard_map/ppermute | solution.py:447
  101.4 2.0 %shard_map.124.refs_2_ = f32[9,320,320]{2,1,0:T(8,128)} custom-call(f32[4,40,768]{2,1,0:T(8,128)S(1)} %convert_multiply_fusion.5.refs_0_, f32[4,40,768]{2,1,0:T(8,128)S(1)} %convert_multiply_fusion.4.refs_1_, f32[4,40,768]{2,1,0:T(8,128)S(1)} %convert_multiply_fusion.3.refs_2_, f32[4,40,768]{2,1,0:T(8,128)S(1)} %convert_multiply_fusion.2.refs_3_, ...), custom_call_target="tpu_custom_call" | custom-call | bytes 5898240 | tf_op jit(solution)/shard_map/pallas_call | solution.py:635
  (94 shorter events, 33.6 us)
Async XLA Ops:
  2.6 22.1 %collective-permute-start.8 = (bf16[320,512]{1,0:T(8,128)(2,1)}, bf16[320,512]{1,0:T(8,128)(2,1)S(1)}, u32[]{:S(2)}, u32[]{:S(2)}) collective-permute-start(bf16[320,512]{1,0:T(8,128)(2,1)} %get-tuple-element.53), channel_id=1, source_target_pairs={{1,2},{2,1},{3,4},{4,3},{5,6},{6,5},{9,10},{10,9},{11,12},{12,11},... | collective-permute-start | bytes 983048 | tf_op jit(solution)/shard_map/ppermute | solution.py:506
  3.3 21.4 %collective-permute-start.9 = (bf16[320,512]{1,0:T(8,128)(2,1)S(1)}, bf16[320,512]{1,0:T(8,128)(2,1)S(1)}, u32[]{:S(2)}, u32[]{:S(2)}) collective-permute-start(bf16[320,512]{1,0:T(8,128)(2,1)S(1)} %get-tuple-element.52), channel_id=1, source_target_pairs={{0,1},{1,0},{2,3},{3,2},{4,5},{5,4},{6,7},{7,6},{8,9},{9,8},{10,11... | collective-permute-start | bytes 983048 | tf_op jit(solution)/shard_map/ppermute | solution.py:438
  14.3 6.2 %collective-permute-start.1 = (f32[8,320]{1,0:T(8,128)S(1)}, f32[8,320]{1,0:T(8,128)S(1)}, u32[]{:S(2)}, u32[]{:S(2)}) collective-permute-start(f32[8,320]{1,0:T(8,128)S(1)} %shard_map.113.refs_0_), channel_id=1, source_target_pairs={{0,2},{1,3},{2,0},{3,1},{4,6},{5,7},{6,4},{7,5},{8,10},{9,11},{10,... | collective-permute-start | bytes 30728 | tf_op jit(solution)/shard_map/ppermute | solution.py:438
  17.1 5.5 %collective-permute-start.3 = (f32[8,320]{1,0:T(8,128)S(1)}, f32[8,320]{1,0:T(8,128)S(1)}, u32[]{:S(2)}, u32[]{:S(2)}) collective-permute-start(f32[8,320]{1,0:T(8,128)S(1)} %shard_map.113.refs_0_), channel_id=1, source_target_pairs={{0,6},{1,7},{2,4},{3,5},{4,2},{5,3},{6,0},{7,1},{8,14},{9,15},{10,... | collective-permute-start | bytes 30728 | tf_op jit(solution)/shard_map/ppermute | solution.py:438
  28.7 9.4 %collective-permute-start.15 = (f32[2,4,40,768]{3,2,1,0:T(8,128)S(1)}, f32[2,4,40,768]{3,2,1,0:T(8,128)S(1)}, u32[]{:S(2)}, u32[]{:S(2)}) collective-permute-start(f32[2,4,40,768]{3,2,1,0:T(8,128)S(1)} %get-tuple-element.41), channel_id=1, source_target_pairs={{0,1},{1,0},{2,3},{3,2},{4,5},{5,4},{6,7},{7,6},{8,9},{9,8},{10,11... | collective-permute-start | bytes 2949128 | tf_op jit(solution)/shard_map/ppermute | solution.py:438
  28.8 11.8 %collective-permute-start.14 = (f32[2,4,40,768]{3,2,1,0:T(8,128)S(1)}, f32[2,4,40,768]{3,2,1,0:T(8,128)S(1)}, u32[]{:S(2)}, u32[]{:S(2)}) collective-permute-start(f32[2,4,40,768]{3,2,1,0:T(8,128)S(1)} %get-tuple-element.40), channel_id=1, source_target_pairs={{0,1},{1,0},{2,3},{3,2},{4,5},{5,4},{6,7},{7,6},{8,9},{9,8},{10,11... | collective-permute-start | bytes 2949128 | tf_op jit(solution)/shard_map/ppermute | solution.py:438
  30.8 48.6 %collective-permute-start.4 = (bf16[320,512]{1,0:T(8,128)(2,1)S(1)}, bf16[320,512]{1,0:T(8,128)(2,1)S(1)}, u32[]{:S(2)}, u32[]{:S(2)}) collective-permute-start(bf16[320,512]{1,0:T(8,128)(2,1)S(1)} %get-tuple-element.55), channel_id=1, source_target_pairs={{1,2},{2,1},{3,4},{4,3},{5,6},{6,5},{9,10},{10,9},{11,12},{12,11},... | collective-permute-start | bytes 983048 | tf_op jit(solution)/shard_map/ppermute | solution.py:506
  31.5 49.5 %collective-permute-start.5 = (bf16[320,512]{1,0:T(8,128)(2,1)S(1)}, bf16[320,512]{1,0:T(8,128)(2,1)S(1)}, u32[]{:S(2)}, u32[]{:S(2)}) collective-permute-start(bf16[320,512]{1,0:T(8,128)(2,1)S(1)} %get-tuple-element.54), channel_id=1, source_target_pairs={{0,1},{1,0},{2,3},{3,2},{4,5},{5,4},{6,7},{7,6},{8,9},{9,8},{10,11... | collective-permute-start | bytes 983048 | tf_op jit(solution)/shard_map/ppermute | solution.py:438
  38.8 8.9 %collective-permute-start.16 = (f16[2,4,40,768]{3,2,1,0:T(8,128)(2,1)S(1)}, f16[2,4,40,768]{3,2,1,0:T(8,128)(2,1)S(1)}, u32[]{:S(2)}, u32[]{:S(2)}) collective-permute-start(f16[2,4,40,768]{3,2,1,0:T(8,128)(2,1)S(1)} %multiply_convert_fusion), channel_id=1, source_target_pairs={{0,8},{1,17},{2,10},{3,19},{4,12},{5,21},{6,14},{7,23},{8,0},{9,25... | collective-permute-start | bytes 1474568 | tf_op jit(solution)/shard_map/ppermute | solution.py:447
  49.1 6.3 %collective-permute-start.17 = (f16[1,4,40,768]{3,2,1,0:T(8,128)(2,1)S(1)}, f16[1,4,40,768]{3,2,1,0:T(8,128)(2,1)S(1)}, u32[]{:S(2)}, u32[]{:S(2)}) collective-permute-start(f16[1,4,40,768]{3,2,1,0:T(8,128)(2,1)S(1)} %fusion.1), channel_id=1, source_target_pairs={{0,16},{1,9},{2,18},{3,11},{4,20},{5,13},{6,22},{7,15},{8,24},{9,1... | collective-permute-start | bytes 737288 | tf_op jit(solution)/shard_map/ppermute | solution.py:447
  56.7 10.0 %collective-permute-start.20 = (f16[40,768]{1,0:T(8,128)(2,1)S(1)}, f16[40,768]{1,0:T(8,128)(2,1)S(1)}, u32[]{:S(2)}, u32[]{:S(2)}) collective-permute-start(f16[40,768]{1,0:T(8,128)(2,1)S(1)} %get-tuple-element.57), channel_id=1, source_target_pairs={{0,6},{1,7},{2,4},{3,5},{4,2},{5,3},{6,0},{7,1},{8,14},{9,15},{10,... | collective-permute-start | bytes 184328 | tf_op jit(solution)/shard_map/ppermute | solution.py:438
  58.4 8.4 %collective-permute-start.19 = (f16[40,768]{1,0:T(8,128)(2,1)S(1)}, f16[40,768]{1,0:T(8,128)(2,1)S(1)}, u32[]{:S(2)}, u32[]{:S(2)}) collective-permute-start(f16[40,768]{1,0:T(8,128)(2,1)S(1)} %get-tuple-element.58), channel_id=1, source_target_pairs={{0,4},{1,5},{2,6},{3,7},{4,0},{5,1},{6,2},{7,3},{8,12},{9,13},{10,... | collective-permute-start | bytes 184328 | tf_op jit(solution)/shard_map/ppermute | solution.py:438
  59.4 7.4 %collective-permute-start.18 = (f16[40,768]{1,0:T(8,128)(2,1)S(1)}, f16[40,768]{1,0:T(8,128)(2,1)S(1)}, u32[]{:S(2)}, u32[]{:S(2)}) collective-permute-start(f16[40,768]{1,0:T(8,128)(2,1)S(1)} %get-tuple-element.56), channel_id=1, source_target_pairs={{0,2},{1,3},{2,0},{3,1},{4,6},{5,7},{6,4},{7,5},{8,10},{9,11},{10,... | collective-permute-start | bytes 184328 | tf_op jit(solution)/shard_map/ppermute | solution.py:438
  68.1 6.8 %collective-permute-start.23 = (f16[40,768]{1,0:T(8,128)(2,1)S(1)}, f16[40,768]{1,0:T(8,128)(2,1)S(1)}, u32[]{:S(2)}, u32[]{:S(2)}) collective-permute-start(f16[40,768]{1,0:T(8,128)(2,1)S(1)} %fusion.11), channel_id=1, source_target_pairs={{0,6},{1,7},{2,4},{3,5},{4,2},{5,3},{6,0},{7,1},{8,14},{9,15},{10,... | collective-permute-start | bytes 184328 | tf_op jit(solution)/shard_map/ppermute | solution.py:438
  69.8 7.2 %collective-permute-start.22 = (f16[40,768]{1,0:T(8,128)(2,1)S(1)}, f16[40,768]{1,0:T(8,128)(2,1)S(1)}, u32[]{:S(2)}, u32[]{:S(2)}) collective-permute-start(f16[40,768]{1,0:T(8,128)(2,1)S(1)} %fusion.11), channel_id=1, source_target_pairs={{0,4},{1,5},{2,6},{3,7},{4,0},{5,1},{6,2},{7,3},{8,12},{9,13},{10,... | collective-permute-start | bytes 184328 | tf_op jit(solution)/shard_map/ppermute | solution.py:438
  69.9 7.2 %collective-permute-start.21 = (f16[40,768]{1,0:T(8,128)(2,1)S(1)}, f16[40,768]{1,0:T(8,128)(2,1)S(1)}, u32[]{:S(2)}, u32[]{:S(2)}) collective-permute-start(f16[40,768]{1,0:T(8,128)(2,1)S(1)} %fusion.11), channel_id=1, source_target_pairs={{0,2},{1,3},{2,0},{3,1},{4,6},{5,7},{6,4},{7,5},{8,10},{9,11},{10,... | collective-permute-start | bytes 184328 | tf_op jit(solution)/shard_map/ppermute | solution.py:438
  74.9 12.8 %collective-permute-start.11 = (f32[8,320]{1,0:T(8,128)S(1)}, f32[8,320]{1,0:T(8,128)S(1)}, u32[]{:S(2)}, u32[]{:S(2)}) collective-permute-start(f32[8,320]{1,0:T(8,128)S(1)} %add.63.refs_0_), channel_id=1, source_target_pairs={{0,2},{1,3},{2,0},{3,1},{4,6},{5,7},{6,4},{7,5},{8,10},{9,11},{10,... | collective-permute-start | bytes 30728 | tf_op jit(solution)/shard_map/ppermute | solution.py:438
  77.0 10.8 %collective-permute-start.12 = (f32[8,320]{1,0:T(8,128)S(1)}, f32[8,320]{1,0:T(8,128)S(1)}, u32[]{:S(2)}, u32[]{:S(2)}) collective-permute-start(f32[8,320]{1,0:T(8,128)S(1)} %add.63.refs_0_), channel_id=1, source_target_pairs={{0,4},{1,5},{2,6},{3,7},{4,0},{5,1},{6,2},{7,3},{8,12},{9,13},{10,... | collective-permute-start | bytes 30728 | tf_op jit(solution)/shard_map/ppermute | solution.py:438
  77.1 10.6 %collective-permute-start.13 = (f32[8,320]{1,0:T(8,128)S(1)}, f32[8,320]{1,0:T(8,128)S(1)}, u32[]{:S(2)}, u32[]{:S(2)}) collective-permute-start(f32[8,320]{1,0:T(8,128)S(1)} %add.63.refs_0_), channel_id=1, source_target_pairs={{0,6},{1,7},{2,4},{3,5},{4,2},{5,3},{6,0},{7,1},{8,14},{9,15},{10,... | collective-permute-start | bytes 30728 | tf_op jit(solution)/shard_map/ppermute | solution.py:438
  79.4 14.1 %collective-permute-start.24 = (f16[4,40,768]{2,1,0:T(8,128)(2,1)S(1)}, f16[4,40,768]{2,1,0:T(8,128)(2,1)S(1)}, u32[]{:S(2)}, u32[]{:S(2)}) collective-permute-start(f16[4,40,768]{2,1,0:T(8,128)(2,1)S(1)} %pad_maximum_fusion), channel_id=1, source_target_pairs={{0,16},{1,9},{2,18},{3,11},{4,20},{5,13},{6,22},{7,15},{8,24},{9,1... | collective-permute-start | bytes 737288 | tf_op jit(solution)/shard_map/ppermute | solution.py:447
  91.4 6.2 %collective-permute-start.27 = (f16[4,40,768]{2,1,0:T(8,128)(2,1)S(1)}, f16[4,40,768]{2,1,0:T(8,128)(2,1)S(1)}, u32[]{:S(2)}, u32[]{:S(2)}) collective-permute-start(f16[4,40,768]{2,1,0:T(8,128)(2,1)S(1)} %pad_maximum_fusion), channel_id=1, source_target_pairs={{0,8},{1,17},{2,10},{3,19},{4,12},{5,21},{6,14},{7,23},{8,0},{9,25... | collective-permute-start | bytes 737288 | tf_op jit(solution)/shard_map/ppermute | solution.py:447
  93.4 4.8 %collective-permute-start.28 = (f16[4,40,768]{2,1,0:T(8,128)(2,1)S(1)}, f16[4,40,768]{2,1,0:T(8,128)(2,1)S(1)}, u32[]{:S(2)}, u32[]{:S(2)}) collective-permute-start(f16[4,40,768]{2,1,0:T(8,128)(2,1)S(1)} %pad_maximum_fusion), channel_id=1, source_target_pairs={{0,1},{1,0},{2,3},{3,2},{4,5},{5,4},{6,7},{7,6},{8,9},{9,8},{10,11... | collective-permute-start | bytes 737288 | tf_op jit(solution)/shard_map/ppermute | solution.py:438
  93.5 6.7 %collective-permute-start.25 = (f16[4,40,768]{2,1,0:T(8,128)(2,1)S(1)}, f16[4,40,768]{2,1,0:T(8,128)(2,1)S(1)}, u32[]{:S(2)}, u32[]{:S(2)}) collective-permute-start(f16[4,40,768]{2,1,0:T(8,128)(2,1)S(1)} %collective-permute-done.24), channel_id=1, source_target_pairs={{0,8},{1,17},{2,10},{3,19},{4,12},{5,21},{6,14},{7,23},{8,0},{9,25... | collective-permute-start | bytes 737288 | tf_op jit(solution)/shard_map/ppermute | solution.py:447
  94.8 5.4 %collective-permute-start.29 = (f16[4,40,768]{2,1,0:T(8,128)(2,1)S(1)}, f16[4,40,768]{2,1,0:T(8,128)(2,1)S(1)}, u32[]{:S(2)}, u32[]{:S(2)}) collective-permute-start(f16[4,40,768]{2,1,0:T(8,128)(2,1)S(1)} %collective-permute-done.24), channel_id=1, source_target_pairs={{0,1},{1,0},{2,3},{3,2},{4,5},{5,4},{6,7},{7,6},{8,9},{9,8},{10,11... | collective-permute-start | bytes 737288 | tf_op jit(solution)/shard_map/ppermute | solution.py:438
  (15 other events, 157.9 us)

commit v10 on v9

--- a/solution.py
+++ b/solution.py
@@ -492,7 +492,10 @@
     )
     partner = swap_space(own, 1)
     pair = call(
-        functools.partial(merge_body, local_count, None), small, (own, partner), limit=4 << 20
+        functools.partial(merge_body, local_count, None),
+        small,
+        (jnp.maximum(own, jnp.finfo(f32).min), partner),
+        limit=4 << 20,
     )
     parts = [pair]
     for mask in range(1, zones):

time: 106 us -> 104 us (0.981)
  local copies, waits for them, and re-layouts: 2.75 us -> 0.13 us
  other arithmetic: 10.4 us -> 12.4 us
  waiting for transfers between devices: 25 us -> 23.3 us
    squeeze x2, local copies, waits for them, and re-layouts: 2 us -> 0.09 us  [edges(): lax.dynamic_index_in_dim(cells, row_count - 1 - far_row, 0, keepdims=False)]
    ppermute x22, waiting for transfers between devices: 7.8 us -> 6.7 us  [swap_space(): return lax.ppermute(cells, 'space', [(i, i ^ mask) for i in range(count)])]
  transfers between devices with their start and end apart: 31 -> 31, of which waited for: 10 -> 10; matrix products, arithmetic and copies ran while one was open for 10% -> 12% of each run, Pallas kernels for 25% -> 21%
where the time goes in v10:
time: 104 us
  starting transfers between devices  34 us (33%)
  Pallas kernels  31.8 us (31%)
  waiting for transfers between devices  23.3 us (22%)
  other arithmetic  12.4 us (12%)
  between operations  1.89 us (2%)
    pallas_call x14, Pallas kernels, call(): pl.pallas_call(body, out_shape=tuple(outs) if many else outs, in_specs=li...  28.6 us
    ppermute x22, starting transfers between devices, swap_space(): return lax.ppermute(cells, 'space', [(i, i ^ mask) for i in range(count)])  22.7 us
    ppermute x7, waiting for transfers between devices, swap_image(): return lax.ppermute(cells, ('dp', 'space'), pairs)  16.6 us
    ppermute x7, starting transfers between devices, swap_image(): return lax.ppermute(cells, ('dp', 'space'), pairs)  9.86 us
    ppermute x22, waiting for transfers between devices, swap_space(): return lax.ppermute(cells, 'space', [(i, i ^ mask) for i in range(count)])  6.7 us
    mul x8, other arithmetic, place(): cells.append(piece.astype(f32) * line_back)  5.69 us
    pallas_call x2, Pallas kernels, place(): pl.pallas_call(functools.partial(place_body, (zones, height, width), half...  3.19 us
  transfers between devices with their start and end apart: 31, of which 10 were waited for; matrix products, arithmetic and copies ran while one was open for 12% of the time, Pallas kernels for 21%

profile of v10, /device:TPU:0, one launch (start us, length us, event | category | flops | bytes accessed | tf_op | source)
XLA Modules:
  0.0 103.7 jit_solution(2100552490049581659)
XLA Ops:
  0.7 4.4 %shard_map.112 = f32[8,320]{1,0:T(8,128)} custom-call(bf16[4,320,512]{2,1,0:T(8,128)(2,1)} %bitcast.61, bf16[4,320,512]{2,1,0:T(8,128)(2,1)} %bitcast.58), custom_call_target="tpu_custom_call" | custom-call | flops 39321600 | bytes 2621440 | tf_op jit(solution)/shard_map/pallas_call | solution.py:42
  6.4 4.1 %collective-permute-start.9 = (bf16[320,512]{1,0:T(8,128)(2,1)S(1)}, bf16[320,512]{1,0:T(8,128)(2,1)S(1)}, u32[]{:S(2)}, u32[]{:S(2)}) collective-permute-start(bf16[320,512]{1,0:T(8,128)(2,1)S(1)} %get-tuple-element.52), channel_id=1, source_target_pairs={{0,1},{1,0},{2,3},{3,2},{4,5},{5,4},{6,7},{7,6},{8,9},{9,8},{10,11... | collective-permute-start | bytes 983048 | tf_op jit(solution)/shard_map/ppermute | solution.py:438
  11.3 1.6 %collective-permute-start.1 = (f32[8,320]{1,0:T(8,128)S(1)}, f32[8,320]{1,0:T(8,128)S(1)}, u32[]{:S(2)}, u32[]{:S(2)}) collective-permute-start(f32[8,320]{1,0:T(8,128)S(1)} %shard_map.113.refs_0_), channel_id=1, source_target_pairs={{0,2},{1,3},{2,0},{3,1},{4,6},{5,7},{6,4},{7,5},{8,10},{9,11},{10,... | collective-permute-start | bytes 30728 | tf_op jit(solution)/shard_map/ppermute | solution.py:438
  17.6 2.1 %collective-permute-done.3.refs_3_ = f32[8,320]{1,0:T(8,128)S(1)} collective-permute-done((f32[8,320]{1,0:T(8,128)S(1)}, f32[8,320]{1,0:T(8,128)S(1)}, u32[]{:S(2)}, u32[]{:S(2)}) %collective-permute-start.3) | collective-permute-done | bytes 10272 | tf_op jit(solution)/shard_map/ppermute | solution.py:438
  19.7 2.0 %shard_map.115 = (bf16[320,2048]{1,0:T(8,128)(2,1)S(1)}, f32[320,960]{1,0:T(8,128)S(1)}, f32[8,384]{1,0:T(8,128)S(1)}) custom-call(bf16[4,320,512]{2,1,0:T(8,128)(2,1)S(1)} %bitcast.62, bf16[960,2048]{1,0:T(8,128)(2,1)S(1)} %get-tuple-element.28.taps_ref, f32[8,320]{1,0:T(8,128)S(1)} %shard_map.114.stats_ref, f32[320]{0:T(512)S(1)} %copy-done.3, ...), custom_call_target="tpu_custom_call" | custom-call | flops 1258291200 | bytes 5242880 | tf_op jit(solution)/shard_map/pallas_call | solution.py:42
  21.8 4.0 %shard_map.119 = (f32[4,4,40,768]{3,2,1,0:T(8,128)S(1)}, f32[2,4,40,768]{3,2,1,0:T(8,128)S(1)}, f32[2,4,40,768]{3,2,1,0:T(8,128)S(1)}, bf16[960,1024]{1,0:T(8,128)(2,1)S(1)}) custom-call(bf16[320,2048]{1,0:T(8,128)(2,1)S(1)} %get-tuple-element.30.act_ref, bf16[960,2048]{1,0:T(8,128)(2,1)S(1)} %get-tuple-element.28.taps_ref, ...), custom_call_target="tpu_custom_call" | custom-call | flops 3774873600 | bytes 5242880 | tf_op jit(solution)/shard_map/pallas_call | solution.py:42
  32.3 2.2 %collective-permute-done.7.other_ref = f32[8,384]{1,0:T(8,128)S(1)} collective-permute-done((f32[8,384]{1,0:T(8,128)S(1)}, f32[8,384]{1,0:T(8,128)S(1)}, u32[]{:S(2)}, u32[]{:S(2)}) %collective-permute-start.7) | collective-permute-done | bytes 12320 | tf_op jit(solution)/shard_map/ppermute | solution.py:447
  35.9 1.6 %collective-permute-start.16 = (f16[2,4,40,768]{3,2,1,0:T(8,128)(2,1)S(1)}, f16[2,4,40,768]{3,2,1,0:T(8,128)(2,1)S(1)}, u32[]{:S(2)}, u32[]{:S(2)}) collective-permute-start(f16[2,4,40,768]{3,2,1,0:T(8,128)(2,1)S(1)} %multiply_convert_fusion), channel_id=1, source_target_pairs={{0,8},{1,17},{2,10},{3,19},{4,12},{5,21},{6,14},{7,23},{8,0},{9,25... | collective-permute-start | bytes 1474568 | tf_op jit(solution)/shard_map/ppermute | solution.py:447
  37.9 6.9 %collective-permute-done.16 = f16[2,4,40,768]{3,2,1,0:T(8,128)(2,1)S(1)} collective-permute-done((f16[2,4,40,768]{3,2,1,0:T(8,128)(2,1)S(1)}, f16[2,4,40,768]{3,2,1,0:T(8,128)(2,1)S(1)}, u32[]{:S(2)}, u32[]{:S(2)}) %collective-permute-start.16) | collective-permute-done | bytes 491552 | tf_op jit(solution)/shard_map/ppermute | solution.py:447
  46.2 1.6 %collective-permute-start.17 = (f16[1,4,40,768]{3,2,1,0:T(8,128)(2,1)S(1)}, f16[1,4,40,768]{3,2,1,0:T(8,128)(2,1)S(1)}, u32[]{:S(2)}, u32[]{:S(2)}) collective-permute-start(f16[1,4,40,768]{3,2,1,0:T(8,128)(2,1)S(1)} %fusion.1), channel_id=1, source_target_pairs={{0,16},{1,9},{2,18},{3,11},{4,20},{5,13},{6,22},{7,15},{8,24},{9,1... | collective-permute-start | bytes 737288 | tf_op jit(solution)/shard_map/ppermute | solution.py:447
  48.5 4.0 %collective-permute-done.17 = f16[1,4,40,768]{3,2,1,0:T(8,128)(2,1)S(1)} collective-permute-done((f16[1,4,40,768]{3,2,1,0:T(8,128)(2,1)S(1)}, f16[1,4,40,768]{3,2,1,0:T(8,128)(2,1)S(1)}, u32[]{:S(2)}, u32[]{:S(2)}) %collective-permute-start.17) | collective-permute-done | bytes 245792 | tf_op jit(solution)/shard_map/ppermute | solution.py:447
  53.8 1.6 %collective-permute-start.20 = (f16[40,768]{1,0:T(8,128)(2,1)S(1)}, f16[40,768]{1,0:T(8,128)(2,1)S(1)}, u32[]{:S(2)}, u32[]{:S(2)}) collective-permute-start(f16[40,768]{1,0:T(8,128)(2,1)S(1)} %get-tuple-element.57), channel_id=1, source_target_pairs={{0,6},{1,7},{2,4},{3,5},{4,2},{5,3},{6,0},{7,1},{8,14},{9,15},{10,... | collective-permute-start | bytes 184328 | tf_op jit(solution)/shard_map/ppermute | solution.py:438
  56.7 1.6 %collective-permute-start.18 = (f16[40,768]{1,0:T(8,128)(2,1)S(1)}, f16[40,768]{1,0:T(8,128)(2,1)S(1)}, u32[]{:S(2)}, u32[]{:S(2)}) collective-permute-start(f16[40,768]{1,0:T(8,128)(2,1)S(1)} %get-tuple-element.56), channel_id=1, source_target_pairs={{0,2},{1,3},{2,0},{3,1},{4,6},{5,7},{6,4},{7,5},{8,10},{9,11},{10,... | collective-permute-start | bytes 184328 | tf_op jit(solution)/shard_map/ppermute | solution.py:438
  58.3 5.4 %shard_map.120 = (f32[4,320,512]{2,1,0:T(8,128)S(1)}, f32[8,320]{1,0:T(8,128)S(1)}) custom-call(bf16[4,320,512]{2,1,0:T(8,128)(2,1)S(1)} %bitcast.63, bf16[960,2048]{1,0:T(8,128)(2,1)S(1)} %get-tuple-element.28.taps_ref, bf16[960,1024]{1,0:T(8,128)(2,1)S(1)} %get-tuple-element.35.edge_ref, f32[8,320]{1,0:T(8,128)S(1)} %shard_map.114.stats_ref, ...), custom_call_target="tpu_custom_call" | custom-call | flops 3774873600 | bytes 5242880 | tf_op jit(solution)/shard_map/pallas_call | solution.py:42
  65.3 1.6 %collective-permute-start.23 = (f16[40,768]{1,0:T(8,128)(2,1)S(1)}, f16[40,768]{1,0:T(8,128)(2,1)S(1)}, u32[]{:S(2)}, u32[]{:S(2)}) collective-permute-start(f16[40,768]{1,0:T(8,128)(2,1)S(1)} %fusion.11), channel_id=1, source_target_pairs={{0,6},{1,7},{2,4},{3,5},{4,2},{5,3},{6,0},{7,1},{8,14},{9,15},{10,... | collective-permute-start | bytes 184328 | tf_op jit(solution)/shard_map/ppermute | solution.py:438
  67.2 2.5 %collective-permute-start.21 = (f16[40,768]{1,0:T(8,128)(2,1)S(1)}, f16[40,768]{1,0:T(8,128)(2,1)S(1)}, u32[]{:S(2)}, u32[]{:S(2)}) collective-permute-start(f16[40,768]{1,0:T(8,128)(2,1)S(1)} %fusion.11), channel_id=1, source_target_pairs={{0,2},{1,3},{2,0},{3,1},{4,6},{5,7},{6,4},{7,5},{8,10},{9,11},{10,... | collective-permute-start | bytes 184328 | tf_op jit(solution)/shard_map/ppermute | solution.py:438
  69.8 2.3 %collective-permute-done.23 = f16[40,768]{1,0:T(8,128)(2,1)S(1)} collective-permute-done((f16[40,768]{1,0:T(8,128)(2,1)S(1)}, f16[40,768]{1,0:T(8,128)(2,1)S(1)}, u32[]{:S(2)}, u32[]{:S(2)}) %collective-permute-start.23) | collective-permute-done | bytes 61472 | tf_op jit(solution)/shard_map/ppermute | solution.py:438
  72.1 2.0 %collective-permute-done.22 = f16[40,768]{1,0:T(8,128)(2,1)S(1)} collective-permute-done((f16[40,768]{1,0:T(8,128)(2,1)S(1)}, f16[40,768]{1,0:T(8,128)(2,1)S(1)}, u32[]{:S(2)}, u32[]{:S(2)}) %collective-permute-start.22) | collective-permute-done | bytes 61472 | tf_op jit(solution)/shard_map/ppermute | solution.py:438
  74.2 2.3 %collective-permute-start.13 = (f32[8,320]{1,0:T(8,128)S(1)}, f32[8,320]{1,0:T(8,128)S(1)}, u32[]{:S(2)}, u32[]{:S(2)}) collective-permute-start(f32[8,320]{1,0:T(8,128)S(1)} %add.63.refs_0_), channel_id=1, source_target_pairs={{0,6},{1,7},{2,4},{3,5},{4,2},{5,3},{6,0},{7,1},{8,14},{9,15},{10,... | collective-permute-start | bytes 30728 | tf_op jit(solution)/shard_map/ppermute | solution.py:438
  76.6 1.6 %collective-permute-start.24 = (f16[4,40,768]{2,1,0:T(8,128)(2,1)S(1)}, f16[4,40,768]{2,1,0:T(8,128)(2,1)S(1)}, u32[]{:S(2)}, u32[]{:S(2)}) collective-permute-start(f16[4,40,768]{2,1,0:T(8,128)(2,1)S(1)} %pad_maximum_fusion), channel_id=1, source_target_pairs={{0,16},{1,9},{2,18},{3,11},{4,20},{5,13},{6,22},{7,15},{8,24},{9,1... | collective-permute-start | bytes 737288 | tf_op jit(solution)/shard_map/ppermute | solution.py:447
  78.2 6.7 %shard_map.118 = bf16[4,320,512]{2,1,0:T(8,128)(2,1)} custom-call(bf16[320,2048]{1,0:T(8,128)(2,1)S(1)} %get-tuple-element.30.act_ref, bf16[4,320,512]{2,1,0:T(8,128)(2,1)S(1)} %bitcast.64, bf16[320,512]{1,0:T(8,128)(2,1)S(1)} %collective-permute-done.4.outer_ref, bf16[320,512]{1,0:T(8,128)(2,1)S(1)} %collective-permute-done.5.inner_ref, ...), custom_call_target="tpu_custom_call" | custom-call | flops 3774873600 | bytes 5242880 | tf_op jit(solution)/shard_map/pallas_call | solution.py:42
  86.1 2.5 %shard_map.123 = bf16[4,320,512]{2,1,0:T(8,128)(2,1)} custom-call(f32[4,320,512]{2,1,0:T(8,128)S(1)} %get-tuple-element.36.grad_ref, bf16[4,320,512]{2,1,0:T(8,128)(2,1)S(1)} %bitcast.65, bf16[4,320,512]{2,1,0:T(8,128)(2,1)S(1)} %bitcast.60, f32[8,320]{1,0:T(8,128)S(1)} %shard_map.114.stats_ref, f32[8,320]{1,0:T(8,128)S(1)} %shard_map.122.sums_ref.total_ref), custom_call_target="tpu_custom_call" | custom-call | flops 13107200 | bytes 6553600 | tf_op jit(solution)/shard_map/pallas_call | solution.py:42
  92.4 2.4 %collective-permute-done.27 = f16[4,40,768]{2,1,0:T(8,128)(2,1)S(1)} collective-permute-done((f16[4,40,768]{2,1,0:T(8,128)(2,1)S(1)}, f16[4,40,768]{2,1,0:T(8,128)(2,1)S(1)}, u32[]{:S(2)}, u32[]{:S(2)}) %collective-permute-start.27) | collective-permute-done | bytes 245792 | tf_op jit(solution)/shard_map/ppermute | solution.py:447
  98.9 2.0 %shard_map.124.refs_2_ = f32[9,320,320]{2,1,0:T(8,128)} custom-call(f32[4,40,768]{2,1,0:T(8,128)S(1)} %convert_multiply_fusion.5.refs_0_, f32[4,40,768]{2,1,0:T(8,128)S(1)} %convert_multiply_fusion.4.refs_1_, f32[4,40,768]{2,1,0:T(8,128)S(1)} %convert_multiply_fusion.3.refs_2_, f32[4,40,768]{2,1,0:T(8,128)S(1)} %convert_multiply_fusion.2.refs_3_, ...), custom_call_target="tpu_custom_call" | custom-call | bytes 5898240 | tf_op jit(solution)/shard_map/pallas_call | solution.py:638
  (93 shorter events, 32.9 us)
Async XLA Ops:
  5.1 6.2 %collective-permute-start = (f32[8,320]{1,0:T(8,128)}, f32[8,320]{1,0:T(8,128)S(1)}, u32[]{:S(2)}, u32[]{:S(2)}) collective-permute-start(f32[8,320]{1,0:T(8,128)} %shard_map.112), channel_id=1, source_target_pairs={{0,1},{1,0},{2,3},{3,2},{4,5},{5,4},{6,7},{7,6},{8,9},{9,8},{10,11... | collective-permute-start | bytes 30728 | tf_op jit(solution)/shard_map/ppermute | solution.py:438
  5.7 16.1 %collective-permute-start.8 = (bf16[320,512]{1,0:T(8,128)(2,1)S(1)}, bf16[320,512]{1,0:T(8,128)(2,1)S(1)}, u32[]{:S(2)}, u32[]{:S(2)}) collective-permute-start(bf16[320,512]{1,0:T(8,128)(2,1)S(1)} %get-tuple-element.53), channel_id=1, source_target_pairs={{1,2},{2,1},{3,4},{4,3},{5,6},{6,5},{9,10},{10,9},{11,12},{12,11},... | collective-permute-start | bytes 983048 | tf_op jit(solution)/shard_map/ppermute | solution.py:509
  6.4 15.4 %collective-permute-start.9 = (bf16[320,512]{1,0:T(8,128)(2,1)S(1)}, bf16[320,512]{1,0:T(8,128)(2,1)S(1)}, u32[]{:S(2)}, u32[]{:S(2)}) collective-permute-start(bf16[320,512]{1,0:T(8,128)(2,1)S(1)} %get-tuple-element.52), channel_id=1, source_target_pairs={{0,1},{1,0},{2,3},{3,2},{4,5},{5,4},{6,7},{7,6},{8,9},{9,8},{10,11... | collective-permute-start | bytes 983048 | tf_op jit(solution)/shard_map/ppermute | solution.py:438
  11.3 6.1 %collective-permute-start.1 = (f32[8,320]{1,0:T(8,128)S(1)}, f32[8,320]{1,0:T(8,128)S(1)}, u32[]{:S(2)}, u32[]{:S(2)}) collective-permute-start(f32[8,320]{1,0:T(8,128)S(1)} %shard_map.113.refs_0_), channel_id=1, source_target_pairs={{0,2},{1,3},{2,0},{3,1},{4,6},{5,7},{6,4},{7,5},{8,10},{9,11},{10,... | collective-permute-start | bytes 30728 | tf_op jit(solution)/shard_map/ppermute | solution.py:438
  14.2 5.5 %collective-permute-start.3 = (f32[8,320]{1,0:T(8,128)S(1)}, f32[8,320]{1,0:T(8,128)S(1)}, u32[]{:S(2)}, u32[]{:S(2)}) collective-permute-start(f32[8,320]{1,0:T(8,128)S(1)} %shard_map.113.refs_0_), channel_id=1, source_target_pairs={{0,6},{1,7},{2,4},{3,5},{4,2},{5,3},{6,0},{7,1},{8,14},{9,15},{10,... | collective-permute-start | bytes 30728 | tf_op jit(solution)/shard_map/ppermute | solution.py:438
  25.8 9.3 %collective-permute-start.15 = (f32[2,4,40,768]{3,2,1,0:T(8,128)S(1)}, f32[2,4,40,768]{3,2,1,0:T(8,128)S(1)}, u32[]{:S(2)}, u32[]{:S(2)}) collective-permute-start(f32[2,4,40,768]{3,2,1,0:T(8,128)S(1)} %get-tuple-element.41), channel_id=1, source_target_pairs={{0,1},{1,0},{2,3},{3,2},{4,5},{5,4},{6,7},{7,6},{8,9},{9,8},{10,11... | collective-permute-start | bytes 2949128 | tf_op jit(solution)/shard_map/ppermute | solution.py:438
  25.8 11.9 %collective-permute-start.14 = (f32[2,4,40,768]{3,2,1,0:T(8,128)S(1)}, f32[2,4,40,768]{3,2,1,0:T(8,128)S(1)}, u32[]{:S(2)}, u32[]{:S(2)}) collective-permute-start(f32[2,4,40,768]{3,2,1,0:T(8,128)S(1)} %get-tuple-element.40), channel_id=1, source_target_pairs={{0,1},{1,0},{2,3},{3,2},{4,5},{5,4},{6,7},{7,6},{8,9},{9,8},{10,11... | collective-permute-start | bytes 2949128 | tf_op jit(solution)/shard_map/ppermute | solution.py:438
  27.9 48.7 %collective-permute-start.4 = (bf16[320,512]{1,0:T(8,128)(2,1)S(1)}, bf16[320,512]{1,0:T(8,128)(2,1)S(1)}, u32[]{:S(2)}, u32[]{:S(2)}) collective-permute-start(bf16[320,512]{1,0:T(8,128)(2,1)S(1)} %get-tuple-element.55), channel_id=1, source_target_pairs={{1,2},{2,1},{3,4},{4,3},{5,6},{6,5},{9,10},{10,9},{11,12},{12,11},... | collective-permute-start | bytes 983048 | tf_op jit(solution)/shard_map/ppermute | solution.py:509
  28.6 49.6 %collective-permute-start.5 = (bf16[320,512]{1,0:T(8,128)(2,1)S(1)}, bf16[320,512]{1,0:T(8,128)(2,1)S(1)}, u32[]{:S(2)}, u32[]{:S(2)}) collective-permute-start(bf16[320,512]{1,0:T(8,128)(2,1)S(1)} %get-tuple-element.54), channel_id=1, source_target_pairs={{0,1},{1,0},{2,3},{3,2},{4,5},{5,4},{6,7},{7,6},{8,9},{9,8},{10,11... | collective-permute-start | bytes 983048 | tf_op jit(solution)/shard_map/ppermute | solution.py:438
  35.9 8.9 %collective-permute-start.16 = (f16[2,4,40,768]{3,2,1,0:T(8,128)(2,1)S(1)}, f16[2,4,40,768]{3,2,1,0:T(8,128)(2,1)S(1)}, u32[]{:S(2)}, u32[]{:S(2)}) collective-permute-start(f16[2,4,40,768]{3,2,1,0:T(8,128)(2,1)S(1)} %multiply_convert_fusion), channel_id=1, source_target_pairs={{0,8},{1,17},{2,10},{3,19},{4,12},{5,21},{6,14},{7,23},{8,0},{9,25... | collective-permute-start | bytes 1474568 | tf_op jit(solution)/shard_map/ppermute | solution.py:447
  46.2 6.3 %collective-permute-start.17 = (f16[1,4,40,768]{3,2,1,0:T(8,128)(2,1)S(1)}, f16[1,4,40,768]{3,2,1,0:T(8,128)(2,1)S(1)}, u32[]{:S(2)}, u32[]{:S(2)}) collective-permute-start(f16[1,4,40,768]{3,2,1,0:T(8,128)(2,1)S(1)} %fusion.1), channel_id=1, source_target_pairs={{0,16},{1,9},{2,18},{3,11},{4,20},{5,13},{6,22},{7,15},{8,24},{9,1... | collective-permute-start | bytes 737288 | tf_op jit(solution)/shard_map/ppermute | solution.py:447
  53.8 9.9 %collective-permute-start.20 = (f16[40,768]{1,0:T(8,128)(2,1)S(1)}, f16[40,768]{1,0:T(8,128)(2,1)S(1)}, u32[]{:S(2)}, u32[]{:S(2)}) collective-permute-start(f16[40,768]{1,0:T(8,128)(2,1)S(1)} %get-tuple-element.57), channel_id=1, source_target_pairs={{0,6},{1,7},{2,4},{3,5},{4,2},{5,3},{6,0},{7,1},{8,14},{9,15},{10,... | collective-permute-start | bytes 184328 | tf_op jit(solution)/shard_map/ppermute | solution.py:438
  55.4 8.4 %collective-permute-start.19 = (f16[40,768]{1,0:T(8,128)(2,1)S(1)}, f16[40,768]{1,0:T(8,128)(2,1)S(1)}, u32[]{:S(2)}, u32[]{:S(2)}) collective-permute-start(f16[40,768]{1,0:T(8,128)(2,1)S(1)} %get-tuple-element.58), channel_id=1, source_target_pairs={{0,4},{1,5},{2,6},{3,7},{4,0},{5,1},{6,2},{7,3},{8,12},{9,13},{10,... | collective-permute-start | bytes 184328 | tf_op jit(solution)/shard_map/ppermute | solution.py:438
  56.7 7.2 %collective-permute-start.18 = (f16[40,768]{1,0:T(8,128)(2,1)S(1)}, f16[40,768]{1,0:T(8,128)(2,1)S(1)}, u32[]{:S(2)}, u32[]{:S(2)}) collective-permute-start(f16[40,768]{1,0:T(8,128)(2,1)S(1)} %get-tuple-element.56), channel_id=1, source_target_pairs={{0,2},{1,3},{2,0},{3,1},{4,6},{5,7},{6,4},{7,5},{8,10},{9,11},{10,... | collective-permute-start | bytes 184328 | tf_op jit(solution)/shard_map/ppermute | solution.py:438
  65.3 6.8 %collective-permute-start.23 = (f16[40,768]{1,0:T(8,128)(2,1)S(1)}, f16[40,768]{1,0:T(8,128)(2,1)S(1)}, u32[]{:S(2)}, u32[]{:S(2)}) collective-permute-start(f16[40,768]{1,0:T(8,128)(2,1)S(1)} %fusion.11), channel_id=1, source_target_pairs={{0,6},{1,7},{2,4},{3,5},{4,2},{5,3},{6,0},{7,1},{8,14},{9,15},{10,... | collective-permute-start | bytes 184328 | tf_op jit(solution)/shard_map/ppermute | solution.py:438
  66.8 7.3 %collective-permute-start.22 = (f16[40,768]{1,0:T(8,128)(2,1)S(1)}, f16[40,768]{1,0:T(8,128)(2,1)S(1)}, u32[]{:S(2)}, u32[]{:S(2)}) collective-permute-start(f16[40,768]{1,0:T(8,128)(2,1)S(1)} %fusion.11), channel_id=1, source_target_pairs={{0,4},{1,5},{2,6},{3,7},{4,0},{5,1},{6,2},{7,3},{8,12},{9,13},{10,... | collective-permute-start | bytes 184328 | tf_op jit(solution)/shard_map/ppermute | solution.py:438
  67.2 7.0 %collective-permute-start.21 = (f16[40,768]{1,0:T(8,128)(2,1)S(1)}, f16[40,768]{1,0:T(8,128)(2,1)S(1)}, u32[]{:S(2)}, u32[]{:S(2)}) collective-permute-start(f16[40,768]{1,0:T(8,128)(2,1)S(1)} %fusion.11), channel_id=1, source_target_pairs={{0,2},{1,3},{2,0},{3,1},{4,6},{5,7},{6,4},{7,5},{8,10},{9,11},{10,... | collective-permute-start | bytes 184328 | tf_op jit(solution)/shard_map/ppermute | solution.py:438
  72.1 12.8 %collective-permute-start.11 = (f32[8,320]{1,0:T(8,128)S(1)}, f32[8,320]{1,0:T(8,128)S(1)}, u32[]{:S(2)}, u32[]{:S(2)}) collective-permute-start(f32[8,320]{1,0:T(8,128)S(1)} %add.63.refs_0_), channel_id=1, source_target_pairs={{0,2},{1,3},{2,0},{3,1},{4,6},{5,7},{6,4},{7,5},{8,10},{9,11},{10,... | collective-permute-start | bytes 30728 | tf_op jit(solution)/shard_map/ppermute | solution.py:438
  74.1 10.8 %collective-permute-start.12 = (f32[8,320]{1,0:T(8,128)S(1)}, f32[8,320]{1,0:T(8,128)S(1)}, u32[]{:S(2)}, u32[]{:S(2)}) collective-permute-start(f32[8,320]{1,0:T(8,128)S(1)} %add.63.refs_0_), channel_id=1, source_target_pairs={{0,4},{1,5},{2,6},{3,7},{4,0},{5,1},{6,2},{7,3},{8,12},{9,13},{10,... | collective-permute-start | bytes 30728 | tf_op jit(solution)/shard_map/ppermute | solution.py:438
  74.2 10.7 %collective-permute-start.13 = (f32[8,320]{1,0:T(8,128)S(1)}, f32[8,320]{1,0:T(8,128)S(1)}, u32[]{:S(2)}, u32[]{:S(2)}) collective-permute-start(f32[8,320]{1,0:T(8,128)S(1)} %add.63.refs_0_), channel_id=1, source_target_pairs={{0,6},{1,7},{2,4},{3,5},{4,2},{5,3},{6,0},{7,1},{8,14},{9,15},{10,... | collective-permute-start | bytes 30728 | tf_op jit(solution)/shard_map/ppermute | solution.py:438
  76.6 14.3 %collective-permute-start.24 = (f16[4,40,768]{2,1,0:T(8,128)(2,1)S(1)}, f16[4,40,768]{2,1,0:T(8,128)(2,1)S(1)}, u32[]{:S(2)}, u32[]{:S(2)}) collective-permute-start(f16[4,40,768]{2,1,0:T(8,128)(2,1)S(1)} %pad_maximum_fusion), channel_id=1, source_target_pairs={{0,16},{1,9},{2,18},{3,11},{4,20},{5,13},{6,22},{7,15},{8,24},{9,1... | collective-permute-start | bytes 737288 | tf_op jit(solution)/shard_map/ppermute | solution.py:447
  88.6 6.2 %collective-permute-start.27 = (f16[4,40,768]{2,1,0:T(8,128)(2,1)S(1)}, f16[4,40,768]{2,1,0:T(8,128)(2,1)S(1)}, u32[]{:S(2)}, u32[]{:S(2)}) collective-permute-start(f16[4,40,768]{2,1,0:T(8,128)(2,1)S(1)} %pad_maximum_fusion), channel_id=1, source_target_pairs={{0,8},{1,17},{2,10},{3,19},{4,12},{5,21},{6,14},{7,23},{8,0},{9,25... | collective-permute-start | bytes 737288 | tf_op jit(solution)/shard_map/ppermute | solution.py:447
  90.9 6.5 %collective-permute-start.25 = (f16[4,40,768]{2,1,0:T(8,128)(2,1)S(1)}, f16[4,40,768]{2,1,0:T(8,128)(2,1)S(1)}, u32[]{:S(2)}, u32[]{:S(2)}) collective-permute-start(f16[4,40,768]{2,1,0:T(8,128)(2,1)S(1)} %collective-permute-done.24), channel_id=1, source_target_pairs={{0,8},{1,17},{2,10},{3,19},{4,12},{5,21},{6,14},{7,23},{8,0},{9,25... | collective-permute-start | bytes 737288 | tf_op jit(solution)/shard_map/ppermute | solution.py:447
  92.2 5.2 %collective-permute-start.29 = (f16[4,40,768]{2,1,0:T(8,128)(2,1)S(1)}, f16[4,40,768]{2,1,0:T(8,128)(2,1)S(1)}, u32[]{:S(2)}, u32[]{:S(2)}) collective-permute-start(f16[4,40,768]{2,1,0:T(8,128)(2,1)S(1)} %collective-permute-done.24), channel_id=1, source_target_pairs={{0,1},{1,0},{2,3},{3,2},{4,5},{5,4},{6,7},{7,6},{8,9},{9,8},{10,11... | collective-permute-start | bytes 737288 | tf_op jit(solution)/shard_map/ppermute | solution.py:438
  (14 other events, 144.7 us)

commit v11 on v10

--- a/solution.py
+++ b/solution.py
@@ -623,18 +623,20 @@
         for piece in pieces:
             arrived.append(swap_image(piece, masks))
         pieces = pieces + arrived
-    crossed = []
-    for piece in pieces:
-        crossed.append(swap_space(piece, 1))
+    wide = {}
+    for number, piece in enumerate(pieces):
+        wide[False, number] = piece.astype(f32) * line_back
+        final = number == len(pieces) - 1
+        crossed = swap_space(piece if final else wide[False, number], 1)
+        if final:
+            crossed = crossed.astype(f32) * line_back
+        wide[True, number] = crossed
     half_blocks = blocks // 2
     numbers = list(range(half_blocks))
 
     def place(chosen, before):
         count = len(chosen)
-        cells = []
-        for is_crossed, rest in chosen:
-            piece = crossed[rest] if is_crossed else pieces[rest]
-            cells.append(piece.astype(f32) * line_back)
+        cells = [wide[key] for key in chosen]
         return pl.pallas_call(
             functools.partial(place_body, (zones, height, width), half_blocks, chosen),
             out_shape=jax.ShapeDtypeStruct((9, channels, channels), f32),
@@ -654,9 +656,11 @@
             ),
         )(*cells, *before)
 
-    early = [(side, rest) for side in (False, True) for rest in numbers[:-1]]
+    late = [(False, numbers[-1]), (True, numbers[-1]), (True, 1)][: 2 + (half_blocks > 2)]
+    early = [(side, rest) for side in (False, True) for rest in numbers]
+    early = [key for key in early if key not in late]
     weight_grad = place(early, ())
-    weight_grad = place([(False, numbers[-1]), (True, numbers[-1])], (weight_grad,))
+    weight_grad = place(late, (weight_grad,))
     weight_grad = weight_grad.reshape(3, 3, channels, channels)
 
     half_count = channels // 2

time: 104 us -> 102 us (0.981)
  starting transfers between devices: 34 us -> 36.7 us
  other arithmetic: 12.4 us -> 10.3 us
  waiting for transfers between devices: 23.3 us -> 21.3 us
    ppermute x7, waiting for transfers between devices: 16.6 us -> 12 us  [swap_image(): return lax.ppermute(cells, ('dp', 'space'), pairs)]
    ppermute x22, starting transfers between devices: 22.7 us -> 25.5 us  [swap_space(): return lax.ppermute(cells, 'space', [(i, i ^ mask) for i in range(count)])]
    ppermute x22, waiting for transfers between devices: 6.7 us -> 9.29 us  [swap_space(): return lax.ppermute(cells, 'space', [(i, i ^ mask) for i in range(count)])]
    mul x8 -> x5, other arithmetic: 5.69 us -> 3.44 us  [the longest x4 2.76 us: slab_program(): wide[False, number] = piece.astype(f32) * line_back]
  transfers between devices with their start and end apart: 31 -> 31, of which waited for: 10 -> 13; matrix products, arithmetic and copies ran while one was open for 12% -> 10% of each run, Pallas kernels for 21% -> 21%
where the time goes in v11:
time: 102 us
  starting transfers between devices  36.7 us (36%)
  Pallas kernels  31.5 us (31%)
  waiting for transfers between devices  21.3 us (21%)
  other arithmetic  10.3 us (10%)
  between operations  1.77 us (2%)
    pallas_call x14, Pallas kernels, call(): pl.pallas_call(body, out_shape=tuple(outs) if many else outs, in_specs=li...  28.3 us
    ppermute x22, starting transfers between devices, swap_space(): return lax.ppermute(cells, 'space', [(i, i ^ mask) for i in range(count)])  25.5 us
    ppermute x7, waiting for transfers between devices, swap_image(): return lax.ppermute(cells, ('dp', 'space'), pairs)  12 us
    ppermute x7, starting transfers between devices, swap_image(): return lax.ppermute(cells, ('dp', 'space'), pairs)  9.81 us
    ppermute x22, waiting for transfers between devices, swap_space(): return lax.ppermute(cells, 'space', [(i, i ^ mask) for i in range(count)])  9.29 us
    pallas_call x2, Pallas kernels, place(): pl.pallas_call(functools.partial(place_body, (zones, height, width), half...  3.2 us
    mul x4, other arithmetic, slab_program(): wide[False, number] = piece.astype(f32) * line_back  2.76 us
  transfers between devices with their start and end apart: 31, of which 13 were waited for; matrix products, arithmetic and copies ran while one was open for 10% of the time, Pallas kernels for 21%

profile of v11, /device:TPU:0, one launch (start us, length us, event | category | flops | bytes accessed | tf_op | source)
XLA Modules:
  0.0 101.9 jit_solution(14542250934166036003)
XLA Ops:
  0.7 4.4 %shard_map.112 = f32[8,320]{1,0:T(8,128)} custom-call(bf16[4,320,512]{2,1,0:T(8,128)(2,1)} %bitcast.61, bf16[4,320,512]{2,1,0:T(8,128)(2,1)} %bitcast.58), custom_call_target="tpu_custom_call" | custom-call | flops 39321600 | bytes 2621440 | tf_op jit(solution)/shard_map/pallas_call | solution.py:42
  6.4 4.1 %collective-permute-start.9 = (bf16[320,512]{1,0:T(8,128)(2,1)S(1)}, bf16[320,512]{1,0:T(8,128)(2,1)S(1)}, u32[]{:S(2)}, u32[]{:S(2)}) collective-permute-start(bf16[320,512]{1,0:T(8,128)(2,1)S(1)} %get-tuple-element.52), channel_id=1, source_target_pairs={{0,1},{1,0},{2,3},{3,2},{4,5},{5,4},{6,7},{7,6},{8,9},{9,8},{10,11... | collective-permute-start | bytes 983048 | tf_op jit(solution)/shard_map/ppermute | solution.py:438
  11.3 1.6 %collective-permute-start.1 = (f32[8,320]{1,0:T(8,128)S(1)}, f32[8,320]{1,0:T(8,128)S(1)}, u32[]{:S(2)}, u32[]{:S(2)}) collective-permute-start(f32[8,320]{1,0:T(8,128)S(1)} %shard_map.113.refs_0_), channel_id=1, source_target_pairs={{0,2},{1,3},{2,0},{3,1},{4,6},{5,7},{6,4},{7,5},{8,10},{9,11},{10,... | collective-permute-start | bytes 30728 | tf_op jit(solution)/shard_map/ppermute | solution.py:438
  17.6 2.1 %collective-permute-done.3.refs_3_ = f32[8,320]{1,0:T(8,128)S(1)} collective-permute-done((f32[8,320]{1,0:T(8,128)S(1)}, f32[8,320]{1,0:T(8,128)S(1)}, u32[]{:S(2)}, u32[]{:S(2)}) %collective-permute-start.3) | collective-permute-done | bytes 10272 | tf_op jit(solution)/shard_map/ppermute | solution.py:438
  19.7 2.0 %shard_map.115 = (bf16[320,2048]{1,0:T(8,128)(2,1)S(1)}, f32[320,960]{1,0:T(8,128)S(1)}, f32[8,384]{1,0:T(8,128)S(1)}) custom-call(bf16[4,320,512]{2,1,0:T(8,128)(2,1)S(1)} %bitcast.62, bf16[960,2048]{1,0:T(8,128)(2,1)S(1)} %get-tuple-element.28.taps_ref, f32[8,320]{1,0:T(8,128)S(1)} %shard_map.114.stats_ref, f32[320]{0:T(512)S(1)} %copy-done.3, ...), custom_call_target="tpu_custom_call" | custom-call | flops 1258291200 | bytes 5242880 | tf_op jit(solution)/shard_map/pallas_call | solution.py:42
  21.8 4.0 %shard_map.119 = (f32[4,4,40,768]{3,2,1,0:T(8,128)S(1)}, f32[2,4,40,768]{3,2,1,0:T(8,128)S(1)}, f32[2,4,40,768]{3,2,1,0:T(8,128)S(1)}, bf16[960,1024]{1,0:T(8,128)(2,1)S(1)}) custom-call(bf16[320,2048]{1,0:T(8,128)(2,1)S(1)} %get-tuple-element.30.act_ref, bf16[960,2048]{1,0:T(8,128)(2,1)S(1)} %get-tuple-element.28.taps_ref, ...), custom_call_target="tpu_custom_call" | custom-call | flops 3774873600 | bytes 5242880 | tf_op jit(solution)/shard_map/pallas_call | solution.py:42
  27.8 2.2 %collective-permute-done.6.other_ref = f32[8,384]{1,0:T(8,128)S(1)} collective-permute-done((f32[8,384]{1,0:T(8,128)S(1)}, f32[8,384]{1,0:T(8,128)S(1)}, u32[]{:S(2)}, u32[]{:S(2)}) %collective-permute-start.6) | collective-permute-done | bytes 12320 | tf_op jit(solution)/shard_map/ppermute | solution.py:447
  31.5 1.5 %collective-permute-start.16 = (f16[2,4,40,768]{3,2,1,0:T(8,128)(2,1)S(1)}, f16[2,4,40,768]{3,2,1,0:T(8,128)(2,1)S(1)}, u32[]{:S(2)}, u32[]{:S(2)}) collective-permute-start(f16[2,4,40,768]{3,2,1,0:T(8,128)(2,1)S(1)} %multiply_convert_fusion), channel_id=1, source_target_pairs={{0,8},{1,17},{2,10},{3,19},{4,12},{5,21},{6,14},{7,23},{8,0},{9,25... | collective-permute-start | bytes 1474568 | tf_op jit(solution)/shard_map/ppermute | solution.py:447
  36.7 2.2 %collective-permute-done.7.other_ref = f32[8,384]{1,0:T(8,128)S(1)} collective-permute-done((f32[8,384]{1,0:T(8,128)S(1)}, f32[8,384]{1,0:T(8,128)S(1)}, u32[]{:S(2)}, u32[]{:S(2)}) %collective-permute-start.7) | collective-permute-done | bytes 12320 | tf_op jit(solution)/shard_map/ppermute | solution.py:447
  40.6 1.5 %fusion.1 = f16[1,4,40,768]{3,2,1,0:T(8,128)(2,1)S(1)} fusion(f32[2,4,40,768]{3,2,1,0:T(8,128)S(1)} %slice_add_fusion, f16[2,4,40,768]{3,2,1,0:T(8,128)(2,1)S(1)} %collective-permute-done.16, f32[]{:T(128)} %bitcast.21, f32[]{:T(128)} %bitcast.20), kind=kLoop, calls=%fused_computation.5 | loop fusion | flops 614400 | bytes 983048 | tf_op jit(solution)/shard_map/convert_element_type | solution.py:604
  42.1 1.6 %collective-permute-start.17 = (f16[1,4,40,768]{3,2,1,0:T(8,128)(2,1)S(1)}, f16[1,4,40,768]{3,2,1,0:T(8,128)(2,1)S(1)}, u32[]{:S(2)}, u32[]{:S(2)}) collective-permute-start(f16[1,4,40,768]{3,2,1,0:T(8,128)(2,1)S(1)} %fusion.1), channel_id=1, source_target_pairs={{0,16},{1,9},{2,18},{3,11},{4,20},{5,13},{6,22},{7,15},{8,24},{9,1... | collective-permute-start | bytes 737288 | tf_op jit(solution)/shard_map/ppermute | solution.py:447
  44.4 4.0 %collective-permute-done.17 = f16[1,4,40,768]{3,2,1,0:T(8,128)(2,1)S(1)} collective-permute-done((f16[1,4,40,768]{3,2,1,0:T(8,128)(2,1)S(1)}, f16[1,4,40,768]{3,2,1,0:T(8,128)(2,1)S(1)}, u32[]{:S(2)}, u32[]{:S(2)}) %collective-permute-start.17) | collective-permute-done | bytes 245792 | tf_op jit(solution)/shard_map/ppermute | solution.py:447
  49.8 1.6 %collective-permute-start.20 = (f16[40,768]{1,0:T(8,128)(2,1)S(1)}, f16[40,768]{1,0:T(8,128)(2,1)S(1)}, u32[]{:S(2)}, u32[]{:S(2)}) collective-permute-start(f16[40,768]{1,0:T(8,128)(2,1)S(1)} %get-tuple-element.57), channel_id=1, source_target_pairs={{0,6},{1,7},{2,4},{3,5},{4,2},{5,3},{6,0},{7,1},{8,14},{9,15},{10,... | collective-permute-start | bytes 184328 | tf_op jit(solution)/shard_map/ppermute | solution.py:438
  51.3 2.9 %collective-permute-start.18 = (f16[40,768]{1,0:T(8,128)(2,1)S(1)}, f16[40,768]{1,0:T(8,128)(2,1)S(1)}, u32[]{:S(2)}, u32[]{:S(2)}) collective-permute-start(f16[40,768]{1,0:T(8,128)(2,1)S(1)} %get-tuple-element.56), channel_id=1, source_target_pairs={{0,2},{1,3},{2,0},{3,1},{4,6},{5,7},{6,4},{7,5},{8,10},{9,11},{10,... | collective-permute-start | bytes 184328 | tf_op jit(solution)/shard_map/ppermute | solution.py:438
  54.3 1.6 %collective-permute-done.20 = f16[40,768]{1,0:T(8,128)(2,1)S(1)} collective-permute-done((f16[40,768]{1,0:T(8,128)(2,1)S(1)}, f16[40,768]{1,0:T(8,128)(2,1)S(1)}, u32[]{:S(2)}, u32[]{:S(2)}) %collective-permute-start.20) | collective-permute-done | bytes 61472 | tf_op jit(solution)/shard_map/ppermute | solution.py:438
  58.5 1.7 %collective-permute-start.23 = (f16[40,768]{1,0:T(8,128)(2,1)S(1)}, f16[40,768]{1,0:T(8,128)(2,1)S(1)}, u32[]{:S(2)}, u32[]{:S(2)}) collective-permute-start(f16[40,768]{1,0:T(8,128)(2,1)S(1)} %fusion.11), channel_id=1, source_target_pairs={{0,6},{1,7},{2,4},{3,5},{4,2},{5,3},{6,0},{7,1},{8,14},{9,15},{10,... | collective-permute-start | bytes 184328 | tf_op jit(solution)/shard_map/ppermute | solution.py:438
  61.3 1.7 %collective-permute-start.21 = (f16[40,768]{1,0:T(8,128)(2,1)S(1)}, f16[40,768]{1,0:T(8,128)(2,1)S(1)}, u32[]{:S(2)}, u32[]{:S(2)}) collective-permute-start(f16[40,768]{1,0:T(8,128)(2,1)S(1)} %fusion.11), channel_id=1, source_target_pairs={{0,2},{1,3},{2,0},{3,1},{4,6},{5,7},{6,4},{7,5},{8,10},{9,11},{10,... | collective-permute-start | bytes 184328 | tf_op jit(solution)/shard_map/ppermute | solution.py:438
  66.3 1.6 %collective-permute-start.24 = (f16[4,40,768]{2,1,0:T(8,128)(2,1)S(1)}, f16[4,40,768]{2,1,0:T(8,128)(2,1)S(1)}, u32[]{:S(2)}, u32[]{:S(2)}) collective-permute-start(f16[4,40,768]{2,1,0:T(8,128)(2,1)S(1)} %pad_maximum_fusion), channel_id=1, source_target_pairs={{0,16},{1,9},{2,18},{3,11},{4,20},{5,13},{6,22},{7,15},{8,24},{9,1... | collective-permute-start | bytes 737288 | tf_op jit(solution)/shard_map/ppermute | solution.py:447
  67.9 5.4 %shard_map.120 = (f32[4,320,512]{2,1,0:T(8,128)S(1)}, f32[8,320]{1,0:T(8,128)S(1)}) custom-call(bf16[4,320,512]{2,1,0:T(8,128)(2,1)S(1)} %bitcast.63, bf16[960,2048]{1,0:T(8,128)(2,1)S(1)} %get-tuple-element.28.taps_ref, bf16[960,1024]{1,0:T(8,128)(2,1)S(1)} %get-tuple-element.35.edge_ref, f32[8,320]{1,0:T(8,128)S(1)} %shard_map.114.stats_ref, ...), custom_call_target="tpu_custom_call" | custom-call | flops 3774873600 | bytes 5242880 | tf_op jit(solution)/shard_map/pallas_call | solution.py:42
  79.1 2.7 %collective-permute-done.28 = f16[4,40,768]{2,1,0:T(8,128)(2,1)S(1)} collective-permute-done((f16[4,40,768]{2,1,0:T(8,128)(2,1)S(1)}, f16[4,40,768]{2,1,0:T(8,128)(2,1)S(1)}, u32[]{:S(2)}, u32[]{:S(2)}) %collective-permute-start.28) | collective-permute-done | bytes 245792 | tf_op jit(solution)/shard_map/ppermute | solution.py:447
  83.9 2.0 %collective-permute-start.13 = (f32[8,320]{1,0:T(8,128)S(1)}, f32[8,320]{1,0:T(8,128)S(1)}, u32[]{:S(2)}, u32[]{:S(2)}) collective-permute-start(f32[8,320]{1,0:T(8,128)S(1)} %add.63.refs_0_), channel_id=1, source_target_pairs={{0,6},{1,7},{2,4},{3,5},{4,2},{5,3},{6,0},{7,1},{8,14},{9,15},{10,... | collective-permute-start | bytes 30728 | tf_op jit(solution)/shard_map/ppermute | solution.py:438
  86.9 6.7 %shard_map.118 = bf16[4,320,512]{2,1,0:T(8,128)(2,1)} custom-call(bf16[320,2048]{1,0:T(8,128)(2,1)S(1)} %get-tuple-element.30.act_ref, bf16[4,320,512]{2,1,0:T(8,128)(2,1)S(1)} %bitcast.64, bf16[320,512]{1,0:T(8,128)(2,1)S(1)} %collective-permute-done.4.outer_ref, bf16[320,512]{1,0:T(8,128)(2,1)S(1)} %collective-permute-done.5.inner_ref, ...), custom_call_target="tpu_custom_call" | custom-call | flops 3774873600 | bytes 5242880 | tf_op jit(solution)/shard_map/pallas_call | solution.py:42
  94.9 2.2 %shard_map.123 = bf16[4,320,512]{2,1,0:T(8,128)(2,1)} custom-call(f32[4,320,512]{2,1,0:T(8,128)S(1)} %get-tuple-element.36.grad_ref, bf16[4,320,512]{2,1,0:T(8,128)(2,1)S(1)} %bitcast.65, bf16[4,320,512]{2,1,0:T(8,128)(2,1)S(1)} %bitcast.60, f32[8,320]{1,0:T(8,128)S(1)} %shard_map.114.stats_ref, f32[8,320]{1,0:T(8,128)S(1)} %shard_map.122.sums_ref.total_ref), custom_call_target="tpu_custom_call" | custom-call | flops 13107200 | bytes 6553600 | tf_op jit(solution)/shard_map/pallas_call | solution.py:42
  98.5 1.8 %shard_map.124.refs_3_ = f32[9,320,320]{2,1,0:T(8,128)} custom-call(f32[4,40,768]{2,1,0:T(8,128)S(1)} %convert_multiply_fusion.1.refs_0_, f32[4,40,768]{2,1,0:T(8,128)S(1)} %convert_multiply_fusion.2.refs_1_, f32[4,40,768]{2,1,0:T(8,128)S(1)} %convert_multiply_fusion.refs_2_, f32[4,40,768]{2,1,0:T(8,128)S(1)} %collective-permute-done.29.refs_3_, ...), custom_call_target="tpu_custom_call" | custom-call | bytes 4915200 | tf_op jit(solution)/shard_map/pallas_call | solution.py:640
  (90 shorter events, 36.9 us)
Async XLA Ops:
  5.1 6.2 %collective-permute-start = (f32[8,320]{1,0:T(8,128)}, f32[8,320]{1,0:T(8,128)S(1)}, u32[]{:S(2)}, u32[]{:S(2)}) collective-permute-start(f32[8,320]{1,0:T(8,128)} %shard_map.112), channel_id=1, source_target_pairs={{0,1},{1,0},{2,3},{3,2},{4,5},{5,4},{6,7},{7,6},{8,9},{9,8},{10,11... | collective-permute-start | bytes 30728 | tf_op jit(solution)/shard_map/ppermute | solution.py:438
  5.7 16.1 %collective-permute-start.8 = (bf16[320,512]{1,0:T(8,128)(2,1)S(1)}, bf16[320,512]{1,0:T(8,128)(2,1)S(1)}, u32[]{:S(2)}, u32[]{:S(2)}) collective-permute-start(bf16[320,512]{1,0:T(8,128)(2,1)S(1)} %get-tuple-element.53), channel_id=1, source_target_pairs={{1,2},{2,1},{3,4},{4,3},{5,6},{6,5},{9,10},{10,9},{11,12},{12,11},... | collective-permute-start | bytes 983048 | tf_op jit(solution)/shard_map/ppermute | solution.py:509
  6.4 15.4 %collective-permute-start.9 = (bf16[320,512]{1,0:T(8,128)(2,1)S(1)}, bf16[320,512]{1,0:T(8,128)(2,1)S(1)}, u32[]{:S(2)}, u32[]{:S(2)}) collective-permute-start(bf16[320,512]{1,0:T(8,128)(2,1)S(1)} %get-tuple-element.52), channel_id=1, source_target_pairs={{0,1},{1,0},{2,3},{3,2},{4,5},{5,4},{6,7},{7,6},{8,9},{9,8},{10,11... | collective-permute-start | bytes 983048 | tf_op jit(solution)/shard_map/ppermute | solution.py:438
  11.3 6.1 %collective-permute-start.1 = (f32[8,320]{1,0:T(8,128)S(1)}, f32[8,320]{1,0:T(8,128)S(1)}, u32[]{:S(2)}, u32[]{:S(2)}) collective-permute-start(f32[8,320]{1,0:T(8,128)S(1)} %shard_map.113.refs_0_), channel_id=1, source_target_pairs={{0,2},{1,3},{2,0},{3,1},{4,6},{5,7},{6,4},{7,5},{8,10},{9,11},{10,... | collective-permute-start | bytes 30728 | tf_op jit(solution)/shard_map/ppermute | solution.py:438
  14.2 5.5 %collective-permute-start.3 = (f32[8,320]{1,0:T(8,128)S(1)}, f32[8,320]{1,0:T(8,128)S(1)}, u32[]{:S(2)}, u32[]{:S(2)}) collective-permute-start(f32[8,320]{1,0:T(8,128)S(1)} %shard_map.113.refs_0_), channel_id=1, source_target_pairs={{0,6},{1,7},{2,4},{3,5},{4,2},{5,3},{6,0},{7,1},{8,14},{9,15},{10,... | collective-permute-start | bytes 30728 | tf_op jit(solution)/shard_map/ppermute | solution.py:438
  25.9 13.6 %collective-permute-start.14 = (f32[2,4,40,768]{3,2,1,0:T(8,128)S(1)}, f32[2,4,40,768]{3,2,1,0:T(8,128)S(1)}, u32[]{:S(2)}, u32[]{:S(2)}) collective-permute-start(f32[2,4,40,768]{3,2,1,0:T(8,128)S(1)} %get-tuple-element.40), channel_id=1, source_target_pairs={{0,1},{1,0},{2,3},{3,2},{4,5},{5,4},{6,7},{7,6},{8,9},{9,8},{10,11... | collective-permute-start | bytes 2949128 | tf_op jit(solution)/shard_map/ppermute | solution.py:438
  31.5 9.0 %collective-permute-start.16 = (f16[2,4,40,768]{3,2,1,0:T(8,128)(2,1)S(1)}, f16[2,4,40,768]{3,2,1,0:T(8,128)(2,1)S(1)}, u32[]{:S(2)}, u32[]{:S(2)}) collective-permute-start(f16[2,4,40,768]{3,2,1,0:T(8,128)(2,1)S(1)} %multiply_convert_fusion), channel_id=1, source_target_pairs={{0,8},{1,17},{2,10},{3,19},{4,12},{5,21},{6,14},{7,23},{8,0},{9,25... | collective-permute-start | bytes 1474568 | tf_op jit(solution)/shard_map/ppermute | solution.py:447
  33.1 50.7 %collective-permute-start.4 = (bf16[320,512]{1,0:T(8,128)(2,1)S(1)}, bf16[320,512]{1,0:T(8,128)(2,1)S(1)}, u32[]{:S(2)}, u32[]{:S(2)}) collective-permute-start(bf16[320,512]{1,0:T(8,128)(2,1)S(1)} %get-tuple-element.55), channel_id=1, source_target_pairs={{1,2},{2,1},{3,4},{4,3},{5,6},{6,5},{9,10},{10,9},{11,12},{12,11},... | collective-permute-start | bytes 983048 | tf_op jit(solution)/shard_map/ppermute | solution.py:509
  33.8 52.1 %collective-permute-start.5 = (bf16[320,512]{1,0:T(8,128)(2,1)S(1)}, bf16[320,512]{1,0:T(8,128)(2,1)S(1)}, u32[]{:S(2)}, u32[]{:S(2)}) collective-permute-start(bf16[320,512]{1,0:T(8,128)(2,1)S(1)} %get-tuple-element.54), channel_id=1, source_target_pairs={{0,1},{1,0},{2,3},{3,2},{4,5},{5,4},{6,7},{7,6},{8,9},{9,8},{10,11... | collective-permute-start | bytes 983048 | tf_op jit(solution)/shard_map/ppermute | solution.py:438
  42.1 6.3 %collective-permute-start.17 = (f16[1,4,40,768]{3,2,1,0:T(8,128)(2,1)S(1)}, f16[1,4,40,768]{3,2,1,0:T(8,128)(2,1)S(1)}, u32[]{:S(2)}, u32[]{:S(2)}) collective-permute-start(f16[1,4,40,768]{3,2,1,0:T(8,128)(2,1)S(1)} %fusion.1), channel_id=1, source_target_pairs={{0,16},{1,9},{2,18},{3,11},{4,20},{5,13},{6,22},{7,15},{8,24},{9,1... | collective-permute-start | bytes 737288 | tf_op jit(solution)/shard_map/ppermute | solution.py:447
  49.8 6.1 %collective-permute-start.20 = (f16[40,768]{1,0:T(8,128)(2,1)S(1)}, f16[40,768]{1,0:T(8,128)(2,1)S(1)}, u32[]{:S(2)}, u32[]{:S(2)}) collective-permute-start(f16[40,768]{1,0:T(8,128)(2,1)S(1)} %get-tuple-element.57), channel_id=1, source_target_pairs={{0,6},{1,7},{2,4},{3,5},{4,2},{5,3},{6,0},{7,1},{8,14},{9,15},{10,... | collective-permute-start | bytes 184328 | tf_op jit(solution)/shard_map/ppermute | solution.py:438
  51.3 5.8 %collective-permute-start.19 = (f16[40,768]{1,0:T(8,128)(2,1)S(1)}, f16[40,768]{1,0:T(8,128)(2,1)S(1)}, u32[]{:S(2)}, u32[]{:S(2)}) collective-permute-start(f16[40,768]{1,0:T(8,128)(2,1)S(1)} %get-tuple-element.58), channel_id=1, source_target_pairs={{0,4},{1,5},{2,6},{3,7},{4,0},{5,1},{6,2},{7,3},{8,12},{9,13},{10,... | collective-permute-start | bytes 184328 | tf_op jit(solution)/shard_map/ppermute | solution.py:438
  51.3 5.8 %collective-permute-start.18 = (f16[40,768]{1,0:T(8,128)(2,1)S(1)}, f16[40,768]{1,0:T(8,128)(2,1)S(1)}, u32[]{:S(2)}, u32[]{:S(2)}) collective-permute-start(f16[40,768]{1,0:T(8,128)(2,1)S(1)} %get-tuple-element.56), channel_id=1, source_target_pairs={{0,2},{1,3},{2,0},{3,1},{4,6},{5,7},{6,4},{7,5},{8,10},{9,11},{10,... | collective-permute-start | bytes 184328 | tf_op jit(solution)/shard_map/ppermute | solution.py:438
  58.5 6.1 %collective-permute-start.23 = (f16[40,768]{1,0:T(8,128)(2,1)S(1)}, f16[40,768]{1,0:T(8,128)(2,1)S(1)}, u32[]{:S(2)}, u32[]{:S(2)}) collective-permute-start(f16[40,768]{1,0:T(8,128)(2,1)S(1)} %fusion.11), channel_id=1, source_target_pairs={{0,6},{1,7},{2,4},{3,5},{4,2},{5,3},{6,0},{7,1},{8,14},{9,15},{10,... | collective-permute-start | bytes 184328 | tf_op jit(solution)/shard_map/ppermute | solution.py:438
  60.2 5.8 %collective-permute-start.22 = (f16[40,768]{1,0:T(8,128)(2,1)S(1)}, f16[40,768]{1,0:T(8,128)(2,1)S(1)}, u32[]{:S(2)}, u32[]{:S(2)}) collective-permute-start(f16[40,768]{1,0:T(8,128)(2,1)S(1)} %fusion.11), channel_id=1, source_target_pairs={{0,4},{1,5},{2,6},{3,7},{4,0},{5,1},{6,2},{7,3},{8,12},{9,13},{10,... | collective-permute-start | bytes 184328 | tf_op jit(solution)/shard_map/ppermute | solution.py:438
  66.3 11.5 %collective-permute-start.24 = (f16[4,40,768]{2,1,0:T(8,128)(2,1)S(1)}, f16[4,40,768]{2,1,0:T(8,128)(2,1)S(1)}, u32[]{:S(2)}, u32[]{:S(2)}) collective-permute-start(f16[4,40,768]{2,1,0:T(8,128)(2,1)S(1)} %pad_maximum_fusion), channel_id=1, source_target_pairs={{0,16},{1,9},{2,18},{3,11},{4,20},{5,13},{6,22},{7,15},{8,24},{9,1... | collective-permute-start | bytes 737288 | tf_op jit(solution)/shard_map/ppermute | solution.py:447
  74.6 11.4 %collective-permute-start.11 = (f32[8,320]{1,0:T(8,128)S(1)}, f32[8,320]{1,0:T(8,128)S(1)}, u32[]{:S(2)}, u32[]{:S(2)}) collective-permute-start(f32[8,320]{1,0:T(8,128)S(1)} %add.63.refs_0_), channel_id=1, source_target_pairs={{0,2},{1,3},{2,0},{3,1},{4,6},{5,7},{6,4},{7,5},{8,10},{9,11},{10,... | collective-permute-start | bytes 30728 | tf_op jit(solution)/shard_map/ppermute | solution.py:438
  75.6 6.2 %collective-permute-start.28 = (f16[4,40,768]{2,1,0:T(8,128)(2,1)S(1)}, f16[4,40,768]{2,1,0:T(8,128)(2,1)S(1)}, u32[]{:S(2)}, u32[]{:S(2)}) collective-permute-start(f16[4,40,768]{2,1,0:T(8,128)(2,1)S(1)} %pad_maximum_fusion), channel_id=1, source_target_pairs={{0,8},{1,17},{2,10},{3,19},{4,12},{5,21},{6,14},{7,23},{8,0},{9,25... | collective-permute-start | bytes 737288 | tf_op jit(solution)/shard_map/ppermute | solution.py:447
  77.8 8.7 %collective-permute-start.25 = (f16[4,40,768]{2,1,0:T(8,128)(2,1)S(1)}, f16[4,40,768]{2,1,0:T(8,128)(2,1)S(1)}, u32[]{:S(2)}, u32[]{:S(2)}) collective-permute-start(f16[4,40,768]{2,1,0:T(8,128)(2,1)S(1)} %collective-permute-done.24), channel_id=1, source_target_pairs={{0,8},{1,17},{2,10},{3,19},{4,12},{5,21},{6,14},{7,23},{8,0},{9,25... | collective-permute-start | bytes 737288 | tf_op jit(solution)/shard_map/ppermute | solution.py:447
  83.9 9.8 %collective-permute-start.13 = (f32[8,320]{1,0:T(8,128)S(1)}, f32[8,320]{1,0:T(8,128)S(1)}, u32[]{:S(2)}, u32[]{:S(2)}) collective-permute-start(f32[8,320]{1,0:T(8,128)S(1)} %add.63.refs_0_), channel_id=1, source_target_pairs={{0,6},{1,7},{2,4},{3,5},{4,2},{5,3},{6,0},{7,1},{8,14},{9,15},{10,... | collective-permute-start | bytes 30728 | tf_op jit(solution)/shard_map/ppermute | solution.py:438
  85.9 12.6 %collective-permute-start.29 = (f32[4,40,768]{2,1,0:T(8,128)S(1)}, f32[4,40,768]{2,1,0:T(8,128)S(1)}, u32[]{:S(2)}, u32[]{:S(2)}) collective-permute-start(f32[4,40,768]{2,1,0:T(8,128)S(1)} %convert_multiply_fusion.1.refs_0_), channel_id=1, source_target_pairs={{0,1},{1,0},{2,3},{3,2},{4,5},{5,4},{6,7},{7,6},{8,9},{9,8},{10,11... | collective-permute-start | bytes 1474568 | tf_op jit(solution)/shard_map/ppermute | solution.py:438
  85.9 14.4 %collective-permute-start.27 = (f32[4,40,768]{2,1,0:T(8,128)S(1)}, f32[4,40,768]{2,1,0:T(8,128)S(1)}, u32[]{:S(2)}, u32[]{:S(2)}) collective-permute-start(f32[4,40,768]{2,1,0:T(8,128)S(1)} %convert_multiply_fusion.2.refs_1_), channel_id=1, source_target_pairs={{0,1},{1,0},{2,3},{3,2},{4,5},{5,4},{6,7},{7,6},{8,9},{9,8},{10,11... | collective-permute-start | bytes 1474568 | tf_op jit(solution)/shard_map/ppermute | solution.py:438
  86.4 12.1 %collective-permute-start.30 = (f32[4,40,768]{2,1,0:T(8,128)S(1)}, f32[4,40,768]{2,1,0:T(8,128)S(1)}, u32[]{:S(2)}, u32[]{:S(2)}) collective-permute-start(f32[4,40,768]{2,1,0:T(8,128)S(1)} %convert_multiply_fusion.refs_2_), channel_id=1, source_target_pairs={{0,1},{1,0},{2,3},{3,2},{4,5},{5,4},{6,7},{7,6},{8,9},{9,8},{10,11... | collective-permute-start | bytes 1474568 | tf_op jit(solution)/shard_map/ppermute | solution.py:438
  86.5 11.3 %collective-permute-start.26 = (f16[4,40,768]{2,1,0:T(8,128)(2,1)S(1)}, f16[4,40,768]{2,1,0:T(8,128)(2,1)S(1)}, u32[]{:S(2)}, u32[]{:S(2)}) collective-permute-start(f16[4,40,768]{2,1,0:T(8,128)(2,1)S(1)} %collective-permute-done.25), channel_id=1, source_target_pairs={{0,1},{1,0},{2,3},{3,2},{4,5},{5,4},{6,7},{7,6},{8,9},{9,8},{10,11... | collective-permute-start | bytes 737288 | tf_op jit(solution)/shard_map/ppermute | solution.py:438
  (14 other events, 172.0 us)
